TPU v7x, 256 devices: a whole 4x4x8 slice. The times are simulated.
256 devices in a mesh: depth: 16 (over z, core), rows: 4 (over x), cols: 4 (over y).
Axes of the slice: x: 4, y: 4, z: 8, core: 2. Of those that a mesh axis runs over, the one named last changes fastest.
Arguments:
- section_states: float32 [16, 128, 64, 256], P('depth', 'rows', 'cols'), may hold values from -6 to 6
- weights: bfloat16 [32, 3, 3, 256, 256], P('depth'), may hold values from -0.125 to 0.125
Outputs:
- fine_states: float32 [32, 128, 64, 256], P('depth', 'rows', 'cols')
- coarse_states: float32 [16, 128, 64, 256], P('depth', 'rows', 'cols')
All inputs are finite; a program needn't handle non-finite values.
Results may differ from a plain program's by a relative error of at most 0.002.
Values may be sent and summed in bfloat16 or wider, within the bound.
No kernel may reach another device: no remote copies, remote signals or barrier semaphores. Data moves between devices by JAX's collectives and lax.ppermute only.
A program may use at most 64 MiB of HBM per device.

v0:
```python
import jax
import jax.numpy as jnp
from jax import lax
from jax.sharding import PartitionSpec as P


def padded_2(shard, sides, width):
    for axis, dim in sides:
        size, length = (lax.axis_size(axis), shard.shape[dim])
        up = [(i, (i + 1) % size) for i in range(size - 1)]
        down = [(j, i) for i, j in up]
        last = lax.slice_in_dim(shard, length - width, length, axis=dim)
        initial = lax.slice_in_dim(shard, 0, width, axis=dim)
        before = lax.ppermute(last, axis, up)
        after = lax.ppermute(initial, axis, down)
        shard = jnp.concatenate([before, shard, after], axis=dim)
    return shard


def shifted_2(block, axis, distance):
    devices = range(lax.axis_size(axis))
    route = [(i - distance, i) for i in devices if i - distance in devices]
    return lax.ppermute(block, axis, route)


def activate(field):
    return jax.nn.silu(field).astype(jnp.bfloat16)


def apply_stencil(padded, flat_weight, out_rows, out_cols):
    channels = padded.shape[2]
    patches = jnp.concatenate(
        [
            padded[shift_row : shift_row + out_rows, shift_col : shift_col + out_cols]
            for shift_row in range(3)
            for shift_col in range(3)
        ],
        axis=2,
    )
    summed = jnp.dot(
        patches.reshape(out_rows * out_cols, 9 * channels),
        flat_weight,
        preferred_element_type=jnp.float32,
    )
    return summed.reshape(out_rows, out_cols, channels)


def section_pass(anchor, first_weight, second_weight, step_size):
    rows_here, cols_here, channels = anchor.shape
    first_act = padded_2(activate(anchor), (("rows", 0), ("cols", 1)), 1)
    first_slope = apply_stencil(first_act, first_weight, rows_here, cols_here)
    middle = anchor + step_size * first_slope
    second_act = padded_2(activate(middle), (("rows", 0), ("cols", 1)), 1)
    second_slope = apply_stencil(second_act, second_weight, rows_here, cols_here)
    ending = middle + step_size * second_slope
    return (first_slope, middle, ending)


def on_device(section_states, weights):
    rows_here, cols_here, channels = (
        section_states.shape[1],
        section_states.shape[2],
        section_states.shape[3],
    )
    ndepth = lax.axis_size("depth")
    position = lax.axis_index("depth")
    step_size = 2.0 / (2 * ndepth)
    first_weight = weights[0].reshape(9 * channels, channels)
    second_weight = weights[1].reshape(9 * channels, channels)
    anchor = section_states[0]
    first_slope, middle, ending = section_pass(anchor, first_weight, second_weight, step_size)
    jump = ending - (anchor + 2.0 * step_size * first_slope)

    def chain_turn(step_index, current):
        padded = padded_2(activate(current), (("rows", 0), ("cols", 1)), 1)
        advanced = (
            current
            + 2.0 * step_size * apply_stencil(padded, first_weight, rows_here, cols_here)
            + jump
        )
        shifted = shifted_2(advanced, "depth", 1)
        return jnp.where(position == 0, anchor, shifted)

    corrected = lax.fori_loop(0, ndepth - 1, chain_turn, anchor)
    final_slope, final_middle, final_ending = section_pass(
        corrected, first_weight, second_weight, step_size
    )
    fine_states = jnp.stack([final_middle, final_ending])
    return (fine_states, corrected[None])


def solution(mesh):
    in_specs = (P("depth", "rows", "cols", None), P("depth", None, None, None, None))
    out_specs = (P("depth", "rows", "cols", None), P("depth", "rows", "cols", None))
    return jax.shard_map(
        on_device, mesh=mesh, in_specs=in_specs, out_specs=out_specs, check_vma=False
    )
```

profile of v0, /device:TPU:154, one launch (start us, length us, event | category | flops | bytes accessed | tf_op | source)
XLA Modules:
  0.0 543.1 jit_solution(3713697297819363275)
XLA Ops:
  34.8 4.2 collective-permute-done.11
  41.3 462.1 %while.12 = (s32[]{:T(128)}, f32[32,16,256]{2,1,0:T(8,128)S(1)}, pred[]{:T(512)}, bf16[2304,256]{1,0:T(8,128)(2,1)S(1)}, f32[32,16,256]{2,1,0:T(8,128)S(1)}, /*index=5*/f32[32,16,256]{2,1,0:T(8,128)S(1)}, s32[]{:T(128)}) while((s32[]{:T(128)}, f32[32,16,256]{2,1,0:T(8,128)S(1)}, pred[]{:T(512)}, bf16[2304,256]{1,0:T(8,128)(2,1)S(1)}, ...), condition=%wide.region_1.2_spmd, body=%wide.region_0.1_spmd.sunk | while | flops 609335296 | bytes 18118960 | solution.py:84
  53.8 4.2 collective-permute-done.3
  61.6 9.8 %collective-permute-done.4 = f32[32,16,256]{2,1,0:T(8,128)S(1)} collective-permute-done((f32[32,16,256]{2,1,0:T(8,128)S(1)}, f32[32,16,256]{2,1,0:T(8,128)S(1)}, u32[]{:S(2)}, u32[]{:S(2)}) %collective-permute-start.4) | collective-permute-done | bytes 524320 | tf_op jit(solution)/shard_map/while/body/eval_jaxpr/ppermute | solution.py:23
  75.4 3.9 collective-permute-start.1
  84.9 4.2 collective-permute-done.3
  92.7 9.8 %collective-permute-done.4 = f32[32,16,256]{2,1,0:T(8,128)S(1)} collective-permute-done((f32[32,16,256]{2,1,0:T(8,128)S(1)}, f32[32,16,256]{2,1,0:T(8,128)S(1)}, u32[]{:S(2)}, u32[]{:S(2)}) %collective-permute-start.4) | collective-permute-done | bytes 524320 | tf_op jit(solution)/shard_map/while/body/eval_jaxpr/ppermute | solution.py:23
  106.5 3.9 collective-permute-start.1
  115.6 4.2 collective-permute-done.3
  123.4 9.8 %collective-permute-done.4 = f32[32,16,256]{2,1,0:T(8,128)S(1)} collective-permute-done((f32[32,16,256]{2,1,0:T(8,128)S(1)}, f32[32,16,256]{2,1,0:T(8,128)S(1)}, u32[]{:S(2)}, u32[]{:S(2)}) %collective-permute-start.4) | collective-permute-done | bytes 524320 | tf_op jit(solution)/shard_map/while/body/eval_jaxpr/ppermute | solution.py:23
  137.2 3.9 collective-permute-start.1
  146.3 4.2 collective-permute-done.3
  154.1 9.8 %collective-permute-done.4 = f32[32,16,256]{2,1,0:T(8,128)S(1)} collective-permute-done((f32[32,16,256]{2,1,0:T(8,128)S(1)}, f32[32,16,256]{2,1,0:T(8,128)S(1)}, u32[]{:S(2)}, u32[]{:S(2)}) %collective-permute-start.4) | collective-permute-done | bytes 524320 | tf_op jit(solution)/shard_map/while/body/eval_jaxpr/ppermute | solution.py:23
  167.9 3.9 collective-permute-start.1
  177.0 4.2 collective-permute-done.3
  184.8 9.8 %collective-permute-done.4 = f32[32,16,256]{2,1,0:T(8,128)S(1)} collective-permute-done((f32[32,16,256]{2,1,0:T(8,128)S(1)}, f32[32,16,256]{2,1,0:T(8,128)S(1)}, u32[]{:S(2)}, u32[]{:S(2)}) %collective-permute-start.4) | collective-permute-done | bytes 524320 | tf_op jit(solution)/shard_map/while/body/eval_jaxpr/ppermute | solution.py:23
  198.6 3.9 collective-permute-start.1
  207.7 4.2 collective-permute-done.3
  215.5 9.8 %collective-permute-done.4 = f32[32,16,256]{2,1,0:T(8,128)S(1)} collective-permute-done((f32[32,16,256]{2,1,0:T(8,128)S(1)}, f32[32,16,256]{2,1,0:T(8,128)S(1)}, u32[]{:S(2)}, u32[]{:S(2)}) %collective-permute-start.4) | collective-permute-done | bytes 524320 | tf_op jit(solution)/shard_map/while/body/eval_jaxpr/ppermute | solution.py:23
  229.3 3.9 collective-permute-start.1
  238.4 4.2 collective-permute-done.3
  246.1 9.8 %collective-permute-done.4 = f32[32,16,256]{2,1,0:T(8,128)S(1)} collective-permute-done((f32[32,16,256]{2,1,0:T(8,128)S(1)}, f32[32,16,256]{2,1,0:T(8,128)S(1)}, u32[]{:S(2)}, u32[]{:S(2)}) %collective-permute-start.4) | collective-permute-done | bytes 524320 | tf_op jit(solution)/shard_map/while/body/eval_jaxpr/ppermute | solution.py:23
  260.0 3.9 collective-permute-start.1
  269.1 4.2 collective-permute-done.3
  276.8 9.8 %collective-permute-done.4 = f32[32,16,256]{2,1,0:T(8,128)S(1)} collective-permute-done((f32[32,16,256]{2,1,0:T(8,128)S(1)}, f32[32,16,256]{2,1,0:T(8,128)S(1)}, u32[]{:S(2)}, u32[]{:S(2)}) %collective-permute-start.4) | collective-permute-done | bytes 524320 | tf_op jit(solution)/shard_map/while/body/eval_jaxpr/ppermute | solution.py:23
  290.6 3.9 collective-permute-start.1
  299.8 4.2 collective-permute-done.3
  307.5 9.8 %collective-permute-done.4 = f32[32,16,256]{2,1,0:T(8,128)S(1)} collective-permute-done((f32[32,16,256]{2,1,0:T(8,128)S(1)}, f32[32,16,256]{2,1,0:T(8,128)S(1)}, u32[]{:S(2)}, u32[]{:S(2)}) %collective-permute-start.4) | collective-permute-done | bytes 524320 | tf_op jit(solution)/shard_map/while/body/eval_jaxpr/ppermute | solution.py:23
  321.3 3.9 collective-permute-start.1
  330.5 4.2 collective-permute-done.3
  338.2 9.8 %collective-permute-done.4 = f32[32,16,256]{2,1,0:T(8,128)S(1)} collective-permute-done((f32[32,16,256]{2,1,0:T(8,128)S(1)}, f32[32,16,256]{2,1,0:T(8,128)S(1)}, u32[]{:S(2)}, u32[]{:S(2)}) %collective-permute-start.4) | collective-permute-done | bytes 524320 | tf_op jit(solution)/shard_map/while/body/eval_jaxpr/ppermute | solution.py:23
  352.0 3.9 collective-permute-start.1
  361.2 4.2 collective-permute-done.3
  368.9 9.8 %collective-permute-done.4 = f32[32,16,256]{2,1,0:T(8,128)S(1)} collective-permute-done((f32[32,16,256]{2,1,0:T(8,128)S(1)}, f32[32,16,256]{2,1,0:T(8,128)S(1)}, u32[]{:S(2)}, u32[]{:S(2)}) %collective-permute-start.4) | collective-permute-done | bytes 524320 | tf_op jit(solution)/shard_map/while/body/eval_jaxpr/ppermute | solution.py:23
  382.7 3.9 collective-permute-start.1
  391.9 4.2 collective-permute-done.3
  399.6 9.8 %collective-permute-done.4 = f32[32,16,256]{2,1,0:T(8,128)S(1)} collective-permute-done((f32[32,16,256]{2,1,0:T(8,128)S(1)}, f32[32,16,256]{2,1,0:T(8,128)S(1)}, u32[]{:S(2)}, u32[]{:S(2)}) %collective-permute-start.4) | collective-permute-done | bytes 524320 | tf_op jit(solution)/shard_map/while/body/eval_jaxpr/ppermute | solution.py:23
  413.4 3.9 collective-permute-start.1
  422.5 4.2 collective-permute-done.3
  430.3 9.8 %collective-permute-done.4 = f32[32,16,256]{2,1,0:T(8,128)S(1)} collective-permute-done((f32[32,16,256]{2,1,0:T(8,128)S(1)}, f32[32,16,256]{2,1,0:T(8,128)S(1)}, u32[]{:S(2)}, u32[]{:S(2)}) %collective-permute-start.4) | collective-permute-done | bytes 524320 | tf_op jit(solution)/shard_map/while/body/eval_jaxpr/ppermute | solution.py:23
  453.2 4.2 collective-permute-done.3
  461.0 9.8 %collective-permute-done.4 = f32[32,16,256]{2,1,0:T(8,128)S(1)} collective-permute-done((f32[32,16,256]{2,1,0:T(8,128)S(1)}, f32[32,16,256]{2,1,0:T(8,128)S(1)}, u32[]{:S(2)}, u32[]{:S(2)}) %collective-permute-start.4) | collective-permute-done | bytes 524320 | tf_op jit(solution)/shard_map/while/body/eval_jaxpr/ppermute | solution.py:23
  474.8 3.9 collective-permute-start.1
  483.9 4.2 collective-permute-done.3
  491.7 9.8 %collective-permute-done.4 = f32[32,16,256]{2,1,0:T(8,128)S(1)} collective-permute-done((f32[32,16,256]{2,1,0:T(8,128)S(1)}, f32[32,16,256]{2,1,0:T(8,128)S(1)}, u32[]{:S(2)}, u32[]{:S(2)}) %collective-permute-start.4) | collective-permute-done | bytes 524320 | tf_op jit(solution)/shard_map/while/body/eval_jaxpr/ppermute | solution.py:23
  503.6 3.9 collective-permute-start.13
  516.6 4.2 collective-permute-done.15
  535.6 4.2 collective-permute-done.19
  (455 shorter events, 261.5 us)
Async XLA Ops:
  1.8 5.9 %collective-permute-start.5 = (bf16[1,16,256]{2,1,0:T(8,128)(2,1)S(1)}, bf16[1,16,256]{2,1,0:T(8,128)(2,1)S(1)}, u32[]{:S(2)}, u32[]{:S(2)}) collective-permute-start(bf16[1,16,256]{2,1,0:T(8,128)(2,1)S(1)} %get-tuple-element.117), channel_id=1, source_target_pairs={{0,4},{4,8},{8,12},{1,5},{5,9},{9,13},{2,6},{6,10},{10,14},{3,7},{... | collective-permute-start | bytes 24584 | tf_op jit(solution)/shard_map/ppermute | solution.py:14
  10.8 6.8 %collective-permute-start.8 = (bf16[34,1,256]{2,1,0:T(2,128)(2,1)S(1)}, bf16[34,1,256]{2,1,0:T(2,128)(2,1)S(1)}, u32[]{:S(2)}, u32[]{:S(2)}) collective-permute-start(bf16[34,1,256]{2,1,0:T(2,128)(2,1)S(1)} %get-tuple-element.109), channel_id=1, source_target_pairs={{1,0},{2,1},{3,2},{5,4},{6,5},{7,6},{9,8},{10,9},{11,10},{13,12},{... | collective-permute-start | bytes 52232 | tf_op jit(solution)/shard_map/ppermute | solution.py:15
  13.5 5.8 %collective-permute-start.7 = (bf16[34,1,256]{2,1,0:T(2,128)(2,1)S(1)}, bf16[34,1,256]{2,1,0:T(2,128)(2,1)S(1)}, u32[]{:S(2)}, u32[]{:S(2)}) collective-permute-start(bf16[34,1,256]{2,1,0:T(2,128)(2,1)S(1)} %get-tuple-element.110), channel_id=1, source_target_pairs={{0,1},{1,2},{2,3},{4,5},{5,6},{6,7},{8,9},{9,10},{10,11},{12,13},{... | collective-permute-start | bytes 52232 | tf_op jit(solution)/shard_map/ppermute | solution.py:14
  21.0 5.9 %collective-permute-start.9 = (bf16[1,16,256]{2,1,0:T(8,128)(2,1)S(1)}, bf16[1,16,256]{2,1,0:T(8,128)(2,1)S(1)}, u32[]{:S(2)}, u32[]{:S(2)}) collective-permute-start(bf16[1,16,256]{2,1,0:T(8,128)(2,1)S(1)} %get-tuple-element.115), channel_id=1, source_target_pairs={{0,4},{4,8},{8,12},{1,5},{5,9},{9,13},{2,6},{6,10},{10,14},{3,7},{... | collective-permute-start | bytes 24584 | tf_op jit(solution)/shard_map/ppermute | solution.py:14
  33.2 5.8 %collective-permute-start.11 = (bf16[34,1,256]{2,1,0:T(2,128)(2,1)S(1)}, bf16[34,1,256]{2,1,0:T(2,128)(2,1)S(1)}, u32[]{:S(2)}, u32[]{:S(2)}) collective-permute-start(bf16[34,1,256]{2,1,0:T(2,128)(2,1)S(1)} %get-tuple-element.106), channel_id=1, source_target_pairs={{0,1},{1,2},{2,3},{4,5},{5,6},{6,7},{8,9},{9,10},{10,11},{12,13},{... | collective-permute-start | bytes 52232 | tf_op jit(solution)/shard_map/ppermute | solution.py:14
  41.5 5.9 %collective-permute-start = (bf16[1,16,256]{2,1,0:T(8,128)(2,1)S(1)}, bf16[1,16,256]{2,1,0:T(8,128)(2,1)S(1)}, u32[]{:S(2)}, u32[]{:S(2)}) collective-permute-start(bf16[1,16,256]{2,1,0:T(8,128)(2,1)S(1)} %get-tuple-element.166), channel_id=1, source_target_pairs={{4,0},{8,4},{12,8},{5,1},{9,5},{13,9},{6,2},{10,6},{14,10},{7,3},{... | collective-permute-start | bytes 24584 | tf_op jit(solution)/shard_map/while/body/eval_jaxpr/ppermute | solution.py:15
  52.2 5.8 %collective-permute-start.3 = (bf16[34,1,256]{2,1,0:T(2,128)(2,1)S(1)}, bf16[34,1,256]{2,1,0:T(2,128)(2,1)S(1)}, u32[]{:S(2)}, u32[]{:S(2)}) collective-permute-start(bf16[34,1,256]{2,1,0:T(2,128)(2,1)S(1)} %get-tuple-element.169), channel_id=1, source_target_pairs={{0,1},{1,2},{2,3},{4,5},{5,6},{6,7},{8,9},{9,10},{10,11},{12,13},{... | collective-permute-start | bytes 52232 | tf_op jit(solution)/shard_map/while/body/eval_jaxpr/ppermute | solution.py:14
  59.6 11.7 %collective-permute-start.4 = (f32[32,16,256]{2,1,0:T(8,128)S(1)}, f32[32,16,256]{2,1,0:T(8,128)S(1)}, u32[]{:S(2)}, u32[]{:S(2)}) collective-permute-start(f32[32,16,256]{2,1,0:T(8,128)S(1)} %fusion.44), channel_id=1, source_target_pairs={{0,16},{16,32},{32,48},{48,64},{64,80},{80,96},{96,112},{112,128},... | collective-permute-start | bytes 1572872 | tf_op jit(solution)/shard_map/while/body/eval_jaxpr/ppermute | solution.py:23
  73.4 5.9 %collective-permute-start = (bf16[1,16,256]{2,1,0:T(8,128)(2,1)S(1)}, bf16[1,16,256]{2,1,0:T(8,128)(2,1)S(1)}, u32[]{:S(2)}, u32[]{:S(2)}) collective-permute-start(bf16[1,16,256]{2,1,0:T(8,128)(2,1)S(1)} %get-tuple-element.166), channel_id=1, source_target_pairs={{4,0},{8,4},{12,8},{5,1},{9,5},{13,9},{6,2},{10,6},{14,10},{7,3},{... | collective-permute-start | bytes 24584 | tf_op jit(solution)/shard_map/while/body/eval_jaxpr/ppermute | solution.py:15
  83.3 5.8 %collective-permute-start.3 = (bf16[34,1,256]{2,1,0:T(2,128)(2,1)S(1)}, bf16[34,1,256]{2,1,0:T(2,128)(2,1)S(1)}, u32[]{:S(2)}, u32[]{:S(2)}) collective-permute-start(bf16[34,1,256]{2,1,0:T(2,128)(2,1)S(1)} %get-tuple-element.169), channel_id=1, source_target_pairs={{0,1},{1,2},{2,3},{4,5},{5,6},{6,7},{8,9},{9,10},{10,11},{12,13},{... | collective-permute-start | bytes 52232 | tf_op jit(solution)/shard_map/while/body/eval_jaxpr/ppermute | solution.py:14
  90.8 11.7 %collective-permute-start.4 = (f32[32,16,256]{2,1,0:T(8,128)S(1)}, f32[32,16,256]{2,1,0:T(8,128)S(1)}, u32[]{:S(2)}, u32[]{:S(2)}) collective-permute-start(f32[32,16,256]{2,1,0:T(8,128)S(1)} %fusion.44), channel_id=1, source_target_pairs={{0,16},{16,32},{32,48},{48,64},{64,80},{80,96},{96,112},{112,128},... | collective-permute-start | bytes 1572872 | tf_op jit(solution)/shard_map/while/body/eval_jaxpr/ppermute | solution.py:23
  104.6 5.9 %collective-permute-start = (bf16[1,16,256]{2,1,0:T(8,128)(2,1)S(1)}, bf16[1,16,256]{2,1,0:T(8,128)(2,1)S(1)}, u32[]{:S(2)}, u32[]{:S(2)}) collective-permute-start(bf16[1,16,256]{2,1,0:T(8,128)(2,1)S(1)} %get-tuple-element.166), channel_id=1, source_target_pairs={{4,0},{8,4},{12,8},{5,1},{9,5},{13,9},{6,2},{10,6},{14,10},{7,3},{... | collective-permute-start | bytes 24584 | tf_op jit(solution)/shard_map/while/body/eval_jaxpr/ppermute | solution.py:15
  114.0 5.8 %collective-permute-start.3 = (bf16[34,1,256]{2,1,0:T(2,128)(2,1)S(1)}, bf16[34,1,256]{2,1,0:T(2,128)(2,1)S(1)}, u32[]{:S(2)}, u32[]{:S(2)}) collective-permute-start(bf16[34,1,256]{2,1,0:T(2,128)(2,1)S(1)} %get-tuple-element.169), channel_id=1, source_target_pairs={{0,1},{1,2},{2,3},{4,5},{5,6},{6,7},{8,9},{9,10},{10,11},{12,13},{... | collective-permute-start | bytes 52232 | tf_op jit(solution)/shard_map/while/body/eval_jaxpr/ppermute | solution.py:14
  121.5 11.7 %collective-permute-start.4 = (f32[32,16,256]{2,1,0:T(8,128)S(1)}, f32[32,16,256]{2,1,0:T(8,128)S(1)}, u32[]{:S(2)}, u32[]{:S(2)}) collective-permute-start(f32[32,16,256]{2,1,0:T(8,128)S(1)} %fusion.44), channel_id=1, source_target_pairs={{0,16},{16,32},{32,48},{48,64},{64,80},{80,96},{96,112},{112,128},... | collective-permute-start | bytes 1572872 | tf_op jit(solution)/shard_map/while/body/eval_jaxpr/ppermute | solution.py:23
  135.3 5.9 %collective-permute-start = (bf16[1,16,256]{2,1,0:T(8,128)(2,1)S(1)}, bf16[1,16,256]{2,1,0:T(8,128)(2,1)S(1)}, u32[]{:S(2)}, u32[]{:S(2)}) collective-permute-start(bf16[1,16,256]{2,1,0:T(8,128)(2,1)S(1)} %get-tuple-element.166), channel_id=1, source_target_pairs={{4,0},{8,4},{12,8},{5,1},{9,5},{13,9},{6,2},{10,6},{14,10},{7,3},{... | collective-permute-start | bytes 24584 | tf_op jit(solution)/shard_map/while/body/eval_jaxpr/ppermute | solution.py:15
  144.7 5.8 %collective-permute-start.3 = (bf16[34,1,256]{2,1,0:T(2,128)(2,1)S(1)}, bf16[34,1,256]{2,1,0:T(2,128)(2,1)S(1)}, u32[]{:S(2)}, u32[]{:S(2)}) collective-permute-start(bf16[34,1,256]{2,1,0:T(2,128)(2,1)S(1)} %get-tuple-element.169), channel_id=1, source_target_pairs={{0,1},{1,2},{2,3},{4,5},{5,6},{6,7},{8,9},{9,10},{10,11},{12,13},{... | collective-permute-start | bytes 52232 | tf_op jit(solution)/shard_map/while/body/eval_jaxpr/ppermute | solution.py:14
  152.1 11.7 %collective-permute-start.4 = (f32[32,16,256]{2,1,0:T(8,128)S(1)}, f32[32,16,256]{2,1,0:T(8,128)S(1)}, u32[]{:S(2)}, u32[]{:S(2)}) collective-permute-start(f32[32,16,256]{2,1,0:T(8,128)S(1)} %fusion.44), channel_id=1, source_target_pairs={{0,16},{16,32},{32,48},{48,64},{64,80},{80,96},{96,112},{112,128},... | collective-permute-start | bytes 1572872 | tf_op jit(solution)/shard_map/while/body/eval_jaxpr/ppermute | solution.py:23
  166.0 5.9 %collective-permute-start = (bf16[1,16,256]{2,1,0:T(8,128)(2,1)S(1)}, bf16[1,16,256]{2,1,0:T(8,128)(2,1)S(1)}, u32[]{:S(2)}, u32[]{:S(2)}) collective-permute-start(bf16[1,16,256]{2,1,0:T(8,128)(2,1)S(1)} %get-tuple-element.166), channel_id=1, source_target_pairs={{4,0},{8,4},{12,8},{5,1},{9,5},{13,9},{6,2},{10,6},{14,10},{7,3},{... | collective-permute-start | bytes 24584 | tf_op jit(solution)/shard_map/while/body/eval_jaxpr/ppermute | solution.py:15
  175.4 5.8 %collective-permute-start.3 = (bf16[34,1,256]{2,1,0:T(2,128)(2,1)S(1)}, bf16[34,1,256]{2,1,0:T(2,128)(2,1)S(1)}, u32[]{:S(2)}, u32[]{:S(2)}) collective-permute-start(bf16[34,1,256]{2,1,0:T(2,128)(2,1)S(1)} %get-tuple-element.169), channel_id=1, source_target_pairs={{0,1},{1,2},{2,3},{4,5},{5,6},{6,7},{8,9},{9,10},{10,11},{12,13},{... | collective-permute-start | bytes 52232 | tf_op jit(solution)/shard_map/while/body/eval_jaxpr/ppermute | solution.py:14
  182.8 11.7 %collective-permute-start.4 = (f32[32,16,256]{2,1,0:T(8,128)S(1)}, f32[32,16,256]{2,1,0:T(8,128)S(1)}, u32[]{:S(2)}, u32[]{:S(2)}) collective-permute-start(f32[32,16,256]{2,1,0:T(8,128)S(1)} %fusion.44), channel_id=1, source_target_pairs={{0,16},{16,32},{32,48},{48,64},{64,80},{80,96},{96,112},{112,128},... | collective-permute-start | bytes 1572872 | tf_op jit(solution)/shard_map/while/body/eval_jaxpr/ppermute | solution.py:23
  196.6 5.9 %collective-permute-start = (bf16[1,16,256]{2,1,0:T(8,128)(2,1)S(1)}, bf16[1,16,256]{2,1,0:T(8,128)(2,1)S(1)}, u32[]{:S(2)}, u32[]{:S(2)}) collective-permute-start(bf16[1,16,256]{2,1,0:T(8,128)(2,1)S(1)} %get-tuple-element.166), channel_id=1, source_target_pairs={{4,0},{8,4},{12,8},{5,1},{9,5},{13,9},{6,2},{10,6},{14,10},{7,3},{... | collective-permute-start | bytes 24584 | tf_op jit(solution)/shard_map/while/body/eval_jaxpr/ppermute | solution.py:15
  206.1 5.8 %collective-permute-start.3 = (bf16[34,1,256]{2,1,0:T(2,128)(2,1)S(1)}, bf16[34,1,256]{2,1,0:T(2,128)(2,1)S(1)}, u32[]{:S(2)}, u32[]{:S(2)}) collective-permute-start(bf16[34,1,256]{2,1,0:T(2,128)(2,1)S(1)} %get-tuple-element.169), channel_id=1, source_target_pairs={{0,1},{1,2},{2,3},{4,5},{5,6},{6,7},{8,9},{9,10},{10,11},{12,13},{... | collective-permute-start | bytes 52232 | tf_op jit(solution)/shard_map/while/body/eval_jaxpr/ppermute | solution.py:14
  213.5 11.7 %collective-permute-start.4 = (f32[32,16,256]{2,1,0:T(8,128)S(1)}, f32[32,16,256]{2,1,0:T(8,128)S(1)}, u32[]{:S(2)}, u32[]{:S(2)}) collective-permute-start(f32[32,16,256]{2,1,0:T(8,128)S(1)} %fusion.44), channel_id=1, source_target_pairs={{0,16},{16,32},{32,48},{48,64},{64,80},{80,96},{96,112},{112,128},... | collective-permute-start | bytes 1572872 | tf_op jit(solution)/shard_map/while/body/eval_jaxpr/ppermute | solution.py:23
  227.3 5.9 %collective-permute-start = (bf16[1,16,256]{2,1,0:T(8,128)(2,1)S(1)}, bf16[1,16,256]{2,1,0:T(8,128)(2,1)S(1)}, u32[]{:S(2)}, u32[]{:S(2)}) collective-permute-start(bf16[1,16,256]{2,1,0:T(8,128)(2,1)S(1)} %get-tuple-element.166), channel_id=1, source_target_pairs={{4,0},{8,4},{12,8},{5,1},{9,5},{13,9},{6,2},{10,6},{14,10},{7,3},{... | collective-permute-start | bytes 24584 | tf_op jit(solution)/shard_map/while/body/eval_jaxpr/ppermute | solution.py:15
  236.8 5.8 %collective-permute-start.3 = (bf16[34,1,256]{2,1,0:T(2,128)(2,1)S(1)}, bf16[34,1,256]{2,1,0:T(2,128)(2,1)S(1)}, u32[]{:S(2)}, u32[]{:S(2)}) collective-permute-start(bf16[34,1,256]{2,1,0:T(2,128)(2,1)S(1)} %get-tuple-element.169), channel_id=1, source_target_pairs={{0,1},{1,2},{2,3},{4,5},{5,6},{6,7},{8,9},{9,10},{10,11},{12,13},{... | collective-permute-start | bytes 52232 | tf_op jit(solution)/shard_map/while/body/eval_jaxpr/ppermute | solution.py:14
  244.2 11.7 %collective-permute-start.4 = (f32[32,16,256]{2,1,0:T(8,128)S(1)}, f32[32,16,256]{2,1,0:T(8,128)S(1)}, u32[]{:S(2)}, u32[]{:S(2)}) collective-permute-start(f32[32,16,256]{2,1,0:T(8,128)S(1)} %fusion.44), channel_id=1, source_target_pairs={{0,16},{16,32},{32,48},{48,64},{64,80},{80,96},{96,112},{112,128},... | collective-permute-start | bytes 1572872 | tf_op jit(solution)/shard_map/while/body/eval_jaxpr/ppermute | solution.py:23
  258.0 5.9 %collective-permute-start = (bf16[1,16,256]{2,1,0:T(8,128)(2,1)S(1)}, bf16[1,16,256]{2,1,0:T(8,128)(2,1)S(1)}, u32[]{:S(2)}, u32[]{:S(2)}) collective-permute-start(bf16[1,16,256]{2,1,0:T(8,128)(2,1)S(1)} %get-tuple-element.166), channel_id=1, source_target_pairs={{4,0},{8,4},{12,8},{5,1},{9,5},{13,9},{6,2},{10,6},{14,10},{7,3},{... | collective-permute-start | bytes 24584 | tf_op jit(solution)/shard_map/while/body/eval_jaxpr/ppermute | solution.py:15
  267.5 5.8 %collective-permute-start.3 = (bf16[34,1,256]{2,1,0:T(2,128)(2,1)S(1)}, bf16[34,1,256]{2,1,0:T(2,128)(2,1)S(1)}, u32[]{:S(2)}, u32[]{:S(2)}) collective-permute-start(bf16[34,1,256]{2,1,0:T(2,128)(2,1)S(1)} %get-tuple-element.169), channel_id=1, source_target_pairs={{0,1},{1,2},{2,3},{4,5},{5,6},{6,7},{8,9},{9,10},{10,11},{12,13},{... | collective-permute-start | bytes 52232 | tf_op jit(solution)/shard_map/while/body/eval_jaxpr/ppermute | solution.py:14
  274.9 11.7 %collective-permute-start.4 = (f32[32,16,256]{2,1,0:T(8,128)S(1)}, f32[32,16,256]{2,1,0:T(8,128)S(1)}, u32[]{:S(2)}, u32[]{:S(2)}) collective-permute-start(f32[32,16,256]{2,1,0:T(8,128)S(1)} %fusion.44), channel_id=1, source_target_pairs={{0,16},{16,32},{32,48},{48,64},{64,80},{80,96},{96,112},{112,128},... | collective-permute-start | bytes 1572872 | tf_op jit(solution)/shard_map/while/body/eval_jaxpr/ppermute | solution.py:23
  288.7 5.9 %collective-permute-start = (bf16[1,16,256]{2,1,0:T(8,128)(2,1)S(1)}, bf16[1,16,256]{2,1,0:T(8,128)(2,1)S(1)}, u32[]{:S(2)}, u32[]{:S(2)}) collective-permute-start(bf16[1,16,256]{2,1,0:T(8,128)(2,1)S(1)} %get-tuple-element.166), channel_id=1, source_target_pairs={{4,0},{8,4},{12,8},{5,1},{9,5},{13,9},{6,2},{10,6},{14,10},{7,3},{... | collective-permute-start | bytes 24584 | tf_op jit(solution)/shard_map/while/body/eval_jaxpr/ppermute | solution.py:15
  298.2 5.8 %collective-permute-start.3 = (bf16[34,1,256]{2,1,0:T(2,128)(2,1)S(1)}, bf16[34,1,256]{2,1,0:T(2,128)(2,1)S(1)}, u32[]{:S(2)}, u32[]{:S(2)}) collective-permute-start(bf16[34,1,256]{2,1,0:T(2,128)(2,1)S(1)} %get-tuple-element.169), channel_id=1, source_target_pairs={{0,1},{1,2},{2,3},{4,5},{5,6},{6,7},{8,9},{9,10},{10,11},{12,13},{... | collective-permute-start | bytes 52232 | tf_op jit(solution)/shard_map/while/body/eval_jaxpr/ppermute | solution.py:14
  305.6 11.7 %collective-permute-start.4 = (f32[32,16,256]{2,1,0:T(8,128)S(1)}, f32[32,16,256]{2,1,0:T(8,128)S(1)}, u32[]{:S(2)}, u32[]{:S(2)}) collective-permute-start(f32[32,16,256]{2,1,0:T(8,128)S(1)} %fusion.44), channel_id=1, source_target_pairs={{0,16},{16,32},{32,48},{48,64},{64,80},{80,96},{96,112},{112,128},... | collective-permute-start | bytes 1572872 | tf_op jit(solution)/shard_map/while/body/eval_jaxpr/ppermute | solution.py:23
  319.4 5.9 %collective-permute-start = (bf16[1,16,256]{2,1,0:T(8,128)(2,1)S(1)}, bf16[1,16,256]{2,1,0:T(8,128)(2,1)S(1)}, u32[]{:S(2)}, u32[]{:S(2)}) collective-permute-start(bf16[1,16,256]{2,1,0:T(8,128)(2,1)S(1)} %get-tuple-element.166), channel_id=1, source_target_pairs={{4,0},{8,4},{12,8},{5,1},{9,5},{13,9},{6,2},{10,6},{14,10},{7,3},{... | collective-permute-start | bytes 24584 | tf_op jit(solution)/shard_map/while/body/eval_jaxpr/ppermute | solution.py:15
  328.9 5.8 %collective-permute-start.3 = (bf16[34,1,256]{2,1,0:T(2,128)(2,1)S(1)}, bf16[34,1,256]{2,1,0:T(2,128)(2,1)S(1)}, u32[]{:S(2)}, u32[]{:S(2)}) collective-permute-start(bf16[34,1,256]{2,1,0:T(2,128)(2,1)S(1)} %get-tuple-element.169), channel_id=1, source_target_pairs={{0,1},{1,2},{2,3},{4,5},{5,6},{6,7},{8,9},{9,10},{10,11},{12,13},{... | collective-permute-start | bytes 52232 | tf_op jit(solution)/shard_map/while/body/eval_jaxpr/ppermute | solution.py:14
  336.3 11.7 %collective-permute-start.4 = (f32[32,16,256]{2,1,0:T(8,128)S(1)}, f32[32,16,256]{2,1,0:T(8,128)S(1)}, u32[]{:S(2)}, u32[]{:S(2)}) collective-permute-start(f32[32,16,256]{2,1,0:T(8,128)S(1)} %fusion.44), channel_id=1, source_target_pairs={{0,16},{16,32},{32,48},{48,64},{64,80},{80,96},{96,112},{112,128},... | collective-permute-start | bytes 1572872 | tf_op jit(solution)/shard_map/while/body/eval_jaxpr/ppermute | solution.py:23
  350.1 5.9 %collective-permute-start = (bf16[1,16,256]{2,1,0:T(8,128)(2,1)S(1)}, bf16[1,16,256]{2,1,0:T(8,128)(2,1)S(1)}, u32[]{:S(2)}, u32[]{:S(2)}) collective-permute-start(bf16[1,16,256]{2,1,0:T(8,128)(2,1)S(1)} %get-tuple-element.166), channel_id=1, source_target_pairs={{4,0},{8,4},{12,8},{5,1},{9,5},{13,9},{6,2},{10,6},{14,10},{7,3},{... | collective-permute-start | bytes 24584 | tf_op jit(solution)/shard_map/while/body/eval_jaxpr/ppermute | solution.py:15
  359.6 5.8 %collective-permute-start.3 = (bf16[34,1,256]{2,1,0:T(2,128)(2,1)S(1)}, bf16[34,1,256]{2,1,0:T(2,128)(2,1)S(1)}, u32[]{:S(2)}, u32[]{:S(2)}) collective-permute-start(bf16[34,1,256]{2,1,0:T(2,128)(2,1)S(1)} %get-tuple-element.169), channel_id=1, source_target_pairs={{0,1},{1,2},{2,3},{4,5},{5,6},{6,7},{8,9},{9,10},{10,11},{12,13},{... | collective-permute-start | bytes 52232 | tf_op jit(solution)/shard_map/while/body/eval_jaxpr/ppermute | solution.py:14
  367.0 11.7 %collective-permute-start.4 = (f32[32,16,256]{2,1,0:T(8,128)S(1)}, f32[32,16,256]{2,1,0:T(8,128)S(1)}, u32[]{:S(2)}, u32[]{:S(2)}) collective-permute-start(f32[32,16,256]{2,1,0:T(8,128)S(1)} %fusion.44), channel_id=1, source_target_pairs={{0,16},{16,32},{32,48},{48,64},{64,80},{80,96},{96,112},{112,128},... | collective-permute-start | bytes 1572872 | tf_op jit(solution)/shard_map/while/body/eval_jaxpr/ppermute | solution.py:23
  380.8 5.9 %collective-permute-start = (bf16[1,16,256]{2,1,0:T(8,128)(2,1)S(1)}, bf16[1,16,256]{2,1,0:T(8,128)(2,1)S(1)}, u32[]{:S(2)}, u32[]{:S(2)}) collective-permute-start(bf16[1,16,256]{2,1,0:T(8,128)(2,1)S(1)} %get-tuple-element.166), channel_id=1, source_target_pairs={{4,0},{8,4},{12,8},{5,1},{9,5},{13,9},{6,2},{10,6},{14,10},{7,3},{... | collective-permute-start | bytes 24584 | tf_op jit(solution)/shard_map/while/body/eval_jaxpr/ppermute | solution.py:15
  397.7 11.7 %collective-permute-start.4 = (f32[32,16,256]{2,1,0:T(8,128)S(1)}, f32[32,16,256]{2,1,0:T(8,128)S(1)}, u32[]{:S(2)}, u32[]{:S(2)}) collective-permute-start(f32[32,16,256]{2,1,0:T(8,128)S(1)} %fusion.44), channel_id=1, source_target_pairs={{0,16},{16,32},{32,48},{48,64},{64,80},{80,96},{96,112},{112,128},... | collective-permute-start | bytes 1572872 | tf_op jit(solution)/shard_map/while/body/eval_jaxpr/ppermute | solution.py:23
  411.5 5.9 %collective-permute-start = (bf16[1,16,256]{2,1,0:T(8,128)(2,1)S(1)}, bf16[1,16,256]{2,1,0:T(8,128)(2,1)S(1)}, u32[]{:S(2)}, u32[]{:S(2)}) collective-permute-start(bf16[1,16,256]{2,1,0:T(8,128)(2,1)S(1)} %get-tuple-element.166), channel_id=1, source_target_pairs={{4,0},{8,4},{12,8},{5,1},{9,5},{13,9},{6,2},{10,6},{14,10},{7,3},{... | collective-permute-start | bytes 24584 | tf_op jit(solution)/shard_map/while/body/eval_jaxpr/ppermute | solution.py:15
  428.4 11.7 %collective-permute-start.4 = (f32[32,16,256]{2,1,0:T(8,128)S(1)}, f32[32,16,256]{2,1,0:T(8,128)S(1)}, u32[]{:S(2)}, u32[]{:S(2)}) collective-permute-start(f32[32,16,256]{2,1,0:T(8,128)S(1)} %fusion.44), channel_id=1, source_target_pairs={{0,16},{16,32},{32,48},{48,64},{64,80},{80,96},{96,112},{112,128},... | collective-permute-start | bytes 1572872 | tf_op jit(solution)/shard_map/while/body/eval_jaxpr/ppermute | solution.py:23
  442.2 5.9 %collective-permute-start = (bf16[1,16,256]{2,1,0:T(8,128)(2,1)S(1)}, bf16[1,16,256]{2,1,0:T(8,128)(2,1)S(1)}, u32[]{:S(2)}, u32[]{:S(2)}) collective-permute-start(bf16[1,16,256]{2,1,0:T(8,128)(2,1)S(1)} %get-tuple-element.166), channel_id=1, source_target_pairs={{4,0},{8,4},{12,8},{5,1},{9,5},{13,9},{6,2},{10,6},{14,10},{7,3},{... | collective-permute-start | bytes 24584 | tf_op jit(solution)/shard_map/while/body/eval_jaxpr/ppermute | solution.py:15
  459.1 11.7 %collective-permute-start.4 = (f32[32,16,256]{2,1,0:T(8,128)S(1)}, f32[32,16,256]{2,1,0:T(8,128)S(1)}, u32[]{:S(2)}, u32[]{:S(2)}) collective-permute-start(f32[32,16,256]{2,1,0:T(8,128)S(1)} %fusion.44), channel_id=1, source_target_pairs={{0,16},{16,32},{32,48},{48,64},{64,80},{80,96},{96,112},{112,128},... | collective-permute-start | bytes 1572872 | tf_op jit(solution)/shard_map/while/body/eval_jaxpr/ppermute | solution.py:23
  472.9 5.9 %collective-permute-start = (bf16[1,16,256]{2,1,0:T(8,128)(2,1)S(1)}, bf16[1,16,256]{2,1,0:T(8,128)(2,1)S(1)}, u32[]{:S(2)}, u32[]{:S(2)}) collective-permute-start(bf16[1,16,256]{2,1,0:T(8,128)(2,1)S(1)} %get-tuple-element.166), channel_id=1, source_target_pairs={{4,0},{8,4},{12,8},{5,1},{9,5},{13,9},{6,2},{10,6},{14,10},{7,3},{... | collective-permute-start | bytes 24584 | tf_op jit(solution)/shard_map/while/body/eval_jaxpr/ppermute | solution.py:15
  489.8 11.7 %collective-permute-start.4 = (f32[32,16,256]{2,1,0:T(8,128)S(1)}, f32[32,16,256]{2,1,0:T(8,128)S(1)}, u32[]{:S(2)}, u32[]{:S(2)}) collective-permute-start(f32[32,16,256]{2,1,0:T(8,128)S(1)} %fusion.44), channel_id=1, source_target_pairs={{0,16},{16,32},{32,48},{48,64},{64,80},{80,96},{96,112},{112,128},... | collective-permute-start | bytes 1572872 | tf_op jit(solution)/shard_map/while/body/eval_jaxpr/ppermute | solution.py:23
  503.6 5.9 %collective-permute-start.13 = (bf16[1,16,256]{2,1,0:T(8,128)(2,1)S(1)}, bf16[1,16,256]{2,1,0:T(8,128)(2,1)S(1)}, u32[]{:S(2)}, u32[]{:S(2)}) collective-permute-start(bf16[1,16,256]{2,1,0:T(8,128)(2,1)S(1)} %get-tuple-element.113), channel_id=1, source_target_pairs={{0,4},{4,8},{8,12},{1,5},{5,9},{9,13},{2,6},{6,10},{10,14},{3,7},{... | collective-permute-start | bytes 24584 | tf_op jit(solution)/shard_map/ppermute | solution.py:14
  522.5 5.9 %collective-permute-start.17 = (bf16[1,16,256]{2,1,0:T(8,128)(2,1)S(1)}, bf16[1,16,256]{2,1,0:T(8,128)(2,1)S(1)}, u32[]{:S(2)}, u32[]{:S(2)}) collective-permute-start(bf16[1,16,256]{2,1,0:T(8,128)(2,1)S(1)} %get-tuple-element.111), channel_id=1, source_target_pairs={{0,4},{4,8},{8,12},{1,5},{5,9},{9,13},{2,6},{6,10},{10,14},{3,7},{... | collective-permute-start | bytes 24584 | tf_op jit(solution)/shard_map/ppermute | solution.py:14
  (62 other events, 241.0 us)
where the time goes:
time: 547 us; the launch traced here: 543 us
  waiting for transfers between devices  268 us (49%)
  starting transfers between devices  204 us (37%)
  other arithmetic  30.2 us (6%)
  local copies, waits for them, and re-layouts  22.4 us (4%)
  matrix products  14.8 us (3%)
    ppermute x15, waiting for transfers between devices, shifted_2(): return lax.ppermute(block, axis, route)  147 us
    ppermute x38, waiting for transfers between devices, padded_2(): before = lax.ppermute(last, axis, up)  103 us
    ppermute x38, starting transfers between devices, padded_2(): before = lax.ppermute(last, axis, up)  96.9 us
    ppermute x38, starting transfers between devices, padded_2(): after = lax.ppermute(initial, axis, down)  78.3 us
    ppermute x15, starting transfers between devices, shifted_2(): return lax.ppermute(block, axis, route)  28.8 us
    ppermute x38, waiting for transfers between devices, padded_2(): after = lax.ppermute(initial, axis, down)  18.4 us
    select_n x15, other arithmetic, chain_turn(): return jnp.where(position == 0, anchor, shifted)  16.8 us
    while x105, local copies, waits for them, and re-layouts  15.2 us
  transfers between devices with their start and end apart: 91, of which 71 were waited for; matrix products, arithmetic and copies ran while one was open for 1% of the time, Pallas kernels for 0%

commit v1 on v0

v1 whole, which is shorter than its diff:
```python
import functools

import jax
import jax.numpy as jnp
from jax import lax
from jax.experimental import pallas as pl
from jax.experimental.pallas import tpu as pltpu
from jax.sharding import PartitionSpec as P

AXES = ("depth", "rows", "cols")
HALO = 3
BF16 = jnp.bfloat16
F32 = jnp.float32


def silu(x):
    return x / (1.0 + jnp.exp(-x))


def fill(patch, row, x, valid):
    width, channels = x.shape
    act = jnp.where(valid, silu(x), 0.0)
    column = lax.broadcasted_iota(jnp.int32, (width, channels), 0)
    left = jnp.where(column == 0, 0.0, pltpu.roll(act, 1, 0))
    right = jnp.where(column == width - 1, 0.0, pltpu.roll(act, width - 1, 0))
    for tap, moved in enumerate((left, act, right)):
        patch[row, :, tap * channels : (tap + 1) * channels] = moved.astype(BF16)


def slope(patch, weight, rows):
    width, deep = patch.shape[1:]
    total = None
    for tap in range(3):
        part = jnp.dot(
            patch[tap : tap + rows].reshape(rows * width, deep),
            weight[tap],
            preferred_element_type=F32,
        )
        total = part if total is None else total + part
    return total.reshape(rows, width, -1)


def in_image(strip, row, rows, height):
    place = strip * rows + row
    return (place >= 0) & (place < height)


def head_kernel(step, height, where, pieces, w0, w1, jump, main, top, bottom, strip, middle, patch, w0v, w1v, sems):
    rows = main.shape[0]
    deep = strip.shape[0]
    halo = (deep - rows) // 2
    wide = pieces.shape[2]
    index = where[1]
    loads = [pltpu.make_async_copy(w0, w0v, sems.at[0]), pltpu.make_async_copy(w1, w1v, sems.at[1])]
    loads += [
        pltpu.make_async_copy(pieces.at[k], strip.at[:, pl.ds(k * wide, wide), :], sems.at[2 + k])
        for k in range(pieces.shape[0])
    ]
    for load in loads:
        load.start()
    for load in loads[2:]:
        load.wait()
    main[...] = strip[halo : halo + rows]
    top[...] = strip[halo - HALO : halo].astype(BF16)
    bottom[...] = strip[halo + rows : halo + rows + HALO].astype(BF16)
    for row in range(deep):
        fill(patch, row, strip[row], in_image(index, row - halo, rows, height))
    loads[0].wait()
    first = slope(patch, w0v, deep - 2)
    jump[...] = -step * first[1 : deep - 3]
    middle[...] = strip[1 : deep - 1] + step * first
    for row in range(deep - 2):
        fill(patch, row, middle[row], in_image(index, row + 1 - halo, rows, height))
    loads[1].wait()
    jump[...] += step * slope(patch, w1v, deep - 4)


def turn_kernel(
    turn, step, height, where, main, top, bottom, wa, wb, ja, jb, saved_in, second_in,
    out, out_top, out_bottom, saved, second, state, edge, patch, wav, wbv, jav, jbv, sems,
):
    @pl.when(where[0] == turn)
    def _():
        rows = main.shape[0]
        deep = rows + 2 * HALO
        index = where[1]
        loads = [
            pltpu.make_async_copy(main, state.at[pl.ds(HALO, rows)], sems.at[0]),
            pltpu.make_async_copy(top, edge.at[0], sems.at[1]),
            pltpu.make_async_copy(bottom, edge.at[1], sems.at[2]),
            pltpu.make_async_copy(wa, wav, sems.at[3]),
            pltpu.make_async_copy(ja, jav, sems.at[4]),
            pltpu.make_async_copy(wb, wbv, sems.at[5]),
            pltpu.make_async_copy(jb.at[pl.ds(2, rows)], jbv, sems.at[6]),
        ]
        for load in loads:
            load.start()
        for load in loads[:3]:
            load.wait()
        state[:HALO] = edge[0].astype(F32)
        state[HALO + rows :] = edge[1].astype(F32)
        keep = pltpu.make_async_copy(state.at[pl.ds(1, deep - 2)], saved, sems.at[0])
        keep.start()
        for row in range(deep):
            fill(patch, row, state[row], in_image(index, row - HALO, rows, height))
        loads[3].wait()
        loads[4].wait()
        jav[...] += state[1 : deep - 1] + (2.0 * step) * slope(patch, wav, deep - 2)
        keep_second = pltpu.make_async_copy(jav, second, sems.at[1])
        keep_second.start()
        for row in range(rows + 2):
            fill(patch, row, jav[row + 1], in_image(index, row - 1, rows, height))
        loads[5].wait()
        loads[6].wait()
        out[...] = jav[2 : 2 + rows] + (2.0 * step) * slope(patch, wbv, rows) + jbv[...]
        out_top[...] = out[:HALO].astype(BF16)
        out_bottom[...] = out[rows - HALO :].astype(BF16)
        keep.wait()
        keep_second.wait()


def tail_kernel(step, height, where, mine, other, w0, w1, pieces, state, middle, patch, w0v, w1v, sems):
    rows = pieces.shape[2]
    deep = state.shape[0]
    wide = pieces.shape[3]
    index = where[1]
    loads = [pltpu.make_async_copy(w0, w0v, sems.at[0]), pltpu.make_async_copy(w1, w1v, sems.at[1])]
    for load in loads:
        load.start()
    held = pltpu.make_async_copy(mine, state, sems.at[2])
    sent = pltpu.make_async_copy(other, state, sems.at[2])

    @pl.when(where[2] == 0)
    def _():
        held.start()
        held.wait()

    @pl.when(where[2] != 0)
    def _():
        sent.start()
        sent.wait()

    for row in range(deep):
        fill(patch, row, state[row], in_image(index, row - 2, rows, height))
    loads[0].wait()
    middle[...] = state[1 : deep - 1] + step * slope(patch, w0v, deep - 2)
    for row in range(rows + 2):
        fill(patch, row, middle[row], in_image(index, row - 1, rows, height))
    loads[1].wait()
    ending = middle[1 : 1 + rows] + step * slope(patch, w1v, rows)
    for k in range(pieces.shape[0]):
        cut = slice(k * wide, (k + 1) * wide)
        pieces[k, 0] = state[2 : 2 + rows, cut]
        pieces[k, 1] = middle[1 : 1 + rows, cut]
        pieces[k, 2] = ending[:, cut]


def call(kernel, outs, scratch, inputs, in_vmem, out_vmem, aliases, vmem=60 << 20):
    place = {True: pltpu.VMEM, False: pl.ANY}
    return pl.pallas_call(
        kernel,
        out_shape=[jax.ShapeDtypeStruct(*o) for o in outs],
        in_specs=[pl.BlockSpec(memory_space=pltpu.SMEM)]
        + [pl.BlockSpec(memory_space=place[v]) for v in in_vmem],
        out_specs=[pl.BlockSpec(memory_space=place[v]) for v in out_vmem],
        scratch_shapes=scratch,
        input_output_aliases=aliases,
        compiler_params=pltpu.CompilerParams(vmem_limit_bytes=vmem),
    )(*inputs)


def swap_pieces(pieces, ncols):
    mine = lax.axis_index("cols")
    got = {}
    for shift in (2, 1, 3):
        given = lax.dynamic_index_in_dim(pieces, (mine + shift) % ncols, 0, keepdims=False)
        got[shift] = lax.ppermute(given, "cols", [(c, (c + shift) % ncols) for c in range(ncols)])
    got[0] = lax.dynamic_index_in_dim(pieces, mine, 0, keepdims=False)
    stacked = jnp.stack([got[0], got[1], got[2], got[3]])
    order = (mine - jnp.arange(ncols)) % ncols
    return jnp.stack([lax.dynamic_index_in_dim(stacked, order[k], 0, keepdims=False) for k in range(ncols)])


def on_device(section_states, weights):
    ndepth, nrows, ncols = (lax.axis_size(a) for a in AXES)
    depth, row, col = (lax.axis_index(a) for a in AXES)
    tile = section_states[0]
    tile_rows, tile_cols, channels = tile.shape
    height, width = tile_rows * nrows, tile_cols * ncols
    rows = tile_rows // ncols
    strips = nrows * ncols
    step = 2.0 / (2 * ndepth)
    where = jnp.stack([depth, row * ncols + col, depth % 2]).astype(jnp.int32)
    flat = weights.reshape(2, 3, 3 * channels, channels)
    w0, w1 = flat[0], flat[1]

    def route(src_depths, step_depth, step_strip):
        return [
            (d * strips + s, (d + step_depth) * strips + s + step_strip)
            for d in src_depths
            for s in range(strips)
            if 0 <= s + step_strip < strips
        ]

    even, odd = range(0, ndepth, 2), range(1, ndepth, 2)
    w_second = lax.ppermute(w0, AXES, route(odd, -1, 0))

    halo = HALO + 1
    up = [(i, i + 1) for i in range(nrows - 1)]
    down = [(j, i) for i, j in up]
    before = lax.ppermute(tile[tile_rows - halo :], "rows", up)
    after = lax.ppermute(tile[:halo], "rows", down)
    long = jnp.concatenate([before, tile, after], axis=0)
    pieces = jnp.stack([long[k * rows : k * rows + rows + 2 * halo] for k in range(ncols)])
    pieces = lax.all_to_all(pieces, "cols", 0, 0, tiled=True)

    deep = rows + 2 * halo
    strip = (rows, width, channels)
    edge = (HALO, width, channels)
    patch = lambda n: pltpu.VMEM((n, width, 3 * channels), BF16)
    wv = pltpu.VMEM((3, 3 * channels, channels), BF16)
    vm = lambda n: pltpu.VMEM((n, width, channels), F32)


    jump, main, top, bottom = call(
        functools.partial(head_kernel, step, height),
        [((deep - 4, width, channels), F32), (strip, F32), (edge, BF16), (edge, BF16)],
        [vm(deep), vm(deep - 2), patch(deep), wv, wv, pltpu.SemaphoreType.DMA((6,))],
        (where, pieces, w0, w1),
        (False,) * 3,
        (True,) * 4,
        {},
    )
    jump_second = lax.ppermute(jump, AXES, route(odd, -1, 0))
    long_strip = (rows + 4, width, channels)
    saved = jnp.zeros(long_strip, F32)
    second = jnp.zeros(long_strip, F32)
    for turn in range(0, ndepth, 2):
        out, out_top, out_bottom, saved, second = call(
            functools.partial(turn_kernel, turn, step, height),
            [(strip, F32), (edge, BF16), (edge, BF16), (long_strip, F32), (long_strip, F32)],
            [vm(rows + 2 * HALO), pltpu.VMEM((2, *edge), BF16), patch(rows + 2 * HALO), wv, wv, vm(rows + 4), vm(rows),
             pltpu.SemaphoreType.DMA((7,))],
            (where, main, top, bottom, w0, w_second, jump, jump_second, saved, second),
            (False,) * 9,
            (True, True, True, False, False),
            {8: 3, 9: 4},
        )
        if turn < ndepth - 2:
            main = lax.ppermute(out, AXES, route([turn], 2, 0))
            top = lax.ppermute(out_bottom, AXES, route([turn], 2, 1))
            bottom = lax.ppermute(out_top, AXES, route([turn], 2, -1))
    other = lax.ppermute(second, AXES, route(even, 1, 0))
    (pieces,) = call(
        functools.partial(tail_kernel, step, height),
        [((ncols, 3, rows, tile_cols, channels), F32)],
        [vm(rows + 4), vm(rows + 2), patch(rows + 4), wv, wv, pltpu.SemaphoreType.DMA((3,))],
        (where, saved, other, w0, w1),
        (False,) * 4,
        (True,),
        {},
    )
    whole = [
        lax.all_to_all(pieces[:, k], "cols", 0, 0, tiled=True).reshape(tile_rows, tile_cols, channels)
        for k in range(3)
    ]
    return jnp.stack(whole[1:]), whole[0][None]


def solution(mesh):
    in_specs = (P("depth", "rows", "cols", None), P("depth", None, None, None, None))
    out_specs = (P("depth", "rows", "cols", None), P("depth", "rows", "cols", None))
    return jax.shard_map(
        on_device, mesh=mesh, in_specs=in_specs, out_specs=out_specs, check_vma=False
    )
```

time: 547 us -> 243 us (0.44)
  the two profiles are of different devices: /device:TPU:154 before, /device:TPU:226 now
where the time goes in v1:
time: 243 us; the launch traced here: 242 us
  waiting for transfers between devices  127 us (52%)
  starting transfers between devices  33.7 us (14%)
  Pallas kernels  33.6 us (14%)
  blocking collectives  25.9 us (11%)
  local copies, waits for them, and re-layouts  17.6 us (7%)
  other arithmetic  2.76 us (1%)
    ppermute x7, waiting for transfers between devices, on_device(): top = lax.ppermute(out_bottom, AXES, route([turn], 2, 1))  103 us
    pallas_call x10, Pallas kernels, call(): pl.pallas_call(kernel, out_shape=[jax.ShapeDtypeStruct(*o) for o in outs]...  33.6 us
    all_to_all x2, blocking collectives, on_device(): lax.all_to_all(pieces[:, k], 'cols', 0, 0, tiled=True)  25.9 us
    all_to_all x1, waiting for transfers between devices, on_device(): pieces = lax.all_to_all(pieces, 'cols', 0, 0, tiled=True)  8.86 us
    unnamed x55, local copies, waits for them, and re-layouts  8.37 us
    all_to_all x1, waiting for transfers between devices, on_device(): lax.all_to_all(pieces[:, k], 'cols', 0, 0, tiled=True)  8.05 us
    ppermute x7, starting transfers between devices, on_device(): main = lax.ppermute(out, AXES, route([turn], 2, 0))  5.46 us
    ppermute x7, starting transfers between devices, on_device(): top = lax.ppermute(out_bottom, AXES, route([turn], 2, 1))  5.29 us
  transfers between devices with their start and end apart: 28, of which 6 were waited for; matrix products, arithmetic and copies ran while one was open for 2% of the time, Pallas kernels for 3%

profile of v1, /device:TPU:226, one launch (start us, length us, event | category | flops | bytes accessed | tf_op | source)
XLA Modules:
  0.0 242.2 jit_solution(5518300693779753292)
XLA Ops:
  0.6 0.9 slice_bitcast_fusion.4
  1.6 3.4 %collective-permute-start = (f32[4,16,256]{2,1,0:T(8,128)S(1)}, f32[4,16,256]{2,1,0:T(8,128)S(1)}, u32[]{:S(2)}, u32[]{:S(2)}) collective-permute-start(f32[4,16,256]{2,1,0:T(8,128)S(1)} %get-tuple-element.91), channel_id=1, source_target_pairs={{0,4},{4,8},{8,12},{1,5},{5,9},{9,13},{2,6},{6,10},{10,14},{3,7},{... | collective-permute-start | bytes 196616 | tf_op jit(solution)/shard_map/ppermute | solution.py:211
  5.0 2.4 %collective-permute-start.1 = (f32[4,16,256]{2,1,0:T(8,128)S(1)}, f32[4,16,256]{2,1,0:T(8,128)S(1)}, u32[]{:S(2)}, u32[]{:S(2)}) collective-permute-start(f32[4,16,256]{2,1,0:T(8,128)S(1)} %get-tuple-element.92), channel_id=1, source_target_pairs={{4,0},{8,4},{12,8},{5,1},{9,5},{13,9},{6,2},{10,6},{14,10},{7,3},{... | collective-permute-start | bytes 196616 | tf_op jit(solution)/shard_map/ppermute | solution.py:212
  7.4 1.1 fusion.3
  8.5 2.6 %collective-permute-done.1 = f32[4,16,256]{2,1,0:T(8,128)S(1)} collective-permute-done((f32[4,16,256]{2,1,0:T(8,128)S(1)}, f32[4,16,256]{2,1,0:T(8,128)S(1)}, u32[]{:S(2)}, u32[]{:S(2)}) %collective-permute-start.1) | collective-permute-done | bytes 65568 | tf_op jit(solution)/shard_map/ppermute | solution.py:212
  11.2 1.0 pad_maximum_fusion
  12.2 4.5 %all-to-all-start = ((f32[4,16,16,256]{3,2,1,0:T(8,128)}), f32[4,16,16,256]{3,2,1,0:T(8,128)S(1)}, u32[]{:S(2)}, u32[]{:S(2)}) async-start(f32[4,16,16,256]{3,2,1,0:T(8,128)} %pad_maximum_fusion), calls=%async_computation | async-start | bytes 2097152 | tf_op jit(solution)/shard_map/all_to_all | solution.py:215
  16.7 2.8 %fusion.2 = (bf16[1,3,3,256,256]{4,3,2,1,0:T(8,128)(2,1)}, bf16[1,3,3,256,256]{4,3,2,1,0:T(8,128)(2,1)S(1)}) fusion(bf16[2,3,3,256,256]{4,3,2,1,0:T(8,128)(2,1)} %param.3), kind=kLoop, calls=%fused_computation.12 | loop fusion | bytes 4718592 | tf_op jit(solution)/shard_map/slice | solution.py:195
  19.5 1.3 collective-permute-start.2
  21.5 8.9 %all-to-all-done.pieces = f32[4,16,16,256]{3,2,1,0:T(8,128)S(1)} async-done(((f32[4,16,16,256]{3,2,1,0:T(8,128)}), f32[4,16,16,256]{3,2,1,0:T(8,128)S(1)}, u32[]{:S(2)}, u32[]{:S(2)}) %all-to-all-start) | async-done | bytes 1048608 | tf_op jit(solution)/shard_map/all_to_all | solution.py:215
  30.4 1.0 copy-done.3
  31.3 8.4 %shard_map.41 = (f32[12,64,256]{2,1,0:T(8,128)}, f32[8,64,256]{2,1,0:T(8,128)}, bf16[3,64,256]{2,1,0:T(8,128)(2,1)}, bf16[3,64,256]{2,1,0:T(8,128)(2,1)}) custom-call(s32[3]{0:T(128)} %pad_add_fusion.where, f32[4,16,16,256]{3,2,1,0:T(8,128)} %copy-done.3, bf16[3,768,256]{2,1,0:T(8,128)(2,1)} %bitcast.24, bf16[3,768,256]{2,1,0:T(8,128)(2,1)} %bitcast.34), custom_call_target="tpu_custom_call" | custom-call | tf_op jit(solution)/shard_map/pallas_call | solution.py:160
  39.7 1.3 collective-permute-start.3
  41.0 3.1 %collective-permute-done.3.jb = f32[12,64,256]{2,1,0:T(8,128)S(1)} collective-permute-done((f32[12,64,256]{2,1,0:T(8,128)}, f32[12,64,256]{2,1,0:T(8,128)S(1)}, u32[]{:S(2)}, u32[]{:S(2)}) %collective-permute-start.3) | collective-permute-done | bytes 786464 | tf_op jit(solution)/shard_map/ppermute | solution.py:234
  44.1 1.1 broadcast_1_saved_in_second_in.2.clone.second_in
  45.2 1.0 broadcast_1_saved_in_second_in.2.saved_in
  46.1 1.6 shard_map.42
  47.7 0.7 collective-permute-start.4
  48.4 0.7 collective-permute-start.5
  50.6 1.6 shard_map.43
  52.2 0.7 collective-permute-start.7
  52.9 0.7 collective-permute-start.8
  55.2 1.8 shard_map.44
  56.9 0.7 collective-permute-start.10
  59.9 1.6 shard_map.45
  61.4 0.7 collective-permute-start.13
  62.2 0.7 collective-permute-start.14
  64.4 1.6 shard_map.46
  66.0 0.7 collective-permute-start.16
  68.9 1.6 shard_map.47
  70.5 0.7 collective-permute-start.19
  73.4 1.8 shard_map.48
  75.2 1.3 collective-permute-start.22
  76.5 1.3 collective-permute-start.23
  77.8 1.3 collective-permute-start.24
  79.1 102.6 %collective-permute-done.23.top = bf16[3,64,256]{2,1,0:T(8,128)(2,1)S(1)} collective-permute-done((bf16[3,64,256]{2,1,0:T(8,128)(2,1)}, bf16[3,64,256]{2,1,0:T(8,128)(2,1)S(1)}, u32[]{:S(2)}, u32[]{:S(2)}) %collective-permute-start.23) | collective-permute-done | bytes 98336 | tf_op jit(solution)/shard_map/ppermute | solution.py:251
  182.6 6.5 %shard_map.49 = (f32[8,64,256]{2,1,0:T(8,128)}, bf16[3,64,256]{2,1,0:T(8,128)(2,1)}, bf16[3,64,256]{2,1,0:T(8,128)(2,1)}, f32[12,64,256]{2,1,0:T(8,128)}, f32[12,64,256]{2,1,0:T(8,128)}) custom-call(s32[3]{0:T(128)} %pad_add_fusion.where, f32[8,64,256]{2,1,0:T(8,128)} %copy-done.6, ...), custom_call_target="tpu_custom_call", output_to_operand_aliasing={{3}: (8, {}), {4}: (9, {})} | custom-call | tf_op jit(solution)/shard_map/pallas_call | solution.py:160
  189.1 1.3 collective-permute-start.25
  190.5 2.1 collective-permute-done.25.other
  192.5 0.9 copy-done.5
  193.4 7.2 %shard_map.50 = f32[4,3,8,16,256]{4,3,2,1,0:T(8,128)} custom-call(s32[3]{0:T(128)} %pad_add_fusion.where, f32[12,64,256]{2,1,0:T(8,128)} %get-tuple-element.82.mine, f32[12,64,256]{2,1,0:T(8,128)} %copy-done.5, bf16[3,768,256]{2,1,0:T(8,128)(2,1)} %bitcast.33, bf16[3,768,256]{2,1,0:T(8,128)(2,1)} %bitcast.35), custom_call_target="tpu_custom_call" | custom-call | tf_op jit(solution)/shard_map/pallas_call | solution.py:160
  200.6 2.3 slice_bitcast_fusion
  202.9 14.4 %all_to_all.20 = f32[4,8,16,256]{3,2,1,0:T(8,128)S(1)} all-to-all(f32[4,8,16,256]{3,2,1,0:T(8,128)S(1)} %get-tuple-element.86), channel_id=1, replica_groups=mesh['depth'=16,'rows'=4,'cols'=4] {'cols'}, dimensions={0} | all-to-all | bytes 1048576 | tf_op jit(solution)/shard_map/all_to_all | solution.py:264
  217.3 11.5 %all_to_all.21 = f32[4,8,16,256]{3,2,1,0:T(8,128)S(1)} all-to-all(f32[4,8,16,256]{3,2,1,0:T(8,128)S(1)} %get-tuple-element.87), channel_id=1, replica_groups=mesh['depth'=16,'rows'=4,'cols'=4] {'cols'}, dimensions={0} | all-to-all | bytes 1048576 | tf_op jit(solution)/shard_map/all_to_all | solution.py:264
  228.9 3.5 %all-to-all-start.1 = ((f32[4,8,16,256]{3,2,1,0:T(8,128)}), f32[4,8,16,256]{3,2,1,0:T(8,128)S(1)}, u32[]{:S(2)}, u32[]{:S(2)}) async-start(f32[4,8,16,256]{3,2,1,0:T(8,128)} %get-tuple-element.88), calls=%async_computation.1 | async-start | bytes 1048576 | tf_op jit(solution)/shard_map/all_to_all | solution.py:264
  232.4 8.0 %all-to-all-done.1 = f32[4,8,16,256]{3,2,1,0:T(8,128)S(1)} async-done(((f32[4,8,16,256]{3,2,1,0:T(8,128)}), f32[4,8,16,256]{3,2,1,0:T(8,128)S(1)}, u32[]{:S(2)}, u32[]{:S(2)}) %all-to-all-start.1) | async-done | bytes 524320 | tf_op jit(solution)/shard_map/all_to_all | solution.py:264
  240.4 1.0 pad_maximum_fusion.1
  241.4 0.8 copy.37
  (85 shorter events, 12.5 us)
Async XLA Ops:
  0.6 10.5 %copy-start.4 = (f32[1,32,16,256]{3,2,1,0:T(8,128)S(1)}, f32[1,32,16,256]{3,2,1,0:T(8,128)}, u32[]{:S(2)}) copy-start(f32[1,32,16,256]{3,2,1,0:T(8,128)} %param.2) | copy-start | bytes 1572868
  1.6 6.9 %collective-permute-start = (f32[4,16,256]{2,1,0:T(8,128)S(1)}, f32[4,16,256]{2,1,0:T(8,128)S(1)}, u32[]{:S(2)}, u32[]{:S(2)}) collective-permute-start(f32[4,16,256]{2,1,0:T(8,128)S(1)} %get-tuple-element.91), channel_id=1, source_target_pairs={{0,4},{4,8},{8,12},{1,5},{5,9},{9,13},{2,6},{6,10},{10,14},{3,7},{... | collective-permute-start | bytes 196616 | tf_op jit(solution)/shard_map/ppermute | solution.py:211
  5.0 6.2 %collective-permute-start.1 = (f32[4,16,256]{2,1,0:T(8,128)S(1)}, f32[4,16,256]{2,1,0:T(8,128)S(1)}, u32[]{:S(2)}, u32[]{:S(2)}) collective-permute-start(f32[4,16,256]{2,1,0:T(8,128)S(1)} %get-tuple-element.92), channel_id=1, source_target_pairs={{4,0},{8,4},{12,8},{5,1},{9,5},{13,9},{6,2},{10,6},{14,10},{7,3},{... | collective-permute-start | bytes 196616 | tf_op jit(solution)/shard_map/ppermute | solution.py:212
  12.2 18.1 %all-to-all-start = ((f32[4,16,16,256]{3,2,1,0:T(8,128)}), f32[4,16,16,256]{3,2,1,0:T(8,128)S(1)}, u32[]{:S(2)}, u32[]{:S(2)}) async-start(f32[4,16,16,256]{3,2,1,0:T(8,128)} %pad_maximum_fusion), calls=%async_computation | async-start | bytes 2097152 | tf_op jit(solution)/shard_map/all_to_all | solution.py:215
  19.5 10.8 %copy-start = (bf16[1,3,3,256,256]{4,3,2,1,0:T(8,128)(2,1)}, bf16[1,3,3,256,256]{4,3,2,1,0:T(8,128)(2,1)S(1)}, u32[]{:S(2)}) copy-start(bf16[1,3,3,256,256]{4,3,2,1,0:T(8,128)(2,1)S(1)} %get-tuple-element.85) | copy-start | bytes 3538948
  19.5 21.5 %collective-permute-start.2 = (bf16[3,768,256]{2,1,0:T(8,128)(2,1)S(1)}, bf16[3,768,256]{2,1,0:T(8,128)(2,1)S(1)}, u32[]{:S(2)}, u32[]{:S(2)}) collective-permute-start(bf16[3,768,256]{2,1,0:T(8,128)(2,1)S(1)} %bitcast.23), channel_id=1, source_target_pairs={{16,0},{17,1},{18,2},{19,3},{20,4},{21,5},{22,6},{23,7},{24,8},{25... | collective-permute-start | bytes 3538952 | tf_op jit(solution)/shard_map/ppermute | solution.py:206
  30.4 1.0 copy-start.3
  39.7 4.4 %collective-permute-start.3 = (f32[12,64,256]{2,1,0:T(8,128)}, f32[12,64,256]{2,1,0:T(8,128)S(1)}, u32[]{:S(2)}, u32[]{:S(2)}) collective-permute-start(f32[12,64,256]{2,1,0:T(8,128)} %get-tuple-element.46.ja), channel_id=1, source_target_pairs={{16,0},{17,1},{18,2},{19,3},{20,4},{21,5},{22,6},{23,7},{24,8},{25... | collective-permute-start | bytes 2359304 | tf_op jit(solution)/shard_map/ppermute | solution.py:234
  41.0 5.1 %copy-start.1 = (bf16[3,768,256]{2,1,0:T(8,128)(2,1)}, bf16[3,768,256]{2,1,0:T(8,128)(2,1)S(1)}, u32[]{:S(2)}) copy-start(bf16[3,768,256]{2,1,0:T(8,128)(2,1)S(1)} %collective-permute-done.2.wb) | copy-start | bytes 3538948
  44.1 2.0 copy-start.2
  47.7 2.1 collective-permute-start.4
  48.4 1.4 collective-permute-start.5
  49.1 0.7 collective-permute-start.6
  49.8 0.7 copy-start.21
  49.8 0.8 copy-start.7
  52.2 2.1 collective-permute-start.7
  52.9 1.4 collective-permute-start.8
  53.6 0.7 collective-permute-start.9
  54.3 0.7 copy-start.22
  54.3 0.8 copy-start.8
  56.9 2.1 collective-permute-start.10
  57.6 1.4 collective-permute-start.11
  58.3 0.7 collective-permute-start.12
  59.0 0.7 copy-start.23
  59.0 0.8 copy-start.9
  61.4 2.1 collective-permute-start.13
  62.2 1.4 collective-permute-start.14
  62.8 0.7 collective-permute-start.15
  63.5 0.7 copy-start.24
  63.6 0.8 copy-start.10
  66.0 2.1 collective-permute-start.16
  66.7 1.4 collective-permute-start.17
  67.3 0.7 collective-permute-start.18
  68.0 0.7 copy-start.25
  68.1 0.8 copy-start.11
  70.5 2.1 collective-permute-start.19
  71.2 1.4 collective-permute-start.20
  71.9 0.7 collective-permute-start.21
  72.6 0.7 copy-start.26
  72.6 0.8 copy-start.12
  75.2 106.6 %collective-permute-start.22 = (f32[8,64,256]{2,1,0:T(8,128)}, f32[8,64,256]{2,1,0:T(8,128)S(1)}, u32[]{:S(2)}, u32[]{:S(2)}) collective-permute-start(f32[8,64,256]{2,1,0:T(8,128)} %get-tuple-element.77), channel_id=1, source_target_pairs={{192,224},{193,225},{194,226},{195,227},{196,228},{197,229},{198,2... | collective-permute-start | bytes 1572872 | tf_op jit(solution)/shard_map/ppermute | solution.py:250
  76.5 105.2 %collective-permute-start.23 = (bf16[3,64,256]{2,1,0:T(8,128)(2,1)}, bf16[3,64,256]{2,1,0:T(8,128)(2,1)S(1)}, u32[]{:S(2)}, u32[]{:S(2)}) collective-permute-start(bf16[3,64,256]{2,1,0:T(8,128)(2,1)} %get-tuple-element.78), channel_id=1, source_target_pairs={{192,225},{193,226},{194,227},{195,228},{196,229},{197,230},{198,2... | collective-permute-start | bytes 294920 | tf_op jit(solution)/shard_map/ppermute | solution.py:251
  77.8 103.9 %collective-permute-start.24 = (bf16[3,64,256]{2,1,0:T(8,128)(2,1)}, bf16[3,64,256]{2,1,0:T(8,128)(2,1)S(1)}, u32[]{:S(2)}, u32[]{:S(2)}) collective-permute-start(bf16[3,64,256]{2,1,0:T(8,128)(2,1)} %get-tuple-element.79), channel_id=1, source_target_pairs={{193,224},{194,225},{195,226},{196,227},{197,228},{198,229},{199,2... | collective-permute-start | bytes 294920 | tf_op jit(solution)/shard_map/ppermute | solution.py:252
  181.8 0.7 copy-start.20
  181.8 0.8 copy-start.6
  189.1 3.4 %collective-permute-start.25 = (f32[12,64,256]{2,1,0:T(8,128)}, f32[12,64,256]{2,1,0:T(8,128)S(1)}, u32[]{:S(2)}, u32[]{:S(2)}) collective-permute-start(f32[12,64,256]{2,1,0:T(8,128)} %get-tuple-element.83), channel_id=1, source_target_pairs={{0,16},{1,17},{2,18},{3,19},{4,20},{5,21},{6,22},{7,23},{8,24},{9,... | collective-permute-start | bytes 2359304 | tf_op jit(solution)/shard_map/ppermute | solution.py:253
  192.5 0.9 copy-start.5
  228.9 11.5 %all-to-all-start.1 = ((f32[4,8,16,256]{3,2,1,0:T(8,128)}), f32[4,8,16,256]{3,2,1,0:T(8,128)S(1)}, u32[]{:S(2)}, u32[]{:S(2)}) async-start(f32[4,8,16,256]{3,2,1,0:T(8,128)} %get-tuple-element.88), calls=%async_computation.1 | async-start | bytes 1048576 | tf_op jit(solution)/shard_map/all_to_all | solution.py:264
  (7 other events, 4.4 us)

commit v2 on v0

v2 whole, which is shorter than its diff:
```python
import functools

import jax
import jax.numpy as jnp
from jax import lax
from jax.experimental import pallas as pl
from jax.experimental.pallas import tpu as pltpu
from jax.sharding import PartitionSpec as P

AXES = ("depth", "rows", "cols")
BF16 = jnp.bfloat16
F32 = jnp.float32
KEPT = 2
FIRST, LONG, LAST = 3, 5, 3


def fill(patch, state, rows, first, strip, height):
    width, channels = state.shape[1:]

    def body(row, carry):
        x = state[row]
        place = strip + first + row
        act = x / (1.0 + jnp.exp(-x))
        act = jnp.where((place >= 0) & (place < height), act, 0.0)
        column = lax.broadcasted_iota(jnp.int32, (width, channels), 0)
        left = jnp.where(column == 0, 0.0, pltpu.roll(act, 1, 0))
        right = jnp.where(column == width - 1, 0.0, pltpu.roll(act, width - 1, 0))
        for tap, moved in enumerate((left, act, right)):
            patch[row, :, tap * channels : (tap + 1) * channels] = moved.astype(BF16)
        return carry

    lax.fori_loop(*rows, body, 0)


def slope(patch, weight, first, rows):
    width, deep = patch.shape[1:]
    total = None
    for tap in range(3):
        part = jnp.dot(
            patch[first + tap : first + tap + rows].reshape(rows * width, deep),
            weight[tap],
            preferred_element_type=F32,
        )
        total = part if total is None else total + part
    return total.reshape(rows, width, -1)


def head_kernel(step, height, where, pieces, above, below, w0, w1, main, top, bottom, *rest):
    jumps, (state, middle, patch) = rest[:-3], rest[-3:]
    ncols, rows, wide = pieces.shape[:3]
    halo = above.shape[1]
    deep = rows + 2 * halo
    strip = where[1] * rows
    for k in range(ncols):
        cut = slice(k * wide, (k + 1) * wide)
        state[:halo, cut] = above[k].astype(F32)
        state[halo : halo + rows, cut] = pieces[k]
        state[halo + rows :, cut] = below[k].astype(F32)
    main[...] = state[halo : halo + rows]
    top[...] = state[halo - FIRST : halo].astype(BF16)
    bottom[...] = state[halo + rows : halo + rows + FIRST].astype(BF16)
    fill(patch, state, (0, deep), -halo, strip, height)
    first = slope(patch, w0, 0, deep - 2)
    middle[...] = state[1 : deep - 1] + step * first
    state[1 : deep - 1] = first
    fill(patch, middle, (0, deep - 2), 1 - halo, strip, height)
    jump = step * (slope(patch, w1, 0, deep - 4) - state[2 : deep - 2])
    for ref in jumps:
        cut = (deep - 4 - ref.shape[0]) // 2
        ref[...] = jump[cut : deep - 4 - cut]


def turn_kernel(host, count, last, given, step, height, where, main, top, bottom, *rest):
    weights, jumps = rest[:count], rest[count : 2 * count]
    rest = rest[2 * count + given :]
    kept = count + 1 if last else count
    if not last:
        out, out_top, out_bottom = rest[:3]
        rest = rest[3:]
    saved, (even, odd, patch, sems) = rest[:kept], rest[kept:]

    @pl.when(where[0] == host)
    def _():
        rows, width, channels = main.shape
        halo = top.shape[0]
        strip = where[1] * rows
        states = (even, odd)
        even[:halo] = top[...].astype(F32)
        even[halo : halo + rows] = main[...]
        even[halo + rows :] = bottom[...].astype(F32)
        keep = []
        for k in range(count + 1):
            here, there = states[k % 2], states[(k + 1) % 2]
            near = halo - k
            if k < kept:
                copy = pltpu.make_async_copy(here.at[pl.ds(halo - KEPT, rows + 2 * KEPT)], saved[k], sems.at[k])
                copy.start()
                keep.append(copy)
            if k == count:
                break
            far = near - 1 if k < count - 1 or last else 0
            fill(patch, here, (halo - far - 1, halo + rows + far + 1), -halo, strip, height)
            change = (2.0 * step) * slope(patch, weights[k], halo - far - 1, rows + 2 * far)
            cut = (jumps[k].shape[0] - rows) // 2 - far
            new = here[halo - far : halo + rows + far] + change + jumps[k][cut : cut + rows + 2 * far]
            if k == count - 1 and not last:
                edge = out_top.shape[0]
                out[...] = new
                out_top[...] = new[:edge].astype(BF16)
                out_bottom[...] = new[rows - edge :].astype(BF16)
                break
            if k >= 1:
                keep[k - 1].wait()
            there[halo - far : halo + rows + far] = new
        for copy in keep[max(count - 1, 0) if last else max(count - 2, 0) :]:
            copy.wait()


def tail_kernel(step, height, where, held, one, two, three, w0, w1, coarse, fine, state, middle, patch, sem):
    ncols, rows, wide = coarse.shape[:3]
    deep = state.shape[0]
    strip = where[1] * rows
    for k, source in enumerate((held, one, two, three)):

        @pl.when(where[2] == k)
        def _():
            copy = pltpu.make_async_copy(source, state, sem.at[0])
            copy.start()
            copy.wait()

    fill(patch, state, (0, deep), -KEPT, strip, height)
    middle[...] = state[1 : deep - 1] + step * slope(patch, w0, 0, deep - 2)
    fill(patch, middle, (0, deep - 2), 1 - KEPT, strip, height)
    ending = middle[1 : 1 + rows] + step * slope(patch, w1, 0, rows)
    for k in range(ncols):
        cut = slice(k * wide, (k + 1) * wide)
        coarse[k] = state[KEPT : KEPT + rows, cut]
        fine[k, 0] = middle[1 : 1 + rows, cut]
        fine[k, 1] = ending[:, cut]


def call(kernel, outs, scratch, inputs, vmem_in, vmem_out, aliases, work, vmem=24 << 20):
    place = {True: pltpu.VMEM, False: pl.ANY}
    return pl.pallas_call(
        kernel,
        out_shape=[jax.ShapeDtypeStruct(*o) for o in outs],
        in_specs=[pl.BlockSpec(memory_space=pltpu.SMEM)]
        + [pl.BlockSpec(memory_space=place[v]) for v in vmem_in],
        out_specs=[pl.BlockSpec(memory_space=place[v]) for v in vmem_out],
        scratch_shapes=scratch,
        input_output_aliases=aliases,
        compiler_params=pltpu.CompilerParams(vmem_limit_bytes=vmem),
        cost_estimate=pl.CostEstimate(flops=work, bytes_accessed=1 << 20, transcendentals=0),
    )(*inputs)


def on_device(section_states, weights):
    ndepth, nrows, ncols = (lax.axis_size(a) for a in AXES)
    depth, row, col = (lax.axis_index(a) for a in AXES)
    tile = section_states[0]
    tile_rows, tile_cols, channels = tile.shape
    height, width = tile_rows * nrows, tile_cols * ncols
    rows = tile_rows // ncols
    strips = nrows * ncols
    step = 2.0 / (2 * ndepth)
    flat = weights.reshape(2, 3, 3 * channels, channels)
    w0, w1 = flat[0], flat[1]

    hosts = [0, *range(2, ndepth - 2, 4), ndepth - 2]
    counts = [2] + [4] * (len(hosts) - 2) + [1]
    halos = [FIRST] + [LONG] * (len(hosts) - 2) + [LAST]
    owner = {h + k: k for h, n in zip(hosts, counts) for k in range(n + (n == 1))}
    role = jnp.array([owner[d] for d in range(ndepth)], jnp.int32)[depth]
    where = jnp.stack([depth, row * ncols + col, role]).astype(jnp.int32)

    def route(pairs, shift):
        return [
            (a * strips + s, b * strips + (s + shift))
            for a, b in pairs
            for s in range(strips)
            if 0 <= s + shift < strips
        ]

    def fetch(x, k):
        return lax.ppermute(x, AXES, route([(h + k, h) for h, n in zip(hosts, counts) if n > k], 0))

    def ring(x, shift):
        return lax.ppermute(x, ("rows", "cols"), [(s, (s + shift) % strips) for s in range(strips)])

    pieces = lax.all_to_all(tile.reshape(ncols, rows, tile_cols, channels), "cols", 0, 0, tiled=True)
    near = LONG + 1
    above = ring(pieces[:, rows - near :].astype(BF16), 1)
    below = ring(pieces[:, :near].astype(BF16), -1)
    all_weights = [w0] + [fetch(w0, k) for k in (1, 2, 3)]
    like = lambda n, t=F32: ((n, width, channels), t)
    vm = lambda n: pltpu.VMEM((n, width, channels), F32)
    patch = lambda n: pltpu.VMEM((n, width, 3 * channels), BF16)
    macs = 2 * 9 * channels * channels * width
    deep = rows + 2 * near
    spans = [rows + 2 * (near - 2), rows + 2 * (near - 3), rows + 2 * (near - 4), rows]
    main, top, bottom, *jumps = call(
        functools.partial(head_kernel, step, height),
        [like(rows), like(FIRST, BF16), like(FIRST, BF16)] + [like(n) for n in spans],
        [vm(deep), vm(deep - 2), patch(deep)],
        (where, pieces, above, below, w0, w1),
        (True,) * 5,
        (True,) * 7,
        {},
        macs * (2 * deep - 6),
    )
    all_jumps = [jumps[0]] + [fetch(jumps[k], k) for k in (1, 2, 3)]

    saved = []
    for turn, (host, count, halo) in enumerate(zip(hosts, counts, halos)):
        last = turn == len(hosts) - 1
        kept = count + 1 if last else count
        given = min(len(saved), kept)
        outs = [] if last else [like(rows), like(halos[turn + 1], BF16), like(halos[turn + 1], BF16)]
        inputs = (where, main, top, bottom, *all_weights[:count], *all_jumps[:count], *saved[:given])
        results = call(
            functools.partial(turn_kernel, host, count, last, given, step, height),
            outs + [like(rows + 2 * KEPT)] * kept,
            [vm(rows + 2 * halo), vm(rows + 2 * halo), patch(rows + 2 * halo), pltpu.SemaphoreType.DMA((5,))],
            inputs,
            (True,) * (3 + 2 * count) + (False,) * given,
            (True,) * len(outs) + (False,) * kept,
            {len(inputs) - given + k: len(outs) + k for k in range(given)},
            macs * 11 * count,
        )
        saved[:kept] = results[len(outs) :]
        if not last:
            pair = [(host, hosts[turn + 1])]
            main = lax.ppermute(results[0], AXES, route(pair, 0))
            top = lax.ppermute(results[2], AXES, route(pair, 1))
            bottom = lax.ppermute(results[1], AXES, route(pair, -1))

    def give(k):
        sized = [n + (n == 1) for n in counts]
        return lax.ppermute(saved[k], AXES, route([(h, h + k) for h, n in zip(hosts, sized) if n > k], 0))

    coarse, fine = call(
        functools.partial(tail_kernel, step, height),
        [((ncols, rows, tile_cols, channels), F32), ((ncols, 2, rows, tile_cols, channels), F32)],
        [vm(rows + 4), vm(rows + 2), patch(rows + 4), pltpu.SemaphoreType.DMA((1,))],
        (where, saved[0], give(1), give(2), give(3), w0, w1),
        (False,) * 4 + (True,) * 2,
        (True, True),
        {},
        macs * 18,
    )
    fine = lax.all_to_all(fine, "cols", 0, 0, tiled=True)
    coarse = lax.all_to_all(coarse, "cols", 0, 0, tiled=True)
    fine = fine.transpose(1, 0, 2, 3, 4).reshape(2, tile_rows, tile_cols, channels)
    return fine, coarse.reshape(1, tile_rows, tile_cols, channels)


def solution(mesh):
    in_specs = (P("depth", "rows", "cols", None), P("depth", None, None, None, None))
    out_specs = (P("depth", "rows", "cols", None), P("depth", "rows", "cols", None))
    return jax.shard_map(
        on_device, mesh=mesh, in_specs=in_specs, out_specs=out_specs, check_vma=False
    )
```

time: 547 us -> 208 us (0.38)
  the two profiles are of different devices: /device:TPU:154 before, /device:TPU:162 now
where the time goes in v2:
time: 208 us
  waiting for transfers between devices  116 us (56%)
  Pallas kernels  29.6 us (14%)
  starting transfers between devices  29.2 us (14%)
  blocking collectives  27.8 us (13%)
  local copies, waits for them, and re-layouts  3.38 us (2%)
    ppermute x4, waiting for transfers between devices, on_device(): top = lax.ppermute(results[2], AXES, route(pair, 1))  48.7 us
    ppermute x6, waiting for transfers between devices, fetch(): lax.ppermute(x, AXES, route([(h + k, h) for h, n in zip(hosts, counts) if...  35.6 us
    pallas_call x7, Pallas kernels, call(): pl.pallas_call(kernel, out_shape=[jax.ShapeDtypeStruct(*o) for o in outs]...  29.6 us
    ppermute x3, waiting for transfers between devices, give(): lax.ppermute(saved[k], AXES, route([(h, h + k) for h, n in zip(hosts, siz...  14.9 us
    all_to_all x1, blocking collectives, on_device(): lax.all_to_all(tile.reshape(ncols, rows, tile_cols, channels), 'cols', 0,...  14.1 us
    all_to_all x1, blocking collectives, on_device(): coarse = lax.all_to_all(coarse, 'cols', 0, 0, tiled=True)  13.7 us
    all_to_all x1, waiting for transfers between devices, on_device(): fine = lax.all_to_all(fine, 'cols', 0, 0, tiled=True)  10.9 us
    ppermute x6, starting transfers between devices, fetch(): lax.ppermute(x, AXES, route([(h + k, h) for h, n in zip(hosts, counts) if...  7.75 us
  transfers between devices with their start and end apart: 24, of which 11 were waited for; matrix products, arithmetic and copies ran while one was open for 1% of the time, Pallas kernels for 5%

profile of v2, /device:TPU:162, one launch (start us, length us, event | category | flops | bytes accessed | tf_op | source)
XLA Modules:
  0.0 207.6 jit_solution(13283590985781183346)
XLA Ops:
  0.6 14.1 %all_to_all.15.pieces = f32[4,8,16,256]{3,2,1,0:T(8,128)S(1)} all-to-all(f32[4,8,16,256]{3,2,1,0:T(8,128)} %bitcast.23), channel_id=1, replica_groups=mesh['depth'=16,'rows'=4,'cols'=4] {'cols'}, dimensions={0} | all-to-all | bytes 1048576 | tf_op jit(solution)/shard_map/all_to_all | solution.py:190
  14.8 0.7 fusion.1
  15.5 1.1 collective-permute-start.1
  16.6 0.9 collective-permute-start
  17.7 1.3 collective-permute-start.2
  19.0 0.6 dynamic_slice.3
  19.6 0.7 pad_add_fusion.where
  20.3 1.0 collective-permute-done.1.below
  21.4 3.0 %collective-permute-done.above = bf16[4,6,16,256]{3,2,1,0:T(8,128)(2,1)S(1)} collective-permute-done((bf16[4,6,16,256]{3,2,1,0:T(8,128)(2,1)S(1)}, bf16[4,6,16,256]{3,2,1,0:T(8,128)(2,1)S(1)}, u32[]{:S(2)}, u32[]{:S(2)}) %collective-permute-start) | collective-permute-done | bytes 196640 | tf_op jit(solution)/shard_map/ppermute | solution.py:188
  24.4 7.4 %shard_map.50 = (f32[8,64,256]{2,1,0:T(8,128)S(1)}, bf16[3,64,256]{2,1,0:T(8,128)(2,1)S(1)}, bf16[3,64,256]{2,1,0:T(8,128)(2,1)S(1)}, f32[16,64,256]{2,1,0:T(8,1...) custom-call(s32[3]{0:T(128)S(1)} %pad_add_fusion.where, ...), custom_call_target="tpu_custom_call" | custom-call | flops 2566914048 | bytes 1048576 | tf_op jit(solution)/shard_map/pallas_call | solution.py:144
  31.9 1.3 collective-permute-start.3
  33.1 1.3 collective-permute-start.8
  34.5 1.3 collective-permute-start.7
  35.8 1.3 collective-permute-start.9
  37.1 1.3 collective-permute-start.10
  38.4 1.3 shard_map.51
  39.7 0.7 collective-permute-start.4
  40.4 32.2 %collective-permute-done.10.rest_7_ = f32[8,64,256]{2,1,0:T(8,128)S(1)} collective-permute-done((f32[8,64,256]{2,1,0:T(8,128)S(1)}, f32[8,64,256]{2,1,0:T(8,128)S(1)}, u32[]{:S(2)}, u32[]{:S(2)}) %collective-permute-start.10) | collective-permute-done | bytes 524320 | tf_op jit(solution)/shard_map/ppermute | solution.py:185
  72.6 0.7 collective-permute-start.5
  73.3 0.7 collective-permute-start.6
  74.0 3.4 %collective-permute-done.9.rest_6_ = f32[12,64,256]{2,1,0:T(8,128)S(1)} collective-permute-done((f32[12,64,256]{2,1,0:T(8,128)S(1)}, f32[12,64,256]{2,1,0:T(8,128)S(1)}, u32[]{:S(2)}, u32[]{:S(2)}) %collective-permute-start.9) | collective-permute-done | bytes 786464 | tf_op jit(solution)/shard_map/ppermute | solution.py:185
  77.4 1.3 shard_map.52
  78.7 0.7 collective-permute-start.11
  79.4 0.7 collective-permute-start.12
  80.1 0.7 collective-permute-start.13
  80.8 1.5 shard_map.53
  82.4 1.3 collective-permute-start.14
  83.7 1.3 collective-permute-start.15
  85.0 1.3 collective-permute-start.16
  86.3 46.2 %collective-permute-done.15.top = bf16[5,64,256]{2,1,0:T(8,128)(2,1)S(1)} collective-permute-done((bf16[5,64,256]{2,1,0:T(8,128)(2,1)S(1)}, bf16[5,64,256]{2,1,0:T(8,128)(2,1)S(1)}, u32[]{:S(2)}, u32[]{:S(2)}) %collective-permute-start.15) | collective-permute-done | bytes 163872 | tf_op jit(solution)/shard_map/ppermute | solution.py:234
  132.5 0.8 collective-permute-done.16.bottom
  133.3 12.1 %shard_map.54 = (f32[8,64,256]{2,1,0:T(8,128)S(1)}, bf16[3,64,256]{2,1,0:T(8,128)(2,1)S(1)}, bf16[3,64,256]{2,1,0:T(8,128)(2,1)S(1)}, f32[12,64,256]{2,1,0:T(8,1...) custom-call(s32[3]{0:T(128)S(1)} %pad_add_fusion.where, ...), custom_call_target="tpu_custom_call", output_to_operand_aliasing={{3}: (12, {}), {4}: (13, {}), {5}: (14, {}), {6}: (15, {})} | custom-call | flops 3321888768 | bytes 1048576 | tf_op jit(solution)/shard_map/pallas_call | solution.py:144
  145.4 1.3 collective-permute-start.17
  146.7 1.3 collective-permute-start.18
  148.0 1.3 collective-permute-start.19
  149.3 1.3 collective-permute-start.21
  150.7 1.3 collective-permute-start.22
  152.0 2.4 %collective-permute-done.18.top = bf16[3,64,256]{2,1,0:T(8,128)(2,1)S(1)} collective-permute-done((bf16[3,64,256]{2,1,0:T(8,128)(2,1)S(1)}, bf16[3,64,256]{2,1,0:T(8,128)(2,1)S(1)}, u32[]{:S(2)}, u32[]{:S(2)}) %collective-permute-start.18) | collective-permute-done | bytes 98336 | tf_op jit(solution)/shard_map/ppermute | solution.py:234
  154.4 1.1 collective-permute-done.19.bottom
  156.1 1.3 collective-permute-start.20
  157.4 6.5 %collective-permute-done.21.two = f32[12,64,256]{2,1,0:T(8,128)S(1)} collective-permute-done((f32[12,64,256]{2,1,0:T(8,128)S(1)}, f32[12,64,256]{2,1,0:T(8,128)S(1)}, u32[]{:S(2)}, u32[]{:S(2)}) %collective-permute-start.21) | collective-permute-done | bytes 786464 | tf_op jit(solution)/shard_map/ppermute | solution.py:239
  163.9 8.4 %collective-permute-done.22.three = f32[12,64,256]{2,1,0:T(8,128)S(1)} collective-permute-done((f32[12,64,256]{2,1,0:T(8,128)S(1)}, f32[12,64,256]{2,1,0:T(8,128)S(1)}, u32[]{:S(2)}, u32[]{:S(2)}) %collective-permute-start.22) | collective-permute-done | bytes 786464 | tf_op jit(solution)/shard_map/ppermute | solution.py:239
  172.3 5.3 %shard_map.56 = (f32[4,8,16,256]{3,2,1,0:T(8,128)S(1)}, f32[4,2,8,16,256]{4,3,2,1,0:T(8,128)}) custom-call(s32[3]{0:T(128)S(1)} %pad_add_fusion.where, f32[12,64,256]{2,1,0:T(8,128)S(1)} %get-tuple-element.70.held, f32[12,64,256]{2,1,0:T(8,128)S(1)} %collective-permute-done.20.one, f32[12,64,256]{2,1,0:T(8,128)S(1)} %collective-permute-done.21.two, ...), custom_call_target="tpu_custom_call" | custom-call | flops 1358954496 | bytes 1048576 | tf_op jit(solution)/shard_map/pallas_call | solution.py:144
  177.7 13.7 %all_to_all.16 = f32[4,8,16,256]{3,2,1,0:T(8,128)S(1)} all-to-all(f32[4,8,16,256]{3,2,1,0:T(8,128)S(1)} %get-tuple-element.75), channel_id=1, replica_groups=mesh['depth'=16,'rows'=4,'cols'=4] {'cols'}, dimensions={0} | all-to-all | bytes 1048576 | tf_op jit(solution)/shard_map/all_to_all | solution.py:252
  191.3 3.5 %all-to-all-start.1 = ((f32[4,2,8,16,256]{4,3,2,1,0:T(8,128)}), f32[4,2,8,16,256]{4,3,2,1,0:T(8,128)S(1)}, u32[]{:S(2)}, u32[]{:S(2)}) async-start(f32[4,2,8,16,256]{4,3,2,1,0:T(8,128)} %get-tuple-element.74), calls=%async_computation.1 | async-start | bytes 2097152 | tf_op jit(solution)/shard_map/all_to_all | solution.py:251
  194.9 10.9 %all-to-all-done.1 = f32[4,2,8,16,256]{4,3,2,1,0:T(8,128)S(1)} async-done(((f32[4,2,8,16,256]{4,3,2,1,0:T(8,128)}), f32[4,2,8,16,256]{4,3,2,1,0:T(8,128)S(1)}, u32[]{:S(2)}, u32[]{:S(2)}) %all-to-all-start.1) | async-done | bytes 1048608 | tf_op jit(solution)/shard_map/all_to_all | solution.py:251
  205.7 1.1 copy.17
  206.8 0.8 copy.31
  (20 shorter events, 0.8 us)
Async XLA Ops:
  0.6 16.9 %copy-start = (bf16[2,3,3,256,256]{4,3,2,1,0:T(8,128)(2,1)S(1)}, bf16[2,3,3,256,256]{4,3,2,1,0:T(8,128)(2,1)}, u32[]{:S(2)}) copy-start(bf16[2,3,3,256,256]{4,3,2,1,0:T(8,128)(2,1)} %param.4) | copy-start | bytes 7077892
  15.5 5.9 %collective-permute-start.1 = (bf16[4,6,16,256]{3,2,1,0:T(8,128)(2,1)}, bf16[4,6,16,256]{3,2,1,0:T(8,128)(2,1)S(1)}, u32[]{:S(2)}, u32[]{:S(2)}) collective-permute-start(bf16[4,6,16,256]{3,2,1,0:T(8,128)(2,1)} %get-tuple-element.78), channel_id=1, source_target_pairs={{0,15},{1,0},{2,1},{3,2},{4,3},{5,4},{6,5},{7,6},{8,7},{9,8},{10,9... | collective-permute-start | bytes 589832 | tf_op jit(solution)/shard_map/ppermute | solution.py:188
  16.6 2.4 %copy-start.1 = (s32[16]{0:T(128)S(1)}, s32[16]{0:T(128)}, u32[]{:S(2)}) copy-start(s32[16]{0:T(128)} %constant.20.clone) | copy-start | bytes 196
  16.6 7.8 %collective-permute-start = (bf16[4,6,16,256]{3,2,1,0:T(8,128)(2,1)S(1)}, bf16[4,6,16,256]{3,2,1,0:T(8,128)(2,1)S(1)}, u32[]{:S(2)}, u32[]{:S(2)}) collective-permute-start(bf16[4,6,16,256]{3,2,1,0:T(8,128)(2,1)S(1)} %get-tuple-element.79), channel_id=1, source_target_pairs={{0,1},{1,2},{2,3},{3,4},{4,5},{5,6},{6,7},{7,8},{8,9},{9,10},{10,1... | collective-permute-start | bytes 589832 | tf_op jit(solution)/shard_map/ppermute | solution.py:188
  17.7 19.4 %collective-permute-start.2 = (bf16[3,768,256]{2,1,0:T(8,128)(2,1)S(1)}, bf16[3,768,256]{2,1,0:T(8,128)(2,1)}, u32[]{:S(2)}, u32[]{:S(2)}) collective-permute-start(bf16[3,768,256]{2,1,0:T(8,128)(2,1)S(1)} %bitcast.8), channel_id=1, source_target_pairs={{16,0},{17,1},{18,2},{19,3},{20,4},{21,5},{22,6},{23,7},{24,8},{25... | collective-permute-start | bytes 3538952 | tf_op jit(solution)/shard_map/ppermute | solution.py:185
  31.9 6.5 %collective-permute-start.3 = (f32[14,64,256]{2,1,0:T(8,128)S(1)}, f32[14,64,256]{2,1,0:T(8,128)S(1)}, u32[]{:S(2)}, u32[]{:S(2)}) collective-permute-start(f32[14,64,256]{2,1,0:T(8,128)S(1)} %get-tuple-element.43), channel_id=1, source_target_pairs={{16,0},{17,1},{18,2},{19,3},{20,4},{21,5},{22,6},{23,7},{24,8},{25... | collective-permute-start | bytes 2752520 | tf_op jit(solution)/shard_map/ppermute | solution.py:185
  33.1 40.1 %collective-permute-start.8 = (bf16[3,768,256]{2,1,0:T(8,128)(2,1)S(1)}, bf16[3,768,256]{2,1,0:T(8,128)(2,1)S(1)}, u32[]{:S(2)}, u32[]{:S(2)}) collective-permute-start(bf16[3,768,256]{2,1,0:T(8,128)(2,1)S(1)} %bitcast.10), channel_id=1, source_target_pairs={{80,32},{81,33},{82,34},{83,35},{84,36},{85,37},{86,38},{87,39},{8... | collective-permute-start | bytes 3538952 | tf_op jit(solution)/shard_map/ppermute | solution.py:185
  34.5 39.5 %collective-permute-start.7 = (bf16[3,768,256]{2,1,0:T(8,128)(2,1)S(1)}, bf16[3,768,256]{2,1,0:T(8,128)(2,1)S(1)}, u32[]{:S(2)}, u32[]{:S(2)}) collective-permute-start(bf16[3,768,256]{2,1,0:T(8,128)(2,1)S(1)} %bitcast.11), channel_id=1, source_target_pairs={{64,32},{65,33},{66,34},{67,35},{68,36},{69,37},{70,38},{71,39},{7... | collective-permute-start | bytes 3538952 | tf_op jit(solution)/shard_map/ppermute | solution.py:185
  35.8 41.6 %collective-permute-start.9 = (f32[12,64,256]{2,1,0:T(8,128)S(1)}, f32[12,64,256]{2,1,0:T(8,128)S(1)}, u32[]{:S(2)}, u32[]{:S(2)}) collective-permute-start(f32[12,64,256]{2,1,0:T(8,128)S(1)} %get-tuple-element.47), channel_id=1, source_target_pairs={{64,32},{65,33},{66,34},{67,35},{68,36},{69,37},{70,38},{71,39},{7... | collective-permute-start | bytes 2359304 | tf_op jit(solution)/shard_map/ppermute | solution.py:185
  37.1 35.5 %collective-permute-start.10 = (f32[8,64,256]{2,1,0:T(8,128)S(1)}, f32[8,64,256]{2,1,0:T(8,128)S(1)}, u32[]{:S(2)}, u32[]{:S(2)}) collective-permute-start(f32[8,64,256]{2,1,0:T(8,128)S(1)} %get-tuple-element.48), channel_id=1, source_target_pairs={{80,32},{81,33},{82,34},{83,35},{84,36},{85,37},{86,38},{87,39},{8... | collective-permute-start | bytes 1572872 | tf_op jit(solution)/shard_map/ppermute | solution.py:185
  39.7 37.6 %collective-permute-start.4 = (f32[8,64,256]{2,1,0:T(8,128)S(1)}, f32[8,64,256]{2,1,0:T(8,128)S(1)}, u32[]{:S(2)}, u32[]{:S(2)}) collective-permute-start(f32[8,64,256]{2,1,0:T(8,128)S(1)} %get-tuple-element.44), channel_id=1, source_target_pairs={{0,32},{1,33},{2,34},{3,35},{4,36},{5,37},{6,38},{7,39},{8,40},{9,... | collective-permute-start | bytes 1572872 | tf_op jit(solution)/shard_map/ppermute | solution.py:233
  72.6 4.8 %collective-permute-start.5 = (bf16[5,64,256]{2,1,0:T(8,128)(2,1)S(1)}, bf16[5,64,256]{2,1,0:T(8,128)(2,1)S(1)}, u32[]{:S(2)}, u32[]{:S(2)}) collective-permute-start(bf16[5,64,256]{2,1,0:T(8,128)(2,1)S(1)} %get-tuple-element.45), channel_id=1, source_target_pairs={{0,33},{1,34},{2,35},{3,36},{4,37},{5,38},{6,39},{7,40},{8,41},{9,... | collective-permute-start | bytes 491528 | tf_op jit(solution)/shard_map/ppermute | solution.py:234
  73.3 4.1 %collective-permute-start.6 = (bf16[5,64,256]{2,1,0:T(8,128)(2,1)S(1)}, bf16[5,64,256]{2,1,0:T(8,128)(2,1)S(1)}, u32[]{:S(2)}, u32[]{:S(2)}) collective-permute-start(bf16[5,64,256]{2,1,0:T(8,128)(2,1)S(1)} %get-tuple-element.46), channel_id=1, source_target_pairs={{1,32},{2,33},{3,34},{4,35},{5,36},{6,37},{7,38},{8,39},{9,40},{10... | collective-permute-start | bytes 491528 | tf_op jit(solution)/shard_map/ppermute | solution.py:235
  78.7 2.1 %collective-permute-start.11 = (f32[8,64,256]{2,1,0:T(8,128)S(1)}, f32[8,64,256]{2,1,0:T(8,128)S(1)}, u32[]{:S(2)}, u32[]{:S(2)}) collective-permute-start(f32[8,64,256]{2,1,0:T(8,128)S(1)} %get-tuple-element.51), channel_id=1, source_target_pairs={{32,96},{33,97},{34,98},{35,99},{36,100},{37,101},{38,102},{39,103... | collective-permute-start | bytes 1572872 | tf_op jit(solution)/shard_map/ppermute | solution.py:233
  79.4 1.4 collective-permute-start.12
  80.1 0.7 collective-permute-start.13
  82.4 51.0 %collective-permute-start.14 = (f32[8,64,256]{2,1,0:T(8,128)S(1)}, f32[8,64,256]{2,1,0:T(8,128)S(1)}, u32[]{:S(2)}, u32[]{:S(2)}) collective-permute-start(f32[8,64,256]{2,1,0:T(8,128)S(1)} %get-tuple-element.58), channel_id=1, source_target_pairs={{96,160},{97,161},{98,162},{99,163},{100,164},{101,165},{102,166},... | collective-permute-start | bytes 1572872 | tf_op jit(solution)/shard_map/ppermute | solution.py:233
  83.7 48.8 %collective-permute-start.15 = (bf16[5,64,256]{2,1,0:T(8,128)(2,1)S(1)}, bf16[5,64,256]{2,1,0:T(8,128)(2,1)S(1)}, u32[]{:S(2)}, u32[]{:S(2)}) collective-permute-start(bf16[5,64,256]{2,1,0:T(8,128)(2,1)S(1)} %get-tuple-element.59), channel_id=1, source_target_pairs={{96,161},{97,162},{98,163},{99,164},{100,165},{101,166},{102,167},... | collective-permute-start | bytes 491528 | tf_op jit(solution)/shard_map/ppermute | solution.py:234
  85.0 48.4 %collective-permute-start.16 = (bf16[5,64,256]{2,1,0:T(8,128)(2,1)S(1)}, bf16[5,64,256]{2,1,0:T(8,128)(2,1)S(1)}, u32[]{:S(2)}, u32[]{:S(2)}) collective-permute-start(bf16[5,64,256]{2,1,0:T(8,128)(2,1)S(1)} %get-tuple-element.60), channel_id=1, source_target_pairs={{97,160},{98,161},{99,162},{100,163},{101,164},{102,165},{103,166}... | collective-permute-start | bytes 491528 | tf_op jit(solution)/shard_map/ppermute | solution.py:235
  145.4 10.1 %collective-permute-start.17 = (f32[8,64,256]{2,1,0:T(8,128)S(1)}, f32[8,64,256]{2,1,0:T(8,128)S(1)}, u32[]{:S(2)}, u32[]{:S(2)}) collective-permute-start(f32[8,64,256]{2,1,0:T(8,128)S(1)} %get-tuple-element.65), channel_id=1, source_target_pairs={{160,224},{161,225},{162,226},{163,227},{164,228},{165,229},{166,2... | collective-permute-start | bytes 1572872 | tf_op jit(solution)/shard_map/ppermute | solution.py:233
  146.7 7.7 %collective-permute-start.18 = (bf16[3,64,256]{2,1,0:T(8,128)(2,1)S(1)}, bf16[3,64,256]{2,1,0:T(8,128)(2,1)S(1)}, u32[]{:S(2)}, u32[]{:S(2)}) collective-permute-start(bf16[3,64,256]{2,1,0:T(8,128)(2,1)S(1)} %get-tuple-element.66), channel_id=1, source_target_pairs={{160,225},{161,226},{162,227},{163,228},{164,229},{165,230},{166,2... | collective-permute-start | bytes 294920 | tf_op jit(solution)/shard_map/ppermute | solution.py:234
  148.0 7.5 %collective-permute-start.19 = (bf16[3,64,256]{2,1,0:T(8,128)(2,1)S(1)}, bf16[3,64,256]{2,1,0:T(8,128)(2,1)S(1)}, u32[]{:S(2)}, u32[]{:S(2)}) collective-permute-start(bf16[3,64,256]{2,1,0:T(8,128)(2,1)S(1)} %get-tuple-element.67), channel_id=1, source_target_pairs={{161,224},{162,225},{163,226},{164,227},{165,228},{166,229},{167,2... | collective-permute-start | bytes 294920 | tf_op jit(solution)/shard_map/ppermute | solution.py:235
  149.3 14.6 %collective-permute-start.21 = (f32[12,64,256]{2,1,0:T(8,128)S(1)}, f32[12,64,256]{2,1,0:T(8,128)S(1)}, u32[]{:S(2)}, u32[]{:S(2)}) collective-permute-start(f32[12,64,256]{2,1,0:T(8,128)S(1)} %get-tuple-element.72), channel_id=1, source_target_pairs={{32,64},{33,65},{34,66},{35,67},{36,68},{37,69},{38,70},{39,71},{4... | collective-permute-start | bytes 2359304 | tf_op jit(solution)/shard_map/ppermute | solution.py:239
  150.7 21.7 %collective-permute-start.22 = (f32[12,64,256]{2,1,0:T(8,128)S(1)}, f32[12,64,256]{2,1,0:T(8,128)S(1)}, u32[]{:S(2)}, u32[]{:S(2)}) collective-permute-start(f32[12,64,256]{2,1,0:T(8,128)S(1)} %get-tuple-element.73), channel_id=1, source_target_pairs={{32,80},{33,81},{34,82},{35,83},{36,84},{37,85},{38,86},{39,87},{4... | collective-permute-start | bytes 2359304 | tf_op jit(solution)/shard_map/ppermute | solution.py:239
  156.1 16.3 %collective-permute-start.20 = (f32[12,64,256]{2,1,0:T(8,128)S(1)}, f32[12,64,256]{2,1,0:T(8,128)S(1)}, u32[]{:S(2)}, u32[]{:S(2)}) collective-permute-start(f32[12,64,256]{2,1,0:T(8,128)S(1)} %get-tuple-element.71), channel_id=1, source_target_pairs={{0,16},{1,17},{2,18},{3,19},{4,20},{5,21},{6,22},{7,23},{8,24},{9,... | collective-permute-start | bytes 2359304 | tf_op jit(solution)/shard_map/ppermute | solution.py:239
  191.3 14.4 %all-to-all-start.1 = ((f32[4,2,8,16,256]{4,3,2,1,0:T(8,128)}), f32[4,2,8,16,256]{4,3,2,1,0:T(8,128)S(1)}, u32[]{:S(2)}, u32[]{:S(2)}) async-start(f32[4,2,8,16,256]{4,3,2,1,0:T(8,128)} %get-tuple-element.74), calls=%async_computation.1 | async-start | bytes 2097152 | tf_op jit(solution)/shard_map/all_to_all | solution.py:251

commit v3 on v2

v3 whole, which is shorter than its diff:
```python
import functools

import jax
import jax.numpy as jnp
from jax import lax
from jax.experimental import pallas as pl
from jax.experimental.pallas import tpu as pltpu
from jax.sharding import PartitionSpec as P

AXES = ("depth", "rows", "cols")
BF16 = jnp.bfloat16
F32 = jnp.float32
KEPT = 2
FIRST, LONG, LAST = 3, 5, 3


def fill(patch, state, rows, first, height, columns=None):
    width, channels = state.shape[1:]
    column = lax.broadcasted_iota(jnp.int32, (width, channels), 0)
    if columns is not None:
        place = columns[1] + jnp.where(column < width - 4, column, column - width)
        inside = (place >= 0) & (place < columns[0])

    def body(row, carry):
        x = state[row]
        act = x / (1.0 + jnp.exp(-x))
        act = jnp.where((first + row >= 0) & (first + row < height), act, 0.0)
        if columns is not None:
            act = jnp.where(inside, act, 0.0)
        left = pltpu.roll(act, 1, 0)
        right = pltpu.roll(act, width - 1, 0)
        if columns is None:
            left = jnp.where(column == 0, 0.0, left)
            right = jnp.where(column == width - 1, 0.0, right)
        for tap, moved in enumerate((left, act, right)):
            patch[row, :, tap * channels : (tap + 1) * channels] = moved.astype(BF16)
        return carry

    lax.fori_loop(*rows, body, 0)


def strip_row(rows):
    return (lax.axis_index("rows") * lax.axis_size("cols") + lax.axis_index("cols")) * rows


def slope(patch, weight, first, rows):
    width, deep = patch.shape[1:]
    total = None
    for tap in range(3):
        part = jnp.dot(
            patch[first + tap : first + tap + rows].reshape(rows * width, deep),
            weight[tap],
            preferred_element_type=F32,
        )
        total = part if total is None else total + part
    return total.reshape(rows, width, -1)


def head_kernel(step, height, pieces, above, below, w0, w1, main, top, bottom, *rest):
    jumps, (state, middle, patch) = rest[:-3], rest[-3:]
    ncols, rows, wide = pieces.shape[:3]
    halo = above.shape[1]
    deep = rows + 2 * halo
    strip = strip_row(rows)
    for k in range(ncols):
        cut = slice(k * wide, (k + 1) * wide)
        state[:halo, cut] = above[k].astype(F32)
        state[halo : halo + rows, cut] = pieces[k]
        state[halo + rows :, cut] = below[k].astype(F32)
    main[...] = state[halo : halo + rows]
    top[...] = state[halo - FIRST : halo].astype(BF16)
    bottom[...] = state[halo + rows : halo + rows + FIRST].astype(BF16)
    fill(patch, state, (0, deep), strip - halo, height)
    first = slope(patch, w0, 0, deep - 2)
    middle[...] = state[1 : deep - 1] + step * first
    state[1 : deep - 1] = first
    fill(patch, middle, (0, deep - 2), strip + 1 - halo, height)
    jump = step * (slope(patch, w1, 0, deep - 4) - state[2 : deep - 2])
    for ref in jumps:
        cut = (deep - 4 - ref.shape[0]) // 2
        ref[...] = jump[cut : deep - 4 - cut].astype(ref.dtype)


def turn_kernel(host, count, last, given, step, height, main, top, bottom, *rest):
    weights, jumps = rest[:count], rest[count : 2 * count]
    rest = rest[2 * count + given :]
    kept = count + 1 if last else count
    if not last:
        out, out_top, out_bottom = rest[:3]
        rest = rest[3:]
    saved, (state, patch) = rest[:kept], rest[kept:]

    @pl.when(lax.axis_index("depth") == host)
    def _():
        rows, width, channels = main.shape
        halo = top.shape[0]
        strip = strip_row(rows)
        state[:halo] = top[...].astype(F32)
        state[halo : halo + rows] = main[...]
        state[halo + rows :] = bottom[...].astype(F32)
        saved[0][...] = state[halo - KEPT : halo + rows + KEPT]
        for k in range(count):
            far = halo - k - 1 if k < count - 1 or last else 0
            fill(patch, state, (halo - far - 1, halo + rows + far + 1), strip - halo, height)
            change = (2.0 * step) * slope(patch, weights[k], halo - far - 1, rows + 2 * far)
            cut = (jumps[k].shape[0] - rows) // 2 - far
            jump = jumps[k][cut : cut + rows + 2 * far].astype(F32)
            new = state[halo - far : halo + rows + far] + change + jump
            if k < kept - 1:
                state[halo - far : halo + rows + far] = new
                saved[k + 1][...] = new[far - KEPT : far + rows + KEPT]
            else:
                edge = out_top.shape[0]
                out[...] = new
                out_top[...] = new[:edge].astype(BF16)
                out_bottom[...] = new[rows - edge :].astype(BF16)


def pack_kernel(held, one, two, three, packed, state):
    depth = lax.axis_index("depth")
    role = jnp.where(depth < 2, depth, (depth - 2) % 4)
    for k, source in enumerate((held, one, two, three)):

        @pl.when(role == k)
        def _():
            state[...] = source[...]

    ncols = packed.shape[0]
    deep, width, channels = state.shape
    wide = width // ncols
    rows = deep - 2 * KEPT
    first = lax.axis_index("cols") == 0
    group = lax.broadcasted_iota(jnp.int32, (8, channels), 0)
    span = wide + 8
    for k in range(ncols):
        for row in range(rows + KEPT):
            if row < rows:
                line = lambda a, b: state[KEPT + row, a:b]
            else:
                line = lambda a, b: jnp.where(first, state[row - rows, a:b], state[KEPT + row, a:b])
            mine = line(k * wide, (k + 1) * wide)
            right = line((k + 1) * wide, (k + 1) * wide + 8) if k < ncols - 1 else jnp.zeros((8, channels), F32)
            left = line(k * wide - 8, k * wide) if k > 0 else jnp.zeros((8, channels), F32)
            high = mine.astype(BF16)
            packed[k, row * span : row * span + wide] = high
            packed[k, row * span + wide : (row + 1) * span] = jnp.where(group < 4, right, left).astype(BF16)
            if row < rows:
                start = (rows + KEPT) * span + row * wide
                packed[k, start : start + wide] = (mine - high.astype(F32)).astype(BF16)


def tail_kernel(step, height, width, packed, w0, w1, fine, coarse, state, middle, patch):
    ncols = packed.shape[0]
    tile_rows, wide = coarse.shape[:2]
    rows = tile_rows // ncols
    span = wide + 8
    for k in range(ncols):
        for row in range(rows):
            start = (rows + KEPT) * span + row * wide
            high = packed[k, row * span : (row + 1) * span].astype(F32)
            whole = high[:wide] + packed[k, start : start + wide].astype(F32)
            place = k * rows + row
            coarse[place] = whole
            state[KEPT + place, :wide] = whole
            state[KEPT + place, wide:] = high[wide:]
    for row in range(KEPT):
        cut = slice((rows + row) * span, (rows + row + 1) * span)
        state[row] = packed[0, cut].astype(F32)
        state[KEPT + tile_rows + row] = packed[ncols - 1, cut].astype(F32)
    top = lax.axis_index("rows") * tile_rows
    columns = (width, lax.axis_index("cols") * wide)
    fill(patch, state, (0, tile_rows + 4), top - 2, height, columns)
    middle[...] = state[1 : tile_rows + 3] + step * slope(patch, w0, 0, tile_rows + 2)
    fill(patch, middle, (0, tile_rows + 2), top - 1, height, columns)
    fine[0] = middle[1 : tile_rows + 1, :wide]
    ending = step * slope(patch, w1, 0, tile_rows)
    fine[1] = middle[1 : tile_rows + 1, :wide] + ending[:, :wide]


def call(kernel, outs, scratch, inputs, aliases={}, vmem=16 << 20):
    return pl.pallas_call(
        kernel,
        out_shape=[jax.ShapeDtypeStruct(*o) for o in outs],
        in_specs=[pl.BlockSpec(memory_space=pltpu.VMEM)] * len(inputs),
        out_specs=[pl.BlockSpec(memory_space=pltpu.VMEM)] * len(outs),
        scratch_shapes=scratch,
        input_output_aliases=aliases,
        compiler_params=pltpu.CompilerParams(vmem_limit_bytes=vmem),
    )(*inputs)


def on_device(section_states, weights):
    ndepth, nrows, ncols = (lax.axis_size(a) for a in AXES)
    tile = section_states[0]
    tile_rows, tile_cols, channels = tile.shape
    height, width = tile_rows * nrows, tile_cols * ncols
    rows = tile_rows // ncols
    strips = nrows * ncols
    step = 2.0 / (2 * ndepth)
    flat = weights.reshape(2, 3, 3 * channels, channels)
    w0, w1 = flat[0], flat[1]

    hosts = [0, *range(2, ndepth - 2, 4), ndepth - 2]
    counts = [2] + [4] * (len(hosts) - 2) + [1]
    halos = [FIRST] + [LONG] * (len(hosts) - 2) + [LAST]
    def route(pairs, shift):
        return [
            (a * strips + s, b * strips + (s + shift))
            for a, b in pairs
            for s in range(strips)
            if 0 <= s + shift < strips
        ]

    def fetch(x, k):
        return lax.ppermute(x, AXES, route([(h + k, h) for h, n in zip(hosts, counts) if n > k], 0))

    def ring(x, shift):
        return lax.ppermute(x, ("rows", "cols"), [(s, (s + shift) % strips) for s in range(strips)])

    pieces = lax.all_to_all(tile.reshape(ncols, rows, tile_cols, channels), "cols", 0, 0, tiled=True)
    near = LONG + 1
    above = ring(pieces[:, rows - near :].astype(BF16), 1)
    below = ring(pieces[:, :near].astype(BF16), -1)
    all_weights = [w0] + [fetch(w0, k) for k in (1, 2, 3)]
    like = lambda n, t=F32: ((n, width, channels), t)
    vm = lambda n: pltpu.VMEM((n, width, channels), F32)
    patch = lambda n: pltpu.VMEM((n, width, 3 * channels), BF16)
    deep = rows + 2 * near
    spans = [rows + 2 * (near - 2), rows + 2 * (near - 3), rows + 2 * (near - 4), rows]
    kinds = [F32, F32, BF16, BF16]
    main, top, bottom, *jumps = call(
        functools.partial(head_kernel, step, height),
        [like(rows), like(FIRST, BF16), like(FIRST, BF16)] + [like(n, t) for n, t in zip(spans, kinds)],
        [vm(deep), vm(deep - 2), patch(deep)],
        (pieces, above, below, w0, w1),
    )
    *all_weights[2:], jumps[2], jumps[3] = lax.optimization_barrier((*all_weights[2:], jumps[2], jumps[3]))
    fetched = [fetch(jumps[k], k) for k in (1, 2, 3)]
    main, top, bottom, *fetched = lax.optimization_barrier((main, top, bottom, *fetched))
    all_jumps = [jumps[0], *fetched]

    saved = []
    for turn, (host, count, halo) in enumerate(zip(hosts, counts, halos)):
        last = turn == len(hosts) - 1
        kept = count + 1 if last else count
        given = min(len(saved), kept)
        outs = [] if last else [like(rows), like(halos[turn + 1], BF16), like(halos[turn + 1], BF16)]
        inputs = (main, top, bottom, *all_weights[:count], *all_jumps[:count], *saved[:given])
        results = call(
            functools.partial(turn_kernel, host, count, last, given, step, height),
            outs + [like(rows + 2 * KEPT)] * kept,
            [vm(rows + 2 * halo), patch(rows + 2 * halo)],
            inputs,
            {len(inputs) - given + k: len(outs) + k for k in range(given)},
        )
        saved[:kept] = results[len(outs) :]
        if not last:
            pair = [(host, hosts[turn + 1])]
            main = lax.ppermute(results[0], AXES, route(pair, 0))
            top = lax.ppermute(results[2], AXES, route(pair, 1))
            bottom = lax.ppermute(results[1], AXES, route(pair, -1))

    def give(k):
        sized = [n + (n == 1) for n in counts]
        return lax.ppermute(saved[k], AXES, route([(h, h + k) for h, n in zip(hosts, sized) if n > k], 0))

    span = tile_cols + 8
    pixels = (rows + KEPT) * span + rows * tile_cols
    (packed,) = call(
        pack_kernel,
        [((ncols, pixels, channels), BF16)],
        [vm(rows + 2 * KEPT)],
        (saved[0], give(1), give(2), give(3)),
    )
    packed = lax.all_to_all(packed, "cols", 0, 0, tiled=True)
    tall = lambda n, t=F32, taps=1: pltpu.VMEM((n, span, taps * channels), t)
    fine, coarse = call(
        functools.partial(tail_kernel, step, height, width),
        [((2, *tile.shape), F32), (tile.shape, F32)],
        [tall(tile_rows + 4), tall(tile_rows + 2), tall(tile_rows + 4, BF16, 3)],
        (packed, w0, w1),
    )
    return fine, coarse[None]


def solution(mesh):
    in_specs = (P("depth", "rows", "cols", None), P("depth", None, None, None, None))
    out_specs = (P("depth", "rows", "cols", None), P("depth", "rows", "cols", None))
    return jax.shard_map(
        on_device, mesh=mesh, in_specs=in_specs, out_specs=out_specs, check_vma=False
    )
```

time: 208 us -> 176 us (0.85)
  the two profiles are of different devices: /device:TPU:162 before, /device:TPU:193 now
where the time goes in v3:
time: 176 us; the launch traced here: 175 us
  waiting for transfers between devices  106 us (60%)
  starting transfers between devices  32 us (18%)
  Pallas kernels  19.8 us (11%)
  blocking collectives  13.3 us (8%)
  local copies, waits for them, and re-layouts  1.85 us (1%)
    ppermute x3, waiting for transfers between devices, give(): lax.ppermute(saved[k], AXES, route([(h, h + k) for h, n in zip(hosts, siz...  90.4 us
    pallas_call x8, Pallas kernels, call(): pl.pallas_call(kernel, out_shape=[jax.ShapeDtypeStruct(*o) for o in outs]...  19.8 us
    all_to_all x1, blocking collectives, on_device(): packed = lax.all_to_all(packed, 'cols', 0, 0, tiled=True)  13.3 us
    ppermute x6, starting transfers between devices, fetch(): lax.ppermute(x, AXES, route([(h + k, h) for h, n in zip(hosts, counts) if...  11.7 us
    ppermute x2, waiting for transfers between devices, ring(): lax.ppermute(x, ('rows', 'cols'), [(s, (s + shift) % strips) for s in ran...  9.54 us
    ppermute x6, waiting for transfers between devices, fetch(): lax.ppermute(x, AXES, route([(h + k, h) for h, n in zip(hosts, counts) if...  6.07 us
    ppermute x2, starting transfers between devices, ring(): lax.ppermute(x, ('rows', 'cols'), [(s, (s + shift) % strips) for s in ran...  5.23 us
    all_to_all x1, starting transfers between devices, on_device(): lax.all_to_all(tile.reshape(ncols, rows, tile_cols, channels), 'cols', 0,...  4.2 us
  transfers between devices with their start and end apart: 24, of which 4 were waited for; matrix products, arithmetic and copies ran while one was open for 2% of the time, Pallas kernels for 5%

profile of v3, /device:TPU:193, one launch (start us, length us, event | category | flops | bytes accessed | tf_op | source)
XLA Modules:
  0.0 175.1 jit_solution(8897468179430305321)
XLA Ops:
  0.6 4.2 %all-to-all-start = ((f32[4,8,16,256]{3,2,1,0:T(8,128)}), f32[4,8,16,256]{3,2,1,0:T(8,128)}, u32[]{:S(2)}, u32[]{:S(2)}) async-start(f32[4,8,16,256]{3,2,1,0:T(8,128)} %bitcast.16), calls=%async_computation | async-start | bytes 1048576 | tf_op jit(solution)/shard_map/all_to_all | solution.py:220
  4.8 1.8 %fusion = (bf16[1,3,3,256,256]{4,3,2,1,0:T(8,128)(2,1)S(1)}, bf16[1,3,3,256,256]{4,3,2,1,0:T(8,128)(2,1)S(1)}) fusion(bf16[2,3,3,256,256]{4,3,2,1,0:T(8,128)(2,1)} %param.3), kind=kLoop, calls=%fused_computation | loop fusion | bytes 4718592 | tf_op jit(solution)/shard_map/slice | solution.py:201
  6.7 4.5 %collective-permute-start.4 = (bf16[3,768,256]{2,1,0:T(8,128)(2,1)S(1)}, bf16[3,768,256]{2,1,0:T(8,128)(2,1)}, u32[]{:S(2)}, u32[]{:S(2)}) collective-permute-start(bf16[3,768,256]{2,1,0:T(8,128)(2,1)S(1)} %bitcast.4), channel_id=1, source_target_pairs={{80,32},{81,33},{82,34},{83,35},{84,36},{85,37},{86,38},{87,39},{8... | collective-permute-start | bytes 3538952 | tf_op jit(solution)/shard_map/ppermute | solution.py:215
  11.2 1.7 collective-permute-start.3
  12.9 0.7 collective-permute-start.7
  13.6 0.0 all-to-all-done.pieces
  13.6 1.1 convert.4
  14.7 5.2 %collective-permute-start.1 = (bf16[4,6,16,256]{3,2,1,0:T(8,128)(2,1)S(1)}, bf16[4,6,16,256]{3,2,1,0:T(8,128)(2,1)S(1)}, u32[]{:S(2)}, u32[]{:S(2)}) collective-permute-start(bf16[4,6,16,256]{3,2,1,0:T(8,128)(2,1)S(1)} %get-tuple-element.98), channel_id=1, source_target_pairs={{0,15},{1,0},{2,1},{3,2},{4,3},{5,4},{6,5},{7,6},{8,7},{9,8},{10,9... | collective-permute-start | bytes 589832 | tf_op jit(solution)/shard_map/ppermute | solution.py:218
  19.9 4.3 %collective-permute-done.1.below = bf16[4,6,16,256]{3,2,1,0:T(8,128)(2,1)S(1)} collective-permute-done((bf16[4,6,16,256]{3,2,1,0:T(8,128)(2,1)S(1)}, bf16[4,6,16,256]{3,2,1,0:T(8,128)(2,1)S(1)}, u32[]{:S(2)}, u32[]{:S(2)}) %collective-permute-start.1) | collective-permute-done | bytes 196640 | tf_op jit(solution)/shard_map/ppermute | solution.py:218
  24.3 5.2 %collective-permute-done.above = bf16[4,6,16,256]{3,2,1,0:T(8,128)(2,1)S(1)} collective-permute-done((bf16[4,6,16,256]{3,2,1,0:T(8,128)(2,1)S(1)}, bf16[4,6,16,256]{3,2,1,0:T(8,128)(2,1)S(1)}, u32[]{:S(2)}, u32[]{:S(2)}) %collective-permute-start) | collective-permute-done | bytes 196640 | tf_op jit(solution)/shard_map/ppermute | solution.py:218
  29.5 8.0 %shard_map.41 = (f32[8,64,256]{2,1,0:T(8,128)S(1)}, bf16[3,64,256]{2,1,0:T(8,128)(2,1)S(1)}, bf16[3,64,256]{2,1,0:T(8,128)(2,1)S(1)}, f32[16,64,256]{2,1,0:T(8,1...) custom-call(f32[4,8,16,256]{3,2,1,0:T(8,128)} %all-to-all-done.pieces, ...), custom_call_target="tpu_custom_call" | custom-call | tf_op jit(solution)/shard_map/pallas_call | solution.py:181
  37.4 0.7 collective-permute-start.2
  38.2 0.0 collective-permute-done.4.rest_3_
  38.2 0.7 collective-permute-start.5
  38.9 3.4 %collective-permute-start.6 = (bf16[8,64,256]{2,1,0:T(8,128)(2,1)S(1)}, bf16[8,64,256]{2,1,0:T(8,128)(2,1)S(1)}, u32[]{:S(2)}, u32[]{:S(2)}) collective-permute-start(bf16[8,64,256]{2,1,0:T(8,128)(2,1)S(1)} %get-tuple-element.56), channel_id=1, source_target_pairs={{80,32},{81,33},{82,34},{83,35},{84,36},{85,37},{86,38},{87,39},{8... | collective-permute-start | bytes 786440 | tf_op jit(solution)/shard_map/ppermute | solution.py:215
  42.3 6.1 %collective-permute-done.6.rest_7_ = bf16[8,64,256]{2,1,0:T(8,128)(2,1)S(1)} collective-permute-done((bf16[8,64,256]{2,1,0:T(8,128)(2,1)S(1)}, bf16[8,64,256]{2,1,0:T(8,128)(2,1)S(1)}, u32[]{:S(2)}, u32[]{:S(2)}) %collective-permute-start.6) | collective-permute-done | bytes 262176 | tf_op jit(solution)/shard_map/ppermute | solution.py:215
  48.4 0.0 collective-permute-done.2.rest_3_.rest_5_
  48.4 0.0 collective-permute-done.5.rest_6_
  48.4 0.0 collective-permute-done.7.rest_1_
  48.4 0.7 collective-permute-start.8
  49.1 0.7 collective-permute-start.9
  49.8 0.7 collective-permute-start.10
  50.5 0.0 collective-permute-done.9.top
  50.5 1.6 shard_map.43
  52.1 0.7 collective-permute-start.11
  52.8 0.7 collective-permute-start.12
  53.5 0.7 collective-permute-start.13
  54.2 0.0 collective-permute-done.12.top
  54.2 0.0 collective-permute-done.11.main
  54.2 1.6 shard_map.44
  55.9 0.7 collective-permute-start.14
  56.5 0.7 collective-permute-start.15
  57.2 0.7 collective-permute-start.16
  57.9 0.0 collective-permute-done.16.bottom
  57.9 0.0 collective-permute-done.14.main
  57.9 1.6 shard_map.45
  59.6 0.7 collective-permute-start.17
  60.3 0.7 collective-permute-start.18
  60.9 0.7 collective-permute-start.19
  61.6 0.7 collective-permute-start.21
  62.3 1.3 collective-permute-start.22
  63.6 0.0 collective-permute-done.18.top
  63.6 0.0 collective-permute-done.19.bottom
  63.7 0.7 collective-permute-start.20
  64.4 90.4 %collective-permute-done.22.three = f32[12,64,256]{2,1,0:T(8,128)S(1)} collective-permute-done((f32[12,64,256]{2,1,0:T(8,128)S(1)}, f32[12,64,256]{2,1,0:T(8,128)S(1)}, u32[]{:S(2)}, u32[]{:S(2)}) %collective-permute-start.22) | collective-permute-done | bytes 786464 | tf_op jit(solution)/shard_map/ppermute | solution.py:265
  154.9 0.1 shard_map.47
  155.0 13.3 %all_to_all.10.packed = bf16[4,368,256]{2,1,0:T(8,128)(2,1)S(1)} all-to-all(bf16[4,368,256]{2,1,0:T(8,128)(2,1)S(1)} %shard_map.47), channel_id=1, replica_groups=mesh['depth'=16,'rows'=4,'cols'=4] {'cols'}, dimensions={0} | all-to-all | bytes 1507328 | tf_op jit(solution)/shard_map/all_to_all | solution.py:275
  168.3 6.8 %shard_map.48 = (f32[2,32,16,256]{3,2,1,0:T(8,128)}, f32[32,16,256]{2,1,0:T(8,128)}) custom-call(bf16[4,368,256]{2,1,0:T(8,128)(2,1)S(1)} %all_to_all.10.packed, bf16[3,768,256]{2,1,0:T(8,128)(2,1)S(1)} %bitcast.13, bf16[3,768,256]{2,1,0:T(8,128)(2,1)S(1)} %bitcast.15), custom_call_target="tpu_custom_call" | custom-call | tf_op jit(solution)/shard_map/pallas_call | solution.py:181
  (12 shorter events, 0.1 us)
Async XLA Ops:
  0.6 13.0 %all-to-all-start = ((f32[4,8,16,256]{3,2,1,0:T(8,128)}), f32[4,8,16,256]{3,2,1,0:T(8,128)}, u32[]{:S(2)}, u32[]{:S(2)}) async-start(f32[4,8,16,256]{3,2,1,0:T(8,128)} %bitcast.16), calls=%async_computation | async-start | bytes 1048576 | tf_op jit(solution)/shard_map/all_to_all | solution.py:220
  6.7 31.5 %collective-permute-start.4 = (bf16[3,768,256]{2,1,0:T(8,128)(2,1)S(1)}, bf16[3,768,256]{2,1,0:T(8,128)(2,1)}, u32[]{:S(2)}, u32[]{:S(2)}) collective-permute-start(bf16[3,768,256]{2,1,0:T(8,128)(2,1)S(1)} %bitcast.4), channel_id=1, source_target_pairs={{80,32},{81,33},{82,34},{83,35},{84,36},{85,37},{86,38},{87,39},{8... | collective-permute-start | bytes 3538952 | tf_op jit(solution)/shard_map/ppermute | solution.py:215
  11.2 27.0 %collective-permute-start.3 = (bf16[3,768,256]{2,1,0:T(8,128)(2,1)S(1)}, bf16[3,768,256]{2,1,0:T(8,128)(2,1)}, u32[]{:S(2)}, u32[]{:S(2)}) collective-permute-start(bf16[3,768,256]{2,1,0:T(8,128)(2,1)S(1)} %bitcast.5), channel_id=1, source_target_pairs={{64,32},{65,33},{66,34},{67,35},{68,36},{69,37},{70,38},{71,39},{7... | collective-permute-start | bytes 3538952 | tf_op jit(solution)/shard_map/ppermute | solution.py:215
  12.9 35.5 %collective-permute-start.7 = (bf16[3,768,256]{2,1,0:T(8,128)(2,1)S(1)}, bf16[3,768,256]{2,1,0:T(8,128)(2,1)S(1)}, u32[]{:S(2)}, u32[]{:S(2)}) collective-permute-start(bf16[3,768,256]{2,1,0:T(8,128)(2,1)S(1)} %bitcast.6), channel_id=1, source_target_pairs={{16,0},{17,1},{18,2},{19,3},{20,4},{21,5},{22,6},{23,7},{24,8},{25... | collective-permute-start | bytes 3538952 | tf_op jit(solution)/shard_map/ppermute | solution.py:215
  14.7 9.6 %collective-permute-start.1 = (bf16[4,6,16,256]{3,2,1,0:T(8,128)(2,1)S(1)}, bf16[4,6,16,256]{3,2,1,0:T(8,128)(2,1)S(1)}, u32[]{:S(2)}, u32[]{:S(2)}) collective-permute-start(bf16[4,6,16,256]{3,2,1,0:T(8,128)(2,1)S(1)} %get-tuple-element.98), channel_id=1, source_target_pairs={{0,15},{1,0},{2,1},{3,2},{4,3},{5,4},{6,5},{7,6},{8,7},{9,8},{10,9... | collective-permute-start | bytes 589832 | tf_op jit(solution)/shard_map/ppermute | solution.py:218
  19.9 9.5 %collective-permute-start = (bf16[4,6,16,256]{3,2,1,0:T(8,128)(2,1)S(1)}, bf16[4,6,16,256]{3,2,1,0:T(8,128)(2,1)S(1)}, u32[]{:S(2)}, u32[]{:S(2)}) collective-permute-start(bf16[4,6,16,256]{3,2,1,0:T(8,128)(2,1)S(1)} %get-tuple-element.99), channel_id=1, source_target_pairs={{0,1},{1,2},{2,3},{3,4},{4,5},{5,6},{6,7},{7,8},{8,9},{9,10},{10,1... | collective-permute-start | bytes 589832 | tf_op jit(solution)/shard_map/ppermute | solution.py:218
  37.4 10.9 %collective-permute-start.2 = (f32[14,64,256]{2,1,0:T(8,128)S(1)}, f32[14,64,256]{2,1,0:T(8,128)S(1)}, u32[]{:S(2)}, u32[]{:S(2)}) collective-permute-start(f32[14,64,256]{2,1,0:T(8,128)S(1)} %get-tuple-element.52), channel_id=1, source_target_pairs={{16,0},{17,1},{18,2},{19,3},{20,4},{21,5},{22,6},{23,7},{24,8},{25... | collective-permute-start | bytes 2752520 | tf_op jit(solution)/shard_map/ppermute | solution.py:215
  38.2 10.2 %collective-permute-start.5 = (bf16[12,64,256]{2,1,0:T(8,128)(2,1)S(1)}, bf16[12,64,256]{2,1,0:T(8,128)(2,1)S(1)}, u32[]{:S(2)}, u32[]{:S(2)}) collective-permute-start(bf16[12,64,256]{2,1,0:T(8,128)(2,1)S(1)} %get-tuple-element.55), channel_id=1, source_target_pairs={{64,32},{65,33},{66,34},{67,35},{68,36},{69,37},{70,38},{71,39},{7... | collective-permute-start | bytes 1179656 | tf_op jit(solution)/shard_map/ppermute | solution.py:215
  38.9 9.5 %collective-permute-start.6 = (bf16[8,64,256]{2,1,0:T(8,128)(2,1)S(1)}, bf16[8,64,256]{2,1,0:T(8,128)(2,1)S(1)}, u32[]{:S(2)}, u32[]{:S(2)}) collective-permute-start(bf16[8,64,256]{2,1,0:T(8,128)(2,1)S(1)} %get-tuple-element.56), channel_id=1, source_target_pairs={{80,32},{81,33},{82,34},{83,35},{84,36},{85,37},{86,38},{87,39},{8... | collective-permute-start | bytes 786440 | tf_op jit(solution)/shard_map/ppermute | solution.py:215
  48.4 2.1 %collective-permute-start.8 = (f32[8,64,256]{2,1,0:T(8,128)S(1)}, f32[8,64,256]{2,1,0:T(8,128)S(1)}, u32[]{:S(2)}, u32[]{:S(2)}) collective-permute-start(f32[8,64,256]{2,1,0:T(8,128)S(1)} %get-tuple-element.62), channel_id=1, source_target_pairs={{0,32},{1,33},{2,34},{3,35},{4,36},{5,37},{6,38},{7,39},{8,40},{9,... | collective-permute-start | bytes 1572872 | tf_op jit(solution)/shard_map/ppermute | solution.py:259
  49.1 1.4 collective-permute-start.9
  49.8 0.7 collective-permute-start.10
  52.1 2.1 %collective-permute-start.11 = (f32[8,64,256]{2,1,0:T(8,128)S(1)}, f32[8,64,256]{2,1,0:T(8,128)S(1)}, u32[]{:S(2)}, u32[]{:S(2)}) collective-permute-start(f32[8,64,256]{2,1,0:T(8,128)S(1)} %get-tuple-element.71), channel_id=1, source_target_pairs={{32,96},{33,97},{34,98},{35,99},{36,100},{37,101},{38,102},{39,103... | collective-permute-start | bytes 1572872 | tf_op jit(solution)/shard_map/ppermute | solution.py:259
  52.8 1.4 collective-permute-start.12
  53.5 0.7 collective-permute-start.13
  55.9 2.1 %collective-permute-start.14 = (f32[8,64,256]{2,1,0:T(8,128)S(1)}, f32[8,64,256]{2,1,0:T(8,128)S(1)}, u32[]{:S(2)}, u32[]{:S(2)}) collective-permute-start(f32[8,64,256]{2,1,0:T(8,128)S(1)} %get-tuple-element.78), channel_id=1, source_target_pairs={{96,160},{97,161},{98,162},{99,163},{100,164},{101,165},{102,166},... | collective-permute-start | bytes 1572872 | tf_op jit(solution)/shard_map/ppermute | solution.py:259
  56.5 1.4 collective-permute-start.15
  57.2 0.7 collective-permute-start.16
  59.6 4.1 %collective-permute-start.17 = (f32[8,64,256]{2,1,0:T(8,128)S(1)}, f32[8,64,256]{2,1,0:T(8,128)S(1)}, u32[]{:S(2)}, u32[]{:S(2)}) collective-permute-start(f32[8,64,256]{2,1,0:T(8,128)S(1)} %get-tuple-element.85), channel_id=1, source_target_pairs={{160,224},{161,225},{162,226},{163,227},{164,228},{165,229},{166,2... | collective-permute-start | bytes 1572872 | tf_op jit(solution)/shard_map/ppermute | solution.py:259
  60.3 3.4 %collective-permute-start.18 = (bf16[3,64,256]{2,1,0:T(8,128)(2,1)S(1)}, bf16[3,64,256]{2,1,0:T(8,128)(2,1)S(1)}, u32[]{:S(2)}, u32[]{:S(2)}) collective-permute-start(bf16[3,64,256]{2,1,0:T(8,128)(2,1)S(1)} %get-tuple-element.86), channel_id=1, source_target_pairs={{160,225},{161,226},{162,227},{163,228},{164,229},{165,230},{166,2... | collective-permute-start | bytes 294920 | tf_op jit(solution)/shard_map/ppermute | solution.py:260
  60.9 2.7 %collective-permute-start.19 = (bf16[3,64,256]{2,1,0:T(8,128)(2,1)S(1)}, bf16[3,64,256]{2,1,0:T(8,128)(2,1)S(1)}, u32[]{:S(2)}, u32[]{:S(2)}) collective-permute-start(bf16[3,64,256]{2,1,0:T(8,128)(2,1)S(1)} %get-tuple-element.87), channel_id=1, source_target_pairs={{161,224},{162,225},{163,226},{164,227},{165,228},{166,229},{167,2... | collective-permute-start | bytes 294920 | tf_op jit(solution)/shard_map/ppermute | solution.py:261
  61.6 2.8 %collective-permute-start.21 = (f32[12,64,256]{2,1,0:T(8,128)S(1)}, f32[12,64,256]{2,1,0:T(8,128)S(1)}, u32[]{:S(2)}, u32[]{:S(2)}) collective-permute-start(f32[12,64,256]{2,1,0:T(8,128)S(1)} %get-tuple-element.92), channel_id=1, source_target_pairs={{32,64},{33,65},{34,66},{35,67},{36,68},{37,69},{38,70},{39,71},{4... | collective-permute-start | bytes 2359304 | tf_op jit(solution)/shard_map/ppermute | solution.py:265
  62.3 92.5 %collective-permute-start.22 = (f32[12,64,256]{2,1,0:T(8,128)S(1)}, f32[12,64,256]{2,1,0:T(8,128)S(1)}, u32[]{:S(2)}, u32[]{:S(2)}) collective-permute-start(f32[12,64,256]{2,1,0:T(8,128)S(1)} %get-tuple-element.93), channel_id=1, source_target_pairs={{32,80},{33,81},{34,82},{35,83},{36,84},{37,85},{38,86},{39,87},{4... | collective-permute-start | bytes 2359304 | tf_op jit(solution)/shard_map/ppermute | solution.py:265
  63.7 91.2 %collective-permute-start.20 = (f32[12,64,256]{2,1,0:T(8,128)S(1)}, f32[12,64,256]{2,1,0:T(8,128)S(1)}, u32[]{:S(2)}, u32[]{:S(2)}) collective-permute-start(f32[12,64,256]{2,1,0:T(8,128)S(1)} %get-tuple-element.91), channel_id=1, source_target_pairs={{0,16},{1,17},{2,18},{3,19},{4,20},{5,21},{6,22},{7,23},{8,24},{9,... | collective-permute-start | bytes 2359304 | tf_op jit(solution)/shard_map/ppermute | solution.py:265

commit v4 on v3

v4 whole, which is shorter than its diff:
```python
import functools

import jax
import jax.numpy as jnp
from jax import lax
from jax.experimental import pallas as pl
from jax.experimental.pallas import tpu as pltpu
from jax.sharding import PartitionSpec as P

AXES = ("depth", "rows", "cols")
BF16 = jnp.bfloat16
F32 = jnp.float32
KEPT = 2
SLOTS = {"prev": -1, "own": 0, "core": 1, "next": 2}
JUMP_HALO = {"prev": 4, "own": 3, "core": 2, "next": 0}


CHUNK = 2


def fill_row(patch, row, x, valid, inside=None):
    width, channels = x.shape
    act = x / (1.0 + jnp.exp(-x))
    act = jnp.where(valid, act, 0.0)
    if inside is not None:
        act = jnp.where(inside, act, 0.0)
    left = pltpu.roll(act, 1, 0)
    right = pltpu.roll(act, width - 1, 0)
    if inside is None:
        column = lax.broadcasted_iota(jnp.int32, (width, channels), 0)
        left = jnp.where(column == 0, 0.0, left)
        right = jnp.where(column == width - 1, 0.0, right)
    for tap, moved in enumerate((left, act, right)):
        patch[row, :, tap * channels : (tap + 1) * channels] = moved.astype(BF16)


def fill(patch, state, rows, first, height, inside=None):
    def body(row, carry):
        fill_row(patch, row, state[row], (first + row >= 0) & (first + row < height), inside)
        return carry

    lax.fori_loop(0, rows, body, 0, unroll=2)


def slopes(patch, weight, first, rows, emit, chunk=CHUNK):
    width, deep = patch.shape[1:]
    for start in range(first, first + rows, chunk):
        count = min(chunk, first + rows - start)
        total = None
        for tap in range(3):
            part = jnp.dot(
                patch[start + tap - 1 : start + tap - 1 + count].reshape(count * width, deep),
                weight[tap],
                preferred_element_type=F32,
            )
            total = part if total is None else total + part
        total = total.reshape(count, width, -1)
        for k in range(count):
            emit(start + k, total[k])


def strip_row(rows):
    return (lax.axis_index("rows") * lax.axis_size("cols") + lax.axis_index("cols")) * rows


def head_kernel(step, height, pieces, above, below, w0, w1, main, top, bottom, *rest):
    jumps, (state, first, patch, second) = rest[:-4], rest[-4:]
    ncols, rows, wide = pieces.shape[:3]
    halo = above.shape[1]
    deep = rows + 2 * halo
    origin = strip_row(rows) - halo
    for k in range(ncols):
        cut = slice(k * wide, (k + 1) * wide)
        state[:halo, cut] = above[k].astype(F32)
        state[halo : halo + rows, cut] = pieces[k]
        state[halo + rows :, cut] = below[k].astype(F32)
    main[...] = state[halo : halo + rows]
    top[...] = state[halo - top.shape[0] : halo].astype(BF16)
    bottom[...] = state[halo + rows : halo + rows + bottom.shape[0]].astype(BF16)
    fill(patch, state, deep, origin, height)

    def to_middle(row, slope):
        first[row] = slope
        valid = (origin + row >= 0) & (origin + row < height)
        fill_row(second, row, state[row] + step * slope, valid)

    def to_jump(row, slope):
        jump = step * (slope - first[row])
        for ref in jumps:
            place = row - (deep - ref.shape[0]) // 2
            if 0 <= place < ref.shape[0]:
                ref[place] = jump.astype(ref.dtype)

    slopes(patch, w0, 1, deep - 2, to_middle)
    slopes(second, w1, 2, deep - 4, to_jump)


def turn_kernel(host, count, kept, given, last, step, height, main, top, bottom, *rest):
    weights, jumps = rest[:count], rest[count : 2 * count]
    rest = rest[2 * count + given :]
    if not last:
        out, out_top, out_bottom = rest[:3]
        rest = rest[3:]
    saved, (state, *patches) = rest[:kept], rest[kept:]

    @pl.when(lax.axis_index("depth") == host)
    def _():
        rows, width, channels = main.shape
        halo = top.shape[0]
        origin = strip_row(rows) - halo
        state[:halo] = top[...].astype(F32)
        state[halo : halo + rows] = main[...]
        state[halo + rows :] = bottom[...].astype(F32)
        saved[0][...] = state[halo - KEPT : halo + rows + KEPT]
        fill(patches[0], state, rows + 2 * halo, origin, height)
        for k in range(count):
            ends = k == count - 1
            far = 0 if ends and not last else halo - k - 1
            cut = halo - (jumps[k].shape[0] - rows) // 2

            def advance(row, slope):
                new = state[row] + (2.0 * step) * slope + jumps[k][row - cut].astype(F32)
                if k < kept - 1 and halo - KEPT <= row < halo + rows + KEPT:
                    saved[k + 1][row - halo + KEPT] = new
                if not ends:
                    state[row] = new
                    fill_row(patches[(k + 1) % 2], row, new, (origin + row >= 0) & (origin + row < height))
                elif not last:
                    place, edge = row - halo, out_top.shape[0]
                    out[place] = new
                    if place < edge:
                        out_top[place] = new.astype(BF16)
                    if place >= rows - edge:
                        out_bottom[place - rows + edge] = new.astype(BF16)

            slopes(patches[k % 2], weights[k], halo - far, rows + 2 * far, advance)


def pack_kernel(own, core, after, prev, packed, state):
    depth = lax.axis_index("depth")
    final = 4 * ((lax.axis_size("depth") - 1) // 4) + 2
    role = jnp.where(depth < final, depth % 4, depth - final)
    for k, source in enumerate((own, core, after, prev)):

        @pl.when(role == k)
        def _():
            state[...] = source[...]

    ncols = packed.shape[0]
    deep, width, channels = state.shape
    wide = width // ncols
    rows = deep - 2 * KEPT
    first = lax.axis_index("cols") == 0
    group = lax.broadcasted_iota(jnp.int32, (8, channels), 0)
    span = wide + 8
    for k in range(ncols):
        for row in range(rows + KEPT):
            if row < rows:
                line = lambda a, b: state[KEPT + row, a:b]
            else:
                line = lambda a, b: jnp.where(first, state[row - rows, a:b], state[KEPT + row, a:b])
            mine = line(k * wide, (k + 1) * wide)
            right = line((k + 1) * wide, (k + 1) * wide + 8) if k < ncols - 1 else jnp.zeros((8, channels), F32)
            left = line(k * wide - 8, k * wide) if k > 0 else jnp.zeros((8, channels), F32)
            high = mine.astype(BF16)
            packed[k, row * span : row * span + wide] = high
            packed[k, row * span + wide : (row + 1) * span] = jnp.where(group < 4, right, left).astype(BF16)
            if row < rows:
                start = (rows + KEPT) * span + row * wide
                packed[k, start : start + wide] = (mine - high.astype(F32)).astype(BF16)


def tail_kernel(step, height, width, packed, w0, w1, fine, coarse, state, patch, second):
    ncols = packed.shape[0]
    tile_rows, wide = coarse.shape[:2]
    rows = tile_rows // ncols
    span = wide + 8
    for k in range(ncols):
        for row in range(rows):
            start = (rows + KEPT) * span + row * wide
            high = packed[k, row * span : (row + 1) * span].astype(F32)
            whole = high[:wide] + packed[k, start : start + wide].astype(F32)
            place = k * rows + row
            coarse[place] = whole
            state[KEPT + place, :wide] = whole
            state[KEPT + place, wide:] = high[wide:]
    for row in range(KEPT):
        cut = slice((rows + row) * span, (rows + row + 1) * span)
        state[row] = packed[0, cut].astype(F32)
        state[KEPT + tile_rows + row] = packed[ncols - 1, cut].astype(F32)
    top = lax.axis_index("rows") * tile_rows - KEPT
    column = lax.broadcasted_iota(jnp.int32, (span, state.shape[2]), 0)
    place = lax.axis_index("cols") * wide + jnp.where(column < span - 4, column, column - span)
    inside = (place >= 0) & (place < width)
    fill(patch, state, tile_rows + 2 * KEPT, top, height, inside)

    def to_middle(row, slope):
        middle = state[row] + step * slope
        if KEPT <= row < KEPT + tile_rows:
            fine[0, row - KEPT] = middle[:wide]
        fill_row(second, row, middle, (top + row >= 0) & (top + row < height), inside)

    def to_ending(row, slope):
        fine[1, row - KEPT] = fine[0, row - KEPT] + step * slope[:wide]

    slopes(patch, w0, 1, tile_rows + 2, to_middle, 2 * CHUNK)
    slopes(second, w1, 2, tile_rows, to_ending, 2 * CHUNK)


def call(kernel, outs, scratch, inputs, aliases={}, vmem=12 << 20):
    return pl.pallas_call(
        kernel,
        out_shape=[jax.ShapeDtypeStruct(*o) for o in outs],
        in_specs=[pl.BlockSpec(memory_space=pltpu.VMEM)] * len(inputs),
        out_specs=[pl.BlockSpec(memory_space=pltpu.VMEM)] * len(outs),
        scratch_shapes=scratch,
        input_output_aliases=aliases,
        compiler_params=pltpu.CompilerParams(vmem_limit_bytes=vmem),
    )(*inputs)


def on_device(section_states, weights):
    ndepth, nrows, ncols = (lax.axis_size(a) for a in AXES)
    tile = section_states[0]
    tile_rows, tile_cols, channels = tile.shape
    height, width = tile_rows * nrows, tile_cols * ncols
    rows = tile_rows // ncols
    strips = nrows * ncols
    step = 2.0 / (2 * ndepth)
    flat = weights.reshape(2, 3, 3 * channels, channels)
    w0, w1 = flat[0], flat[1]

    hosts = [*range(0, ndepth, 4), ndepth - 2]
    visits = [["own", "core", "next"]] + [["prev", "own", "core", "next"]] * (len(hosts) - 2) + [["own"]]
    visits[-2] = ["prev", "own", "core"]
    halos = [len(v) + 1 for v in visits]
    halos[-1] += 1

    def route(pairs, shift):
        return [
            (a * strips + s, b * strips + (s + shift))
            for a, b in pairs
            for s in range(strips)
            if 0 <= s + shift < strips
        ]

    def fetch(x, slot):
        away = SLOTS[slot]
        return lax.ppermute(x, AXES, route([(h + away, h) for h, v in zip(hosts, visits) if slot in v], 0))

    def ring(x, shift):
        return lax.ppermute(x, ("rows", "cols"), [(s, (s + shift) % strips) for s in range(strips)])

    pieces = lax.all_to_all(tile.reshape(ncols, rows, tile_cols, channels), "cols", 0, 0, tiled=True)
    near = JUMP_HALO["prev"] + 2
    above = ring(pieces[:, rows - near :].astype(BF16), 1)
    below = ring(pieces[:, :near].astype(BF16), -1)
    far = ("core", "next", "prev")
    all_weights = {"own": w0} | {slot: fetch(w0, slot) for slot in far}
    like = lambda n, t=F32: ((n, width, channels), t)
    vm = lambda n: pltpu.VMEM((n, width, channels), F32)
    patch = lambda n: pltpu.VMEM((n, width, 3 * channels), BF16)
    deep = rows + 2 * near
    kinds = {"prev": BF16, "own": F32, "core": F32, "next": BF16}
    main, top, bottom, *jumps = call(
        functools.partial(head_kernel, step, height),
        [like(rows), like(halos[0], BF16), like(halos[0], BF16)]
        + [like(rows + 2 * JUMP_HALO[slot], kinds[slot]) for slot in SLOTS],
        [vm(deep), vm(deep), patch(deep), patch(deep)],
        (pieces, above, below, w0, w1),
    )
    all_jumps = dict(zip(SLOTS, jumps))
    all_jumps |= {slot: fetch(all_jumps[slot], slot) for slot in far}
    main, top, bottom, all_weights["prev"] = lax.optimization_barrier((main, top, bottom, all_weights["prev"]))

    saved = {}
    for turn, (host, visit, halo) in enumerate(zip(hosts, visits, halos)):
        last = turn == len(hosts) - 1
        keeps = [*visit, "core"] if last else visit
        given = [slot for slot in keeps if slot in saved]
        outs = [] if last else [like(rows), like(halos[turn + 1], BF16), like(halos[turn + 1], BF16)]
        inputs = (
            main, top, bottom,
            *(all_weights[slot] for slot in visit),
            *(all_jumps[slot] for slot in visit),
            *(saved[slot] for slot in given),
        )
        results = call(
            functools.partial(turn_kernel, host, len(visit), len(keeps), len(given), last, step, height),
            outs + [like(rows + 2 * KEPT)] * len(keeps),
            [vm(rows + 2 * halo), patch(rows + 2 * halo), patch(rows + 2 * halo)],
            inputs,
            {len(inputs) - len(given) + k: len(outs) + keeps.index(slot) for k, slot in enumerate(given)},
        )
        saved |= zip(keeps, results[len(outs) :])
        if not last:
            pair = [(host, hosts[turn + 1])]
            main = lax.ppermute(results[0], AXES, route(pair, 0))
            top = lax.ppermute(results[2], AXES, route(pair, 1))
            bottom = lax.ppermute(results[1], AXES, route(pair, -1))

    visits[-1] = ["own", "core"]

    def give(slot):
        away = SLOTS[slot]
        return lax.ppermute(saved[slot], AXES, route([(h, h + away) for h, v in zip(hosts, visits) if slot in v], 0))

    span = tile_cols + 8
    pixels = (rows + KEPT) * span + rows * tile_cols
    (packed,) = call(
        pack_kernel,
        [((ncols, pixels, channels), BF16)],
        [vm(rows + 2 * KEPT)],
        (saved["own"], give("core"), give("next"), give("prev")),
    )
    packed = lax.all_to_all(packed, "cols", 0, 0, tiled=True)
    tall = lambda n, t=F32, taps=1: pltpu.VMEM((n, span, taps * channels), t)
    fine, coarse = call(
        functools.partial(tail_kernel, step, height, width),
        [((2, *tile.shape), F32), (tile.shape, F32)],
        [tall(tile_rows + 4), tall(tile_rows + 4, BF16, 3), tall(tile_rows + 4, BF16, 3)],
        (packed, w0, w1),
    )
    return fine, coarse[None]


def solution(mesh):
    in_specs = (P("depth", "rows", "cols", None), P("depth", None, None, None, None))
    out_specs = (P("depth", "rows", "cols", None), P("depth", "rows", "cols", None))
    return jax.shard_map(
        on_device, mesh=mesh, in_specs=in_specs, out_specs=out_specs, check_vma=False
    )
```

time: 176 us -> 140 us (0.80)
  the two profiles are of different devices: /device:TPU:193 before, /device:TPU:226 now
where the time goes in v4:
time: 140 us; the launch traced here: 138 us
  waiting for transfers between devices  77.8 us (56%)
  starting transfers between devices  24.5 us (18%)
  Pallas kernels  15.6 us (11%)
  blocking collectives  15.1 us (11%)
  local copies, waits for them, and re-layouts  2.88 us (2%)
    ppermute x4, waiting for transfers between devices, on_device(): top = lax.ppermute(results[2], AXES, route(pair, 1))  65.5 us
    pallas_call x8, Pallas kernels, call(): pl.pallas_call(kernel, out_shape=[jax.ShapeDtypeStruct(*o) for o in outs]...  15.6 us
    all_to_all x1, blocking collectives, on_device(): packed = lax.all_to_all(packed, 'cols', 0, 0, tiled=True)  15.1 us
    ppermute x2, waiting for transfers between devices, ring(): lax.ppermute(x, ('rows', 'cols'), [(s, (s + shift) % strips) for s in ran...  6.89 us
    ppermute x6, starting transfers between devices, fetch(): lax.ppermute(x, AXES, route([(h + away, h) for h, v in zip(hosts, visits)...  5.24 us
    all_to_all x1, starting transfers between devices, on_device(): lax.all_to_all(tile.reshape(ncols, rows, tile_cols, channels), 'cols', 0,...  4.48 us
    all_to_all x1, waiting for transfers between devices, on_device(): lax.all_to_all(tile.reshape(ncols, rows, tile_cols, channels), 'cols', 0,...  3.57 us
    ppermute x4, starting transfers between devices, on_device(): main = lax.ppermute(results[0], AXES, route(pair, 0))  3.34 us
  transfers between devices with their start and end apart: 24, of which 5 were waited for; matrix products, arithmetic and copies ran while one was open for 3% of the time, Pallas kernels for 6%

profile of v4, /device:TPU:226, one launch (start us, length us, event | category | flops | bytes accessed | tf_op | source)
XLA Modules:
  0.0 138.1 jit_solution(1797710807767308726)
XLA Ops:
  0.6 4.5 %all-to-all-start = ((f32[4,8,16,256]{3,2,1,0:T(8,128)}), f32[4,8,16,256]{3,2,1,0:T(8,128)}, u32[]{:S(2)}, u32[]{:S(2)}) async-start(f32[4,8,16,256]{3,2,1,0:T(8,128)} %bitcast.16), calls=%async_computation | async-start | bytes 1048576 | tf_op jit(solution)/shard_map/all_to_all | solution.py:254
  5.1 2.8 %fusion = (bf16[1,3,3,256,256]{4,3,2,1,0:T(8,128)(2,1)}, bf16[1,3,3,256,256]{4,3,2,1,0:T(8,128)(2,1)S(1)}) fusion(bf16[2,3,3,256,256]{4,3,2,1,0:T(8,128)(2,1)} %param.3), kind=kLoop, calls=%fused_computation | loop fusion | bytes 4718592 | tf_op jit(solution)/shard_map/slice | solution.py:231
  7.9 1.7 %collective-permute-start.4 = (bf16[3,768,256]{2,1,0:T(8,128)(2,1)S(1)}, bf16[3,768,256]{2,1,0:T(8,128)(2,1)}, u32[]{:S(2)}, u32[]{:S(2)}) collective-permute-start(bf16[3,768,256]{2,1,0:T(8,128)(2,1)S(1)} %bitcast.4), channel_id=1, source_target_pairs={{32,0},{33,1},{34,2},{35,3},{36,4},{37,5},{38,6},{39,7},{40,8},{41... | collective-permute-start | bytes 3538952 | tf_op jit(solution)/shard_map/ppermute | solution.py:249
  9.6 0.7 collective-permute-start.3
  10.4 0.7 collective-permute-start.2
  11.1 3.6 %all-to-all-done.pieces = f32[4,8,16,256]{3,2,1,0:T(8,128)} async-done(((f32[4,8,16,256]{3,2,1,0:T(8,128)}), f32[4,8,16,256]{3,2,1,0:T(8,128)}, u32[]{:S(2)}, u32[]{:S(2)}) %all-to-all-start) | async-done | bytes 524320 | tf_op jit(solution)/shard_map/all_to_all | solution.py:254
  14.7 1.2 convert.4
  15.9 1.2 collective-permute-start.1
  17.1 0.9 collective-permute-start
  18.0 3.6 %collective-permute-done.1.below = bf16[4,6,16,256]{3,2,1,0:T(8,128)(2,1)S(1)} collective-permute-done((bf16[4,6,16,256]{3,2,1,0:T(8,128)(2,1)S(1)}, bf16[4,6,16,256]{3,2,1,0:T(8,128)(2,1)S(1)}, u32[]{:S(2)}, u32[]{:S(2)}) %collective-permute-start.1) | collective-permute-done | bytes 196640 | tf_op jit(solution)/shard_map/ppermute | solution.py:252
  21.6 3.2 %collective-permute-done.above = bf16[4,6,16,256]{3,2,1,0:T(8,128)(2,1)S(1)} collective-permute-done((bf16[4,6,16,256]{3,2,1,0:T(8,128)(2,1)S(1)}, bf16[4,6,16,256]{3,2,1,0:T(8,128)(2,1)S(1)}, u32[]{:S(2)}, u32[]{:S(2)}) %collective-permute-start) | collective-permute-done | bytes 196640 | tf_op jit(solution)/shard_map/ppermute | solution.py:252
  24.9 4.7 %shard_map.41 = (f32[8,64,256]{2,1,0:T(8,128)S(1)}, bf16[4,64,256]{2,1,0:T(8,128)(2,1)S(1)}, bf16[4,64,256]{2,1,0:T(8,128)(2,1)S(1)}, bf16[16,64,256]{2,1,0:T(8,...) custom-call(f32[4,8,16,256]{3,2,1,0:T(8,128)} %all-to-all-done.pieces, ...), custom_call_target="tpu_custom_call" | custom-call | tf_op jit(solution)/shard_map/pallas_call | solution.py:211
  29.6 0.7 collective-permute-start.5
  30.3 0.7 collective-permute-start.6
  31.0 0.0 collective-permute-done.2.rest_0_
  31.0 0.7 collective-permute-start.10
  31.7 0.0 collective-permute-done.6.rest_5_.rest_7_
  31.7 0.0 collective-permute-done.4.rest_2_.rest_3_
  31.7 0.0 collective-permute-done.5.rest_4_.rest_6_.rest_5_
  31.7 1.3 shard_map.42
  33.0 0.7 collective-permute-start.7
  33.7 0.7 collective-permute-start.8
  34.4 0.7 collective-permute-start.9
  35.1 0.0 collective-permute-done.8.top
  35.1 0.0 collective-permute-done.9.bottom
  35.1 1.3 shard_map.43
  36.4 0.7 collective-permute-start.11
  37.1 0.7 collective-permute-start.12
  37.7 0.7 collective-permute-start.13
  38.4 0.0 collective-permute-done.13.bottom
  38.4 0.0 collective-permute-done.11.main
  38.5 1.3 shard_map.44
  39.7 0.7 collective-permute-start.14
  40.4 0.7 collective-permute-start.15
  41.1 0.7 collective-permute-start.16
  41.8 0.2 shard_map.45
  42.1 1.3 collective-permute-start.17
  43.4 1.3 collective-permute-start.18
  44.7 1.3 collective-permute-start.19
  46.0 0.7 collective-permute-start.21
  46.7 0.7 collective-permute-start.22
  47.4 65.5 %collective-permute-done.18.top = bf16[3,64,256]{2,1,0:T(8,128)(2,1)S(1)} collective-permute-done((bf16[3,64,256]{2,1,0:T(8,128)(2,1)S(1)}, bf16[3,64,256]{2,1,0:T(8,128)(2,1)S(1)}, u32[]{:S(2)}, u32[]{:S(2)}) %collective-permute-start.18) | collective-permute-done | bytes 98336 | tf_op jit(solution)/shard_map/ppermute | solution.py:299
  112.9 1.7 %shard_map.46 = (f32[12,64,256]{2,1,0:T(8,128)S(1)}, f32[12,64,256]{2,1,0:T(8,128)S(1)}) custom-call(f32[8,64,256]{2,1,0:T(8,128)S(1)} %collective-permute-done.17.main, bf16[3,64,256]{2,1,0:T(8,128)(2,1)S(1)} %collective-permute-done.18.top, bf16[3,64,256]{2,1,0:T(8,128)(2,1)S(1)} %collective-permute-done.19.bottom, ...), custom_call_target="tpu_custom_call", output_to_operand_aliasing={{0}: (5, {}), {1}: (6, {})} | custom-call | tf_op jit(solution)/shard_map/pallas_call | solution.py:211
  114.6 1.3 collective-permute-start.20
  115.9 1.8 %collective-permute-done.20.core = f32[12,64,256]{2,1,0:T(8,128)S(1)} collective-permute-done((f32[12,64,256]{2,1,0:T(8,128)S(1)}, f32[12,64,256]{2,1,0:T(8,128)S(1)}, u32[]{:S(2)}, u32[]{:S(2)}) %collective-permute-start.20) | collective-permute-done | bytes 786464 | tf_op jit(solution)/shard_map/ppermute | solution.py:306
  117.8 0.1 shard_map.47
  117.9 15.1 %all_to_all.10.packed = bf16[4,368,256]{2,1,0:T(8,128)(2,1)S(1)} all-to-all(bf16[4,368,256]{2,1,0:T(8,128)(2,1)S(1)} %shard_map.47), channel_id=1, replica_groups=mesh['depth'=16,'rows'=4,'cols'=4] {'cols'}, dimensions={0} | all-to-all | bytes 1507328 | tf_op jit(solution)/shard_map/all_to_all | solution.py:316
  133.1 5.1 %shard_map.48 = (f32[2,32,16,256]{3,2,1,0:T(8,128)}, f32[32,16,256]{2,1,0:T(8,128)}) custom-call(bf16[4,368,256]{2,1,0:T(8,128)(2,1)S(1)} %all_to_all.10.packed, bf16[3,768,256]{2,1,0:T(8,128)(2,1)S(1)} %bitcast.13, bf16[3,768,256]{2,1,0:T(8,128)(2,1)S(1)} %bitcast.15), custom_call_target="tpu_custom_call" | custom-call | tf_op jit(solution)/shard_map/pallas_call | solution.py:211
  (14 shorter events, 0.1 us)
Async XLA Ops:
  0.6 14.1 %all-to-all-start = ((f32[4,8,16,256]{3,2,1,0:T(8,128)}), f32[4,8,16,256]{3,2,1,0:T(8,128)}, u32[]{:S(2)}, u32[]{:S(2)}) async-start(f32[4,8,16,256]{3,2,1,0:T(8,128)} %bitcast.16), calls=%async_computation | async-start | bytes 1048576 | tf_op jit(solution)/shard_map/all_to_all | solution.py:254
  7.9 23.8 %collective-permute-start.4 = (bf16[3,768,256]{2,1,0:T(8,128)(2,1)S(1)}, bf16[3,768,256]{2,1,0:T(8,128)(2,1)}, u32[]{:S(2)}, u32[]{:S(2)}) collective-permute-start(bf16[3,768,256]{2,1,0:T(8,128)(2,1)S(1)} %bitcast.4), channel_id=1, source_target_pairs={{32,0},{33,1},{34,2},{35,3},{36,4},{37,5},{38,6},{39,7},{40,8},{41... | collective-permute-start | bytes 3538952 | tf_op jit(solution)/shard_map/ppermute | solution.py:249
  9.6 22.1 %collective-permute-start.3 = (bf16[3,768,256]{2,1,0:T(8,128)(2,1)S(1)}, bf16[3,768,256]{2,1,0:T(8,128)(2,1)S(1)}, u32[]{:S(2)}, u32[]{:S(2)}) collective-permute-start(bf16[3,768,256]{2,1,0:T(8,128)(2,1)S(1)} %bitcast.5), channel_id=1, source_target_pairs={{16,0},{17,1},{18,2},{19,3},{20,4},{21,5},{22,6},{23,7},{24,8},{25... | collective-permute-start | bytes 3538952 | tf_op jit(solution)/shard_map/ppermute | solution.py:249
  10.4 20.6 %collective-permute-start.2 = (bf16[3,768,256]{2,1,0:T(8,128)(2,1)S(1)}, bf16[3,768,256]{2,1,0:T(8,128)(2,1)S(1)}, u32[]{:S(2)}, u32[]{:S(2)}) collective-permute-start(bf16[3,768,256]{2,1,0:T(8,128)(2,1)S(1)} %bitcast.6), channel_id=1, source_target_pairs={{48,64},{49,65},{50,66},{51,67},{52,68},{53,69},{54,70},{55,71},{5... | collective-permute-start | bytes 3538952 | tf_op jit(solution)/shard_map/ppermute | solution.py:249
  14.7 10.2 %copy-start = (bf16[1,3,3,256,256]{4,3,2,1,0:T(8,128)(2,1)S(1)}, bf16[1,3,3,256,256]{4,3,2,1,0:T(8,128)(2,1)}, u32[]{:S(2)}) copy-start(bf16[1,3,3,256,256]{4,3,2,1,0:T(8,128)(2,1)} %get-tuple-element.84) | copy-start | bytes 3538948
  15.9 5.7 %collective-permute-start.1 = (bf16[4,6,16,256]{3,2,1,0:T(8,128)(2,1)S(1)}, bf16[4,6,16,256]{3,2,1,0:T(8,128)(2,1)S(1)}, u32[]{:S(2)}, u32[]{:S(2)}) collective-permute-start(bf16[4,6,16,256]{3,2,1,0:T(8,128)(2,1)S(1)} %get-tuple-element.86), channel_id=1, source_target_pairs={{0,15},{1,0},{2,1},{3,2},{4,3},{5,4},{6,5},{7,6},{8,7},{9,8},{10,9... | collective-permute-start | bytes 589832 | tf_op jit(solution)/shard_map/ppermute | solution.py:252
  17.1 7.8 %collective-permute-start = (bf16[4,6,16,256]{3,2,1,0:T(8,128)(2,1)S(1)}, bf16[4,6,16,256]{3,2,1,0:T(8,128)(2,1)S(1)}, u32[]{:S(2)}, u32[]{:S(2)}) collective-permute-start(bf16[4,6,16,256]{3,2,1,0:T(8,128)(2,1)S(1)} %get-tuple-element.87), channel_id=1, source_target_pairs={{0,1},{1,2},{2,3},{3,4},{4,5},{5,6},{6,7},{7,8},{8,9},{9,10},{10,1... | collective-permute-start | bytes 589832 | tf_op jit(solution)/shard_map/ppermute | solution.py:252
  29.6 2.2 %collective-permute-start.5 = (f32[12,64,256]{2,1,0:T(8,128)S(1)}, f32[12,64,256]{2,1,0:T(8,128)S(1)}, u32[]{:S(2)}, u32[]{:S(2)}) collective-permute-start(f32[12,64,256]{2,1,0:T(8,128)S(1)} %get-tuple-element.50), channel_id=1, source_target_pairs={{16,0},{17,1},{18,2},{19,3},{20,4},{21,5},{22,6},{23,7},{24,8},{25... | collective-permute-start | bytes 2359304 | tf_op jit(solution)/shard_map/ppermute | solution.py:249
  30.3 1.4 %collective-permute-start.6 = (bf16[8,64,256]{2,1,0:T(8,128)(2,1)S(1)}, bf16[8,64,256]{2,1,0:T(8,128)(2,1)S(1)}, u32[]{:S(2)}, u32[]{:S(2)}) collective-permute-start(bf16[8,64,256]{2,1,0:T(8,128)(2,1)S(1)} %get-tuple-element.51), channel_id=1, source_target_pairs={{32,0},{33,1},{34,2},{35,3},{36,4},{37,5},{38,6},{39,7},{40,8},{41... | collective-permute-start | bytes 786440 | tf_op jit(solution)/shard_map/ppermute | solution.py:249
  31.0 4.1 %collective-permute-start.10 = (bf16[16,64,256]{2,1,0:T(8,128)(2,1)S(1)}, bf16[16,64,256]{2,1,0:T(8,128)(2,1)S(1)}, u32[]{:S(2)}, u32[]{:S(2)}) collective-permute-start(bf16[16,64,256]{2,1,0:T(8,128)(2,1)S(1)} %get-tuple-element.56), channel_id=1, source_target_pairs={{48,64},{49,65},{50,66},{51,67},{52,68},{53,69},{54,70},{55,71},{5... | collective-permute-start | bytes 1572872 | tf_op jit(solution)/shard_map/ppermute | solution.py:249
  33.0 2.1 %collective-permute-start.7 = (f32[8,64,256]{2,1,0:T(8,128)S(1)}, f32[8,64,256]{2,1,0:T(8,128)S(1)}, u32[]{:S(2)}, u32[]{:S(2)}) collective-permute-start(f32[8,64,256]{2,1,0:T(8,128)S(1)} %get-tuple-element.52), channel_id=1, source_target_pairs={{0,64},{1,65},{2,66},{3,67},{4,68},{5,69},{6,70},{7,71},{8,72},{9,... | collective-permute-start | bytes 1572872 | tf_op jit(solution)/shard_map/ppermute | solution.py:298
  33.7 1.4 collective-permute-start.8
  34.4 0.7 collective-permute-start.9
  36.4 2.1 %collective-permute-start.11 = (f32[8,64,256]{2,1,0:T(8,128)S(1)}, f32[8,64,256]{2,1,0:T(8,128)S(1)}, u32[]{:S(2)}, u32[]{:S(2)}) collective-permute-start(f32[8,64,256]{2,1,0:T(8,128)S(1)} %get-tuple-element.60), channel_id=1, source_target_pairs={{64,128},{65,129},{66,130},{67,131},{68,132},{69,133},{70,134},{71... | collective-permute-start | bytes 1572872 | tf_op jit(solution)/shard_map/ppermute | solution.py:298
  37.1 1.4 collective-permute-start.12
  37.7 0.7 collective-permute-start.13
  39.7 2.1 %collective-permute-start.14 = (f32[8,64,256]{2,1,0:T(8,128)S(1)}, f32[8,64,256]{2,1,0:T(8,128)S(1)}, u32[]{:S(2)}, u32[]{:S(2)}) collective-permute-start(f32[8,64,256]{2,1,0:T(8,128)S(1)} %get-tuple-element.67), channel_id=1, source_target_pairs={{128,192},{129,193},{130,194},{131,195},{132,196},{133,197},{134,1... | collective-permute-start | bytes 1572872 | tf_op jit(solution)/shard_map/ppermute | solution.py:298
  40.4 1.4 collective-permute-start.15
  41.1 0.7 collective-permute-start.16
  42.1 70.8 %collective-permute-start.17 = (f32[8,64,256]{2,1,0:T(8,128)S(1)}, f32[8,64,256]{2,1,0:T(8,128)S(1)}, u32[]{:S(2)}, u32[]{:S(2)}) collective-permute-start(f32[8,64,256]{2,1,0:T(8,128)S(1)} %get-tuple-element.73), channel_id=1, source_target_pairs={{192,224},{193,225},{194,226},{195,227},{196,228},{197,229},{198,2... | collective-permute-start | bytes 1572872 | tf_op jit(solution)/shard_map/ppermute | solution.py:298
  43.4 69.5 %collective-permute-start.18 = (bf16[3,64,256]{2,1,0:T(8,128)(2,1)S(1)}, bf16[3,64,256]{2,1,0:T(8,128)(2,1)S(1)}, u32[]{:S(2)}, u32[]{:S(2)}) collective-permute-start(bf16[3,64,256]{2,1,0:T(8,128)(2,1)S(1)} %get-tuple-element.74), channel_id=1, source_target_pairs={{192,225},{193,226},{194,227},{195,228},{196,229},{197,230},{198,2... | collective-permute-start | bytes 294920 | tf_op jit(solution)/shard_map/ppermute | solution.py:299
  44.7 68.2 %collective-permute-start.19 = (bf16[3,64,256]{2,1,0:T(8,128)(2,1)S(1)}, bf16[3,64,256]{2,1,0:T(8,128)(2,1)S(1)}, u32[]{:S(2)}, u32[]{:S(2)}) collective-permute-start(bf16[3,64,256]{2,1,0:T(8,128)(2,1)S(1)} %get-tuple-element.75), channel_id=1, source_target_pairs={{193,224},{194,225},{195,226},{196,227},{197,228},{198,229},{199,2... | collective-permute-start | bytes 294920 | tf_op jit(solution)/shard_map/ppermute | solution.py:300
  46.0 70.0 %collective-permute-start.21 = (f32[12,64,256]{2,1,0:T(8,128)S(1)}, f32[12,64,256]{2,1,0:T(8,128)S(1)}, u32[]{:S(2)}, u32[]{:S(2)}) collective-permute-start(f32[12,64,256]{2,1,0:T(8,128)S(1)} %get-tuple-element.80), channel_id=1, source_target_pairs={{0,32},{1,33},{2,34},{3,35},{4,36},{5,37},{6,38},{7,39},{8,40},{9,... | collective-permute-start | bytes 2359304 | tf_op jit(solution)/shard_map/ppermute | solution.py:306
  46.7 69.3 %collective-permute-start.22 = (f32[12,64,256]{2,1,0:T(8,128)S(1)}, f32[12,64,256]{2,1,0:T(8,128)S(1)}, u32[]{:S(2)}, u32[]{:S(2)}) collective-permute-start(f32[12,64,256]{2,1,0:T(8,128)S(1)} %get-tuple-element.81), channel_id=1, source_target_pairs={{64,48},{65,49},{66,50},{67,51},{68,52},{69,53},{70,54},{71,55},{7... | collective-permute-start | bytes 2359304 | tf_op jit(solution)/shard_map/ppermute | solution.py:306
  114.6 3.2 %collective-permute-start.20 = (f32[12,64,256]{2,1,0:T(8,128)S(1)}, f32[12,64,256]{2,1,0:T(8,128)S(1)}, u32[]{:S(2)}, u32[]{:S(2)}) collective-permute-start(f32[12,64,256]{2,1,0:T(8,128)S(1)} %get-tuple-element.79), channel_id=1, source_target_pairs={{0,16},{1,17},{2,18},{3,19},{4,20},{5,21},{6,22},{7,23},{8,24},{9,... | collective-permute-start | bytes 2359304 | tf_op jit(solution)/shard_map/ppermute | solution.py:306

commit v5 on v4

--- a/solution.py
+++ b/solution.py
@@ -63,6 +63,16 @@
     return (lax.axis_index("rows") * lax.axis_size("cols") + lax.axis_index("cols")) * rows
 
 
+def hold_kernel(given, held):
+    held[...] = given[...]
+
+
+def edge_kernel(pieces, low, high):
+    rows, count = pieces.shape[1], low.shape[1]
+    low[...] = pieces[:, :count].astype(BF16)
+    high[...] = pieces[:, rows - count :].astype(BF16)
+
+
 def head_kernel(step, height, pieces, above, below, w0, w1, main, top, bottom, *rest):
     jumps, (state, first, patch, second) = rest[:-4], rest[-4:]
     ncols, rows, wide = pieces.shape[:3]
@@ -95,7 +105,10 @@
     slopes(second, w1, 2, deep - 4, to_jump)
 
 
-def turn_kernel(host, count, kept, given, last, step, height, main, top, bottom, *rest):
+def turn_kernel(host, rows, count, kept, given, last, step, height, *rest):
+    outs = 0 if last else 3
+    begin = len(rest) - (2 * count + given + outs + kept + 3)
+    start, rest = rest[:begin], rest[begin:]
     weights, jumps = rest[:count], rest[count : 2 * count]
     rest = rest[2 * count + given :]
     if not last:
@@ -105,13 +118,17 @@
 
     @pl.when(lax.axis_index("depth") == host)
     def _():
-        rows, width, channels = main.shape
-        halo = top.shape[0]
+        halo = (state.shape[0] - rows) // 2
         origin = strip_row(rows) - halo
-        state[:halo] = top[...].astype(F32)
-        state[halo : halo + rows] = main[...]
-        state[halo + rows :] = bottom[...].astype(F32)
-        saved[0][...] = state[halo - KEPT : halo + rows + KEPT]
+        if len(start) == 1:
+            state[...] = start[0][...]
+        else:
+            main, top, bottom = start
+            state[:halo] = top[...].astype(F32)
+            state[halo : halo + rows] = main[...]
+            state[halo + rows :] = bottom[...].astype(F32)
+        if kept:
+            saved[0][...] = state[halo - KEPT : halo + rows + KEPT]
         fill(patches[0], state, rows + 2 * halo, origin, height)
         for k in range(count):
             ends = k == count - 1
@@ -253,9 +270,9 @@
 
     pieces = lax.all_to_all(tile.reshape(ncols, rows, tile_cols, channels), "cols", 0, 0, tiled=True)
     near = JUMP_HALO["prev"] + 2
-    above = ring(pieces[:, rows - near :].astype(BF16), 1)
-    below = ring(pieces[:, :near].astype(BF16), -1)
-    far = ("core", "next", "prev")
+    low, high = call(edge_kernel, [((ncols, near, tile_cols, channels), BF16)] * 2, [], (pieces,))
+    above, below = ring(high, 1), ring(low, -1)
+    far = ("next", "core", "prev")
     all_weights = {"own": w0} | {slot: fetch(w0, slot) for slot in far}
     like = lambda n, t=F32: ((n, width, channels), t)
     vm = lambda n: pltpu.VMEM((n, width, channels), F32)
@@ -274,30 +291,38 @@
     main, top, bottom, all_weights["prev"] = lax.optimization_barrier((main, top, bottom, all_weights["prev"]))
 
     saved = {}
-    for turn, (host, visit, halo) in enumerate(zip(hosts, visits, halos)):
-        last = turn == len(hosts) - 1
-        keeps = [*visit, "core"] if last else visit
+    start = (main, top, bottom)
+    turns = list(zip(hosts, visits, halos))
+    turns[:1] = [(hosts[0], visits[0][:-1], halos[0]), (hosts[0], visits[0][-1:], KEPT)]
+    for turn, (host, visit, halo) in enumerate(turns):
+        last = turn in (0, len(turns) - 1)
+        keeps = [] if turn == 1 else [*visit, "next" if turn == 0 else "core"] if last else visit
         given = [slot for slot in keeps if slot in saved]
-        outs = [] if last else [like(rows), like(halos[turn + 1], BF16), like(halos[turn + 1], BF16)]
+        outs = [] if last else [like(rows)] + [like(turns[turn + 1][2], BF16)] * 2
         inputs = (
-            main, top, bottom,
+            *start,
             *(all_weights[slot] for slot in visit),
             *(all_jumps[slot] for slot in visit),
             *(saved[slot] for slot in given),
         )
         results = call(
-            functools.partial(turn_kernel, host, len(visit), len(keeps), len(given), last, step, height),
+            functools.partial(turn_kernel, host, rows, len(visit), len(keeps), len(given), last, step, height),
             outs + [like(rows + 2 * KEPT)] * len(keeps),
             [vm(rows + 2 * halo), patch(rows + 2 * halo), patch(rows + 2 * halo)],
             inputs,
             {len(inputs) - len(given) + k: len(outs) + keeps.index(slot) for k, slot in enumerate(given)},
         )
         saved |= zip(keeps, results[len(outs) :])
-        if not last:
-            pair = [(host, hosts[turn + 1])]
+        if turn == 0:
+            start = (saved["next"],)
+            weight = all_weights["next"]
+            (all_weights["next"],) = call(hold_kernel, [(weight.shape, BF16)], [], (weight,))
+        elif not last:
+            pair = [(host, turns[turn + 1][0])]
             main = lax.ppermute(results[0], AXES, route(pair, 0))
             top = lax.ppermute(results[2], AXES, route(pair, 1))
             bottom = lax.ppermute(results[1], AXES, route(pair, -1))
+            start = (main, top, bottom)
 
     visits[-1] = ["own", "core"]
 

time: 140 us -> 136 us (0.971)
  waiting for transfers between devices: 77.8 us -> 72 us
  starting transfers between devices: 24.5 us -> 26.7 us
  blocking collectives: 15.1 us -> 17.2 us
    ppermute x2, waiting for transfers between devices: 6.89 us -> 3.65 us  [ring(): lax.ppermute(x, ('rows', 'cols'), [(s, (s + shift) % strips) for s in ran...]
    ppermute x4, waiting for transfers between devices: 65.5 us -> 62.8 us  [on_device(): top = lax.ppermute(results[2], AXES, route(pair, 1))]
    ppermute x2, starting transfers between devices: 2.1 us -> 4.21 us  [ring(): lax.ppermute(x, ('rows', 'cols'), [(s, (s + shift) % strips) for s in ran...]
    all_to_all x1, blocking collectives: 15.1 us -> 17.2 us  [on_device(): packed = lax.all_to_all(packed, 'cols', 0, 0, tiled=True)]
    pallas_call x8 -> x11, Pallas kernels: 15.6 us -> 14.4 us  [call(): pl.pallas_call(kernel, out_shape=[jax.ShapeDtypeStruct(*o) for o in outs]...]
  transfers between devices with their start and end apart: 24 -> 24, of which waited for: 5 -> 5; matrix products, arithmetic and copies ran while one was open for 3% -> 2% of each run, Pallas kernels for 6% -> 6%
where the time goes in v5:
time: 136 us; the launch traced here: 135 us
  waiting for transfers between devices  72 us (53%)
  starting transfers between devices  26.7 us (20%)
  blocking collectives  17.2 us (13%)
  Pallas kernels  14.4 us (11%)
  local copies, waits for them, and re-layouts  4.13 us (3%)
    ppermute x4, waiting for transfers between devices, on_device(): top = lax.ppermute(results[2], AXES, route(pair, 1))  62.8 us
    all_to_all x1, blocking collectives, on_device(): packed = lax.all_to_all(packed, 'cols', 0, 0, tiled=True)  17.2 us
    pallas_call x11, Pallas kernels, call(): pl.pallas_call(kernel, out_shape=[jax.ShapeDtypeStruct(*o) for o in outs]...  14.4 us
    ppermute x6, starting transfers between devices, fetch(): lax.ppermute(x, AXES, route([(h + away, h) for h, v in zip(hosts, visits)...  5.22 us
    all_to_all x1, starting transfers between devices, on_device(): lax.all_to_all(tile.reshape(ncols, rows, tile_cols, channels), 'cols', 0,...  4.48 us
    ppermute x2, starting transfers between devices, ring(): lax.ppermute(x, ('rows', 'cols'), [(s, (s + shift) % strips) for s in ran...  4.21 us
    ppermute x2, waiting for transfers between devices, ring(): lax.ppermute(x, ('rows', 'cols'), [(s, (s + shift) % strips) for s in ran...  3.65 us
    all_to_all x1, waiting for transfers between devices, on_device(): lax.all_to_all(tile.reshape(ncols, rows, tile_cols, channels), 'cols', 0,...  3.57 us
  transfers between devices with their start and end apart: 24, of which 5 were waited for; matrix products, arithmetic and copies ran while one was open for 2% of the time, Pallas kernels for 6%

profile of v5, /device:TPU:226, one launch (start us, length us, event | category | flops | bytes accessed | tf_op | source)
XLA Modules:
  0.0 135.5 jit_solution(8471499798951593621)
XLA Ops:
  0.6 4.5 %all-to-all-start = ((f32[4,8,16,256]{3,2,1,0:T(8,128)}), f32[4,8,16,256]{3,2,1,0:T(8,128)}, u32[]{:S(2)}, u32[]{:S(2)}) async-start(f32[4,8,16,256]{3,2,1,0:T(8,128)} %bitcast.16), calls=%async_computation | async-start | bytes 1048576 | tf_op jit(solution)/shard_map/all_to_all | solution.py:271
  5.1 2.9 %fusion = (bf16[1,3,3,256,256]{4,3,2,1,0:T(8,128)(2,1)}, bf16[1,3,3,256,256]{4,3,2,1,0:T(8,128)(2,1)S(1)}) fusion(bf16[2,3,3,256,256]{4,3,2,1,0:T(8,128)(2,1)} %param.3), kind=kLoop, calls=%fused_computation | loop fusion | bytes 4718592 | tf_op jit(solution)/shard_map/slice | solution.py:248
  8.0 0.7 collective-permute-start.2
  8.7 1.7 %collective-permute-start.5 = (bf16[3,768,256]{2,1,0:T(8,128)(2,1)S(1)}, bf16[3,768,256]{2,1,0:T(8,128)(2,1)}, u32[]{:S(2)}, u32[]{:S(2)}) collective-permute-start(bf16[3,768,256]{2,1,0:T(8,128)(2,1)S(1)} %bitcast.5), channel_id=1, source_target_pairs={{32,0},{33,1},{34,2},{35,3},{36,4},{37,5},{38,6},{39,7},{40,8},{41... | collective-permute-start | bytes 3538952 | tf_op jit(solution)/shard_map/ppermute | solution.py:266
  10.4 0.7 collective-permute-start.3
  11.1 3.6 %all-to-all-done.pieces = f32[4,8,16,256]{3,2,1,0:T(8,128)} async-done(((f32[4,8,16,256]{3,2,1,0:T(8,128)}), f32[4,8,16,256]{3,2,1,0:T(8,128)}, u32[]{:S(2)}, u32[]{:S(2)}) %all-to-all-start) | async-done | bytes 524320 | tf_op jit(solution)/shard_map/all_to_all | solution.py:271
  14.7 1.1 shard_map.41
  15.8 0.6 collective-permute-start
  16.4 3.6 %collective-permute-start.1 = (bf16[4,6,16,256]{3,2,1,0:T(8,128)(2,1)S(1)}, bf16[4,6,16,256]{3,2,1,0:T(8,128)(2,1)S(1)}, u32[]{:S(2)}, u32[]{:S(2)}) collective-permute-start(bf16[4,6,16,256]{3,2,1,0:T(8,128)(2,1)S(1)} %get-tuple-element.46), channel_id=1, source_target_pairs={{0,15},{1,0},{2,1},{3,2},{4,3},{5,4},{6,5},{7,6},{8,7},{9,8},{10,9... | collective-permute-start | bytes 589832 | tf_op jit(solution)/shard_map/ppermute | solution.py:269
  20.0 3.6 %collective-permute-done.above = bf16[4,6,16,256]{3,2,1,0:T(8,128)(2,1)S(1)} collective-permute-done((bf16[4,6,16,256]{3,2,1,0:T(8,128)(2,1)S(1)}, bf16[4,6,16,256]{3,2,1,0:T(8,128)(2,1)S(1)}, u32[]{:S(2)}, u32[]{:S(2)}) %collective-permute-start) | collective-permute-done | bytes 196640 | tf_op jit(solution)/shard_map/ppermute | solution.py:269
  23.6 1.3 copy-done
  24.9 4.7 %shard_map.42 = (f32[8,64,256]{2,1,0:T(8,128)S(1)}, bf16[4,64,256]{2,1,0:T(8,128)(2,1)S(1)}, bf16[4,64,256]{2,1,0:T(8,128)(2,1)S(1)}, bf16[16,64,256]{2,1,0:T(8,...) custom-call(f32[4,8,16,256]{3,2,1,0:T(8,128)} %all-to-all-done.pieces, ...), custom_call_target="tpu_custom_call" | custom-call | tf_op jit(solution)/shard_map/pallas_call | solution.py:228
  29.6 0.7 collective-permute-start.4
  30.3 0.7 collective-permute-start.6
  31.0 0.7 collective-permute-start.10
  31.7 0.0 collective-permute-done.5.given
  31.7 1.3 shard_map.44.rest_1_.rest_6_
  33.0 0.0 collective-permute-done.3.rest_4_.rest_5_
  33.1 0.0 collective-permute-done.6.rest_2_.rest_10_
  33.1 0.7 collective-permute-start.7
  33.8 0.7 collective-permute-start.8
  34.5 0.7 collective-permute-start.9
  35.2 0.0 collective-permute-done.8.rest_1_
  35.2 0.2 shard_map.46
  35.4 0.7 collective-permute-start.11
  36.1 0.7 collective-permute-start.12
  36.8 0.7 collective-permute-start.13
  37.5 0.0 collective-permute-done.13.rest_2_
  37.5 0.0 collective-permute-done.11.rest_0_
  37.6 0.7 collective-permute-start.14
  38.3 0.7 collective-permute-start.15
  38.9 0.7 collective-permute-start.16
  39.6 0.0 collective-permute-done.16.rest_2_
  39.6 0.0 collective-permute-done.14.rest_0_
  39.6 0.2 shard_map.48
  39.9 1.3 collective-permute-start.17
  41.2 1.3 collective-permute-start.18
  42.5 1.3 collective-permute-start.19
  43.8 0.7 collective-permute-start.21
  44.5 0.7 collective-permute-start.22
  45.2 62.8 %collective-permute-done.18.rest_1_ = bf16[3,64,256]{2,1,0:T(8,128)(2,1)S(1)} collective-permute-done((bf16[3,64,256]{2,1,0:T(8,128)(2,1)S(1)}, bf16[3,64,256]{2,1,0:T(8,128)(2,1)S(1)}, u32[]{:S(2)}, u32[]{:S(2)}) %collective-permute-start.18) | collective-permute-done | bytes 98336 | tf_op jit(solution)/shard_map/ppermute | solution.py:323
  108.0 0.1 collective-permute-done.19.rest_2_
  108.1 1.7 %shard_map.49 = (f32[12,64,256]{2,1,0:T(8,128)S(1)}, f32[12,64,256]{2,1,0:T(8,128)S(1)}) custom-call(f32[8,64,256]{2,1,0:T(8,128)S(1)} %collective-permute-done.17.rest_0_, bf16[3,64,256]{2,1,0:T(8,128)(2,1)S(1)} %collective-permute-done.18.rest_1_, ...), custom_call_target="tpu_custom_call", output_to_operand_aliasing={{0}: (5, {}), {1}: (6, {})} | custom-call | tf_op jit(solution)/shard_map/pallas_call | solution.py:228
  109.8 1.3 collective-permute-start.20
  111.2 1.8 %collective-permute-done.20.core = f32[12,64,256]{2,1,0:T(8,128)S(1)} collective-permute-done((f32[12,64,256]{2,1,0:T(8,128)S(1)}, f32[12,64,256]{2,1,0:T(8,128)S(1)}, u32[]{:S(2)}, u32[]{:S(2)}) %collective-permute-start.20) | collective-permute-done | bytes 786464 | tf_op jit(solution)/shard_map/ppermute | solution.py:331
  113.0 0.1 shard_map.50
  113.2 17.2 %all_to_all.10.packed = bf16[4,368,256]{2,1,0:T(8,128)(2,1)S(1)} all-to-all(bf16[4,368,256]{2,1,0:T(8,128)(2,1)S(1)} %shard_map.50), channel_id=1, replica_groups=mesh['depth'=16,'rows'=4,'cols'=4] {'cols'}, dimensions={0} | all-to-all | bytes 1507328 | tf_op jit(solution)/shard_map/all_to_all | solution.py:341
  130.4 5.0 %shard_map.51 = (f32[2,32,16,256]{3,2,1,0:T(8,128)}, f32[32,16,256]{2,1,0:T(8,128)}) custom-call(bf16[4,368,256]{2,1,0:T(8,128)(2,1)S(1)} %all_to_all.10.packed, bf16[3,768,256]{2,1,0:T(8,128)(2,1)S(1)} %bitcast.13, bf16[3,768,256]{2,1,0:T(8,128)(2,1)S(1)} %bitcast.15), custom_call_target="tpu_custom_call" | custom-call | tf_op jit(solution)/shard_map/pallas_call | solution.py:228
  (17 shorter events, 0.1 us)
Async XLA Ops:
  0.6 14.1 %all-to-all-start = ((f32[4,8,16,256]{3,2,1,0:T(8,128)}), f32[4,8,16,256]{3,2,1,0:T(8,128)}, u32[]{:S(2)}, u32[]{:S(2)}) async-start(f32[4,8,16,256]{3,2,1,0:T(8,128)} %bitcast.16), calls=%async_computation | async-start | bytes 1048576 | tf_op jit(solution)/shard_map/all_to_all | solution.py:271
  8.0 23.0 %collective-permute-start.2 = (bf16[3,768,256]{2,1,0:T(8,128)(2,1)S(1)}, bf16[3,768,256]{2,1,0:T(8,128)(2,1)S(1)}, u32[]{:S(2)}, u32[]{:S(2)}) collective-permute-start(bf16[3,768,256]{2,1,0:T(8,128)(2,1)S(1)} %bitcast.4), channel_id=1, source_target_pairs={{48,64},{49,65},{50,66},{51,67},{52,68},{53,69},{54,70},{55,71},{5... | collective-permute-start | bytes 3538952 | tf_op jit(solution)/shard_map/ppermute | solution.py:266
  8.7 23.0 %collective-permute-start.5 = (bf16[3,768,256]{2,1,0:T(8,128)(2,1)S(1)}, bf16[3,768,256]{2,1,0:T(8,128)(2,1)}, u32[]{:S(2)}, u32[]{:S(2)}) collective-permute-start(bf16[3,768,256]{2,1,0:T(8,128)(2,1)S(1)} %bitcast.5), channel_id=1, source_target_pairs={{32,0},{33,1},{34,2},{35,3},{36,4},{37,5},{38,6},{39,7},{40,8},{41... | collective-permute-start | bytes 3538952 | tf_op jit(solution)/shard_map/ppermute | solution.py:266
  10.4 22.7 %collective-permute-start.3 = (bf16[3,768,256]{2,1,0:T(8,128)(2,1)S(1)}, bf16[3,768,256]{2,1,0:T(8,128)(2,1)S(1)}, u32[]{:S(2)}, u32[]{:S(2)}) collective-permute-start(bf16[3,768,256]{2,1,0:T(8,128)(2,1)S(1)} %bitcast.6), channel_id=1, source_target_pairs={{16,0},{17,1},{18,2},{19,3},{20,4},{21,5},{22,6},{23,7},{24,8},{25... | collective-permute-start | bytes 3538952 | tf_op jit(solution)/shard_map/ppermute | solution.py:266
  15.8 7.9 %collective-permute-start = (bf16[4,6,16,256]{3,2,1,0:T(8,128)(2,1)S(1)}, bf16[4,6,16,256]{3,2,1,0:T(8,128)(2,1)S(1)}, u32[]{:S(2)}, u32[]{:S(2)}) collective-permute-start(bf16[4,6,16,256]{3,2,1,0:T(8,128)(2,1)S(1)} %get-tuple-element.45), channel_id=1, source_target_pairs={{0,1},{1,2},{2,3},{3,4},{4,5},{5,6},{6,7},{7,8},{8,9},{9,10},{10,1... | collective-permute-start | bytes 589832 | tf_op jit(solution)/shard_map/ppermute | solution.py:269
  16.4 7.2 %collective-permute-start.1 = (bf16[4,6,16,256]{3,2,1,0:T(8,128)(2,1)S(1)}, bf16[4,6,16,256]{3,2,1,0:T(8,128)(2,1)S(1)}, u32[]{:S(2)}, u32[]{:S(2)}) collective-permute-start(bf16[4,6,16,256]{3,2,1,0:T(8,128)(2,1)S(1)} %get-tuple-element.46), channel_id=1, source_target_pairs={{0,15},{1,0},{2,1},{3,2},{4,3},{5,4},{6,5},{7,6},{8,7},{9,8},{10,9... | collective-permute-start | bytes 589832 | tf_op jit(solution)/shard_map/ppermute | solution.py:269
  23.6 1.3 copy-start
  29.6 3.5 %collective-permute-start.4 = (f32[12,64,256]{2,1,0:T(8,128)S(1)}, f32[12,64,256]{2,1,0:T(8,128)S(1)}, u32[]{:S(2)}, u32[]{:S(2)}) collective-permute-start(f32[12,64,256]{2,1,0:T(8,128)S(1)} %get-tuple-element.54), channel_id=1, source_target_pairs={{16,0},{17,1},{18,2},{19,3},{20,4},{21,5},{22,6},{23,7},{24,8},{25... | collective-permute-start | bytes 2359304 | tf_op jit(solution)/shard_map/ppermute | solution.py:266
  30.3 2.8 %collective-permute-start.6 = (bf16[8,64,256]{2,1,0:T(8,128)(2,1)S(1)}, bf16[8,64,256]{2,1,0:T(8,128)(2,1)S(1)}, u32[]{:S(2)}, u32[]{:S(2)}) collective-permute-start(bf16[8,64,256]{2,1,0:T(8,128)(2,1)S(1)} %get-tuple-element.56), channel_id=1, source_target_pairs={{32,0},{33,1},{34,2},{35,3},{36,4},{37,5},{38,6},{39,7},{40,8},{41... | collective-permute-start | bytes 786440 | tf_op jit(solution)/shard_map/ppermute | solution.py:266
  31.0 4.2 %collective-permute-start.10 = (bf16[16,64,256]{2,1,0:T(8,128)(2,1)S(1)}, bf16[16,64,256]{2,1,0:T(8,128)(2,1)S(1)}, u32[]{:S(2)}, u32[]{:S(2)}) collective-permute-start(bf16[16,64,256]{2,1,0:T(8,128)(2,1)S(1)} %get-tuple-element.61), channel_id=1, source_target_pairs={{48,64},{49,65},{50,66},{51,67},{52,68},{53,69},{54,70},{55,71},{5... | collective-permute-start | bytes 1572872 | tf_op jit(solution)/shard_map/ppermute | solution.py:266
  33.1 2.1 %collective-permute-start.7 = (f32[8,64,256]{2,1,0:T(8,128)S(1)}, f32[8,64,256]{2,1,0:T(8,128)S(1)}, u32[]{:S(2)}, u32[]{:S(2)}) collective-permute-start(f32[8,64,256]{2,1,0:T(8,128)S(1)} %get-tuple-element.57), channel_id=1, source_target_pairs={{0,64},{1,65},{2,66},{3,67},{4,68},{5,69},{6,70},{7,71},{8,72},{9,... | collective-permute-start | bytes 1572872 | tf_op jit(solution)/shard_map/ppermute | solution.py:322
  33.8 1.4 %collective-permute-start.8 = (bf16[5,64,256]{2,1,0:T(8,128)(2,1)S(1)}, bf16[5,64,256]{2,1,0:T(8,128)(2,1)S(1)}, u32[]{:S(2)}, u32[]{:S(2)}) collective-permute-start(bf16[5,64,256]{2,1,0:T(8,128)(2,1)S(1)} %get-tuple-element.58), channel_id=1, source_target_pairs={{0,65},{1,66},{2,67},{3,68},{4,69},{5,70},{6,71},{7,72},{8,73},{9,... | collective-permute-start | bytes 491528 | tf_op jit(solution)/shard_map/ppermute | solution.py:323
  34.5 0.7 collective-permute-start.9
  35.4 2.1 %collective-permute-start.11 = (f32[8,64,256]{2,1,0:T(8,128)S(1)}, f32[8,64,256]{2,1,0:T(8,128)S(1)}, u32[]{:S(2)}, u32[]{:S(2)}) collective-permute-start(f32[8,64,256]{2,1,0:T(8,128)S(1)} %get-tuple-element.64), channel_id=1, source_target_pairs={{64,128},{65,129},{66,130},{67,131},{68,132},{69,133},{70,134},{71... | collective-permute-start | bytes 1572872 | tf_op jit(solution)/shard_map/ppermute | solution.py:322
  36.1 1.4 %collective-permute-start.12 = (bf16[5,64,256]{2,1,0:T(8,128)(2,1)S(1)}, bf16[5,64,256]{2,1,0:T(8,128)(2,1)S(1)}, u32[]{:S(2)}, u32[]{:S(2)}) collective-permute-start(bf16[5,64,256]{2,1,0:T(8,128)(2,1)S(1)} %get-tuple-element.65), channel_id=1, source_target_pairs={{64,129},{65,130},{66,131},{67,132},{68,133},{69,134},{70,135},{71... | collective-permute-start | bytes 491528 | tf_op jit(solution)/shard_map/ppermute | solution.py:323
  36.8 0.7 collective-permute-start.13
  37.6 2.1 %collective-permute-start.14 = (f32[8,64,256]{2,1,0:T(8,128)S(1)}, f32[8,64,256]{2,1,0:T(8,128)S(1)}, u32[]{:S(2)}, u32[]{:S(2)}) collective-permute-start(f32[8,64,256]{2,1,0:T(8,128)S(1)} %get-tuple-element.71), channel_id=1, source_target_pairs={{128,192},{129,193},{130,194},{131,195},{132,196},{133,197},{134,1... | collective-permute-start | bytes 1572872 | tf_op jit(solution)/shard_map/ppermute | solution.py:322
  38.3 1.4 %collective-permute-start.15 = (bf16[4,64,256]{2,1,0:T(8,128)(2,1)S(1)}, bf16[4,64,256]{2,1,0:T(8,128)(2,1)S(1)}, u32[]{:S(2)}, u32[]{:S(2)}) collective-permute-start(bf16[4,64,256]{2,1,0:T(8,128)(2,1)S(1)} %get-tuple-element.72), channel_id=1, source_target_pairs={{128,193},{129,194},{130,195},{131,196},{132,197},{133,198},{134,1... | collective-permute-start | bytes 393224 | tf_op jit(solution)/shard_map/ppermute | solution.py:323
  38.9 0.7 collective-permute-start.16
  39.9 68.2 %collective-permute-start.17 = (f32[8,64,256]{2,1,0:T(8,128)S(1)}, f32[8,64,256]{2,1,0:T(8,128)S(1)}, u32[]{:S(2)}, u32[]{:S(2)}) collective-permute-start(f32[8,64,256]{2,1,0:T(8,128)S(1)} %get-tuple-element.77), channel_id=1, source_target_pairs={{192,224},{193,225},{194,226},{195,227},{196,228},{197,229},{198,2... | collective-permute-start | bytes 1572872 | tf_op jit(solution)/shard_map/ppermute | solution.py:322
  41.2 66.8 %collective-permute-start.18 = (bf16[3,64,256]{2,1,0:T(8,128)(2,1)S(1)}, bf16[3,64,256]{2,1,0:T(8,128)(2,1)S(1)}, u32[]{:S(2)}, u32[]{:S(2)}) collective-permute-start(bf16[3,64,256]{2,1,0:T(8,128)(2,1)S(1)} %get-tuple-element.78), channel_id=1, source_target_pairs={{192,225},{193,226},{194,227},{195,228},{196,229},{197,230},{198,2... | collective-permute-start | bytes 294920 | tf_op jit(solution)/shard_map/ppermute | solution.py:323
  42.5 65.6 %collective-permute-start.19 = (bf16[3,64,256]{2,1,0:T(8,128)(2,1)S(1)}, bf16[3,64,256]{2,1,0:T(8,128)(2,1)S(1)}, u32[]{:S(2)}, u32[]{:S(2)}) collective-permute-start(bf16[3,64,256]{2,1,0:T(8,128)(2,1)S(1)} %get-tuple-element.79), channel_id=1, source_target_pairs={{193,224},{194,225},{195,226},{196,227},{197,228},{198,229},{199,2... | collective-permute-start | bytes 294920 | tf_op jit(solution)/shard_map/ppermute | solution.py:324
  43.8 67.4 %collective-permute-start.21 = (f32[12,64,256]{2,1,0:T(8,128)S(1)}, f32[12,64,256]{2,1,0:T(8,128)S(1)}, u32[]{:S(2)}, u32[]{:S(2)}) collective-permute-start(f32[12,64,256]{2,1,0:T(8,128)S(1)} %get-tuple-element.84), channel_id=1, source_target_pairs={{0,32},{1,33},{2,34},{3,35},{4,36},{5,37},{6,38},{7,39},{8,40},{9,... | collective-permute-start | bytes 2359304 | tf_op jit(solution)/shard_map/ppermute | solution.py:331
  44.5 66.7 %collective-permute-start.22 = (f32[12,64,256]{2,1,0:T(8,128)S(1)}, f32[12,64,256]{2,1,0:T(8,128)S(1)}, u32[]{:S(2)}, u32[]{:S(2)}) collective-permute-start(f32[12,64,256]{2,1,0:T(8,128)S(1)} %get-tuple-element.85), channel_id=1, source_target_pairs={{64,48},{65,49},{66,50},{67,51},{68,52},{69,53},{70,54},{71,55},{7... | collective-permute-start | bytes 2359304 | tf_op jit(solution)/shard_map/ppermute | solution.py:331
  109.8 3.2 %collective-permute-start.20 = (f32[12,64,256]{2,1,0:T(8,128)S(1)}, f32[12,64,256]{2,1,0:T(8,128)S(1)}, u32[]{:S(2)}, u32[]{:S(2)}) collective-permute-start(f32[12,64,256]{2,1,0:T(8,128)S(1)} %get-tuple-element.83), channel_id=1, source_target_pairs={{0,16},{1,17},{2,18},{3,19},{4,20},{5,21},{6,22},{7,23},{8,24},{9,... | collective-permute-start | bytes 2359304 | tf_op jit(solution)/shard_map/ppermute | solution.py:331
  113.2 17.3 %copy-start.1 = (bf16[1,3,3,256,256]{4,3,2,1,0:T(8,128)(2,1)S(1)}, bf16[1,3,3,256,256]{4,3,2,1,0:T(8,128)(2,1)}, u32[]{:S(2)}) copy-start(bf16[1,3,3,256,256]{4,3,2,1,0:T(8,128)(2,1)} %get-tuple-element.88) | copy-start | bytes 3538948

commit v6 on v5

--- a/solution.py
+++ b/solution.py
@@ -73,8 +73,10 @@
     high[...] = pieces[:, rows - count :].astype(BF16)
 
 
-def head_kernel(step, height, pieces, above, below, w0, w1, main, top, bottom, *rest):
-    jumps, (state, first, patch, second) = rest[:-4], rest[-4:]
+def head_kernel(step, height, pieces, above, below, w0, layers, main, top, bottom, *rest):
+    jumps, (state, first, patch, second, w1, sem) = rest[:-6], rest[-6:]
+    load = pltpu.make_async_copy(layers.at[1], w1, sem.at[0])
+    load.start()
     ncols, rows, wide = pieces.shape[:3]
     halo = above.shape[1]
     deep = rows + 2 * halo
@@ -102,18 +104,19 @@
                 ref[place] = jump.astype(ref.dtype)
 
     slopes(patch, w0, 1, deep - 2, to_middle)
+    load.wait()
     slopes(second, w1, 2, deep - 4, to_jump)
 
 
 def turn_kernel(host, rows, count, kept, given, last, step, height, *rest):
-    outs = 0 if last else 3
+    outs = 0 if last else 4
     begin = len(rest) - (2 * count + given + outs + kept + 3)
     start, rest = rest[:begin], rest[begin:]
     weights, jumps = rest[:count], rest[count : 2 * count]
     rest = rest[2 * count + given :]
     if not last:
-        out, out_top, out_bottom = rest[:3]
-        rest = rest[3:]
+        out, out_top, out_bottom, left = rest[:4]
+        rest = rest[4:]
     saved, (state, *patches) = rest[:kept], rest[kept:]
 
     @pl.when(lax.axis_index("depth") == host)
@@ -125,7 +128,7 @@
         else:
             main, top, bottom = start
             state[:halo] = top[...].astype(F32)
-            state[halo : halo + rows] = main[...]
+            state[halo : halo + rows] = main[...].astype(F32)
             state[halo + rows :] = bottom[...].astype(F32)
         if kept:
             saved[0][...] = state[halo - KEPT : halo + rows + KEPT]
@@ -144,13 +147,31 @@
                     fill_row(patches[(k + 1) % 2], row, new, (origin + row >= 0) & (origin + row < height))
                 elif not last:
                     place, edge = row - halo, out_top.shape[0]
-                    out[place] = new
+                    high = new.astype(BF16)
+                    out[place] = high
+                    left[place] = (new - high.astype(F32)).astype(left.dtype)
                     if place < edge:
-                        out_top[place] = new.astype(BF16)
+                        out_top[place] = high
                     if place >= rows - edge:
-                        out_bottom[place - rows + edge] = new.astype(BF16)
+                        out_bottom[place - rows + edge] = high
 
             slopes(patches[k % 2], weights[k], halo - far, rows + 2 * far, advance)
+
+
+def settle_kernel(host, sends, low, *rest):
+    if sends:
+        left, rest = rest[0], rest[1:]
+    kept = len(rest) // 2 if not sends else (len(rest) - 1) // 2
+    given, outs = rest[:kept], rest[kept:]
+
+    @pl.when(lax.axis_index("depth") == host)
+    def _():
+        rows = low.shape[0]
+        part = low[...].astype(F32)
+        if sends:
+            outs[0][...] = (left[...] + part).astype(BF16)
+        for old, new in zip(given, outs[1:] if sends else outs):
+            new[KEPT : KEPT + rows] = old[KEPT : KEPT + rows] + part
 
 
 def pack_kernel(own, core, after, prev, packed, state):
@@ -187,7 +208,10 @@
                 packed[k, start : start + wide] = (mine - high.astype(F32)).astype(BF16)
 
 
-def tail_kernel(step, height, width, packed, w0, w1, fine, coarse, state, patch, second):
+def tail_kernel(step, height, width, packed, layers, fine, coarse, state, patch, second, held, sems):
+    loads = [pltpu.make_async_copy(layers.at[k], held.at[k], sems.at[k]) for k in range(2)]
+    for load in loads:
+        load.start()
     ncols = packed.shape[0]
     tile_rows, wide = coarse.shape[:2]
     rows = tile_rows // ncols
@@ -220,19 +244,22 @@
     def to_ending(row, slope):
         fine[1, row - KEPT] = fine[0, row - KEPT] + step * slope[:wide]
 
-    slopes(patch, w0, 1, tile_rows + 2, to_middle, 2 * CHUNK)
-    slopes(second, w1, 2, tile_rows, to_ending, 2 * CHUNK)
-
-
-def call(kernel, outs, scratch, inputs, aliases={}, vmem=12 << 20):
+    loads[0].wait()
+    slopes(patch, held.at[0], 1, tile_rows + 2, to_middle, 2 * CHUNK)
+    loads[1].wait()
+    slopes(second, held.at[1], 2, tile_rows, to_ending, 2 * CHUNK)
+
+
+def call(kernel, outs, scratch, inputs, aliases={}, far=None, vmem=12 << 20, work=0):
     return pl.pallas_call(
         kernel,
         out_shape=[jax.ShapeDtypeStruct(*o) for o in outs],
-        in_specs=[pl.BlockSpec(memory_space=pltpu.VMEM)] * len(inputs),
+        in_specs=[pl.BlockSpec(memory_space=pl.ANY if k == far else pltpu.VMEM) for k in range(len(inputs))],
         out_specs=[pl.BlockSpec(memory_space=pltpu.VMEM)] * len(outs),
         scratch_shapes=scratch,
         input_output_aliases=aliases,
         compiler_params=pltpu.CompilerParams(vmem_limit_bytes=vmem),
+        cost_estimate=pl.CostEstimate(flops=work, bytes_accessed=0, transcendentals=0) if work else None,
     )(*inputs)
 
 
@@ -245,7 +272,8 @@
     strips = nrows * ncols
     step = 2.0 / (2 * ndepth)
     flat = weights.reshape(2, 3, 3 * channels, channels)
-    w0, w1 = flat[0], flat[1]
+    w0 = flat[0]
+    held = pltpu.VMEM(w0.shape, BF16)
 
     hosts = [*range(0, ndepth, 4), ndepth - 2]
     visits = [["own", "core", "next"]] + [["prev", "own", "core", "next"]] * (len(hosts) - 2) + [["own"]]
@@ -261,9 +289,10 @@
             if 0 <= s + shift < strips
         ]
 
-    def fetch(x, slot):
+    def fetch(x, slot, only=hosts):
         away = SLOTS[slot]
-        return lax.ppermute(x, AXES, route([(h + away, h) for h, v in zip(hosts, visits) if slot in v], 0))
+        pairs = [(h + away, h) for h, v in zip(hosts, visits) if slot in v and h in only]
+        return lax.ppermute(x, AXES, route(pairs, 0))
 
     def ring(x, shift):
         return lax.ppermute(x, ("rows", "cols"), [(s, (s + shift) % strips) for s in range(strips)])
@@ -283,11 +312,13 @@
         functools.partial(head_kernel, step, height),
         [like(rows), like(halos[0], BF16), like(halos[0], BF16)]
         + [like(rows + 2 * JUMP_HALO[slot], kinds[slot]) for slot in SLOTS],
-        [vm(deep), vm(deep), patch(deep), patch(deep)],
-        (pieces, above, below, w0, w1),
+        [vm(deep), vm(deep), patch(deep), patch(deep), held, pltpu.SemaphoreType.DMA((1,))],
+        (pieces, above, below, w0, flat),
+        far=4,
     )
     all_jumps = dict(zip(SLOTS, jumps))
-    all_jumps |= {slot: fetch(all_jumps[slot], slot) for slot in far}
+    first_jump = fetch(all_jumps["next"], "next", hosts[:1])
+    all_jumps |= {slot: fetch(all_jumps[slot], slot, hosts[1:] if slot == "next" else hosts) for slot in far}
     main, top, bottom, all_weights["prev"] = lax.optimization_barrier((main, top, bottom, all_weights["prev"]))
 
     saved = {}
@@ -298,11 +329,12 @@
         last = turn in (0, len(turns) - 1)
         keeps = [] if turn == 1 else [*visit, "next" if turn == 0 else "core"] if last else visit
         given = [slot for slot in keeps if slot in saved]
-        outs = [] if last else [like(rows)] + [like(turns[turn + 1][2], BF16)] * 2
+        left = like(rows, BF16 if turn == 1 else F32)
+        outs = [] if last else [like(rows, BF16)] + [like(turns[turn + 1][2], BF16)] * 2 + [left]
         inputs = (
             *start,
             *(all_weights[slot] for slot in visit),
-            *(all_jumps[slot] for slot in visit),
+            *(first_jump if turn == 1 else all_jumps[slot] for slot in visit),
             *(saved[slot] for slot in given),
         )
         results = call(
@@ -311,17 +343,31 @@
             [vm(rows + 2 * halo), patch(rows + 2 * halo), patch(rows + 2 * halo)],
             inputs,
             {len(inputs) - len(given) + k: len(outs) + keeps.index(slot) for k, slot in enumerate(given)},
+            work=20_000_000_000 if turn > 1 else 0,
         )
         saved |= zip(keeps, results[len(outs) :])
         if turn == 0:
             start = (saved["next"],)
             weight = all_weights["next"]
             (all_weights["next"],) = call(hold_kernel, [(weight.shape, BF16)], [], (weight,))
-        elif not last:
+            continue
+        if turn > 1:
+            inputs = (low, *(() if last else results[3:4]), *(saved[slot] for slot in keeps))
+            settled = call(
+                functools.partial(settle_kernel, host, not last),
+                ([] if last else [like(rows, BF16)]) + [like(rows + 2 * KEPT)] * len(keeps),
+                [],
+                inputs,
+                {len(inputs) - len(keeps) + k: int(not last) + k for k in range(len(keeps))},
+                work=20_000_000_000,
+            )
+            saved |= zip(keeps, settled[int(not last) :])
+        if not last:
             pair = [(host, turns[turn + 1][0])]
             main = lax.ppermute(results[0], AXES, route(pair, 0))
             top = lax.ppermute(results[2], AXES, route(pair, 1))
             bottom = lax.ppermute(results[1], AXES, route(pair, -1))
+            low = lax.ppermute(results[3] if turn == 1 else settled[0], AXES, route(pair, 0))
             start = (main, top, bottom)
 
     visits[-1] = ["own", "core"]
@@ -343,8 +389,10 @@
     fine, coarse = call(
         functools.partial(tail_kernel, step, height, width),
         [((2, *tile.shape), F32), (tile.shape, F32)],
-        [tall(tile_rows + 4), tall(tile_rows + 4, BF16, 3), tall(tile_rows + 4, BF16, 3)],
-        (packed, w0, w1),
+        [tall(tile_rows + 4), tall(tile_rows + 4, BF16, 3), tall(tile_rows + 4, BF16, 3)]
+        + [pltpu.VMEM(flat.shape, BF16), pltpu.SemaphoreType.DMA((2,))],
+        (packed, flat),
+        far=1,
     )
     return fine, coarse[None]
 

time: 136 us -> 130 us (0.956)
  waiting for transfers between devices: 72 us -> 55.6 us
  Pallas kernels: 14.4 us -> 21.6 us
  starting transfers between devices: 26.7 us -> 32.5 us
  local copies, waits for them, and re-layouts: 4.13 us -> 1.5 us
    ppermute x4, waiting for transfers between devices: 62.8 us -> 41.9 us  [on_device(): top = lax.ppermute(results[2], AXES, route(pair, 1))]
    pallas_call x11 -> x15, Pallas kernels: 14.4 us -> 21.6 us  [call(): pl.pallas_call(kernel, out_shape=[jax.ShapeDtypeStruct(*o) for o in outs]...]
    ppermute x6 -> x11, starting transfers between devices: 5.22 us -> 11.2 us  [the longest x7 7.83 us: fetch(): return lax.ppermute(x, AXES, route(pairs, 0))]
    all_to_all x1, waiting for transfers between devices: 3.57 us -> 6.21 us  [on_device(): lax.all_to_all(tile.reshape(ncols, rows, tile_cols, channels), 'cols', 0,...]
  transfers between devices with their start and end apart: 24 -> 29, of which waited for: 5 -> 6; matrix products, arithmetic and copies ran while one was open for 2% -> 0% of each run, Pallas kernels for 6% -> 12%
where the time goes in v6:
time: 130 us; the launch traced here: 129 us
  waiting for transfers between devices  55.6 us (43%)
  starting transfers between devices  32.5 us (25%)
  Pallas kernels  21.6 us (17%)
  blocking collectives  16.9 us (13%)
  local copies, waits for them, and re-layouts  1.5 us (1%)
    ppermute x4, waiting for transfers between devices, on_device(): top = lax.ppermute(results[2], AXES, route(pair, 1))  41.9 us
    pallas_call x15, Pallas kernels, call(): pl.pallas_call(kernel, out_shape=[jax.ShapeDtypeStruct(*o) for o in outs]...  21.6 us
    all_to_all x1, blocking collectives, on_device(): packed = lax.all_to_all(packed, 'cols', 0, 0, tiled=True)  16.9 us
    ppermute x7, starting transfers between devices, fetch(): return lax.ppermute(x, AXES, route(pairs, 0))  7.83 us
    all_to_all x1, waiting for transfers between devices, on_device(): lax.all_to_all(tile.reshape(ncols, rows, tile_cols, channels), 'cols', 0,...  6.21 us
    all_to_all x1, starting transfers between devices, on_device(): lax.all_to_all(tile.reshape(ncols, rows, tile_cols, channels), 'cols', 0,...  4.46 us
    ppermute x2, starting transfers between devices, ring(): lax.ppermute(x, ('rows', 'cols'), [(s, (s + shift) % strips) for s in ran...  4.21 us
    ppermute x2, waiting for transfers between devices, ring(): lax.ppermute(x, ('rows', 'cols'), [(s, (s + shift) % strips) for s in ran...  3.65 us
  transfers between devices with their start and end apart: 29, of which 6 were waited for; matrix products, arithmetic and copies ran while one was open for 0% of the time, Pallas kernels for 12%

profile of v6, /device:TPU:226, one launch (start us, length us, event | category | flops | bytes accessed | tf_op | source)
XLA Modules:
  0.0 129.4 jit_solution(2601431196423352036)
XLA Ops:
  0.6 1.5 %slice.4 = bf16[1,3,3,256,256]{4,3,2,1,0:T(8,128)(2,1)S(1)} slice(bf16[2,3,3,256,256]{4,3,2,1,0:T(8,128)(2,1)} %param.3), slice={[0:1], [0:3], [0:3], [0:256], [0:256]} | slice | bytes 2359296 | tf_op jit(solution)/shard_map/slice | solution.py:275
  2.1 1.7 %collective-permute-start.2 = (bf16[3,768,256]{2,1,0:T(8,128)(2,1)S(1)}, bf16[3,768,256]{2,1,0:T(8,128)(2,1)}, u32[]{:S(2)}, u32[]{:S(2)}) collective-permute-start(bf16[3,768,256]{2,1,0:T(8,128)(2,1)S(1)} %bitcast.6), channel_id=1, source_target_pairs={{48,64},{49,65},{50,66},{51,67},{52,68},{53,69},{54,70},{55,71},{5... | collective-permute-start | bytes 3538952 | tf_op jit(solution)/shard_map/ppermute | solution.py:295
  3.8 4.5 %all-to-all-start = ((f32[4,8,16,256]{3,2,1,0:T(8,128)}), f32[4,8,16,256]{3,2,1,0:T(8,128)}, u32[]{:S(2)}, u32[]{:S(2)}) async-start(f32[4,8,16,256]{3,2,1,0:T(8,128)} %bitcast.15), calls=%async_computation | async-start | bytes 1048576 | tf_op jit(solution)/shard_map/all_to_all | solution.py:300
  8.3 1.7 %collective-permute-start.5 = (bf16[3,768,256]{2,1,0:T(8,128)(2,1)S(1)}, bf16[3,768,256]{2,1,0:T(8,128)(2,1)}, u32[]{:S(2)}, u32[]{:S(2)}) collective-permute-start(bf16[3,768,256]{2,1,0:T(8,128)(2,1)S(1)} %bitcast.7), channel_id=1, source_target_pairs={{32,0},{33,1},{34,2},{35,3},{36,4},{37,5},{38,6},{39,7},{40,8},{41... | collective-permute-start | bytes 3538952 | tf_op jit(solution)/shard_map/ppermute | solution.py:295
  10.0 1.7 %collective-permute-start.3 = (bf16[3,768,256]{2,1,0:T(8,128)(2,1)S(1)}, bf16[3,768,256]{2,1,0:T(8,128)(2,1)}, u32[]{:S(2)}, u32[]{:S(2)}) collective-permute-start(bf16[3,768,256]{2,1,0:T(8,128)(2,1)S(1)} %bitcast.8), channel_id=1, source_target_pairs={{16,0},{17,1},{18,2},{19,3},{20,4},{21,5},{22,6},{23,7},{24,8},{25... | collective-permute-start | bytes 3538952 | tf_op jit(solution)/shard_map/ppermute | solution.py:295
  11.7 6.2 %all-to-all-done.pieces = f32[4,8,16,256]{3,2,1,0:T(8,128)} async-done(((f32[4,8,16,256]{3,2,1,0:T(8,128)}), f32[4,8,16,256]{3,2,1,0:T(8,128)}, u32[]{:S(2)}, u32[]{:S(2)}) %all-to-all-start) | async-done | bytes 524320 | tf_op jit(solution)/shard_map/all_to_all | solution.py:300
  17.9 1.1 shard_map.41
  19.0 0.6 collective-permute-start
  19.6 3.6 %collective-permute-start.1 = (bf16[4,6,16,256]{3,2,1,0:T(8,128)(2,1)S(1)}, bf16[4,6,16,256]{3,2,1,0:T(8,128)(2,1)S(1)}, u32[]{:S(2)}, u32[]{:S(2)}) collective-permute-start(bf16[4,6,16,256]{3,2,1,0:T(8,128)(2,1)S(1)} %get-tuple-element.66), channel_id=1, source_target_pairs={{0,15},{1,0},{2,1},{3,2},{4,3},{5,4},{6,5},{7,6},{8,7},{9,8},{10,9... | collective-permute-start | bytes 589832 | tf_op jit(solution)/shard_map/ppermute | solution.py:298
  23.2 3.6 %collective-permute-done.above = bf16[4,6,16,256]{3,2,1,0:T(8,128)(2,1)S(1)} collective-permute-done((bf16[4,6,16,256]{3,2,1,0:T(8,128)(2,1)S(1)}, bf16[4,6,16,256]{3,2,1,0:T(8,128)(2,1)S(1)}, u32[]{:S(2)}, u32[]{:S(2)}) %collective-permute-start) | collective-permute-done | bytes 196640 | tf_op jit(solution)/shard_map/ppermute | solution.py:298
  26.8 5.2 %shard_map.42 = (f32[8,64,256]{2,1,0:T(8,128)S(1)}, bf16[4,64,256]{2,1,0:T(8,128)(2,1)S(1)}, bf16[4,64,256]{2,1,0:T(8,128)(2,1)S(1)}, bf16[16,64,256]{2,1,0:T(8,...) custom-call(f32[4,8,16,256]{3,2,1,0:T(8,128)} %all-to-all-done.pieces, ...), custom_call_target="tpu_custom_call" | custom-call | tf_op jit(solution)/shard_map/pallas_call | solution.py:254
  32.1 0.7 collective-permute-start.4
  32.8 0.7 collective-permute-start.6
  33.5 0.7 collective-permute-start.11
  34.2 0.7 collective-permute-start.12
  34.9 1.3 %shard_map.44.rest_1_.rest_6_ = bf16[3,768,256]{2,1,0:T(8,128)(2,1)S(1)} custom-call(bf16[3,768,256]{2,1,0:T(8,128)(2,1)} %collective-permute-done.5.given), custom_call_target="tpu_custom_call" | custom-call | tf_op jit(solution)/shard_map/pallas_call | solution.py:254
  36.3 1.3 shard_map.43
  37.5 0.7 collective-permute-start.8
  38.2 0.7 collective-permute-start.9
  38.9 0.7 collective-permute-start.10
  39.6 0.7 collective-permute-start.7
  40.3 1.6 %shard_map.46 = (bf16[8,64,256]{2,1,0:T(8,128)(2,1)S(1)}, bf16[5,64,256]{2,1,0:T(8,128)(2,1)S(1)}, bf16[5,64,256]{2,1,0:T(8,128)(2,1)S(1)}, f32[8,64,256]{2,1,0:...) custom-call(bf16[8,64,256]{2,1,0:T(8,128)(2,1)S(1)} %collective-perm, ...), custom_call_target="tpu_custom_call", output_to_operand_aliasing={{5}: (11, {}), {6}: (12, {}), {7}: (13, {})} | custom-call | flops 20000000000 | tf_op jit(solution)/shard_map/pallas_call | solution.py:254
  41.9 0.7 collective-permute-start.15
  42.6 0.7 collective-permute-start.16
  43.3 0.7 collective-permute-start.14
  44.0 0.7 collective-permute-start.13
  44.7 1.6 %shard_map.48 = (bf16[8,64,256]{2,1,0:T(8,128)(2,1)S(1)}, bf16[4,64,256]{2,1,0:T(8,128)(2,1)S(1)}, bf16[4,64,256]{2,1,0:T(8,128)(2,1)S(1)}, f32[8,64,256]{2,1,0:...) custom-call(bf16[8,64,256]{2,1,0:T(8,128)(2,1)S(1)} %collective-perm, ...), custom_call_target="tpu_custom_call", output_to_operand_aliasing={{4}: (11, {}), {5}: (12, {}), {6}: (13, {}), {7}: (14, {})} | custom-call | flops 20000000000 | tf_op jit(solution)/shard_map/pallas_call | solution.py:254
  46.4 0.7 collective-permute-start.19
  47.0 0.7 collective-permute-start.20
  47.7 0.7 collective-permute-start.18
  48.4 0.7 collective-permute-start.17
  49.1 0.7 collective-permute-start.26
  49.9 1.6 %shard_map.50 = (bf16[8,64,256]{2,1,0:T(8,128)(2,1)S(1)}, bf16[3,64,256]{2,1,0:T(8,128)(2,1)S(1)}, bf16[3,64,256]{2,1,0:T(8,128)(2,1)S(1)}, f32[8,64,256]{2,1,0:...) custom-call(bf16[8,64,256]{2,1,0:T(8,128)(2,1)S(1)} %collective-perm, ...), custom_call_target="tpu_custom_call", output_to_operand_aliasing={{4}: (9, {}), {5}: (10, {}), {6}: (11, {})} | custom-call | flops 20000000000 | tf_op jit(solution)/shard_map/pallas_call | solution.py:254
  51.5 1.3 collective-permute-start.23
  52.8 1.3 collective-permute-start.24
  54.1 1.3 collective-permute-start.22
  55.4 1.3 collective-permute-start.21
  56.7 41.9 %collective-permute-done.23.rest_1_ = bf16[3,64,256]{2,1,0:T(8,128)(2,1)S(1)} collective-permute-done((bf16[3,64,256]{2,1,0:T(8,128)(2,1)S(1)}, bf16[3,64,256]{2,1,0:T(8,128)(2,1)S(1)}, u32[]{:S(2)}, u32[]{:S(2)}) %collective-permute-start.23) | collective-permute-done | bytes 98336 | tf_op jit(solution)/shard_map/ppermute | solution.py:368
  98.6 0.7 collective-permute-start.27
  99.3 0.8 collective-permute-done.22.rest_0_
  100.2 1.7 %shard_map.52 = (f32[12,64,256]{2,1,0:T(8,128)S(1)}, f32[12,64,256]{2,1,0:T(8,128)S(1)}) custom-call(bf16[8,64,256]{2,1,0:T(8,128)(2,1)S(1)} %collective-permute-done.22.rest_0_, bf16[3,64,256]{2,1,0:T(8,128)(2,1)S(1)} %collective-permute-done.23.rest_1_, ...), custom_call_target="tpu_custom_call", output_to_operand_aliasing={{0}: (5, {}), {1}: (6, {})} | custom-call | flops 20000000000 | tf_op jit(solution)/shard_map/pallas_call | solution.py:254
  101.9 1.1 collective-permute-done.21.low
  103.0 0.2 shard_map.53
  103.2 1.3 %collective-permute-start.25 = (f32[12,64,256]{2,1,0:T(8,128)S(1)}, f32[12,64,256]{2,1,0:T(8,128)S(1)}, u32[]{:S(2)}, u32[]{:S(2)}) collective-permute-start(f32[12,64,256]{2,1,0:T(8,128)S(1)} %get-tuple-element.123), channel_id=1, source_target_pairs={{0,16},{1,17},{2,18},{3,19},{4,20},{5,21},{6,22},{7,23},{8,24},{9,... | collective-permute-start | bytes 2359304 | tf_op jit(solution)/shard_map/ppermute | solution.py:377
  104.5 1.8 %collective-permute-done.25.core = f32[12,64,256]{2,1,0:T(8,128)S(1)} collective-permute-done((f32[12,64,256]{2,1,0:T(8,128)S(1)}, f32[12,64,256]{2,1,0:T(8,128)S(1)}, u32[]{:S(2)}, u32[]{:S(2)}) %collective-permute-start.25) | collective-permute-done | bytes 786464 | tf_op jit(solution)/shard_map/ppermute | solution.py:377
  106.4 0.1 shard_map.54
  106.5 16.9 %all_to_all.10.packed = bf16[4,368,256]{2,1,0:T(8,128)(2,1)S(1)} all-to-all(bf16[4,368,256]{2,1,0:T(8,128)(2,1)S(1)} %shard_map.54), channel_id=1, replica_groups=mesh['depth'=16,'rows'=4,'cols'=4] {'cols'}, dimensions={0} | all-to-all | bytes 1507328 | tf_op jit(solution)/shard_map/all_to_all | solution.py:387
  123.5 5.7 %shard_map.55 = (f32[2,32,16,256]{3,2,1,0:T(8,128)}, f32[32,16,256]{2,1,0:T(8,128)}) custom-call(bf16[4,368,256]{2,1,0:T(8,128)(2,1)S(1)} %all_to_all.10.packed, bf16[2,3,768,256]{3,2,1,0:T(8,128)(2,1)S(1)} %bitcast.5), custom_call_target="tpu_custom_call" | custom-call | tf_op jit(solution)/shard_map/pallas_call | solution.py:254
  (29 shorter events, 0.1 us)
Async XLA Ops:
  0.6 26.2 %copy-start = (bf16[2,3,3,256,256]{4,3,2,1,0:T(8,128)(2,1)S(1)}, bf16[2,3,3,256,256]{4,3,2,1,0:T(8,128)(2,1)}, u32[]{:S(2)}) copy-start(bf16[2,3,3,256,256]{4,3,2,1,0:T(8,128)(2,1)} %param.3) | copy-start | bytes 7077892
  2.1 31.3 %collective-permute-start.2 = (bf16[3,768,256]{2,1,0:T(8,128)(2,1)S(1)}, bf16[3,768,256]{2,1,0:T(8,128)(2,1)}, u32[]{:S(2)}, u32[]{:S(2)}) collective-permute-start(bf16[3,768,256]{2,1,0:T(8,128)(2,1)S(1)} %bitcast.6), channel_id=1, source_target_pairs={{48,64},{49,65},{50,66},{51,67},{52,68},{53,69},{54,70},{55,71},{5... | collective-permute-start | bytes 3538952 | tf_op jit(solution)/shard_map/ppermute | solution.py:295
  3.8 14.0 %all-to-all-start = ((f32[4,8,16,256]{3,2,1,0:T(8,128)}), f32[4,8,16,256]{3,2,1,0:T(8,128)}, u32[]{:S(2)}, u32[]{:S(2)}) async-start(f32[4,8,16,256]{3,2,1,0:T(8,128)} %bitcast.15), calls=%async_computation | async-start | bytes 1048576 | tf_op jit(solution)/shard_map/all_to_all | solution.py:300
  8.3 25.9 %collective-permute-start.5 = (bf16[3,768,256]{2,1,0:T(8,128)(2,1)S(1)}, bf16[3,768,256]{2,1,0:T(8,128)(2,1)}, u32[]{:S(2)}, u32[]{:S(2)}) collective-permute-start(bf16[3,768,256]{2,1,0:T(8,128)(2,1)S(1)} %bitcast.7), channel_id=1, source_target_pairs={{32,0},{33,1},{34,2},{35,3},{36,4},{37,5},{38,6},{39,7},{40,8},{41... | collective-permute-start | bytes 3538952 | tf_op jit(solution)/shard_map/ppermute | solution.py:295
  10.0 26.2 %collective-permute-start.3 = (bf16[3,768,256]{2,1,0:T(8,128)(2,1)S(1)}, bf16[3,768,256]{2,1,0:T(8,128)(2,1)}, u32[]{:S(2)}, u32[]{:S(2)}) collective-permute-start(bf16[3,768,256]{2,1,0:T(8,128)(2,1)S(1)} %bitcast.8), channel_id=1, source_target_pairs={{16,0},{17,1},{18,2},{19,3},{20,4},{21,5},{22,6},{23,7},{24,8},{25... | collective-permute-start | bytes 3538952 | tf_op jit(solution)/shard_map/ppermute | solution.py:295
  19.0 7.9 %collective-permute-start = (bf16[4,6,16,256]{3,2,1,0:T(8,128)(2,1)S(1)}, bf16[4,6,16,256]{3,2,1,0:T(8,128)(2,1)S(1)}, u32[]{:S(2)}, u32[]{:S(2)}) collective-permute-start(bf16[4,6,16,256]{3,2,1,0:T(8,128)(2,1)S(1)} %get-tuple-element.65), channel_id=1, source_target_pairs={{0,1},{1,2},{2,3},{3,4},{4,5},{5,6},{6,7},{7,8},{8,9},{9,10},{10,1... | collective-permute-start | bytes 589832 | tf_op jit(solution)/shard_map/ppermute | solution.py:298
  19.6 7.2 %collective-permute-start.1 = (bf16[4,6,16,256]{3,2,1,0:T(8,128)(2,1)S(1)}, bf16[4,6,16,256]{3,2,1,0:T(8,128)(2,1)S(1)}, u32[]{:S(2)}, u32[]{:S(2)}) collective-permute-start(bf16[4,6,16,256]{3,2,1,0:T(8,128)(2,1)S(1)} %get-tuple-element.66), channel_id=1, source_target_pairs={{0,15},{1,0},{2,1},{3,2},{4,3},{5,4},{6,5},{7,6},{8,7},{9,8},{10,9... | collective-permute-start | bytes 589832 | tf_op jit(solution)/shard_map/ppermute | solution.py:298
  32.1 4.2 %collective-permute-start.4 = (f32[12,64,256]{2,1,0:T(8,128)S(1)}, f32[12,64,256]{2,1,0:T(8,128)S(1)}, u32[]{:S(2)}, u32[]{:S(2)}) collective-permute-start(f32[12,64,256]{2,1,0:T(8,128)S(1)} %get-tuple-element.74), channel_id=1, source_target_pairs={{16,0},{17,1},{18,2},{19,3},{20,4},{21,5},{22,6},{23,7},{24,8},{25... | collective-permute-start | bytes 2359304 | tf_op jit(solution)/shard_map/ppermute | solution.py:295
  32.8 4.7 %collective-permute-start.6 = (bf16[8,64,256]{2,1,0:T(8,128)(2,1)S(1)}, bf16[8,64,256]{2,1,0:T(8,128)(2,1)S(1)}, u32[]{:S(2)}, u32[]{:S(2)}) collective-permute-start(bf16[8,64,256]{2,1,0:T(8,128)(2,1)S(1)} %get-tuple-element.76), channel_id=1, source_target_pairs={{32,0},{33,1},{34,2},{35,3},{36,4},{37,5},{38,6},{39,7},{40,8},{41... | collective-permute-start | bytes 786440 | tf_op jit(solution)/shard_map/ppermute | solution.py:295
  33.5 6.8 %collective-permute-start.11 = (bf16[16,64,256]{2,1,0:T(8,128)(2,1)S(1)}, bf16[16,64,256]{2,1,0:T(8,128)(2,1)S(1)}, u32[]{:S(2)}, u32[]{:S(2)}) collective-permute-start(bf16[16,64,256]{2,1,0:T(8,128)(2,1)S(1)} %get-tuple-element.82), channel_id=1, source_target_pairs={{48,64},{49,65},{50,66},{51,67},{52,68},{53,69},{54,70},{55,71},{5... | collective-permute-start | bytes 1572872 | tf_op jit(solution)/shard_map/ppermute | solution.py:295
  34.2 5.4 %collective-permute-start.12 = (bf16[8,64,256]{2,1,0:T(8,128)(2,1)S(1)}, bf16[8,64,256]{2,1,0:T(8,128)(2,1)S(1)}, u32[]{:S(2)}, u32[]{:S(2)}) collective-permute-start(bf16[8,64,256]{2,1,0:T(8,128)(2,1)S(1)} %get-tuple-element.76), channel_id=1, source_target_pairs={{96,64},{97,65},{98,66},{99,67},{100,68},{101,69},{102,70},{103,71... | collective-permute-start | bytes 786440 | tf_op jit(solution)/shard_map/ppermute | solution.py:295
  37.5 2.8 %collective-permute-start.8 = (bf16[8,64,256]{2,1,0:T(8,128)(2,1)S(1)}, bf16[8,64,256]{2,1,0:T(8,128)(2,1)S(1)}, u32[]{:S(2)}, u32[]{:S(2)}) collective-permute-start(bf16[8,64,256]{2,1,0:T(8,128)(2,1)S(1)} %get-tuple-element.78), channel_id=1, source_target_pairs={{0,64},{1,65},{2,66},{3,67},{4,68},{5,69},{6,70},{7,71},{8,72},{9,... | collective-permute-start | bytes 786440 | tf_op jit(solution)/shard_map/ppermute | solution.py:367
  38.2 2.1 %collective-permute-start.9 = (bf16[5,64,256]{2,1,0:T(8,128)(2,1)S(1)}, bf16[5,64,256]{2,1,0:T(8,128)(2,1)S(1)}, u32[]{:S(2)}, u32[]{:S(2)}) collective-permute-start(bf16[5,64,256]{2,1,0:T(8,128)(2,1)S(1)} %get-tuple-element.79), channel_id=1, source_target_pairs={{0,65},{1,66},{2,67},{3,68},{4,69},{5,70},{6,71},{7,72},{8,73},{9,... | collective-permute-start | bytes 491528 | tf_op jit(solution)/shard_map/ppermute | solution.py:368
  38.9 1.4 %collective-permute-start.10 = (bf16[5,64,256]{2,1,0:T(8,128)(2,1)S(1)}, bf16[5,64,256]{2,1,0:T(8,128)(2,1)S(1)}, u32[]{:S(2)}, u32[]{:S(2)}) collective-permute-start(bf16[5,64,256]{2,1,0:T(8,128)(2,1)S(1)} %get-tuple-element.80), channel_id=1, source_target_pairs={{1,64},{2,65},{3,66},{4,67},{5,68},{6,69},{7,70},{8,71},{9,72},{10... | collective-permute-start | bytes 491528 | tf_op jit(solution)/shard_map/ppermute | solution.py:369
  39.6 4.4 %collective-permute-start.7 = (bf16[8,64,256]{2,1,0:T(8,128)(2,1)S(1)}, bf16[8,64,256]{2,1,0:T(8,128)(2,1)S(1)}, u32[]{:S(2)}, u32[]{:S(2)}) collective-permute-start(bf16[8,64,256]{2,1,0:T(8,128)(2,1)S(1)} %get-tuple-element.77), channel_id=1, source_target_pairs={{0,64},{1,65},{2,66},{3,67},{4,68},{5,69},{6,70},{7,71},{8,72},{9,... | collective-permute-start | bytes 786440 | tf_op jit(solution)/shard_map/ppermute | solution.py:370
  41.9 2.8 %collective-permute-start.15 = (bf16[5,64,256]{2,1,0:T(8,128)(2,1)S(1)}, bf16[5,64,256]{2,1,0:T(8,128)(2,1)S(1)}, u32[]{:S(2)}, u32[]{:S(2)}) collective-permute-start(bf16[5,64,256]{2,1,0:T(8,128)(2,1)S(1)} %get-tuple-element.92), channel_id=1, source_target_pairs={{64,129},{65,130},{66,131},{67,132},{68,133},{69,134},{70,135},{71... | collective-permute-start | bytes 491528 | tf_op jit(solution)/shard_map/ppermute | solution.py:368
  42.6 2.1 %collective-permute-start.16 = (bf16[5,64,256]{2,1,0:T(8,128)(2,1)S(1)}, bf16[5,64,256]{2,1,0:T(8,128)(2,1)S(1)}, u32[]{:S(2)}, u32[]{:S(2)}) collective-permute-start(bf16[5,64,256]{2,1,0:T(8,128)(2,1)S(1)} %get-tuple-element.93), channel_id=1, source_target_pairs={{65,128},{66,129},{67,130},{68,131},{69,132},{70,133},{71,134},{72... | collective-permute-start | bytes 491528 | tf_op jit(solution)/shard_map/ppermute | solution.py:369
  43.3 1.4 %collective-permute-start.14 = (bf16[8,64,256]{2,1,0:T(8,128)(2,1)S(1)}, bf16[8,64,256]{2,1,0:T(8,128)(2,1)S(1)}, u32[]{:S(2)}, u32[]{:S(2)}) collective-permute-start(bf16[8,64,256]{2,1,0:T(8,128)(2,1)S(1)} %get-tuple-element.91), channel_id=1, source_target_pairs={{64,128},{65,129},{66,130},{67,131},{68,132},{69,133},{70,134},{71... | collective-permute-start | bytes 786440 | tf_op jit(solution)/shard_map/ppermute | solution.py:367
  44.0 4.4 %collective-permute-start.13 = (bf16[8,64,256]{2,1,0:T(8,128)(2,1)S(1)}, bf16[8,64,256]{2,1,0:T(8,128)(2,1)S(1)}, u32[]{:S(2)}, u32[]{:S(2)}) collective-permute-start(bf16[8,64,256]{2,1,0:T(8,128)(2,1)S(1)} %get-tuple-element.90), channel_id=1, source_target_pairs={{64,128},{65,129},{66,130},{67,131},{68,132},{69,133},{70,134},{71... | collective-permute-start | bytes 786440 | tf_op jit(solution)/shard_map/ppermute | solution.py:370
  46.4 3.5 %collective-permute-start.19 = (bf16[4,64,256]{2,1,0:T(8,128)(2,1)S(1)}, bf16[4,64,256]{2,1,0:T(8,128)(2,1)S(1)}, u32[]{:S(2)}, u32[]{:S(2)}) collective-permute-start(bf16[4,64,256]{2,1,0:T(8,128)(2,1)S(1)} %get-tuple-element.105), channel_id=1, source_target_pairs={{128,193},{129,194},{130,195},{131,196},{132,197},{133,198},{134,1... | collective-permute-start | bytes 393224 | tf_op jit(solution)/shard_map/ppermute | solution.py:368
  47.0 2.8 %collective-permute-start.20 = (bf16[4,64,256]{2,1,0:T(8,128)(2,1)S(1)}, bf16[4,64,256]{2,1,0:T(8,128)(2,1)S(1)}, u32[]{:S(2)}, u32[]{:S(2)}) collective-permute-start(bf16[4,64,256]{2,1,0:T(8,128)(2,1)S(1)} %get-tuple-element.106), channel_id=1, source_target_pairs={{129,192},{130,193},{131,194},{132,195},{133,196},{134,197},{135,1... | collective-permute-start | bytes 393224 | tf_op jit(solution)/shard_map/ppermute | solution.py:369
  47.7 2.1 %collective-permute-start.18 = (bf16[8,64,256]{2,1,0:T(8,128)(2,1)S(1)}, bf16[8,64,256]{2,1,0:T(8,128)(2,1)S(1)}, u32[]{:S(2)}, u32[]{:S(2)}) collective-permute-start(bf16[8,64,256]{2,1,0:T(8,128)(2,1)S(1)} %get-tuple-element.104), channel_id=1, source_target_pairs={{128,192},{129,193},{130,194},{131,195},{132,196},{133,197},{134,1... | collective-permute-start | bytes 786440 | tf_op jit(solution)/shard_map/ppermute | solution.py:367
  48.4 7.0 %collective-permute-start.17 = (bf16[8,64,256]{2,1,0:T(8,128)(2,1)S(1)}, bf16[8,64,256]{2,1,0:T(8,128)(2,1)S(1)}, u32[]{:S(2)}, u32[]{:S(2)}) collective-permute-start(bf16[8,64,256]{2,1,0:T(8,128)(2,1)S(1)} %get-tuple-element.103), channel_id=1, source_target_pairs={{128,192},{129,193},{130,194},{131,195},{132,196},{133,197},{134,1... | collective-permute-start | bytes 786440 | tf_op jit(solution)/shard_map/ppermute | solution.py:370
  49.1 55.4 %collective-permute-start.26 = (f32[12,64,256]{2,1,0:T(8,128)S(1)}, f32[12,64,256]{2,1,0:T(8,128)S(1)}, u32[]{:S(2)}, u32[]{:S(2)}) collective-permute-start(f32[12,64,256]{2,1,0:T(8,128)S(1)} %get-tuple-element.124), channel_id=1, source_target_pairs={{0,32},{1,33},{2,34},{3,35},{4,36},{5,37},{6,38},{7,39},{8,40},{9,... | collective-permute-start | bytes 2359304 | tf_op jit(solution)/shard_map/ppermute | solution.py:377
  51.5 47.1 %collective-permute-start.23 = (bf16[3,64,256]{2,1,0:T(8,128)(2,1)S(1)}, bf16[3,64,256]{2,1,0:T(8,128)(2,1)S(1)}, u32[]{:S(2)}, u32[]{:S(2)}) collective-permute-start(bf16[3,64,256]{2,1,0:T(8,128)(2,1)S(1)} %get-tuple-element.116), channel_id=1, source_target_pairs={{192,225},{193,226},{194,227},{195,228},{196,229},{197,230},{198,2... | collective-permute-start | bytes 294920 | tf_op jit(solution)/shard_map/ppermute | solution.py:368
  52.8 46.5 %collective-permute-start.24 = (bf16[3,64,256]{2,1,0:T(8,128)(2,1)S(1)}, bf16[3,64,256]{2,1,0:T(8,128)(2,1)S(1)}, u32[]{:S(2)}, u32[]{:S(2)}) collective-permute-start(bf16[3,64,256]{2,1,0:T(8,128)(2,1)S(1)} %get-tuple-element.117), channel_id=1, source_target_pairs={{193,224},{194,225},{195,226},{196,227},{197,228},{198,229},{199,2... | collective-permute-start | bytes 294920 | tf_op jit(solution)/shard_map/ppermute | solution.py:369
  54.1 46.1 %collective-permute-start.22 = (bf16[8,64,256]{2,1,0:T(8,128)(2,1)S(1)}, bf16[8,64,256]{2,1,0:T(8,128)(2,1)S(1)}, u32[]{:S(2)}, u32[]{:S(2)}) collective-permute-start(bf16[8,64,256]{2,1,0:T(8,128)(2,1)S(1)} %get-tuple-element.115), channel_id=1, source_target_pairs={{192,224},{193,225},{194,226},{195,227},{196,228},{197,229},{198,2... | collective-permute-start | bytes 786440 | tf_op jit(solution)/shard_map/ppermute | solution.py:367
  55.4 47.6 %collective-permute-start.21 = (bf16[8,64,256]{2,1,0:T(8,128)(2,1)S(1)}, bf16[8,64,256]{2,1,0:T(8,128)(2,1)S(1)}, u32[]{:S(2)}, u32[]{:S(2)}) collective-permute-start(bf16[8,64,256]{2,1,0:T(8,128)(2,1)S(1)} %get-tuple-element.114), channel_id=1, source_target_pairs={{192,224},{193,225},{194,226},{195,227},{196,228},{197,229},{198,2... | collective-permute-start | bytes 786440 | tf_op jit(solution)/shard_map/ppermute | solution.py:370
  98.6 5.9 %collective-permute-start.27 = (f32[12,64,256]{2,1,0:T(8,128)S(1)}, f32[12,64,256]{2,1,0:T(8,128)S(1)}, u32[]{:S(2)}, u32[]{:S(2)}) collective-permute-start(f32[12,64,256]{2,1,0:T(8,128)S(1)} %get-tuple-element.125), channel_id=1, source_target_pairs={{64,48},{65,49},{66,50},{67,51},{68,52},{69,53},{70,54},{71,55},{7... | collective-permute-start | bytes 2359304 | tf_op jit(solution)/shard_map/ppermute | solution.py:377
  103.2 3.2 %collective-permute-start.25 = (f32[12,64,256]{2,1,0:T(8,128)S(1)}, f32[12,64,256]{2,1,0:T(8,128)S(1)}, u32[]{:S(2)}, u32[]{:S(2)}) collective-permute-start(f32[12,64,256]{2,1,0:T(8,128)S(1)} %get-tuple-element.123), channel_id=1, source_target_pairs={{0,16},{1,17},{2,18},{3,19},{4,20},{5,21},{6,22},{7,23},{8,24},{9,... | collective-permute-start | bytes 2359304 | tf_op jit(solution)/shard_map/ppermute | solution.py:377

commit v7 on v6

--- a/solution.py
+++ b/solution.py
@@ -63,20 +63,14 @@
     return (lax.axis_index("rows") * lax.axis_size("cols") + lax.axis_index("cols")) * rows
 
 
-def hold_kernel(given, held):
-    held[...] = given[...]
-
-
 def edge_kernel(pieces, low, high):
     rows, count = pieces.shape[1], low.shape[1]
     low[...] = pieces[:, :count].astype(BF16)
     high[...] = pieces[:, rows - count :].astype(BF16)
 
 
-def head_kernel(step, height, pieces, above, below, w0, layers, main, top, bottom, *rest):
-    jumps, (state, first, patch, second, w1, sem) = rest[:-6], rest[-6:]
-    load = pltpu.make_async_copy(layers.at[1], w1, sem.at[0])
-    load.start()
+def head_kernel(step, height, pieces, above, below, layers, main, top, bottom, *rest):
+    jumps, (state, first, patch, second) = rest[:-4], rest[-4:]
     ncols, rows, wide = pieces.shape[:3]
     halo = above.shape[1]
     deep = rows + 2 * halo
@@ -103,9 +97,8 @@
             if 0 <= place < ref.shape[0]:
                 ref[place] = jump.astype(ref.dtype)
 
-    slopes(patch, w0, 1, deep - 2, to_middle)
-    load.wait()
-    slopes(second, w1, 2, deep - 4, to_jump)
+    slopes(patch, layers.at[0], 1, deep - 2, to_middle)
+    slopes(second, layers.at[1], 2, deep - 4, to_jump)
 
 
 def turn_kernel(host, rows, count, kept, given, last, step, height, *rest):
@@ -113,6 +106,7 @@
     begin = len(rest) - (2 * count + given + outs + kept + 3)
     start, rest = rest[:begin], rest[begin:]
     weights, jumps = rest[:count], rest[count : 2 * count]
+    weights = [weight.at[0] if len(weight.shape) == 4 else weight for weight in weights]
     rest = rest[2 * count + given :]
     if not last:
         out, out_top, out_bottom, left = rest[:4]
@@ -208,10 +202,7 @@
                 packed[k, start : start + wide] = (mine - high.astype(F32)).astype(BF16)
 
 
-def tail_kernel(step, height, width, packed, layers, fine, coarse, state, patch, second, held, sems):
-    loads = [pltpu.make_async_copy(layers.at[k], held.at[k], sems.at[k]) for k in range(2)]
-    for load in loads:
-        load.start()
+def tail_kernel(step, height, width, packed, layers, fine, coarse, state, patch, second):
     ncols = packed.shape[0]
     tile_rows, wide = coarse.shape[:2]
     rows = tile_rows // ncols
@@ -244,17 +235,15 @@
     def to_ending(row, slope):
         fine[1, row - KEPT] = fine[0, row - KEPT] + step * slope[:wide]
 
-    loads[0].wait()
-    slopes(patch, held.at[0], 1, tile_rows + 2, to_middle, 2 * CHUNK)
-    loads[1].wait()
-    slopes(second, held.at[1], 2, tile_rows, to_ending, 2 * CHUNK)
-
-
-def call(kernel, outs, scratch, inputs, aliases={}, far=None, vmem=12 << 20, work=0):
+    slopes(patch, layers.at[0], 1, tile_rows + 2, to_middle, 2 * CHUNK)
+    slopes(second, layers.at[1], 2, tile_rows, to_ending, 2 * CHUNK)
+
+
+def call(kernel, outs, scratch, inputs, aliases={}, vmem=12 << 20, work=0):
     return pl.pallas_call(
         kernel,
         out_shape=[jax.ShapeDtypeStruct(*o) for o in outs],
-        in_specs=[pl.BlockSpec(memory_space=pl.ANY if k == far else pltpu.VMEM) for k in range(len(inputs))],
+        in_specs=[pl.BlockSpec(memory_space=pltpu.VMEM)] * len(inputs),
         out_specs=[pl.BlockSpec(memory_space=pltpu.VMEM)] * len(outs),
         scratch_shapes=scratch,
         input_output_aliases=aliases,
@@ -273,7 +262,6 @@
     step = 2.0 / (2 * ndepth)
     flat = weights.reshape(2, 3, 3 * channels, channels)
     w0 = flat[0]
-    held = pltpu.VMEM(w0.shape, BF16)
 
     hosts = [*range(0, ndepth, 4), ndepth - 2]
     visits = [["own", "core", "next"]] + [["prev", "own", "core", "next"]] * (len(hosts) - 2) + [["own"]]
@@ -302,7 +290,7 @@
     low, high = call(edge_kernel, [((ncols, near, tile_cols, channels), BF16)] * 2, [], (pieces,))
     above, below = ring(high, 1), ring(low, -1)
     far = ("next", "core", "prev")
-    all_weights = {"own": w0} | {slot: fetch(w0, slot) for slot in far}
+    all_weights = {"own": flat} | {slot: fetch(w0, slot) for slot in far}
     like = lambda n, t=F32: ((n, width, channels), t)
     vm = lambda n: pltpu.VMEM((n, width, channels), F32)
     patch = lambda n: pltpu.VMEM((n, width, 3 * channels), BF16)
@@ -312,9 +300,9 @@
         functools.partial(head_kernel, step, height),
         [like(rows), like(halos[0], BF16), like(halos[0], BF16)]
         + [like(rows + 2 * JUMP_HALO[slot], kinds[slot]) for slot in SLOTS],
-        [vm(deep), vm(deep), patch(deep), patch(deep), held, pltpu.SemaphoreType.DMA((1,))],
-        (pieces, above, below, w0, flat),
-        far=4,
+        [vm(deep), vm(deep), patch(deep), patch(deep)],
+        (pieces, above, below, flat),
+        work=10_000_000_000,
     )
     all_jumps = dict(zip(SLOTS, jumps))
     first_jump = fetch(all_jumps["next"], "next", hosts[:1])
@@ -348,8 +336,6 @@
         saved |= zip(keeps, results[len(outs) :])
         if turn == 0:
             start = (saved["next"],)
-            weight = all_weights["next"]
-            (all_weights["next"],) = call(hold_kernel, [(weight.shape, BF16)], [], (weight,))
             continue
         if turn > 1:
             inputs = (low, *(() if last else results[3:4]), *(saved[slot] for slot in keeps))
@@ -389,10 +375,8 @@
     fine, coarse = call(
         functools.partial(tail_kernel, step, height, width),
         [((2, *tile.shape), F32), (tile.shape, F32)],
-        [tall(tile_rows + 4), tall(tile_rows + 4, BF16, 3), tall(tile_rows + 4, BF16, 3)]
-        + [pltpu.VMEM(flat.shape, BF16), pltpu.SemaphoreType.DMA((2,))],
+        [tall(tile_rows + 4), tall(tile_rows + 4, BF16, 3), tall(tile_rows + 4, BF16, 3)],
         (packed, flat),
-        far=1,
     )
     return fine, coarse[None]
 

time: 130 us -> 129 us (level)
  blocking collectives: 16.9 us -> 29.1 us
  Pallas kernels: 21.6 us -> 11.2 us
  starting transfers between devices: 32.5 us -> 25.2 us
  waiting for transfers between devices: 55.6 us -> 60.2 us
    all_to_all x0 -> x1, blocking collectives: none -> 14 us  [on_device(): lax.all_to_all(tile.reshape(ncols, rows, tile_cols, channels), 'cols', 0,...]
    ppermute x4, waiting for transfers between devices: 41.9 us -> 53.7 us  [on_device(): top = lax.ppermute(results[2], AXES, route(pair, 1))]
    pallas_call x15 -> x14, Pallas kernels: 21.6 us -> 11.2 us  [call(): pl.pallas_call(kernel, out_shape=[jax.ShapeDtypeStruct(*o) for o in outs]...]
    all_to_all x1 -> x0, waiting for transfers between devices: 6.21 us -> none  [on_device(): lax.all_to_all(tile.reshape(ncols, rows, tile_cols, channels), 'cols', 0,...]
    all_to_all x1 -> x0, starting transfers between devices: 4.46 us -> none  [on_device(): lax.all_to_all(tile.reshape(ncols, rows, tile_cols, channels), 'cols', 0,...]
    ppermute x2, waiting for transfers between devices: 3.65 us -> 0.06 us  [ring(): lax.ppermute(x, ('rows', 'cols'), [(s, (s + shift) % strips) for s in ran...]
    ppermute x7, starting transfers between devices: 7.83 us -> 4.97 us  [fetch(): return lax.ppermute(x, AXES, route(pairs, 0))]
    ppermute x4, waiting for transfers between devices: 0.85 us -> 3.45 us  [on_device(): main = lax.ppermute(results[0], AXES, route(pair, 0))]
  transfers between devices with their start and end apart: 29 -> 28, of which waited for: 6 -> 5; matrix products, arithmetic and copies ran while one was open for 0% -> 1% of each run, Pallas kernels for 12% -> 5%
where the time goes in v7:
time: 129 us; the launch traced here: 128 us
  waiting for transfers between devices  60.2 us (47%)
  blocking collectives  29.1 us (23%)
  starting transfers between devices  25.2 us (20%)
  Pallas kernels  11.2 us (9%)
  local copies, waits for them, and re-layouts  1.35 us (1%)
    ppermute x4, waiting for transfers between devices, on_device(): top = lax.ppermute(results[2], AXES, route(pair, 1))  53.7 us
    all_to_all x1, blocking collectives, on_device(): packed = lax.all_to_all(packed, 'cols', 0, 0, tiled=True)  15.1 us
    all_to_all x1, blocking collectives, on_device(): lax.all_to_all(tile.reshape(ncols, rows, tile_cols, channels), 'cols', 0,...  14 us
    pallas_call x14, Pallas kernels, call(): pl.pallas_call(kernel, out_shape=[jax.ShapeDtypeStruct(*o) for o in outs]...  11.2 us
    ppermute x7, starting transfers between devices, fetch(): return lax.ppermute(x, AXES, route(pairs, 0))  4.97 us
    ppermute x2, starting transfers between devices, ring(): lax.ppermute(x, ('rows', 'cols'), [(s, (s + shift) % strips) for s in ran...  4.21 us
    ppermute x4, waiting for transfers between devices, on_device(): main = lax.ppermute(results[0], AXES, route(pair, 0))  3.45 us
    ppermute x4, starting transfers between devices, on_device(): main = lax.ppermute(results[0], AXES, route(pair, 0))  3.32 us
  transfers between devices with their start and end apart: 28, of which 5 were waited for; matrix products, arithmetic and copies ran while one was open for 1% of the time, Pallas kernels for 5%

profile of v7, /device:TPU:226, one launch (start us, length us, event | category | flops | bytes accessed | tf_op | source)
XLA Modules:
  0.0 128.2 jit_solution(13871714088234290450)
XLA Ops:
  0.6 14.0 %all_to_all.10.pieces = f32[4,8,16,256]{3,2,1,0:T(8,128)S(1)} all-to-all(f32[4,8,16,256]{3,2,1,0:T(8,128)} %bitcast.14), channel_id=1, replica_groups=mesh['depth'=16,'rows'=4,'cols'=4] {'cols'}, dimensions={0} | all-to-all | bytes 1048576 | tf_op jit(solution)/shard_map/all_to_all | solution.py:288
  14.6 0.6 collective-permute-start
  15.3 3.6 %collective-permute-start.1 = (bf16[4,6,16,256]{3,2,1,0:T(8,128)(2,1)S(1)}, bf16[4,6,16,256]{3,2,1,0:T(8,128)(2,1)S(1)}, u32[]{:S(2)}, u32[]{:S(2)}) collective-permute-start(bf16[4,6,16,256]{3,2,1,0:T(8,128)(2,1)S(1)} %get-tuple-element.66), channel_id=1, source_target_pairs={{0,15},{1,0},{2,1},{3,2},{4,3},{5,4},{6,5},{7,6},{8,7},{9,8},{10,9... | collective-permute-start | bytes 589832 | tf_op jit(solution)/shard_map/ppermute | solution.py:286
  18.8 1.3 %slice.4 = bf16[1,3,3,256,256]{4,3,2,1,0:T(8,128)(2,1)S(1)} slice(bf16[2,3,3,256,256]{4,3,2,1,0:T(8,128)(2,1)} %param.3), slice={[0:1], [0:3], [0:3], [0:256], [0:256]} | slice | bytes 2359296 | tf_op jit(solution)/shard_map/slice | solution.py:264
  20.2 0.7 collective-permute-start.5
  20.9 0.7 collective-permute-start.3
  21.7 0.7 collective-permute-start.2
  22.4 0.1 collective-permute-done.above
  22.5 3.6 %shard_map.42 = (f32[8,64,256]{2,1,0:T(8,128)S(1)}, bf16[4,64,256]{2,1,0:T(8,128)(2,1)S(1)}, bf16[4,64,256]{2,1,0:T(8,128)(2,1)S(1)}, bf16[16,64,256]{2,1,0:T(8,...) custom-call(f32[4,8,16,256]{3,2,1,0:T(8,128)S(1)} %all_to_all.10.pieces, ...), custom_call_target="tpu_custom_call" | custom-call | flops 10000000000 | tf_op jit(solution)/shard_map/pallas_call | solution.py:243
  26.1 0.7 collective-permute-start.4
  26.8 0.7 collective-permute-start.6
  27.5 0.7 collective-permute-start.11
  28.2 0.0 collective-permute-done.3.rest_4_.rest_5_
  28.2 0.7 collective-permute-start.12
  29.0 0.7 collective-permute-start.8
  29.7 0.7 collective-permute-start.9
  30.4 0.7 collective-permute-start.10
  31.1 0.0 collective-permute-done.12.rest_10_
  31.1 0.7 collective-permute-start.7
  31.8 0.0 collective-permute-done.9.rest_1_
  31.8 0.0 collective-permute-done.10.rest_2_
  31.8 0.2 shard_map.45
  32.0 0.7 collective-permute-start.15
  32.7 0.7 collective-permute-start.16
  33.4 0.7 collective-permute-start.14
  34.1 0.7 collective-permute-start.13
  34.8 0.0 collective-permute-done.15.rest_1_
  34.8 0.7 collective-permute-start.19
  35.5 0.7 collective-permute-start.20
  36.2 0.7 collective-permute-start.18
  36.9 0.7 collective-permute-start.17
  37.6 0.7 collective-permute-start.26
  38.3 0.2 shard_map.49
  38.6 1.3 %collective-permute-start.23 = (bf16[3,64,256]{2,1,0:T(8,128)(2,1)S(1)}, bf16[3,64,256]{2,1,0:T(8,128)(2,1)S(1)}, u32[]{:S(2)}, u32[]{:S(2)}) collective-permute-start(bf16[3,64,256]{2,1,0:T(8,128)(2,1)S(1)} %get-tuple-element.116), channel_id=1, source_target_pairs={{192,225},{193,226},{194,227},{195,228},{196,229},{197,230},{198,2... | collective-permute-start | bytes 294920 | tf_op jit(solution)/shard_map/ppermute | solution.py:354
  39.9 1.3 %collective-permute-start.24 = (bf16[3,64,256]{2,1,0:T(8,128)(2,1)S(1)}, bf16[3,64,256]{2,1,0:T(8,128)(2,1)S(1)}, u32[]{:S(2)}, u32[]{:S(2)}) collective-permute-start(bf16[3,64,256]{2,1,0:T(8,128)(2,1)S(1)} %get-tuple-element.117), channel_id=1, source_target_pairs={{193,224},{194,225},{195,226},{196,227},{197,228},{198,229},{199,2... | collective-permute-start | bytes 294920 | tf_op jit(solution)/shard_map/ppermute | solution.py:355
  41.2 1.3 %collective-permute-start.22 = (bf16[8,64,256]{2,1,0:T(8,128)(2,1)S(1)}, bf16[8,64,256]{2,1,0:T(8,128)(2,1)S(1)}, u32[]{:S(2)}, u32[]{:S(2)}) collective-permute-start(bf16[8,64,256]{2,1,0:T(8,128)(2,1)S(1)} %get-tuple-element.115), channel_id=1, source_target_pairs={{192,224},{193,225},{194,226},{195,227},{196,228},{197,229},{198,2... | collective-permute-start | bytes 786440 | tf_op jit(solution)/shard_map/ppermute | solution.py:353
  42.5 1.3 %collective-permute-start.21 = (bf16[8,64,256]{2,1,0:T(8,128)(2,1)S(1)}, bf16[8,64,256]{2,1,0:T(8,128)(2,1)S(1)}, u32[]{:S(2)}, u32[]{:S(2)}) collective-permute-start(bf16[8,64,256]{2,1,0:T(8,128)(2,1)S(1)} %get-tuple-element.114), channel_id=1, source_target_pairs={{192,224},{193,225},{194,226},{195,227},{196,228},{197,229},{198,2... | collective-permute-start | bytes 786440 | tf_op jit(solution)/shard_map/ppermute | solution.py:356
  43.8 53.7 %collective-permute-done.23.rest_1_ = bf16[3,64,256]{2,1,0:T(8,128)(2,1)S(1)} collective-permute-done((bf16[3,64,256]{2,1,0:T(8,128)(2,1)S(1)}, bf16[3,64,256]{2,1,0:T(8,128)(2,1)S(1)}, u32[]{:S(2)}, u32[]{:S(2)}) %collective-permute-start.23) | collective-permute-done | bytes 98336 | tf_op jit(solution)/shard_map/ppermute | solution.py:354
  97.5 0.7 collective-permute-start.27
  98.2 3.4 %collective-permute-done.22.rest_0_ = bf16[8,64,256]{2,1,0:T(8,128)(2,1)S(1)} collective-permute-done((bf16[8,64,256]{2,1,0:T(8,128)(2,1)S(1)}, bf16[8,64,256]{2,1,0:T(8,128)(2,1)S(1)}, u32[]{:S(2)}, u32[]{:S(2)}) %collective-permute-start.22) | collective-permute-done | bytes 262176 | tf_op jit(solution)/shard_map/ppermute | solution.py:353
  101.7 1.7 %shard_map.51 = (f32[12,64,256]{2,1,0:T(8,128)S(1)}, f32[12,64,256]{2,1,0:T(8,128)S(1)}) custom-call(bf16[8,64,256]{2,1,0:T(8,128)(2,1)S(1)} %collective-permute-done.22.rest_0_, bf16[3,64,256]{2,1,0:T(8,128)(2,1)S(1)} %collective-permute-done.23.rest_1_, ...), custom_call_target="tpu_custom_call", output_to_operand_aliasing={{0}: (5, {}), {1}: (6, {})} | custom-call | flops 20000000000 | tf_op jit(solution)/shard_map/pallas_call | solution.py:243
  103.3 1.1 collective-permute-done.21.low
  104.5 0.2 shard_map.52
  104.6 1.3 %collective-permute-start.25 = (f32[12,64,256]{2,1,0:T(8,128)S(1)}, f32[12,64,256]{2,1,0:T(8,128)S(1)}, u32[]{:S(2)}, u32[]{:S(2)}) collective-permute-start(f32[12,64,256]{2,1,0:T(8,128)S(1)} %get-tuple-element.123), channel_id=1, source_target_pairs={{0,16},{1,17},{2,18},{3,19},{4,20},{5,21},{6,22},{7,23},{8,24},{9,... | collective-permute-start | bytes 2359304 | tf_op jit(solution)/shard_map/ppermute | solution.py:363
  106.0 1.8 %collective-permute-done.25.core = f32[12,64,256]{2,1,0:T(8,128)S(1)} collective-permute-done((f32[12,64,256]{2,1,0:T(8,128)S(1)}, f32[12,64,256]{2,1,0:T(8,128)S(1)}, u32[]{:S(2)}, u32[]{:S(2)}) %collective-permute-start.25) | collective-permute-done | bytes 786464 | tf_op jit(solution)/shard_map/ppermute | solution.py:363
  107.8 0.1 shard_map.53
  108.0 15.1 %all_to_all.11.packed = bf16[4,368,256]{2,1,0:T(8,128)(2,1)S(1)} all-to-all(bf16[4,368,256]{2,1,0:T(8,128)(2,1)S(1)} %shard_map.53), channel_id=1, replica_groups=mesh['depth'=16,'rows'=4,'cols'=4] {'cols'}, dimensions={0} | all-to-all | bytes 1507328 | tf_op jit(solution)/shard_map/all_to_all | solution.py:373
  123.1 5.1 %shard_map.54 = (f32[2,32,16,256]{3,2,1,0:T(8,128)}, f32[32,16,256]{2,1,0:T(8,128)}) custom-call(bf16[4,368,256]{2,1,0:T(8,128)(2,1)S(1)} %all_to_all.11.packed, bf16[2,3,768,256]{3,2,1,0:T(8,128)(2,1)S(1)} %bitcast.10), custom_call_target="tpu_custom_call" | custom-call | tf_op jit(solution)/shard_map/pallas_call | solution.py:243
  (27 shorter events, 0.2 us)
Async XLA Ops:
  14.6 7.9 %collective-permute-start = (bf16[4,6,16,256]{3,2,1,0:T(8,128)(2,1)S(1)}, bf16[4,6,16,256]{3,2,1,0:T(8,128)(2,1)S(1)}, u32[]{:S(2)}, u32[]{:S(2)}) collective-permute-start(bf16[4,6,16,256]{3,2,1,0:T(8,128)(2,1)S(1)} %get-tuple-element.65), channel_id=1, source_target_pairs={{0,1},{1,2},{2,3},{3,4},{4,5},{5,6},{6,7},{7,8},{8,9},{9,10},{10,1... | collective-permute-start | bytes 589832 | tf_op jit(solution)/shard_map/ppermute | solution.py:286
  15.3 7.2 %copy-start = (bf16[2,3,3,256,256]{4,3,2,1,0:T(8,128)(2,1)S(1)}, bf16[2,3,3,256,256]{4,3,2,1,0:T(8,128)(2,1)}, u32[]{:S(2)}) copy-start(bf16[2,3,3,256,256]{4,3,2,1,0:T(8,128)(2,1)} %param.3) | copy-start | bytes 7077892
  15.3 7.2 %collective-permute-start.1 = (bf16[4,6,16,256]{3,2,1,0:T(8,128)(2,1)S(1)}, bf16[4,6,16,256]{3,2,1,0:T(8,128)(2,1)S(1)}, u32[]{:S(2)}, u32[]{:S(2)}) collective-permute-start(bf16[4,6,16,256]{3,2,1,0:T(8,128)(2,1)S(1)} %get-tuple-element.66), channel_id=1, source_target_pairs={{0,15},{1,0},{2,1},{3,2},{4,3},{5,4},{6,5},{7,6},{8,7},{9,8},{10,9... | collective-permute-start | bytes 589832 | tf_op jit(solution)/shard_map/ppermute | solution.py:286
  20.2 8.8 %collective-permute-start.5 = (bf16[3,768,256]{2,1,0:T(8,128)(2,1)S(1)}, bf16[3,768,256]{2,1,0:T(8,128)(2,1)S(1)}, u32[]{:S(2)}, u32[]{:S(2)}) collective-permute-start(bf16[3,768,256]{2,1,0:T(8,128)(2,1)S(1)} %bitcast.11), channel_id=1, source_target_pairs={{32,0},{33,1},{34,2},{35,3},{36,4},{37,5},{38,6},{39,7},{40,8},{41... | collective-permute-start | bytes 3538952 | tf_op jit(solution)/shard_map/ppermute | solution.py:283
  20.9 7.3 %collective-permute-start.3 = (bf16[3,768,256]{2,1,0:T(8,128)(2,1)S(1)}, bf16[3,768,256]{2,1,0:T(8,128)(2,1)S(1)}, u32[]{:S(2)}, u32[]{:S(2)}) collective-permute-start(bf16[3,768,256]{2,1,0:T(8,128)(2,1)S(1)} %bitcast.12), channel_id=1, source_target_pairs={{16,0},{17,1},{18,2},{19,3},{20,4},{21,5},{22,6},{23,7},{24,8},{25... | collective-permute-start | bytes 3538952 | tf_op jit(solution)/shard_map/ppermute | solution.py:283
  21.7 5.9 %collective-permute-start.2 = (bf16[3,768,256]{2,1,0:T(8,128)(2,1)S(1)}, bf16[3,768,256]{2,1,0:T(8,128)(2,1)S(1)}, u32[]{:S(2)}, u32[]{:S(2)}) collective-permute-start(bf16[3,768,256]{2,1,0:T(8,128)(2,1)S(1)} %bitcast.13), channel_id=1, source_target_pairs={{48,64},{49,65},{50,66},{51,67},{52,68},{53,69},{54,70},{55,71},{5... | collective-permute-start | bytes 3538952 | tf_op jit(solution)/shard_map/ppermute | solution.py:283
  26.1 2.8 %collective-permute-start.4 = (f32[12,64,256]{2,1,0:T(8,128)S(1)}, f32[12,64,256]{2,1,0:T(8,128)S(1)}, u32[]{:S(2)}, u32[]{:S(2)}) collective-permute-start(f32[12,64,256]{2,1,0:T(8,128)S(1)} %get-tuple-element.74), channel_id=1, source_target_pairs={{16,0},{17,1},{18,2},{19,3},{20,4},{21,5},{22,6},{23,7},{24,8},{25... | collective-permute-start | bytes 2359304 | tf_op jit(solution)/shard_map/ppermute | solution.py:283
  26.8 2.1 %collective-permute-start.6 = (bf16[8,64,256]{2,1,0:T(8,128)(2,1)S(1)}, bf16[8,64,256]{2,1,0:T(8,128)(2,1)S(1)}, u32[]{:S(2)}, u32[]{:S(2)}) collective-permute-start(bf16[8,64,256]{2,1,0:T(8,128)(2,1)S(1)} %get-tuple-element.76), channel_id=1, source_target_pairs={{32,0},{33,1},{34,2},{35,3},{36,4},{37,5},{38,6},{39,7},{40,8},{41... | collective-permute-start | bytes 786440 | tf_op jit(solution)/shard_map/ppermute | solution.py:283
  27.5 4.2 %collective-permute-start.11 = (bf16[16,64,256]{2,1,0:T(8,128)(2,1)S(1)}, bf16[16,64,256]{2,1,0:T(8,128)(2,1)S(1)}, u32[]{:S(2)}, u32[]{:S(2)}) collective-permute-start(bf16[16,64,256]{2,1,0:T(8,128)(2,1)S(1)} %get-tuple-element.82), channel_id=1, source_target_pairs={{48,64},{49,65},{50,66},{51,67},{52,68},{53,69},{54,70},{55,71},{5... | collective-permute-start | bytes 1572872 | tf_op jit(solution)/shard_map/ppermute | solution.py:283
  28.2 2.8 %collective-permute-start.12 = (bf16[8,64,256]{2,1,0:T(8,128)(2,1)S(1)}, bf16[8,64,256]{2,1,0:T(8,128)(2,1)S(1)}, u32[]{:S(2)}, u32[]{:S(2)}) collective-permute-start(bf16[8,64,256]{2,1,0:T(8,128)(2,1)S(1)} %get-tuple-element.76), channel_id=1, source_target_pairs={{96,64},{97,65},{98,66},{99,67},{100,68},{101,69},{102,70},{103,71... | collective-permute-start | bytes 786440 | tf_op jit(solution)/shard_map/ppermute | solution.py:283
  29.0 2.8 %collective-permute-start.8 = (bf16[8,64,256]{2,1,0:T(8,128)(2,1)S(1)}, bf16[8,64,256]{2,1,0:T(8,128)(2,1)S(1)}, u32[]{:S(2)}, u32[]{:S(2)}) collective-permute-start(bf16[8,64,256]{2,1,0:T(8,128)(2,1)S(1)} %get-tuple-element.78), channel_id=1, source_target_pairs={{0,64},{1,65},{2,66},{3,67},{4,68},{5,69},{6,70},{7,71},{8,72},{9,... | collective-permute-start | bytes 786440 | tf_op jit(solution)/shard_map/ppermute | solution.py:353
  29.7 2.1 %collective-permute-start.9 = (bf16[5,64,256]{2,1,0:T(8,128)(2,1)S(1)}, bf16[5,64,256]{2,1,0:T(8,128)(2,1)S(1)}, u32[]{:S(2)}, u32[]{:S(2)}) collective-permute-start(bf16[5,64,256]{2,1,0:T(8,128)(2,1)S(1)} %get-tuple-element.79), channel_id=1, source_target_pairs={{0,65},{1,66},{2,67},{3,68},{4,69},{5,70},{6,71},{7,72},{8,73},{9,... | collective-permute-start | bytes 491528 | tf_op jit(solution)/shard_map/ppermute | solution.py:354
  30.4 1.4 %collective-permute-start.10 = (bf16[5,64,256]{2,1,0:T(8,128)(2,1)S(1)}, bf16[5,64,256]{2,1,0:T(8,128)(2,1)S(1)}, u32[]{:S(2)}, u32[]{:S(2)}) collective-permute-start(bf16[5,64,256]{2,1,0:T(8,128)(2,1)S(1)} %get-tuple-element.80), channel_id=1, source_target_pairs={{1,64},{2,65},{3,66},{4,67},{5,68},{6,69},{7,70},{8,71},{9,72},{10... | collective-permute-start | bytes 491528 | tf_op jit(solution)/shard_map/ppermute | solution.py:355
  31.1 3.0 %collective-permute-start.7 = (bf16[8,64,256]{2,1,0:T(8,128)(2,1)S(1)}, bf16[8,64,256]{2,1,0:T(8,128)(2,1)S(1)}, u32[]{:S(2)}, u32[]{:S(2)}) collective-permute-start(bf16[8,64,256]{2,1,0:T(8,128)(2,1)S(1)} %get-tuple-element.77), channel_id=1, source_target_pairs={{0,64},{1,65},{2,66},{3,67},{4,68},{5,69},{6,70},{7,71},{8,72},{9,... | collective-permute-start | bytes 786440 | tf_op jit(solution)/shard_map/ppermute | solution.py:356
  32.0 2.8 %collective-permute-start.15 = (bf16[5,64,256]{2,1,0:T(8,128)(2,1)S(1)}, bf16[5,64,256]{2,1,0:T(8,128)(2,1)S(1)}, u32[]{:S(2)}, u32[]{:S(2)}) collective-permute-start(bf16[5,64,256]{2,1,0:T(8,128)(2,1)S(1)} %get-tuple-element.92), channel_id=1, source_target_pairs={{64,129},{65,130},{66,131},{67,132},{68,133},{69,134},{70,135},{71... | collective-permute-start | bytes 491528 | tf_op jit(solution)/shard_map/ppermute | solution.py:354
  32.7 2.1 %collective-permute-start.16 = (bf16[5,64,256]{2,1,0:T(8,128)(2,1)S(1)}, bf16[5,64,256]{2,1,0:T(8,128)(2,1)S(1)}, u32[]{:S(2)}, u32[]{:S(2)}) collective-permute-start(bf16[5,64,256]{2,1,0:T(8,128)(2,1)S(1)} %get-tuple-element.93), channel_id=1, source_target_pairs={{65,128},{66,129},{67,130},{68,131},{69,132},{70,133},{71,134},{72... | collective-permute-start | bytes 491528 | tf_op jit(solution)/shard_map/ppermute | solution.py:355
  33.4 1.4 %collective-permute-start.14 = (bf16[8,64,256]{2,1,0:T(8,128)(2,1)S(1)}, bf16[8,64,256]{2,1,0:T(8,128)(2,1)S(1)}, u32[]{:S(2)}, u32[]{:S(2)}) collective-permute-start(bf16[8,64,256]{2,1,0:T(8,128)(2,1)S(1)} %get-tuple-element.91), channel_id=1, source_target_pairs={{64,128},{65,129},{66,130},{67,131},{68,132},{69,133},{70,134},{71... | collective-permute-start | bytes 786440 | tf_op jit(solution)/shard_map/ppermute | solution.py:353
  34.1 2.8 %collective-permute-start.13 = (bf16[8,64,256]{2,1,0:T(8,128)(2,1)S(1)}, bf16[8,64,256]{2,1,0:T(8,128)(2,1)S(1)}, u32[]{:S(2)}, u32[]{:S(2)}) collective-permute-start(bf16[8,64,256]{2,1,0:T(8,128)(2,1)S(1)} %get-tuple-element.90), channel_id=1, source_target_pairs={{64,128},{65,129},{66,130},{67,131},{68,132},{69,133},{70,134},{71... | collective-permute-start | bytes 786440 | tf_op jit(solution)/shard_map/ppermute | solution.py:356
  34.8 3.5 %collective-permute-start.19 = (bf16[4,64,256]{2,1,0:T(8,128)(2,1)S(1)}, bf16[4,64,256]{2,1,0:T(8,128)(2,1)S(1)}, u32[]{:S(2)}, u32[]{:S(2)}) collective-permute-start(bf16[4,64,256]{2,1,0:T(8,128)(2,1)S(1)} %get-tuple-element.105), channel_id=1, source_target_pairs={{128,193},{129,194},{130,195},{131,196},{132,197},{133,198},{134,1... | collective-permute-start | bytes 393224 | tf_op jit(solution)/shard_map/ppermute | solution.py:354
  35.5 2.8 %collective-permute-start.20 = (bf16[4,64,256]{2,1,0:T(8,128)(2,1)S(1)}, bf16[4,64,256]{2,1,0:T(8,128)(2,1)S(1)}, u32[]{:S(2)}, u32[]{:S(2)}) collective-permute-start(bf16[4,64,256]{2,1,0:T(8,128)(2,1)S(1)} %get-tuple-element.106), channel_id=1, source_target_pairs={{129,192},{130,193},{131,194},{132,195},{133,196},{134,197},{135,1... | collective-permute-start | bytes 393224 | tf_op jit(solution)/shard_map/ppermute | solution.py:355
  36.2 2.1 %collective-permute-start.18 = (bf16[8,64,256]{2,1,0:T(8,128)(2,1)S(1)}, bf16[8,64,256]{2,1,0:T(8,128)(2,1)S(1)}, u32[]{:S(2)}, u32[]{:S(2)}) collective-permute-start(bf16[8,64,256]{2,1,0:T(8,128)(2,1)S(1)} %get-tuple-element.104), channel_id=1, source_target_pairs={{128,192},{129,193},{130,194},{131,195},{132,196},{133,197},{134,1... | collective-permute-start | bytes 786440 | tf_op jit(solution)/shard_map/ppermute | solution.py:353
  36.9 5.6 %collective-permute-start.17 = (bf16[8,64,256]{2,1,0:T(8,128)(2,1)S(1)}, bf16[8,64,256]{2,1,0:T(8,128)(2,1)S(1)}, u32[]{:S(2)}, u32[]{:S(2)}) collective-permute-start(bf16[8,64,256]{2,1,0:T(8,128)(2,1)S(1)} %get-tuple-element.103), channel_id=1, source_target_pairs={{128,192},{129,193},{130,194},{131,195},{132,196},{133,197},{134,1... | collective-permute-start | bytes 786440 | tf_op jit(solution)/shard_map/ppermute | solution.py:356
  37.6 68.4 %collective-permute-start.26 = (f32[12,64,256]{2,1,0:T(8,128)S(1)}, f32[12,64,256]{2,1,0:T(8,128)S(1)}, u32[]{:S(2)}, u32[]{:S(2)}) collective-permute-start(f32[12,64,256]{2,1,0:T(8,128)S(1)} %get-tuple-element.124), channel_id=1, source_target_pairs={{0,32},{1,33},{2,34},{3,35},{4,36},{5,37},{6,38},{7,39},{8,40},{9,... | collective-permute-start | bytes 2359304 | tf_op jit(solution)/shard_map/ppermute | solution.py:363
  38.6 58.9 %collective-permute-start.23 = (bf16[3,64,256]{2,1,0:T(8,128)(2,1)S(1)}, bf16[3,64,256]{2,1,0:T(8,128)(2,1)S(1)}, u32[]{:S(2)}, u32[]{:S(2)}) collective-permute-start(bf16[3,64,256]{2,1,0:T(8,128)(2,1)S(1)} %get-tuple-element.116), channel_id=1, source_target_pairs={{192,225},{193,226},{194,227},{195,228},{196,229},{197,230},{198,2... | collective-permute-start | bytes 294920 | tf_op jit(solution)/shard_map/ppermute | solution.py:354
  39.9 58.3 %collective-permute-start.24 = (bf16[3,64,256]{2,1,0:T(8,128)(2,1)S(1)}, bf16[3,64,256]{2,1,0:T(8,128)(2,1)S(1)}, u32[]{:S(2)}, u32[]{:S(2)}) collective-permute-start(bf16[3,64,256]{2,1,0:T(8,128)(2,1)S(1)} %get-tuple-element.117), channel_id=1, source_target_pairs={{193,224},{194,225},{195,226},{196,227},{197,228},{198,229},{199,2... | collective-permute-start | bytes 294920 | tf_op jit(solution)/shard_map/ppermute | solution.py:355
  41.2 60.5 %collective-permute-start.22 = (bf16[8,64,256]{2,1,0:T(8,128)(2,1)S(1)}, bf16[8,64,256]{2,1,0:T(8,128)(2,1)S(1)}, u32[]{:S(2)}, u32[]{:S(2)}) collective-permute-start(bf16[8,64,256]{2,1,0:T(8,128)(2,1)S(1)} %get-tuple-element.115), channel_id=1, source_target_pairs={{192,224},{193,225},{194,226},{195,227},{196,228},{197,229},{198,2... | collective-permute-start | bytes 786440 | tf_op jit(solution)/shard_map/ppermute | solution.py:353
  42.5 61.9 %collective-permute-start.21 = (bf16[8,64,256]{2,1,0:T(8,128)(2,1)S(1)}, bf16[8,64,256]{2,1,0:T(8,128)(2,1)S(1)}, u32[]{:S(2)}, u32[]{:S(2)}) collective-permute-start(bf16[8,64,256]{2,1,0:T(8,128)(2,1)S(1)} %get-tuple-element.114), channel_id=1, source_target_pairs={{192,224},{193,225},{194,226},{195,227},{196,228},{197,229},{198,2... | collective-permute-start | bytes 786440 | tf_op jit(solution)/shard_map/ppermute | solution.py:356
  97.5 8.5 %collective-permute-start.27 = (f32[12,64,256]{2,1,0:T(8,128)S(1)}, f32[12,64,256]{2,1,0:T(8,128)S(1)}, u32[]{:S(2)}, u32[]{:S(2)}) collective-permute-start(f32[12,64,256]{2,1,0:T(8,128)S(1)} %get-tuple-element.125), channel_id=1, source_target_pairs={{64,48},{65,49},{66,50},{67,51},{68,52},{69,53},{70,54},{71,55},{7... | collective-permute-start | bytes 2359304 | tf_op jit(solution)/shard_map/ppermute | solution.py:363
  104.6 3.2 %collective-permute-start.25 = (f32[12,64,256]{2,1,0:T(8,128)S(1)}, f32[12,64,256]{2,1,0:T(8,128)S(1)}, u32[]{:S(2)}, u32[]{:S(2)}) collective-permute-start(f32[12,64,256]{2,1,0:T(8,128)S(1)} %get-tuple-element.123), channel_id=1, source_target_pairs={{0,16},{1,17},{2,18},{3,19},{4,20},{5,21},{6,22},{7,23},{8,24},{9,... | collective-permute-start | bytes 2359304 | tf_op jit(solution)/shard_map/ppermute | solution.py:363

commit v8 on v7

--- a/solution.py
+++ b/solution.py
@@ -302,12 +302,12 @@
         + [like(rows + 2 * JUMP_HALO[slot], kinds[slot]) for slot in SLOTS],
         [vm(deep), vm(deep), patch(deep), patch(deep)],
         (pieces, above, below, flat),
-        work=10_000_000_000,
+        work=15_000_000_000,
     )
+    *jumps, all_weights["core"] = lax.optimization_barrier((*jumps, all_weights["core"]))
     all_jumps = dict(zip(SLOTS, jumps))
     first_jump = fetch(all_jumps["next"], "next", hosts[:1])
     all_jumps |= {slot: fetch(all_jumps[slot], slot, hosts[1:] if slot == "next" else hosts) for slot in far}
-    main, top, bottom, all_weights["prev"] = lax.optimization_barrier((main, top, bottom, all_weights["prev"]))
 
     saved = {}
     start = (main, top, bottom)

time: 129 us -> 123 us (0.953)
  waiting for transfers between devices: 60.2 us -> 52.1 us
  blocking collectives: 29.1 us -> 31.3 us
    ppermute x4, waiting for transfers between devices: 53.7 us -> 48.6 us  [on_device(): top = lax.ppermute(results[2], AXES, route(pair, 1))]
    ppermute x4, waiting for transfers between devices: 3.45 us -> 0.39 us  [on_device(): main = lax.ppermute(results[0], AXES, route(pair, 0))]
    all_to_all x1, blocking collectives: 15.1 us -> 17.4 us  [on_device(): packed = lax.all_to_all(packed, 'cols', 0, 0, tiled=True)]
where the time goes in v8:
time: 123 us; the launch traced here: 122 us
  waiting for transfers between devices  52.1 us (42%)
  blocking collectives  31.3 us (25%)
  starting transfers between devices  25.2 us (20%)
  Pallas kernels  11.2 us (9%)
  local copies, waits for them, and re-layouts  1.35 us (1%)
    ppermute x4, waiting for transfers between devices, on_device(): top = lax.ppermute(results[2], AXES, route(pair, 1))  48.6 us
    all_to_all x1, blocking collectives, on_device(): packed = lax.all_to_all(packed, 'cols', 0, 0, tiled=True)  17.4 us
    all_to_all x1, blocking collectives, on_device(): lax.all_to_all(tile.reshape(ncols, rows, tile_cols, channels), 'cols', 0,...  14 us
    pallas_call x14, Pallas kernels, call(): pl.pallas_call(kernel, out_shape=[jax.ShapeDtypeStruct(*o) for o in outs]...  11.2 us
    ppermute x7, starting transfers between devices, fetch(): return lax.ppermute(x, AXES, route(pairs, 0))  4.97 us
    ppermute x2, starting transfers between devices, ring(): lax.ppermute(x, ('rows', 'cols'), [(s, (s + shift) % strips) for s in ran...  4.21 us
    ppermute x4, starting transfers between devices, on_device(): main = lax.ppermute(results[0], AXES, route(pair, 0))  3.32 us
    ppermute x4, starting transfers between devices, on_device(): lax.ppermute(results[3] if turn == 1 else settled[0], AXES, route(pair, 0))  3.32 us
  transfers between devices with their start and end apart: 28, of which 5 were waited for; matrix products, arithmetic and copies ran while one was open for 1% of the time, Pallas kernels for 5%

profile of v8, /device:TPU:226, one launch (start us, length us, event | category | flops | bytes accessed | tf_op | source)
XLA Modules:
  0.0 122.3 jit_solution(10776395555456063841)
XLA Ops:
  0.6 14.0 %all_to_all.10.pieces = f32[4,8,16,256]{3,2,1,0:T(8,128)S(1)} all-to-all(f32[4,8,16,256]{3,2,1,0:T(8,128)} %bitcast.14), channel_id=1, replica_groups=mesh['depth'=16,'rows'=4,'cols'=4] {'cols'}, dimensions={0} | all-to-all | bytes 1048576 | tf_op jit(solution)/shard_map/all_to_all | solution.py:288
  14.6 0.6 collective-permute-start
  15.3 3.6 %collective-permute-start.1 = (bf16[4,6,16,256]{3,2,1,0:T(8,128)(2,1)S(1)}, bf16[4,6,16,256]{3,2,1,0:T(8,128)(2,1)S(1)}, u32[]{:S(2)}, u32[]{:S(2)}) collective-permute-start(bf16[4,6,16,256]{3,2,1,0:T(8,128)(2,1)S(1)} %get-tuple-element.67), channel_id=1, source_target_pairs={{0,15},{1,0},{2,1},{3,2},{4,3},{5,4},{6,5},{7,6},{8,7},{9,8},{10,9... | collective-permute-start | bytes 589832 | tf_op jit(solution)/shard_map/ppermute | solution.py:286
  18.8 1.3 %slice.4 = bf16[1,3,3,256,256]{4,3,2,1,0:T(8,128)(2,1)S(1)} slice(bf16[2,3,3,256,256]{4,3,2,1,0:T(8,128)(2,1)} %param.3), slice={[0:1], [0:3], [0:3], [0:256], [0:256]} | slice | bytes 2359296 | tf_op jit(solution)/shard_map/slice | solution.py:264
  20.2 0.7 collective-permute-start.10
  20.9 0.7 collective-permute-start.4
  21.7 0.7 collective-permute-start.2
  22.4 0.1 collective-permute-done.above
  22.5 0.0 collective-permute-done.1.below
  22.5 3.6 %shard_map.42 = (f32[8,64,256]{2,1,0:T(8,128)S(1)}, bf16[4,64,256]{2,1,0:T(8,128)(2,1)S(1)}, bf16[4,64,256]{2,1,0:T(8,128)(2,1)S(1)}, bf16[16,64,256]{2,1,0:T(8,...) custom-call(f32[4,8,16,256]{3,2,1,0:T(8,128)S(1)} %all_to_all.10.pieces, ...), custom_call_target="tpu_custom_call" | custom-call | flops 15000000512 | tf_op jit(solution)/shard_map/pallas_call | solution.py:243
  26.1 0.7 collective-permute-start.3
  26.8 0.7 collective-permute-start.5
  27.5 0.7 collective-permute-start.11
  28.2 0.7 collective-permute-start.12
  29.0 0.0 collective-permute-done.5.rest_2_
  29.0 0.7 collective-permute-start.7
  29.7 0.7 collective-permute-start.8
  30.4 0.0 collective-permute-done.10.rest_3_
  30.4 0.7 collective-permute-start.9
  31.1 0.7 collective-permute-start.6
  31.7 0.0 collective-permute-done.11.rest_7_.rest_6_
  31.8 0.0 collective-permute-done.7.rest_0_
  31.8 0.2 shard_map.45
  32.0 0.7 collective-permute-start.15
  32.7 0.7 collective-permute-start.16
  33.4 0.7 collective-permute-start.14
  34.1 0.7 collective-permute-start.13
  34.8 0.7 collective-permute-start.19
  35.5 0.7 collective-permute-start.20
  36.2 0.7 collective-permute-start.18
  36.9 0.7 collective-permute-start.17
  37.6 0.7 collective-permute-start.26
  38.3 0.2 shard_map.49
  38.6 1.3 %collective-permute-start.23 = (bf16[3,64,256]{2,1,0:T(8,128)(2,1)S(1)}, bf16[3,64,256]{2,1,0:T(8,128)(2,1)S(1)}, u32[]{:S(2)}, u32[]{:S(2)}) collective-permute-start(bf16[3,64,256]{2,1,0:T(8,128)(2,1)S(1)} %get-tuple-element.118), channel_id=1, source_target_pairs={{192,225},{193,226},{194,227},{195,228},{196,229},{197,230},{198,2... | collective-permute-start | bytes 294920 | tf_op jit(solution)/shard_map/ppermute | solution.py:354
  39.9 1.3 %collective-permute-start.24 = (bf16[3,64,256]{2,1,0:T(8,128)(2,1)S(1)}, bf16[3,64,256]{2,1,0:T(8,128)(2,1)S(1)}, u32[]{:S(2)}, u32[]{:S(2)}) collective-permute-start(bf16[3,64,256]{2,1,0:T(8,128)(2,1)S(1)} %get-tuple-element.119), channel_id=1, source_target_pairs={{193,224},{194,225},{195,226},{196,227},{197,228},{198,229},{199,2... | collective-permute-start | bytes 294920 | tf_op jit(solution)/shard_map/ppermute | solution.py:355
  41.2 1.3 %collective-permute-start.22 = (bf16[8,64,256]{2,1,0:T(8,128)(2,1)S(1)}, bf16[8,64,256]{2,1,0:T(8,128)(2,1)S(1)}, u32[]{:S(2)}, u32[]{:S(2)}) collective-permute-start(bf16[8,64,256]{2,1,0:T(8,128)(2,1)S(1)} %get-tuple-element.117), channel_id=1, source_target_pairs={{192,224},{193,225},{194,226},{195,227},{196,228},{197,229},{198,2... | collective-permute-start | bytes 786440 | tf_op jit(solution)/shard_map/ppermute | solution.py:353
  42.5 1.3 %collective-permute-start.21 = (bf16[8,64,256]{2,1,0:T(8,128)(2,1)S(1)}, bf16[8,64,256]{2,1,0:T(8,128)(2,1)S(1)}, u32[]{:S(2)}, u32[]{:S(2)}) collective-permute-start(bf16[8,64,256]{2,1,0:T(8,128)(2,1)S(1)} %get-tuple-element.116), channel_id=1, source_target_pairs={{192,224},{193,225},{194,226},{195,227},{196,228},{197,229},{198,2... | collective-permute-start | bytes 786440 | tf_op jit(solution)/shard_map/ppermute | solution.py:356
  43.8 48.6 %collective-permute-done.23.rest_1_ = bf16[3,64,256]{2,1,0:T(8,128)(2,1)S(1)} collective-permute-done((bf16[3,64,256]{2,1,0:T(8,128)(2,1)S(1)}, bf16[3,64,256]{2,1,0:T(8,128)(2,1)S(1)}, u32[]{:S(2)}, u32[]{:S(2)}) %collective-permute-start.23) | collective-permute-done | bytes 98336 | tf_op jit(solution)/shard_map/ppermute | solution.py:354
  92.4 0.7 collective-permute-start.27
  93.1 0.4 collective-permute-done.22.rest_0_
  93.5 1.7 %shard_map.51 = (f32[12,64,256]{2,1,0:T(8,128)S(1)}, f32[12,64,256]{2,1,0:T(8,128)S(1)}) custom-call(bf16[8,64,256]{2,1,0:T(8,128)(2,1)S(1)} %collective-permute-done.22.rest_0_, bf16[3,64,256]{2,1,0:T(8,128)(2,1)S(1)} %collective-permute-done.23.rest_1_, ...), custom_call_target="tpu_custom_call", output_to_operand_aliasing={{0}: (5, {}), {1}: (6, {})} | custom-call | flops 20000000000 | tf_op jit(solution)/shard_map/pallas_call | solution.py:243
  95.2 1.1 collective-permute-done.21.low
  96.3 0.2 shard_map.52
  96.5 1.3 %collective-permute-start.25 = (f32[12,64,256]{2,1,0:T(8,128)S(1)}, f32[12,64,256]{2,1,0:T(8,128)S(1)}, u32[]{:S(2)}, u32[]{:S(2)}) collective-permute-start(f32[12,64,256]{2,1,0:T(8,128)S(1)} %get-tuple-element.125), channel_id=1, source_target_pairs={{0,16},{1,17},{2,18},{3,19},{4,20},{5,21},{6,22},{7,23},{8,24},{9,... | collective-permute-start | bytes 2359304 | tf_op jit(solution)/shard_map/ppermute | solution.py:363
  97.9 1.8 %collective-permute-done.25.core = f32[12,64,256]{2,1,0:T(8,128)S(1)} collective-permute-done((f32[12,64,256]{2,1,0:T(8,128)S(1)}, f32[12,64,256]{2,1,0:T(8,128)S(1)}, u32[]{:S(2)}, u32[]{:S(2)}) %collective-permute-start.25) | collective-permute-done | bytes 786464 | tf_op jit(solution)/shard_map/ppermute | solution.py:363
  99.7 0.1 shard_map.53
  99.8 17.4 %all_to_all.11.packed = bf16[4,368,256]{2,1,0:T(8,128)(2,1)S(1)} all-to-all(bf16[4,368,256]{2,1,0:T(8,128)(2,1)S(1)} %shard_map.53), channel_id=1, replica_groups=mesh['depth'=16,'rows'=4,'cols'=4] {'cols'}, dimensions={0} | all-to-all | bytes 1507328 | tf_op jit(solution)/shard_map/all_to_all | solution.py:373
  117.2 5.1 %shard_map.54 = (f32[2,32,16,256]{3,2,1,0:T(8,128)}, f32[32,16,256]{2,1,0:T(8,128)}) custom-call(bf16[4,368,256]{2,1,0:T(8,128)(2,1)S(1)} %all_to_all.11.packed, bf16[2,3,768,256]{3,2,1,0:T(8,128)(2,1)S(1)} %bitcast.10), custom_call_target="tpu_custom_call" | custom-call | tf_op jit(solution)/shard_map/pallas_call | solution.py:243
  (27 shorter events, 0.2 us)
Async XLA Ops:
  14.6 7.9 %collective-permute-start = (bf16[4,6,16,256]{3,2,1,0:T(8,128)(2,1)S(1)}, bf16[4,6,16,256]{3,2,1,0:T(8,128)(2,1)S(1)}, u32[]{:S(2)}, u32[]{:S(2)}) collective-permute-start(bf16[4,6,16,256]{3,2,1,0:T(8,128)(2,1)S(1)} %get-tuple-element.66), channel_id=1, source_target_pairs={{0,1},{1,2},{2,3},{3,4},{4,5},{5,6},{6,7},{7,8},{8,9},{9,10},{10,1... | collective-permute-start | bytes 589832 | tf_op jit(solution)/shard_map/ppermute | solution.py:286
  15.3 7.2 %copy-start = (bf16[2,3,3,256,256]{4,3,2,1,0:T(8,128)(2,1)S(1)}, bf16[2,3,3,256,256]{4,3,2,1,0:T(8,128)(2,1)}, u32[]{:S(2)}) copy-start(bf16[2,3,3,256,256]{4,3,2,1,0:T(8,128)(2,1)} %param.3) | copy-start | bytes 7077892
  15.3 7.2 %collective-permute-start.1 = (bf16[4,6,16,256]{3,2,1,0:T(8,128)(2,1)S(1)}, bf16[4,6,16,256]{3,2,1,0:T(8,128)(2,1)S(1)}, u32[]{:S(2)}, u32[]{:S(2)}) collective-permute-start(bf16[4,6,16,256]{3,2,1,0:T(8,128)(2,1)S(1)} %get-tuple-element.67), channel_id=1, source_target_pairs={{0,15},{1,0},{2,1},{3,2},{4,3},{5,4},{6,5},{7,6},{8,7},{9,8},{10,9... | collective-permute-start | bytes 589832 | tf_op jit(solution)/shard_map/ppermute | solution.py:286
  20.2 10.2 %collective-permute-start.10 = (bf16[3,768,256]{2,1,0:T(8,128)(2,1)S(1)}, bf16[3,768,256]{2,1,0:T(8,128)(2,1)S(1)}, u32[]{:S(2)}, u32[]{:S(2)}) collective-permute-start(bf16[3,768,256]{2,1,0:T(8,128)(2,1)S(1)} %bitcast.11), channel_id=1, source_target_pairs={{48,64},{49,65},{50,66},{51,67},{52,68},{53,69},{54,70},{55,71},{5... | collective-permute-start | bytes 3538952 | tf_op jit(solution)/shard_map/ppermute | solution.py:283
  20.9 8.0 %collective-permute-start.4 = (bf16[3,768,256]{2,1,0:T(8,128)(2,1)S(1)}, bf16[3,768,256]{2,1,0:T(8,128)(2,1)S(1)}, u32[]{:S(2)}, u32[]{:S(2)}) collective-permute-start(bf16[3,768,256]{2,1,0:T(8,128)(2,1)S(1)} %bitcast.12), channel_id=1, source_target_pairs={{32,0},{33,1},{34,2},{35,3},{36,4},{37,5},{38,6},{39,7},{40,8},{41... | collective-permute-start | bytes 3538952 | tf_op jit(solution)/shard_map/ppermute | solution.py:283
  21.7 4.4 %collective-permute-start.2 = (bf16[3,768,256]{2,1,0:T(8,128)(2,1)S(1)}, bf16[3,768,256]{2,1,0:T(8,128)(2,1)S(1)}, u32[]{:S(2)}, u32[]{:S(2)}) collective-permute-start(bf16[3,768,256]{2,1,0:T(8,128)(2,1)S(1)} %bitcast.13), channel_id=1, source_target_pairs={{16,0},{17,1},{18,2},{19,3},{20,4},{21,5},{22,6},{23,7},{24,8},{25... | collective-permute-start | bytes 3538952 | tf_op jit(solution)/shard_map/ppermute | solution.py:283
  26.1 2.1 %collective-permute-start.3 = (f32[12,64,256]{2,1,0:T(8,128)S(1)}, f32[12,64,256]{2,1,0:T(8,128)S(1)}, u32[]{:S(2)}, u32[]{:S(2)}) collective-permute-start(f32[12,64,256]{2,1,0:T(8,128)S(1)} %get-tuple-element.77), channel_id=1, source_target_pairs={{16,0},{17,1},{18,2},{19,3},{20,4},{21,5},{22,6},{23,7},{24,8},{25... | collective-permute-start | bytes 2359304 | tf_op jit(solution)/shard_map/ppermute | solution.py:283
  26.8 2.1 %collective-permute-start.5 = (bf16[8,64,256]{2,1,0:T(8,128)(2,1)S(1)}, bf16[8,64,256]{2,1,0:T(8,128)(2,1)S(1)}, u32[]{:S(2)}, u32[]{:S(2)}) collective-permute-start(bf16[8,64,256]{2,1,0:T(8,128)(2,1)S(1)} %get-tuple-element.79), channel_id=1, source_target_pairs={{32,0},{33,1},{34,2},{35,3},{36,4},{37,5},{38,6},{39,7},{40,8},{41... | collective-permute-start | bytes 786440 | tf_op jit(solution)/shard_map/ppermute | solution.py:283
  27.5 4.2 %collective-permute-start.11 = (bf16[16,64,256]{2,1,0:T(8,128)(2,1)S(1)}, bf16[16,64,256]{2,1,0:T(8,128)(2,1)S(1)}, u32[]{:S(2)}, u32[]{:S(2)}) collective-permute-start(bf16[16,64,256]{2,1,0:T(8,128)(2,1)S(1)} %get-tuple-element.84), channel_id=1, source_target_pairs={{48,64},{49,65},{50,66},{51,67},{52,68},{53,69},{54,70},{55,71},{5... | collective-permute-start | bytes 1572872 | tf_op jit(solution)/shard_map/ppermute | solution.py:283
  28.2 2.8 %collective-permute-start.12 = (bf16[8,64,256]{2,1,0:T(8,128)(2,1)S(1)}, bf16[8,64,256]{2,1,0:T(8,128)(2,1)S(1)}, u32[]{:S(2)}, u32[]{:S(2)}) collective-permute-start(bf16[8,64,256]{2,1,0:T(8,128)(2,1)S(1)} %get-tuple-element.79), channel_id=1, source_target_pairs={{96,64},{97,65},{98,66},{99,67},{100,68},{101,69},{102,70},{103,71... | collective-permute-start | bytes 786440 | tf_op jit(solution)/shard_map/ppermute | solution.py:283
  29.0 2.8 %collective-permute-start.7 = (bf16[8,64,256]{2,1,0:T(8,128)(2,1)S(1)}, bf16[8,64,256]{2,1,0:T(8,128)(2,1)S(1)}, u32[]{:S(2)}, u32[]{:S(2)}) collective-permute-start(bf16[8,64,256]{2,1,0:T(8,128)(2,1)S(1)} %get-tuple-element.81), channel_id=1, source_target_pairs={{0,64},{1,65},{2,66},{3,67},{4,68},{5,69},{6,70},{7,71},{8,72},{9,... | collective-permute-start | bytes 786440 | tf_op jit(solution)/shard_map/ppermute | solution.py:353
  29.7 2.1 %collective-permute-start.8 = (bf16[5,64,256]{2,1,0:T(8,128)(2,1)S(1)}, bf16[5,64,256]{2,1,0:T(8,128)(2,1)S(1)}, u32[]{:S(2)}, u32[]{:S(2)}) collective-permute-start(bf16[5,64,256]{2,1,0:T(8,128)(2,1)S(1)} %get-tuple-element.82), channel_id=1, source_target_pairs={{0,65},{1,66},{2,67},{3,68},{4,69},{5,70},{6,71},{7,72},{8,73},{9,... | collective-permute-start | bytes 491528 | tf_op jit(solution)/shard_map/ppermute | solution.py:354
  30.4 1.4 %collective-permute-start.9 = (bf16[5,64,256]{2,1,0:T(8,128)(2,1)S(1)}, bf16[5,64,256]{2,1,0:T(8,128)(2,1)S(1)}, u32[]{:S(2)}, u32[]{:S(2)}) collective-permute-start(bf16[5,64,256]{2,1,0:T(8,128)(2,1)S(1)} %get-tuple-element.83), channel_id=1, source_target_pairs={{1,64},{2,65},{3,66},{4,67},{5,68},{6,69},{7,70},{8,71},{9,72},{10... | collective-permute-start | bytes 491528 | tf_op jit(solution)/shard_map/ppermute | solution.py:355
  31.1 3.0 %collective-permute-start.6 = (bf16[8,64,256]{2,1,0:T(8,128)(2,1)S(1)}, bf16[8,64,256]{2,1,0:T(8,128)(2,1)S(1)}, u32[]{:S(2)}, u32[]{:S(2)}) collective-permute-start(bf16[8,64,256]{2,1,0:T(8,128)(2,1)S(1)} %get-tuple-element.80), channel_id=1, source_target_pairs={{0,64},{1,65},{2,66},{3,67},{4,68},{5,69},{6,70},{7,71},{8,72},{9,... | collective-permute-start | bytes 786440 | tf_op jit(solution)/shard_map/ppermute | solution.py:356
  32.0 2.8 %collective-permute-start.15 = (bf16[5,64,256]{2,1,0:T(8,128)(2,1)S(1)}, bf16[5,64,256]{2,1,0:T(8,128)(2,1)S(1)}, u32[]{:S(2)}, u32[]{:S(2)}) collective-permute-start(bf16[5,64,256]{2,1,0:T(8,128)(2,1)S(1)} %get-tuple-element.94), channel_id=1, source_target_pairs={{64,129},{65,130},{66,131},{67,132},{68,133},{69,134},{70,135},{71... | collective-permute-start | bytes 491528 | tf_op jit(solution)/shard_map/ppermute | solution.py:354
  32.7 2.1 %collective-permute-start.16 = (bf16[5,64,256]{2,1,0:T(8,128)(2,1)S(1)}, bf16[5,64,256]{2,1,0:T(8,128)(2,1)S(1)}, u32[]{:S(2)}, u32[]{:S(2)}) collective-permute-start(bf16[5,64,256]{2,1,0:T(8,128)(2,1)S(1)} %get-tuple-element.95), channel_id=1, source_target_pairs={{65,128},{66,129},{67,130},{68,131},{69,132},{70,133},{71,134},{72... | collective-permute-start | bytes 491528 | tf_op jit(solution)/shard_map/ppermute | solution.py:355
  33.4 1.4 %collective-permute-start.14 = (bf16[8,64,256]{2,1,0:T(8,128)(2,1)S(1)}, bf16[8,64,256]{2,1,0:T(8,128)(2,1)S(1)}, u32[]{:S(2)}, u32[]{:S(2)}) collective-permute-start(bf16[8,64,256]{2,1,0:T(8,128)(2,1)S(1)} %get-tuple-element.93), channel_id=1, source_target_pairs={{64,128},{65,129},{66,130},{67,131},{68,132},{69,133},{70,134},{71... | collective-permute-start | bytes 786440 | tf_op jit(solution)/shard_map/ppermute | solution.py:353
  34.1 2.8 %collective-permute-start.13 = (bf16[8,64,256]{2,1,0:T(8,128)(2,1)S(1)}, bf16[8,64,256]{2,1,0:T(8,128)(2,1)S(1)}, u32[]{:S(2)}, u32[]{:S(2)}) collective-permute-start(bf16[8,64,256]{2,1,0:T(8,128)(2,1)S(1)} %get-tuple-element.92), channel_id=1, source_target_pairs={{64,128},{65,129},{66,130},{67,131},{68,132},{69,133},{70,134},{71... | collective-permute-start | bytes 786440 | tf_op jit(solution)/shard_map/ppermute | solution.py:356
  34.8 3.5 %collective-permute-start.19 = (bf16[4,64,256]{2,1,0:T(8,128)(2,1)S(1)}, bf16[4,64,256]{2,1,0:T(8,128)(2,1)S(1)}, u32[]{:S(2)}, u32[]{:S(2)}) collective-permute-start(bf16[4,64,256]{2,1,0:T(8,128)(2,1)S(1)} %get-tuple-element.107), channel_id=1, source_target_pairs={{128,193},{129,194},{130,195},{131,196},{132,197},{133,198},{134,1... | collective-permute-start | bytes 393224 | tf_op jit(solution)/shard_map/ppermute | solution.py:354
  35.5 2.8 %collective-permute-start.20 = (bf16[4,64,256]{2,1,0:T(8,128)(2,1)S(1)}, bf16[4,64,256]{2,1,0:T(8,128)(2,1)S(1)}, u32[]{:S(2)}, u32[]{:S(2)}) collective-permute-start(bf16[4,64,256]{2,1,0:T(8,128)(2,1)S(1)} %get-tuple-element.108), channel_id=1, source_target_pairs={{129,192},{130,193},{131,194},{132,195},{133,196},{134,197},{135,1... | collective-permute-start | bytes 393224 | tf_op jit(solution)/shard_map/ppermute | solution.py:355
  36.2 2.1 %collective-permute-start.18 = (bf16[8,64,256]{2,1,0:T(8,128)(2,1)S(1)}, bf16[8,64,256]{2,1,0:T(8,128)(2,1)S(1)}, u32[]{:S(2)}, u32[]{:S(2)}) collective-permute-start(bf16[8,64,256]{2,1,0:T(8,128)(2,1)S(1)} %get-tuple-element.106), channel_id=1, source_target_pairs={{128,192},{129,193},{130,194},{131,195},{132,196},{133,197},{134,1... | collective-permute-start | bytes 786440 | tf_op jit(solution)/shard_map/ppermute | solution.py:353
  36.9 5.6 %collective-permute-start.17 = (bf16[8,64,256]{2,1,0:T(8,128)(2,1)S(1)}, bf16[8,64,256]{2,1,0:T(8,128)(2,1)S(1)}, u32[]{:S(2)}, u32[]{:S(2)}) collective-permute-start(bf16[8,64,256]{2,1,0:T(8,128)(2,1)S(1)} %get-tuple-element.105), channel_id=1, source_target_pairs={{128,192},{129,193},{130,194},{131,195},{132,196},{133,197},{134,1... | collective-permute-start | bytes 786440 | tf_op jit(solution)/shard_map/ppermute | solution.py:356
  37.6 60.3 %collective-permute-start.26 = (f32[12,64,256]{2,1,0:T(8,128)S(1)}, f32[12,64,256]{2,1,0:T(8,128)S(1)}, u32[]{:S(2)}, u32[]{:S(2)}) collective-permute-start(f32[12,64,256]{2,1,0:T(8,128)S(1)} %get-tuple-element.126), channel_id=1, source_target_pairs={{0,32},{1,33},{2,34},{3,35},{4,36},{5,37},{6,38},{7,39},{8,40},{9,... | collective-permute-start | bytes 2359304 | tf_op jit(solution)/shard_map/ppermute | solution.py:363
  38.6 53.8 %collective-permute-start.23 = (bf16[3,64,256]{2,1,0:T(8,128)(2,1)S(1)}, bf16[3,64,256]{2,1,0:T(8,128)(2,1)S(1)}, u32[]{:S(2)}, u32[]{:S(2)}) collective-permute-start(bf16[3,64,256]{2,1,0:T(8,128)(2,1)S(1)} %get-tuple-element.118), channel_id=1, source_target_pairs={{192,225},{193,226},{194,227},{195,228},{196,229},{197,230},{198,2... | collective-permute-start | bytes 294920 | tf_op jit(solution)/shard_map/ppermute | solution.py:354
  39.9 53.2 %collective-permute-start.24 = (bf16[3,64,256]{2,1,0:T(8,128)(2,1)S(1)}, bf16[3,64,256]{2,1,0:T(8,128)(2,1)S(1)}, u32[]{:S(2)}, u32[]{:S(2)}) collective-permute-start(bf16[3,64,256]{2,1,0:T(8,128)(2,1)S(1)} %get-tuple-element.119), channel_id=1, source_target_pairs={{193,224},{194,225},{195,226},{196,227},{197,228},{198,229},{199,2... | collective-permute-start | bytes 294920 | tf_op jit(solution)/shard_map/ppermute | solution.py:355
  41.2 52.3 %collective-permute-start.22 = (bf16[8,64,256]{2,1,0:T(8,128)(2,1)S(1)}, bf16[8,64,256]{2,1,0:T(8,128)(2,1)S(1)}, u32[]{:S(2)}, u32[]{:S(2)}) collective-permute-start(bf16[8,64,256]{2,1,0:T(8,128)(2,1)S(1)} %get-tuple-element.117), channel_id=1, source_target_pairs={{192,224},{193,225},{194,226},{195,227},{196,228},{197,229},{198,2... | collective-permute-start | bytes 786440 | tf_op jit(solution)/shard_map/ppermute | solution.py:353
  42.5 53.8 %collective-permute-start.21 = (bf16[8,64,256]{2,1,0:T(8,128)(2,1)S(1)}, bf16[8,64,256]{2,1,0:T(8,128)(2,1)S(1)}, u32[]{:S(2)}, u32[]{:S(2)}) collective-permute-start(bf16[8,64,256]{2,1,0:T(8,128)(2,1)S(1)} %get-tuple-element.116), channel_id=1, source_target_pairs={{192,224},{193,225},{194,226},{195,227},{196,228},{197,229},{198,2... | collective-permute-start | bytes 786440 | tf_op jit(solution)/shard_map/ppermute | solution.py:356
  92.4 5.4 %collective-permute-start.27 = (f32[12,64,256]{2,1,0:T(8,128)S(1)}, f32[12,64,256]{2,1,0:T(8,128)S(1)}, u32[]{:S(2)}, u32[]{:S(2)}) collective-permute-start(f32[12,64,256]{2,1,0:T(8,128)S(1)} %get-tuple-element.127), channel_id=1, source_target_pairs={{64,48},{65,49},{66,50},{67,51},{68,52},{69,53},{70,54},{71,55},{7... | collective-permute-start | bytes 2359304 | tf_op jit(solution)/shard_map/ppermute | solution.py:363
  96.5 3.2 %collective-permute-start.25 = (f32[12,64,256]{2,1,0:T(8,128)S(1)}, f32[12,64,256]{2,1,0:T(8,128)S(1)}, u32[]{:S(2)}, u32[]{:S(2)}) collective-permute-start(f32[12,64,256]{2,1,0:T(8,128)S(1)} %get-tuple-element.125), channel_id=1, source_target_pairs={{0,16},{1,17},{2,18},{3,19},{4,20},{5,21},{6,22},{7,23},{8,24},{9,... | collective-permute-start | bytes 2359304 | tf_op jit(solution)/shard_map/ppermute | solution.py:363

commit v9 on v8

--- a/solution.py
+++ b/solution.py
@@ -285,12 +285,14 @@
     def ring(x, shift):
         return lax.ppermute(x, ("rows", "cols"), [(s, (s + shift) % strips) for s in range(strips)])
 
+    far = ("next", "core", "prev")
+    all_weights = {"own": flat} | {slot: fetch(w0, slot) for slot in far}
+
     pieces = lax.all_to_all(tile.reshape(ncols, rows, tile_cols, channels), "cols", 0, 0, tiled=True)
     near = JUMP_HALO["prev"] + 2
     low, high = call(edge_kernel, [((ncols, near, tile_cols, channels), BF16)] * 2, [], (pieces,))
     above, below = ring(high, 1), ring(low, -1)
-    far = ("next", "core", "prev")
-    all_weights = {"own": flat} | {slot: fetch(w0, slot) for slot in far}
+    above, below, all_weights["next"] = lax.optimization_barrier((above, below, all_weights["next"]))
     like = lambda n, t=F32: ((n, width, channels), t)
     vm = lambda n: pltpu.VMEM((n, width, channels), F32)
     patch = lambda n: pltpu.VMEM((n, width, 3 * channels), BF16)

time: 123 us -> 122 us (level)
  blocking collectives: 31.3 us -> 29.1 us
  waiting for transfers between devices: 52.1 us -> 53.5 us
    ppermute x4, waiting for transfers between devices: 48.6 us -> 44.9 us  [on_device(): top = lax.ppermute(results[2], AXES, route(pair, 1))]
    ppermute x4, waiting for transfers between devices: 0.39 us -> 3.44 us  [on_device(): main = lax.ppermute(results[0], AXES, route(pair, 0))]
    all_to_all x1, blocking collectives: 17.4 us -> 15.1 us  [on_device(): packed = lax.all_to_all(packed, 'cols', 0, 0, tiled=True)]
    ppermute x2, waiting for transfers between devices: 0.06 us -> 2.17 us  [ring(): lax.ppermute(x, ('rows', 'cols'), [(s, (s + shift) % strips) for s in ran...]
  transfers between devices with their start and end apart: 28 -> 28, of which waited for: 5 -> 5; matrix products, arithmetic and copies ran while one was open for 1% -> 0% of each run, Pallas kernels for 5% -> 5%
where the time goes in v9:
time: 122 us
  waiting for transfers between devices  53.5 us (44%)
  blocking collectives  29.1 us (24%)
  starting transfers between devices  25.2 us (21%)
  Pallas kernels  11.2 us (9%)
  local copies, waits for them, and re-layouts  1.5 us (1%)
    ppermute x4, waiting for transfers between devices, on_device(): top = lax.ppermute(results[2], AXES, route(pair, 1))  44.9 us
    all_to_all x1, blocking collectives, on_device(): packed = lax.all_to_all(packed, 'cols', 0, 0, tiled=True)  15.1 us
    all_to_all x1, blocking collectives, on_device(): lax.all_to_all(tile.reshape(ncols, rows, tile_cols, channels), 'cols', 0,...  14 us
    pallas_call x14, Pallas kernels, call(): pl.pallas_call(kernel, out_shape=[jax.ShapeDtypeStruct(*o) for o in outs]...  11.2 us
    ppermute x7, starting transfers between devices, fetch(): return lax.ppermute(x, AXES, route(pairs, 0))  4.96 us
    ppermute x2, starting transfers between devices, ring(): lax.ppermute(x, ('rows', 'cols'), [(s, (s + shift) % strips) for s in ran...  4.21 us
    ppermute x4, waiting for transfers between devices, on_device(): main = lax.ppermute(results[0], AXES, route(pair, 0))  3.44 us
    ppermute x4, starting transfers between devices, on_device(): main = lax.ppermute(results[0], AXES, route(pair, 0))  3.32 us
  transfers between devices with their start and end apart: 28, of which 5 were waited for; matrix products, arithmetic and copies ran while one was open for 0% of the time, Pallas kernels for 5%

profile of v9, /device:TPU:226, one launch (start us, length us, event | category | flops | bytes accessed | tf_op | source)
XLA Modules:
  0.0 121.6 jit_solution(1477917871989907540)
XLA Ops:
  0.6 1.5 %slice.4 = bf16[1,3,3,256,256]{4,3,2,1,0:T(8,128)(2,1)S(1)} slice(bf16[2,3,3,256,256]{4,3,2,1,0:T(8,128)(2,1)} %param.3), slice={[0:1], [0:3], [0:3], [0:256], [0:256]} | slice | bytes 2359296 | tf_op jit(solution)/shard_map/slice | solution.py:264
  2.1 0.7 collective-permute-start.2
  2.9 14.0 %all_to_all.10.pieces = f32[4,8,16,256]{3,2,1,0:T(8,128)S(1)} all-to-all(f32[4,8,16,256]{3,2,1,0:T(8,128)} %bitcast.14), channel_id=1, replica_groups=mesh['depth'=16,'rows'=4,'cols'=4] {'cols'}, dimensions={0} | all-to-all | bytes 1048576 | tf_op jit(solution)/shard_map/all_to_all | solution.py:291
  16.9 0.6 collective-permute-start
  17.5 3.6 %collective-permute-start.1 = (bf16[4,6,16,256]{3,2,1,0:T(8,128)(2,1)S(1)}, bf16[4,6,16,256]{3,2,1,0:T(8,128)(2,1)S(1)}, u32[]{:S(2)}, u32[]{:S(2)}) collective-permute-start(bf16[4,6,16,256]{3,2,1,0:T(8,128)(2,1)S(1)} %get-tuple-element.70), channel_id=1, source_target_pairs={{0,15},{1,0},{2,1},{3,2},{4,3},{5,4},{6,5},{7,6},{8,7},{9,8},{10,9... | collective-permute-start | bytes 589832 | tf_op jit(solution)/shard_map/ppermute | solution.py:286
  21.1 0.7 collective-permute-start.10
  21.8 0.7 collective-permute-start.3
  22.6 2.2 %collective-permute-done.above = bf16[4,6,16,256]{3,2,1,0:T(8,128)(2,1)S(1)} collective-permute-done((bf16[4,6,16,256]{3,2,1,0:T(8,128)(2,1)S(1)}, bf16[4,6,16,256]{3,2,1,0:T(8,128)(2,1)S(1)}, u32[]{:S(2)}, u32[]{:S(2)}) %collective-permute-start) | collective-permute-done | bytes 196640 | tf_op jit(solution)/shard_map/ppermute | solution.py:286
  24.7 0.0 collective-permute-done.1.below
  24.7 0.0 collective-permute-done.2.rest_1_.rest_6_
  24.7 3.6 %shard_map.42 = (f32[8,64,256]{2,1,0:T(8,128)S(1)}, bf16[4,64,256]{2,1,0:T(8,128)(2,1)S(1)}, bf16[4,64,256]{2,1,0:T(8,128)(2,1)S(1)}, bf16[16,64,256]{2,1,0:T(8,...) custom-call(f32[4,8,16,256]{3,2,1,0:T(8,128)S(1)} %all_to_all.10.pieces, ...), custom_call_target="tpu_custom_call" | custom-call | flops 15000000512 | tf_op jit(solution)/shard_map/pallas_call | solution.py:243
  28.4 0.7 collective-permute-start.4
  29.1 0.7 collective-permute-start.5
  29.8 0.7 collective-permute-start.11
  30.5 0.7 collective-permute-start.12
  31.2 0.0 collective-permute-done.4.rest_6_.rest_9_.rest_8_
  31.3 0.7 collective-permute-start.7
  31.9 0.7 collective-permute-start.8
  32.6 0.7 collective-permute-start.9
  33.3 0.0 collective-permute-done.12.rest_10_
  33.3 0.7 collective-permute-start.6
  34.0 0.0 collective-permute-done.8.rest_1_
  34.0 0.2 shard_map.45
  34.3 0.7 collective-permute-start.15
  34.9 0.7 collective-permute-start.16
  35.6 0.7 collective-permute-start.14
  36.3 0.7 collective-permute-start.13
  37.1 0.7 collective-permute-start.19
  37.8 0.7 collective-permute-start.20
  38.4 0.7 collective-permute-start.18
  39.2 0.7 collective-permute-start.17
  39.8 0.7 collective-permute-start.26
  40.6 0.2 shard_map.49
  40.8 1.3 %collective-permute-start.23 = (bf16[3,64,256]{2,1,0:T(8,128)(2,1)S(1)}, bf16[3,64,256]{2,1,0:T(8,128)(2,1)S(1)}, u32[]{:S(2)}, u32[]{:S(2)}) collective-permute-start(bf16[3,64,256]{2,1,0:T(8,128)(2,1)S(1)} %get-tuple-element.124), channel_id=1, source_target_pairs={{192,225},{193,226},{194,227},{195,228},{196,229},{197,230},{198,2... | collective-permute-start | bytes 294920 | tf_op jit(solution)/shard_map/ppermute | solution.py:356
  42.1 1.3 %collective-permute-start.24 = (bf16[3,64,256]{2,1,0:T(8,128)(2,1)S(1)}, bf16[3,64,256]{2,1,0:T(8,128)(2,1)S(1)}, u32[]{:S(2)}, u32[]{:S(2)}) collective-permute-start(bf16[3,64,256]{2,1,0:T(8,128)(2,1)S(1)} %get-tuple-element.125), channel_id=1, source_target_pairs={{193,224},{194,225},{195,226},{196,227},{197,228},{198,229},{199,2... | collective-permute-start | bytes 294920 | tf_op jit(solution)/shard_map/ppermute | solution.py:357
  43.4 1.3 %collective-permute-start.22 = (bf16[8,64,256]{2,1,0:T(8,128)(2,1)S(1)}, bf16[8,64,256]{2,1,0:T(8,128)(2,1)S(1)}, u32[]{:S(2)}, u32[]{:S(2)}) collective-permute-start(bf16[8,64,256]{2,1,0:T(8,128)(2,1)S(1)} %get-tuple-element.123), channel_id=1, source_target_pairs={{192,224},{193,225},{194,226},{195,227},{196,228},{197,229},{198,2... | collective-permute-start | bytes 786440 | tf_op jit(solution)/shard_map/ppermute | solution.py:355
  44.8 1.3 %collective-permute-start.21 = (bf16[8,64,256]{2,1,0:T(8,128)(2,1)S(1)}, bf16[8,64,256]{2,1,0:T(8,128)(2,1)S(1)}, u32[]{:S(2)}, u32[]{:S(2)}) collective-permute-start(bf16[8,64,256]{2,1,0:T(8,128)(2,1)S(1)} %get-tuple-element.122), channel_id=1, source_target_pairs={{192,224},{193,225},{194,226},{195,227},{196,228},{197,229},{198,2... | collective-permute-start | bytes 786440 | tf_op jit(solution)/shard_map/ppermute | solution.py:358
  46.1 44.9 %collective-permute-done.23.rest_1_ = bf16[3,64,256]{2,1,0:T(8,128)(2,1)S(1)} collective-permute-done((bf16[3,64,256]{2,1,0:T(8,128)(2,1)S(1)}, bf16[3,64,256]{2,1,0:T(8,128)(2,1)S(1)}, u32[]{:S(2)}, u32[]{:S(2)}) %collective-permute-start.23) | collective-permute-done | bytes 98336 | tf_op jit(solution)/shard_map/ppermute | solution.py:356
  90.9 0.7 collective-permute-start.27
  91.7 3.4 %collective-permute-done.22.rest_0_ = bf16[8,64,256]{2,1,0:T(8,128)(2,1)S(1)} collective-permute-done((bf16[8,64,256]{2,1,0:T(8,128)(2,1)S(1)}, bf16[8,64,256]{2,1,0:T(8,128)(2,1)S(1)}, u32[]{:S(2)}, u32[]{:S(2)}) %collective-permute-start.22) | collective-permute-done | bytes 262176 | tf_op jit(solution)/shard_map/ppermute | solution.py:355
  95.1 1.7 %shard_map.51 = (f32[12,64,256]{2,1,0:T(8,128)S(1)}, f32[12,64,256]{2,1,0:T(8,128)S(1)}) custom-call(bf16[8,64,256]{2,1,0:T(8,128)(2,1)S(1)} %collective-permute-done.22.rest_0_, bf16[3,64,256]{2,1,0:T(8,128)(2,1)S(1)} %collective-permute-done.23.rest_1_, ...), custom_call_target="tpu_custom_call", output_to_operand_aliasing={{0}: (5, {}), {1}: (6, {})} | custom-call | flops 20000000000 | tf_op jit(solution)/shard_map/pallas_call | solution.py:243
  96.8 1.1 collective-permute-done.21.low
  97.9 0.2 shard_map.52
  98.1 1.3 %collective-permute-start.25 = (f32[12,64,256]{2,1,0:T(8,128)S(1)}, f32[12,64,256]{2,1,0:T(8,128)S(1)}, u32[]{:S(2)}, u32[]{:S(2)}) collective-permute-start(f32[12,64,256]{2,1,0:T(8,128)S(1)} %get-tuple-element.131), channel_id=1, source_target_pairs={{0,16},{1,17},{2,18},{3,19},{4,20},{5,21},{6,22},{7,23},{8,24},{9,... | collective-permute-start | bytes 2359304 | tf_op jit(solution)/shard_map/ppermute | solution.py:365
  99.4 1.8 %collective-permute-done.25.core = f32[12,64,256]{2,1,0:T(8,128)S(1)} collective-permute-done((f32[12,64,256]{2,1,0:T(8,128)S(1)}, f32[12,64,256]{2,1,0:T(8,128)S(1)}, u32[]{:S(2)}, u32[]{:S(2)}) %collective-permute-start.25) | collective-permute-done | bytes 786464 | tf_op jit(solution)/shard_map/ppermute | solution.py:365
  101.3 0.1 shard_map.53
  101.4 15.1 %all_to_all.11.packed = bf16[4,368,256]{2,1,0:T(8,128)(2,1)S(1)} all-to-all(bf16[4,368,256]{2,1,0:T(8,128)(2,1)S(1)} %shard_map.53), channel_id=1, replica_groups=mesh['depth'=16,'rows'=4,'cols'=4] {'cols'}, dimensions={0} | all-to-all | bytes 1507328 | tf_op jit(solution)/shard_map/all_to_all | solution.py:375
  116.6 5.1 %shard_map.54 = (f32[2,32,16,256]{3,2,1,0:T(8,128)}, f32[32,16,256]{2,1,0:T(8,128)}) custom-call(bf16[4,368,256]{2,1,0:T(8,128)(2,1)S(1)} %all_to_all.11.packed, bf16[2,3,768,256]{3,2,1,0:T(8,128)(2,1)S(1)} %bitcast.10), custom_call_target="tpu_custom_call" | custom-call | tf_op jit(solution)/shard_map/pallas_call | solution.py:243
  (27 shorter events, 0.2 us)
Async XLA Ops:
  0.6 24.1 %copy-start = (bf16[2,3,3,256,256]{4,3,2,1,0:T(8,128)(2,1)S(1)}, bf16[2,3,3,256,256]{4,3,2,1,0:T(8,128)(2,1)}, u32[]{:S(2)}) copy-start(bf16[2,3,3,256,256]{4,3,2,1,0:T(8,128)(2,1)} %param.3) | copy-start | bytes 7077892
  2.1 22.6 %collective-permute-start.2 = (bf16[3,768,256]{2,1,0:T(8,128)(2,1)S(1)}, bf16[3,768,256]{2,1,0:T(8,128)(2,1)S(1)}, u32[]{:S(2)}, u32[]{:S(2)}) collective-permute-start(bf16[3,768,256]{2,1,0:T(8,128)(2,1)S(1)} %bitcast.11), channel_id=1, source_target_pairs={{32,0},{33,1},{34,2},{35,3},{36,4},{37,5},{38,6},{39,7},{40,8},{41... | collective-permute-start | bytes 3538952 | tf_op jit(solution)/shard_map/ppermute | solution.py:283
  16.9 7.9 %collective-permute-start = (bf16[4,6,16,256]{3,2,1,0:T(8,128)(2,1)S(1)}, bf16[4,6,16,256]{3,2,1,0:T(8,128)(2,1)S(1)}, u32[]{:S(2)}, u32[]{:S(2)}) collective-permute-start(bf16[4,6,16,256]{3,2,1,0:T(8,128)(2,1)S(1)} %get-tuple-element.69), channel_id=1, source_target_pairs={{0,1},{1,2},{2,3},{3,4},{4,5},{5,6},{6,7},{7,8},{8,9},{9,10},{10,1... | collective-permute-start | bytes 589832 | tf_op jit(solution)/shard_map/ppermute | solution.py:286
  17.5 7.2 %collective-permute-start.1 = (bf16[4,6,16,256]{3,2,1,0:T(8,128)(2,1)S(1)}, bf16[4,6,16,256]{3,2,1,0:T(8,128)(2,1)S(1)}, u32[]{:S(2)}, u32[]{:S(2)}) collective-permute-start(bf16[4,6,16,256]{3,2,1,0:T(8,128)(2,1)S(1)} %get-tuple-element.70), channel_id=1, source_target_pairs={{0,15},{1,0},{2,1},{3,2},{4,3},{5,4},{6,5},{7,6},{8,7},{9,8},{10,9... | collective-permute-start | bytes 589832 | tf_op jit(solution)/shard_map/ppermute | solution.py:286
  21.1 11.5 %collective-permute-start.10 = (bf16[3,768,256]{2,1,0:T(8,128)(2,1)S(1)}, bf16[3,768,256]{2,1,0:T(8,128)(2,1)S(1)}, u32[]{:S(2)}, u32[]{:S(2)}) collective-permute-start(bf16[3,768,256]{2,1,0:T(8,128)(2,1)S(1)} %bitcast.12), channel_id=1, source_target_pairs={{48,64},{49,65},{50,66},{51,67},{52,68},{53,69},{54,70},{55,71},{5... | collective-permute-start | bytes 3538952 | tf_op jit(solution)/shard_map/ppermute | solution.py:283
  21.8 6.6 %collective-permute-start.3 = (bf16[3,768,256]{2,1,0:T(8,128)(2,1)S(1)}, bf16[3,768,256]{2,1,0:T(8,128)(2,1)S(1)}, u32[]{:S(2)}, u32[]{:S(2)}) collective-permute-start(bf16[3,768,256]{2,1,0:T(8,128)(2,1)S(1)} %bitcast.13), channel_id=1, source_target_pairs={{16,0},{17,1},{18,2},{19,3},{20,4},{21,5},{22,6},{23,7},{24,8},{25... | collective-permute-start | bytes 3538952 | tf_op jit(solution)/shard_map/ppermute | solution.py:283
  28.4 2.8 %collective-permute-start.4 = (f32[12,64,256]{2,1,0:T(8,128)S(1)}, f32[12,64,256]{2,1,0:T(8,128)S(1)}, u32[]{:S(2)}, u32[]{:S(2)}) collective-permute-start(f32[12,64,256]{2,1,0:T(8,128)S(1)} %get-tuple-element.82), channel_id=1, source_target_pairs={{16,0},{17,1},{18,2},{19,3},{20,4},{21,5},{22,6},{23,7},{24,8},{25... | collective-permute-start | bytes 2359304 | tf_op jit(solution)/shard_map/ppermute | solution.py:283
  29.1 2.1 %collective-permute-start.5 = (bf16[8,64,256]{2,1,0:T(8,128)(2,1)S(1)}, bf16[8,64,256]{2,1,0:T(8,128)(2,1)S(1)}, u32[]{:S(2)}, u32[]{:S(2)}) collective-permute-start(bf16[8,64,256]{2,1,0:T(8,128)(2,1)S(1)} %get-tuple-element.85), channel_id=1, source_target_pairs={{32,0},{33,1},{34,2},{35,3},{36,4},{37,5},{38,6},{39,7},{40,8},{41... | collective-permute-start | bytes 786440 | tf_op jit(solution)/shard_map/ppermute | solution.py:283
  29.8 4.2 %collective-permute-start.11 = (bf16[16,64,256]{2,1,0:T(8,128)(2,1)S(1)}, bf16[16,64,256]{2,1,0:T(8,128)(2,1)S(1)}, u32[]{:S(2)}, u32[]{:S(2)}) collective-permute-start(bf16[16,64,256]{2,1,0:T(8,128)(2,1)S(1)} %get-tuple-element.90), channel_id=1, source_target_pairs={{48,64},{49,65},{50,66},{51,67},{52,68},{53,69},{54,70},{55,71},{5... | collective-permute-start | bytes 1572872 | tf_op jit(solution)/shard_map/ppermute | solution.py:283
  30.5 2.8 %collective-permute-start.12 = (bf16[8,64,256]{2,1,0:T(8,128)(2,1)S(1)}, bf16[8,64,256]{2,1,0:T(8,128)(2,1)S(1)}, u32[]{:S(2)}, u32[]{:S(2)}) collective-permute-start(bf16[8,64,256]{2,1,0:T(8,128)(2,1)S(1)} %get-tuple-element.85), channel_id=1, source_target_pairs={{96,64},{97,65},{98,66},{99,67},{100,68},{101,69},{102,70},{103,71... | collective-permute-start | bytes 786440 | tf_op jit(solution)/shard_map/ppermute | solution.py:283
  31.3 2.8 %collective-permute-start.7 = (bf16[8,64,256]{2,1,0:T(8,128)(2,1)S(1)}, bf16[8,64,256]{2,1,0:T(8,128)(2,1)S(1)}, u32[]{:S(2)}, u32[]{:S(2)}) collective-permute-start(bf16[8,64,256]{2,1,0:T(8,128)(2,1)S(1)} %get-tuple-element.87), channel_id=1, source_target_pairs={{0,64},{1,65},{2,66},{3,67},{4,68},{5,69},{6,70},{7,71},{8,72},{9,... | collective-permute-start | bytes 786440 | tf_op jit(solution)/shard_map/ppermute | solution.py:355
  31.9 2.1 %collective-permute-start.8 = (bf16[5,64,256]{2,1,0:T(8,128)(2,1)S(1)}, bf16[5,64,256]{2,1,0:T(8,128)(2,1)S(1)}, u32[]{:S(2)}, u32[]{:S(2)}) collective-permute-start(bf16[5,64,256]{2,1,0:T(8,128)(2,1)S(1)} %get-tuple-element.88), channel_id=1, source_target_pairs={{0,65},{1,66},{2,67},{3,68},{4,69},{5,70},{6,71},{7,72},{8,73},{9,... | collective-permute-start | bytes 491528 | tf_op jit(solution)/shard_map/ppermute | solution.py:356
  32.6 1.4 %collective-permute-start.9 = (bf16[5,64,256]{2,1,0:T(8,128)(2,1)S(1)}, bf16[5,64,256]{2,1,0:T(8,128)(2,1)S(1)}, u32[]{:S(2)}, u32[]{:S(2)}) collective-permute-start(bf16[5,64,256]{2,1,0:T(8,128)(2,1)S(1)} %get-tuple-element.89), channel_id=1, source_target_pairs={{1,64},{2,65},{3,66},{4,67},{5,68},{6,69},{7,70},{8,71},{9,72},{10... | collective-permute-start | bytes 491528 | tf_op jit(solution)/shard_map/ppermute | solution.py:357
  33.3 3.0 %collective-permute-start.6 = (bf16[8,64,256]{2,1,0:T(8,128)(2,1)S(1)}, bf16[8,64,256]{2,1,0:T(8,128)(2,1)S(1)}, u32[]{:S(2)}, u32[]{:S(2)}) collective-permute-start(bf16[8,64,256]{2,1,0:T(8,128)(2,1)S(1)} %get-tuple-element.86), channel_id=1, source_target_pairs={{0,64},{1,65},{2,66},{3,67},{4,68},{5,69},{6,70},{7,71},{8,72},{9,... | collective-permute-start | bytes 786440 | tf_op jit(solution)/shard_map/ppermute | solution.py:358
  34.3 2.8 %collective-permute-start.15 = (bf16[5,64,256]{2,1,0:T(8,128)(2,1)S(1)}, bf16[5,64,256]{2,1,0:T(8,128)(2,1)S(1)}, u32[]{:S(2)}, u32[]{:S(2)}) collective-permute-start(bf16[5,64,256]{2,1,0:T(8,128)(2,1)S(1)} %get-tuple-element.100), channel_id=1, source_target_pairs={{64,129},{65,130},{66,131},{67,132},{68,133},{69,134},{70,135},{71... | collective-permute-start | bytes 491528 | tf_op jit(solution)/shard_map/ppermute | solution.py:356
  34.9 2.1 %collective-permute-start.16 = (bf16[5,64,256]{2,1,0:T(8,128)(2,1)S(1)}, bf16[5,64,256]{2,1,0:T(8,128)(2,1)S(1)}, u32[]{:S(2)}, u32[]{:S(2)}) collective-permute-start(bf16[5,64,256]{2,1,0:T(8,128)(2,1)S(1)} %get-tuple-element.101), channel_id=1, source_target_pairs={{65,128},{66,129},{67,130},{68,131},{69,132},{70,133},{71,134},{72... | collective-permute-start | bytes 491528 | tf_op jit(solution)/shard_map/ppermute | solution.py:357
  35.6 1.4 %collective-permute-start.14 = (bf16[8,64,256]{2,1,0:T(8,128)(2,1)S(1)}, bf16[8,64,256]{2,1,0:T(8,128)(2,1)S(1)}, u32[]{:S(2)}, u32[]{:S(2)}) collective-permute-start(bf16[8,64,256]{2,1,0:T(8,128)(2,1)S(1)} %get-tuple-element.99), channel_id=1, source_target_pairs={{64,128},{65,129},{66,130},{67,131},{68,132},{69,133},{70,134},{71... | collective-permute-start | bytes 786440 | tf_op jit(solution)/shard_map/ppermute | solution.py:355
  36.3 2.8 %collective-permute-start.13 = (bf16[8,64,256]{2,1,0:T(8,128)(2,1)S(1)}, bf16[8,64,256]{2,1,0:T(8,128)(2,1)S(1)}, u32[]{:S(2)}, u32[]{:S(2)}) collective-permute-start(bf16[8,64,256]{2,1,0:T(8,128)(2,1)S(1)} %get-tuple-element.98), channel_id=1, source_target_pairs={{64,128},{65,129},{66,130},{67,131},{68,132},{69,133},{70,134},{71... | collective-permute-start | bytes 786440 | tf_op jit(solution)/shard_map/ppermute | solution.py:358
  37.1 3.5 %collective-permute-start.19 = (bf16[4,64,256]{2,1,0:T(8,128)(2,1)S(1)}, bf16[4,64,256]{2,1,0:T(8,128)(2,1)S(1)}, u32[]{:S(2)}, u32[]{:S(2)}) collective-permute-start(bf16[4,64,256]{2,1,0:T(8,128)(2,1)S(1)} %get-tuple-element.113), channel_id=1, source_target_pairs={{128,193},{129,194},{130,195},{131,196},{132,197},{133,198},{134,1... | collective-permute-start | bytes 393224 | tf_op jit(solution)/shard_map/ppermute | solution.py:356
  37.8 2.8 %collective-permute-start.20 = (bf16[4,64,256]{2,1,0:T(8,128)(2,1)S(1)}, bf16[4,64,256]{2,1,0:T(8,128)(2,1)S(1)}, u32[]{:S(2)}, u32[]{:S(2)}) collective-permute-start(bf16[4,64,256]{2,1,0:T(8,128)(2,1)S(1)} %get-tuple-element.114), channel_id=1, source_target_pairs={{129,192},{130,193},{131,194},{132,195},{133,196},{134,197},{135,1... | collective-permute-start | bytes 393224 | tf_op jit(solution)/shard_map/ppermute | solution.py:357
  38.4 2.1 %collective-permute-start.18 = (bf16[8,64,256]{2,1,0:T(8,128)(2,1)S(1)}, bf16[8,64,256]{2,1,0:T(8,128)(2,1)S(1)}, u32[]{:S(2)}, u32[]{:S(2)}) collective-permute-start(bf16[8,64,256]{2,1,0:T(8,128)(2,1)S(1)} %get-tuple-element.112), channel_id=1, source_target_pairs={{128,192},{129,193},{130,194},{131,195},{132,196},{133,197},{134,1... | collective-permute-start | bytes 786440 | tf_op jit(solution)/shard_map/ppermute | solution.py:355
  39.2 5.6 %collective-permute-start.17 = (bf16[8,64,256]{2,1,0:T(8,128)(2,1)S(1)}, bf16[8,64,256]{2,1,0:T(8,128)(2,1)S(1)}, u32[]{:S(2)}, u32[]{:S(2)}) collective-permute-start(bf16[8,64,256]{2,1,0:T(8,128)(2,1)S(1)} %get-tuple-element.111), channel_id=1, source_target_pairs={{128,192},{129,193},{130,194},{131,195},{132,196},{133,197},{134,1... | collective-permute-start | bytes 786440 | tf_op jit(solution)/shard_map/ppermute | solution.py:358
  39.8 59.6 %collective-permute-start.26 = (f32[12,64,256]{2,1,0:T(8,128)S(1)}, f32[12,64,256]{2,1,0:T(8,128)S(1)}, u32[]{:S(2)}, u32[]{:S(2)}) collective-permute-start(f32[12,64,256]{2,1,0:T(8,128)S(1)} %get-tuple-element.132), channel_id=1, source_target_pairs={{0,32},{1,33},{2,34},{3,35},{4,36},{5,37},{6,38},{7,39},{8,40},{9,... | collective-permute-start | bytes 2359304 | tf_op jit(solution)/shard_map/ppermute | solution.py:365
  40.8 50.1 %collective-permute-start.23 = (bf16[3,64,256]{2,1,0:T(8,128)(2,1)S(1)}, bf16[3,64,256]{2,1,0:T(8,128)(2,1)S(1)}, u32[]{:S(2)}, u32[]{:S(2)}) collective-permute-start(bf16[3,64,256]{2,1,0:T(8,128)(2,1)S(1)} %get-tuple-element.124), channel_id=1, source_target_pairs={{192,225},{193,226},{194,227},{195,228},{196,229},{197,230},{198,2... | collective-permute-start | bytes 294920 | tf_op jit(solution)/shard_map/ppermute | solution.py:356
  42.1 49.5 %collective-permute-start.24 = (bf16[3,64,256]{2,1,0:T(8,128)(2,1)S(1)}, bf16[3,64,256]{2,1,0:T(8,128)(2,1)S(1)}, u32[]{:S(2)}, u32[]{:S(2)}) collective-permute-start(bf16[3,64,256]{2,1,0:T(8,128)(2,1)S(1)} %get-tuple-element.125), channel_id=1, source_target_pairs={{193,224},{194,225},{195,226},{196,227},{197,228},{198,229},{199,2... | collective-permute-start | bytes 294920 | tf_op jit(solution)/shard_map/ppermute | solution.py:357
  43.4 51.6 %collective-permute-start.22 = (bf16[8,64,256]{2,1,0:T(8,128)(2,1)S(1)}, bf16[8,64,256]{2,1,0:T(8,128)(2,1)S(1)}, u32[]{:S(2)}, u32[]{:S(2)}) collective-permute-start(bf16[8,64,256]{2,1,0:T(8,128)(2,1)S(1)} %get-tuple-element.123), channel_id=1, source_target_pairs={{192,224},{193,225},{194,226},{195,227},{196,228},{197,229},{198,2... | collective-permute-start | bytes 786440 | tf_op jit(solution)/shard_map/ppermute | solution.py:355
  44.8 53.1 %collective-permute-start.21 = (bf16[8,64,256]{2,1,0:T(8,128)(2,1)S(1)}, bf16[8,64,256]{2,1,0:T(8,128)(2,1)S(1)}, u32[]{:S(2)}, u32[]{:S(2)}) collective-permute-start(bf16[8,64,256]{2,1,0:T(8,128)(2,1)S(1)} %get-tuple-element.122), channel_id=1, source_target_pairs={{192,224},{193,225},{194,226},{195,227},{196,228},{197,229},{198,2... | collective-permute-start | bytes 786440 | tf_op jit(solution)/shard_map/ppermute | solution.py:358
  90.9 8.5 %collective-permute-start.27 = (f32[12,64,256]{2,1,0:T(8,128)S(1)}, f32[12,64,256]{2,1,0:T(8,128)S(1)}, u32[]{:S(2)}, u32[]{:S(2)}) collective-permute-start(f32[12,64,256]{2,1,0:T(8,128)S(1)} %get-tuple-element.133), channel_id=1, source_target_pairs={{64,48},{65,49},{66,50},{67,51},{68,52},{69,53},{70,54},{71,55},{7... | collective-permute-start | bytes 2359304 | tf_op jit(solution)/shard_map/ppermute | solution.py:365
  98.1 3.2 %collective-permute-start.25 = (f32[12,64,256]{2,1,0:T(8,128)S(1)}, f32[12,64,256]{2,1,0:T(8,128)S(1)}, u32[]{:S(2)}, u32[]{:S(2)}) collective-permute-start(f32[12,64,256]{2,1,0:T(8,128)S(1)} %get-tuple-element.131), channel_id=1, source_target_pairs={{0,16},{1,17},{2,18},{3,19},{4,20},{5,21},{6,22},{7,23},{8,24},{9,... | collective-permute-start | bytes 2359304 | tf_op jit(solution)/shard_map/ppermute | solution.py:365

commit v10 on v9

--- a/solution.py
+++ b/solution.py
@@ -292,7 +292,8 @@
     near = JUMP_HALO["prev"] + 2
     low, high = call(edge_kernel, [((ncols, near, tile_cols, channels), BF16)] * 2, [], (pieces,))
     above, below = ring(high, 1), ring(low, -1)
-    above, below, all_weights["next"] = lax.optimization_barrier((above, below, all_weights["next"]))
+    early = [all_weights[slot] for slot in ("next", "prev")]
+    above, below, all_weights["next"], all_weights["prev"] = lax.optimization_barrier((above, below, *early))
     like = lambda n, t=F32: ((n, width, channels), t)
     vm = lambda n: pltpu.VMEM((n, width, channels), F32)
     patch = lambda n: pltpu.VMEM((n, width, 3 * channels), BF16)

time: 122 us -> 123 us (level)
  blocking collectives: 29.1 us -> 30.7 us
    all_to_all x1, blocking collectives: 15.1 us -> 16.8 us  [on_device(): packed = lax.all_to_all(packed, 'cols', 0, 0, tiled=True)]
    ppermute x4, waiting for transfers between devices: 3.44 us -> 2.16 us  [on_device(): main = lax.ppermute(results[0], AXES, route(pair, 0))]
where the time goes in v10:
time: 123 us; the launch traced here: 122 us
  waiting for transfers between devices  52.6 us (43%)
  blocking collectives  30.7 us (25%)
  starting transfers between devices  25.2 us (20%)
  Pallas kernels  11.2 us (9%)
  local copies, waits for them, and re-layouts  1.5 us (1%)
    ppermute x4, waiting for transfers between devices, on_device(): top = lax.ppermute(results[2], AXES, route(pair, 1))  44.6 us
    all_to_all x1, blocking collectives, on_device(): packed = lax.all_to_all(packed, 'cols', 0, 0, tiled=True)  16.8 us
    all_to_all x1, blocking collectives, on_device(): lax.all_to_all(tile.reshape(ncols, rows, tile_cols, channels), 'cols', 0,...  14 us
    pallas_call x14, Pallas kernels, call(): pl.pallas_call(kernel, out_shape=[jax.ShapeDtypeStruct(*o) for o in outs]...  11.2 us
    ppermute x7, starting transfers between devices, fetch(): return lax.ppermute(x, AXES, route(pairs, 0))  4.96 us
    ppermute x2, starting transfers between devices, ring(): lax.ppermute(x, ('rows', 'cols'), [(s, (s + shift) % strips) for s in ran...  4.21 us
    ppermute x4, starting transfers between devices, on_device(): lax.ppermute(results[3] if turn == 1 else settled[0], AXES, route(pair, 0))  3.32 us
    ppermute x4, starting transfers between devices, on_device(): main = lax.ppermute(results[0], AXES, route(pair, 0))  3.32 us
  transfers between devices with their start and end apart: 28, of which 5 were waited for; matrix products, arithmetic and copies ran while one was open for 0% of the time, Pallas kernels for 5%

profile of v10, /device:TPU:226, one launch (start us, length us, event | category | flops | bytes accessed | tf_op | source)
XLA Modules:
  0.0 122.4 jit_solution(4600334189720146958)
XLA Ops:
  0.6 1.5 %slice.4 = bf16[1,3,3,256,256]{4,3,2,1,0:T(8,128)(2,1)S(1)} slice(bf16[2,3,3,256,256]{4,3,2,1,0:T(8,128)(2,1)} %param.3), slice={[0:1], [0:3], [0:3], [0:256], [0:256]} | slice | bytes 2359296 | tf_op jit(solution)/shard_map/slice | solution.py:264
  2.1 0.7 collective-permute-start.3
  2.9 0.7 collective-permute-start.2
  3.6 14.0 %all_to_all.10.pieces = f32[4,8,16,256]{3,2,1,0:T(8,128)S(1)} all-to-all(f32[4,8,16,256]{3,2,1,0:T(8,128)} %bitcast.14), channel_id=1, replica_groups=mesh['depth'=16,'rows'=4,'cols'=4] {'cols'}, dimensions={0} | all-to-all | bytes 1048576 | tf_op jit(solution)/shard_map/all_to_all | solution.py:291
  17.6 0.6 collective-permute-start
  18.3 3.6 %collective-permute-start.1 = (bf16[4,6,16,256]{3,2,1,0:T(8,128)(2,1)S(1)}, bf16[4,6,16,256]{3,2,1,0:T(8,128)(2,1)S(1)}, u32[]{:S(2)}, u32[]{:S(2)}) collective-permute-start(bf16[4,6,16,256]{3,2,1,0:T(8,128)(2,1)S(1)} %get-tuple-element.71), channel_id=1, source_target_pairs={{0,15},{1,0},{2,1},{3,2},{4,3},{5,4},{6,5},{7,6},{8,7},{9,8},{10,9... | collective-permute-start | bytes 589832 | tf_op jit(solution)/shard_map/ppermute | solution.py:286
  21.8 0.7 collective-permute-start.4
  22.6 2.9 %collective-permute-done.above = bf16[4,6,16,256]{3,2,1,0:T(8,128)(2,1)S(1)} collective-permute-done((bf16[4,6,16,256]{3,2,1,0:T(8,128)(2,1)S(1)}, bf16[4,6,16,256]{3,2,1,0:T(8,128)(2,1)S(1)}, u32[]{:S(2)}, u32[]{:S(2)}) %collective-permute-start) | collective-permute-done | bytes 196640 | tf_op jit(solution)/shard_map/ppermute | solution.py:286
  25.5 0.0 collective-permute-done.1.below
  25.5 0.0 collective-permute-done.3.rest_3_
  25.5 0.0 collective-permute-done.2.rest_1_.rest_6_
  25.5 3.6 %shard_map.42 = (f32[8,64,256]{2,1,0:T(8,128)S(1)}, bf16[4,64,256]{2,1,0:T(8,128)(2,1)S(1)}, bf16[4,64,256]{2,1,0:T(8,128)(2,1)S(1)}, bf16[16,64,256]{2,1,0:T(8,...) custom-call(f32[4,8,16,256]{3,2,1,0:T(8,128)S(1)} %all_to_all.10.pieces, ...), custom_call_target="tpu_custom_call" | custom-call | flops 15000000512 | tf_op jit(solution)/shard_map/pallas_call | solution.py:243
  29.1 0.7 collective-permute-start.5
  29.9 0.7 collective-permute-start.6
  30.5 0.7 collective-permute-start.11
  31.3 0.7 collective-permute-start.12
  31.9 0.0 collective-permute-done.5.rest_6_.rest_9_.rest_8_
  32.0 0.7 collective-permute-start.8
  32.7 0.7 collective-permute-start.9
  33.4 0.7 collective-permute-start.10
  34.1 0.0 collective-permute-done.12.rest_10_
  34.1 0.7 collective-permute-start.7
  34.8 0.2 shard_map.45
  35.0 0.7 collective-permute-start.15
  35.7 0.7 collective-permute-start.16
  36.4 0.7 collective-permute-start.14
  37.1 0.7 collective-permute-start.13
  37.8 0.7 collective-permute-start.19
  38.5 0.7 collective-permute-start.20
  39.2 0.7 collective-permute-start.18
  39.9 0.7 collective-permute-start.17
  40.6 0.7 collective-permute-start.26
  41.3 0.2 shard_map.49
  41.6 1.3 %collective-permute-start.23 = (bf16[3,64,256]{2,1,0:T(8,128)(2,1)S(1)}, bf16[3,64,256]{2,1,0:T(8,128)(2,1)S(1)}, u32[]{:S(2)}, u32[]{:S(2)}) collective-permute-start(bf16[3,64,256]{2,1,0:T(8,128)(2,1)S(1)} %get-tuple-element.126), channel_id=1, source_target_pairs={{192,225},{193,226},{194,227},{195,228},{196,229},{197,230},{198,2... | collective-permute-start | bytes 294920 | tf_op jit(solution)/shard_map/ppermute | solution.py:357
  42.9 1.3 %collective-permute-start.24 = (bf16[3,64,256]{2,1,0:T(8,128)(2,1)S(1)}, bf16[3,64,256]{2,1,0:T(8,128)(2,1)S(1)}, u32[]{:S(2)}, u32[]{:S(2)}) collective-permute-start(bf16[3,64,256]{2,1,0:T(8,128)(2,1)S(1)} %get-tuple-element.127), channel_id=1, source_target_pairs={{193,224},{194,225},{195,226},{196,227},{197,228},{198,229},{199,2... | collective-permute-start | bytes 294920 | tf_op jit(solution)/shard_map/ppermute | solution.py:358
  44.2 1.3 %collective-permute-start.22 = (bf16[8,64,256]{2,1,0:T(8,128)(2,1)S(1)}, bf16[8,64,256]{2,1,0:T(8,128)(2,1)S(1)}, u32[]{:S(2)}, u32[]{:S(2)}) collective-permute-start(bf16[8,64,256]{2,1,0:T(8,128)(2,1)S(1)} %get-tuple-element.125), channel_id=1, source_target_pairs={{192,224},{193,225},{194,226},{195,227},{196,228},{197,229},{198,2... | collective-permute-start | bytes 786440 | tf_op jit(solution)/shard_map/ppermute | solution.py:356
  45.5 1.3 %collective-permute-start.21 = (bf16[8,64,256]{2,1,0:T(8,128)(2,1)S(1)}, bf16[8,64,256]{2,1,0:T(8,128)(2,1)S(1)}, u32[]{:S(2)}, u32[]{:S(2)}) collective-permute-start(bf16[8,64,256]{2,1,0:T(8,128)(2,1)S(1)} %get-tuple-element.124), channel_id=1, source_target_pairs={{192,224},{193,225},{194,226},{195,227},{196,228},{197,229},{198,2... | collective-permute-start | bytes 786440 | tf_op jit(solution)/shard_map/ppermute | solution.py:359
  46.8 44.5 %collective-permute-done.23.rest_1_ = bf16[3,64,256]{2,1,0:T(8,128)(2,1)S(1)} collective-permute-done((bf16[3,64,256]{2,1,0:T(8,128)(2,1)S(1)}, bf16[3,64,256]{2,1,0:T(8,128)(2,1)S(1)}, u32[]{:S(2)}, u32[]{:S(2)}) %collective-permute-start.23) | collective-permute-done | bytes 98336 | tf_op jit(solution)/shard_map/ppermute | solution.py:357
  91.4 0.7 collective-permute-start.27
  92.1 2.2 %collective-permute-done.22.rest_0_ = bf16[8,64,256]{2,1,0:T(8,128)(2,1)S(1)} collective-permute-done((bf16[8,64,256]{2,1,0:T(8,128)(2,1)S(1)}, bf16[8,64,256]{2,1,0:T(8,128)(2,1)S(1)}, u32[]{:S(2)}, u32[]{:S(2)}) %collective-permute-start.22) | collective-permute-done | bytes 262176 | tf_op jit(solution)/shard_map/ppermute | solution.py:356
  94.2 1.7 %shard_map.51 = (f32[12,64,256]{2,1,0:T(8,128)S(1)}, f32[12,64,256]{2,1,0:T(8,128)S(1)}) custom-call(bf16[8,64,256]{2,1,0:T(8,128)(2,1)S(1)} %collective-permute-done.22.rest_0_, bf16[3,64,256]{2,1,0:T(8,128)(2,1)S(1)} %collective-permute-done.23.rest_1_, ...), custom_call_target="tpu_custom_call", output_to_operand_aliasing={{0}: (5, {}), {1}: (6, {})} | custom-call | flops 20000000000 | tf_op jit(solution)/shard_map/pallas_call | solution.py:243
  95.9 1.1 collective-permute-done.21.low
  97.0 0.2 shard_map.52
  97.2 1.3 %collective-permute-start.25 = (f32[12,64,256]{2,1,0:T(8,128)S(1)}, f32[12,64,256]{2,1,0:T(8,128)S(1)}, u32[]{:S(2)}, u32[]{:S(2)}) collective-permute-start(f32[12,64,256]{2,1,0:T(8,128)S(1)} %get-tuple-element.133), channel_id=1, source_target_pairs={{0,16},{1,17},{2,18},{3,19},{4,20},{5,21},{6,22},{7,23},{8,24},{9,... | collective-permute-start | bytes 2359304 | tf_op jit(solution)/shard_map/ppermute | solution.py:366
  98.6 1.8 %collective-permute-done.25.core = f32[12,64,256]{2,1,0:T(8,128)S(1)} collective-permute-done((f32[12,64,256]{2,1,0:T(8,128)S(1)}, f32[12,64,256]{2,1,0:T(8,128)S(1)}, u32[]{:S(2)}, u32[]{:S(2)}) %collective-permute-start.25) | collective-permute-done | bytes 786464 | tf_op jit(solution)/shard_map/ppermute | solution.py:366
  100.4 0.1 shard_map.53
  100.6 16.8 %all_to_all.11.packed = bf16[4,368,256]{2,1,0:T(8,128)(2,1)S(1)} all-to-all(bf16[4,368,256]{2,1,0:T(8,128)(2,1)S(1)} %shard_map.53), channel_id=1, replica_groups=mesh['depth'=16,'rows'=4,'cols'=4] {'cols'}, dimensions={0} | all-to-all | bytes 1507328 | tf_op jit(solution)/shard_map/all_to_all | solution.py:376
  117.4 5.1 %shard_map.54 = (f32[2,32,16,256]{3,2,1,0:T(8,128)}, f32[32,16,256]{2,1,0:T(8,128)}) custom-call(bf16[4,368,256]{2,1,0:T(8,128)(2,1)S(1)} %all_to_all.11.packed, bf16[2,3,768,256]{3,2,1,0:T(8,128)(2,1)S(1)} %bitcast.10), custom_call_target="tpu_custom_call" | custom-call | tf_op jit(solution)/shard_map/pallas_call | solution.py:243
  (27 shorter events, 0.2 us)
Async XLA Ops:
  0.6 24.9 %copy-start = (bf16[2,3,3,256,256]{4,3,2,1,0:T(8,128)(2,1)S(1)}, bf16[2,3,3,256,256]{4,3,2,1,0:T(8,128)(2,1)}, u32[]{:S(2)}) copy-start(bf16[2,3,3,256,256]{4,3,2,1,0:T(8,128)(2,1)} %param.3) | copy-start | bytes 7077892
  2.1 23.3 %collective-permute-start.3 = (bf16[3,768,256]{2,1,0:T(8,128)(2,1)S(1)}, bf16[3,768,256]{2,1,0:T(8,128)(2,1)S(1)}, u32[]{:S(2)}, u32[]{:S(2)}) collective-permute-start(bf16[3,768,256]{2,1,0:T(8,128)(2,1)S(1)} %bitcast.11), channel_id=1, source_target_pairs={{48,64},{49,65},{50,66},{51,67},{52,68},{53,69},{54,70},{55,71},{5... | collective-permute-start | bytes 3538952 | tf_op jit(solution)/shard_map/ppermute | solution.py:283
  2.9 22.6 %collective-permute-start.2 = (bf16[3,768,256]{2,1,0:T(8,128)(2,1)S(1)}, bf16[3,768,256]{2,1,0:T(8,128)(2,1)S(1)}, u32[]{:S(2)}, u32[]{:S(2)}) collective-permute-start(bf16[3,768,256]{2,1,0:T(8,128)(2,1)S(1)} %bitcast.12), channel_id=1, source_target_pairs={{32,0},{33,1},{34,2},{35,3},{36,4},{37,5},{38,6},{39,7},{40,8},{41... | collective-permute-start | bytes 3538952 | tf_op jit(solution)/shard_map/ppermute | solution.py:283
  17.6 7.9 %collective-permute-start = (bf16[4,6,16,256]{3,2,1,0:T(8,128)(2,1)S(1)}, bf16[4,6,16,256]{3,2,1,0:T(8,128)(2,1)S(1)}, u32[]{:S(2)}, u32[]{:S(2)}) collective-permute-start(bf16[4,6,16,256]{3,2,1,0:T(8,128)(2,1)S(1)} %get-tuple-element.70), channel_id=1, source_target_pairs={{0,1},{1,2},{2,3},{3,4},{4,5},{5,6},{6,7},{7,8},{8,9},{9,10},{10,1... | collective-permute-start | bytes 589832 | tf_op jit(solution)/shard_map/ppermute | solution.py:286
  18.3 7.2 %collective-permute-start.1 = (bf16[4,6,16,256]{3,2,1,0:T(8,128)(2,1)S(1)}, bf16[4,6,16,256]{3,2,1,0:T(8,128)(2,1)S(1)}, u32[]{:S(2)}, u32[]{:S(2)}) collective-permute-start(bf16[4,6,16,256]{3,2,1,0:T(8,128)(2,1)S(1)} %get-tuple-element.71), channel_id=1, source_target_pairs={{0,15},{1,0},{2,1},{3,2},{4,3},{5,4},{6,5},{7,6},{8,7},{9,8},{10,9... | collective-permute-start | bytes 589832 | tf_op jit(solution)/shard_map/ppermute | solution.py:286
  21.8 7.3 %collective-permute-start.4 = (bf16[3,768,256]{2,1,0:T(8,128)(2,1)S(1)}, bf16[3,768,256]{2,1,0:T(8,128)(2,1)S(1)}, u32[]{:S(2)}, u32[]{:S(2)}) collective-permute-start(bf16[3,768,256]{2,1,0:T(8,128)(2,1)S(1)} %bitcast.13), channel_id=1, source_target_pairs={{16,0},{17,1},{18,2},{19,3},{20,4},{21,5},{22,6},{23,7},{24,8},{25... | collective-permute-start | bytes 3538952 | tf_op jit(solution)/shard_map/ppermute | solution.py:283
  29.1 2.8 %collective-permute-start.5 = (f32[12,64,256]{2,1,0:T(8,128)S(1)}, f32[12,64,256]{2,1,0:T(8,128)S(1)}, u32[]{:S(2)}, u32[]{:S(2)}) collective-permute-start(f32[12,64,256]{2,1,0:T(8,128)S(1)} %get-tuple-element.83), channel_id=1, source_target_pairs={{16,0},{17,1},{18,2},{19,3},{20,4},{21,5},{22,6},{23,7},{24,8},{25... | collective-permute-start | bytes 2359304 | tf_op jit(solution)/shard_map/ppermute | solution.py:283
  29.9 2.1 %collective-permute-start.6 = (bf16[8,64,256]{2,1,0:T(8,128)(2,1)S(1)}, bf16[8,64,256]{2,1,0:T(8,128)(2,1)S(1)}, u32[]{:S(2)}, u32[]{:S(2)}) collective-permute-start(bf16[8,64,256]{2,1,0:T(8,128)(2,1)S(1)} %get-tuple-element.86), channel_id=1, source_target_pairs={{32,0},{33,1},{34,2},{35,3},{36,4},{37,5},{38,6},{39,7},{40,8},{41... | collective-permute-start | bytes 786440 | tf_op jit(solution)/shard_map/ppermute | solution.py:283
  30.5 4.2 %collective-permute-start.11 = (bf16[16,64,256]{2,1,0:T(8,128)(2,1)S(1)}, bf16[16,64,256]{2,1,0:T(8,128)(2,1)S(1)}, u32[]{:S(2)}, u32[]{:S(2)}) collective-permute-start(bf16[16,64,256]{2,1,0:T(8,128)(2,1)S(1)} %get-tuple-element.92), channel_id=1, source_target_pairs={{48,64},{49,65},{50,66},{51,67},{52,68},{53,69},{54,70},{55,71},{5... | collective-permute-start | bytes 1572872 | tf_op jit(solution)/shard_map/ppermute | solution.py:283
  31.3 2.8 %collective-permute-start.12 = (bf16[8,64,256]{2,1,0:T(8,128)(2,1)S(1)}, bf16[8,64,256]{2,1,0:T(8,128)(2,1)S(1)}, u32[]{:S(2)}, u32[]{:S(2)}) collective-permute-start(bf16[8,64,256]{2,1,0:T(8,128)(2,1)S(1)} %get-tuple-element.86), channel_id=1, source_target_pairs={{96,64},{97,65},{98,66},{99,67},{100,68},{101,69},{102,70},{103,71... | collective-permute-start | bytes 786440 | tf_op jit(solution)/shard_map/ppermute | solution.py:283
  32.0 2.8 %collective-permute-start.8 = (bf16[8,64,256]{2,1,0:T(8,128)(2,1)S(1)}, bf16[8,64,256]{2,1,0:T(8,128)(2,1)S(1)}, u32[]{:S(2)}, u32[]{:S(2)}) collective-permute-start(bf16[8,64,256]{2,1,0:T(8,128)(2,1)S(1)} %get-tuple-element.88), channel_id=1, source_target_pairs={{0,64},{1,65},{2,66},{3,67},{4,68},{5,69},{6,70},{7,71},{8,72},{9,... | collective-permute-start | bytes 786440 | tf_op jit(solution)/shard_map/ppermute | solution.py:356
  32.7 2.1 %collective-permute-start.9 = (bf16[5,64,256]{2,1,0:T(8,128)(2,1)S(1)}, bf16[5,64,256]{2,1,0:T(8,128)(2,1)S(1)}, u32[]{:S(2)}, u32[]{:S(2)}) collective-permute-start(bf16[5,64,256]{2,1,0:T(8,128)(2,1)S(1)} %get-tuple-element.89), channel_id=1, source_target_pairs={{0,65},{1,66},{2,67},{3,68},{4,69},{5,70},{6,71},{7,72},{8,73},{9,... | collective-permute-start | bytes 491528 | tf_op jit(solution)/shard_map/ppermute | solution.py:357
  33.4 1.4 %collective-permute-start.10 = (bf16[5,64,256]{2,1,0:T(8,128)(2,1)S(1)}, bf16[5,64,256]{2,1,0:T(8,128)(2,1)S(1)}, u32[]{:S(2)}, u32[]{:S(2)}) collective-permute-start(bf16[5,64,256]{2,1,0:T(8,128)(2,1)S(1)} %get-tuple-element.90), channel_id=1, source_target_pairs={{1,64},{2,65},{3,66},{4,67},{5,68},{6,69},{7,70},{8,71},{9,72},{10... | collective-permute-start | bytes 491528 | tf_op jit(solution)/shard_map/ppermute | solution.py:358
  34.1 3.0 %collective-permute-start.7 = (bf16[8,64,256]{2,1,0:T(8,128)(2,1)S(1)}, bf16[8,64,256]{2,1,0:T(8,128)(2,1)S(1)}, u32[]{:S(2)}, u32[]{:S(2)}) collective-permute-start(bf16[8,64,256]{2,1,0:T(8,128)(2,1)S(1)} %get-tuple-element.87), channel_id=1, source_target_pairs={{0,64},{1,65},{2,66},{3,67},{4,68},{5,69},{6,70},{7,71},{8,72},{9,... | collective-permute-start | bytes 786440 | tf_op jit(solution)/shard_map/ppermute | solution.py:359
  35.0 2.8 %collective-permute-start.15 = (bf16[5,64,256]{2,1,0:T(8,128)(2,1)S(1)}, bf16[5,64,256]{2,1,0:T(8,128)(2,1)S(1)}, u32[]{:S(2)}, u32[]{:S(2)}) collective-permute-start(bf16[5,64,256]{2,1,0:T(8,128)(2,1)S(1)} %get-tuple-element.102), channel_id=1, source_target_pairs={{64,129},{65,130},{66,131},{67,132},{68,133},{69,134},{70,135},{71... | collective-permute-start | bytes 491528 | tf_op jit(solution)/shard_map/ppermute | solution.py:357
  35.7 2.1 %collective-permute-start.16 = (bf16[5,64,256]{2,1,0:T(8,128)(2,1)S(1)}, bf16[5,64,256]{2,1,0:T(8,128)(2,1)S(1)}, u32[]{:S(2)}, u32[]{:S(2)}) collective-permute-start(bf16[5,64,256]{2,1,0:T(8,128)(2,1)S(1)} %get-tuple-element.103), channel_id=1, source_target_pairs={{65,128},{66,129},{67,130},{68,131},{69,132},{70,133},{71,134},{72... | collective-permute-start | bytes 491528 | tf_op jit(solution)/shard_map/ppermute | solution.py:358
  36.4 1.4 %collective-permute-start.14 = (bf16[8,64,256]{2,1,0:T(8,128)(2,1)S(1)}, bf16[8,64,256]{2,1,0:T(8,128)(2,1)S(1)}, u32[]{:S(2)}, u32[]{:S(2)}) collective-permute-start(bf16[8,64,256]{2,1,0:T(8,128)(2,1)S(1)} %get-tuple-element.101), channel_id=1, source_target_pairs={{64,128},{65,129},{66,130},{67,131},{68,132},{69,133},{70,134},{71... | collective-permute-start | bytes 786440 | tf_op jit(solution)/shard_map/ppermute | solution.py:356
  37.1 2.8 %collective-permute-start.13 = (bf16[8,64,256]{2,1,0:T(8,128)(2,1)S(1)}, bf16[8,64,256]{2,1,0:T(8,128)(2,1)S(1)}, u32[]{:S(2)}, u32[]{:S(2)}) collective-permute-start(bf16[8,64,256]{2,1,0:T(8,128)(2,1)S(1)} %get-tuple-element.100), channel_id=1, source_target_pairs={{64,128},{65,129},{66,130},{67,131},{68,132},{69,133},{70,134},{71... | collective-permute-start | bytes 786440 | tf_op jit(solution)/shard_map/ppermute | solution.py:359
  37.8 3.5 %collective-permute-start.19 = (bf16[4,64,256]{2,1,0:T(8,128)(2,1)S(1)}, bf16[4,64,256]{2,1,0:T(8,128)(2,1)S(1)}, u32[]{:S(2)}, u32[]{:S(2)}) collective-permute-start(bf16[4,64,256]{2,1,0:T(8,128)(2,1)S(1)} %get-tuple-element.115), channel_id=1, source_target_pairs={{128,193},{129,194},{130,195},{131,196},{132,197},{133,198},{134,1... | collective-permute-start | bytes 393224 | tf_op jit(solution)/shard_map/ppermute | solution.py:357
  38.5 2.8 %collective-permute-start.20 = (bf16[4,64,256]{2,1,0:T(8,128)(2,1)S(1)}, bf16[4,64,256]{2,1,0:T(8,128)(2,1)S(1)}, u32[]{:S(2)}, u32[]{:S(2)}) collective-permute-start(bf16[4,64,256]{2,1,0:T(8,128)(2,1)S(1)} %get-tuple-element.116), channel_id=1, source_target_pairs={{129,192},{130,193},{131,194},{132,195},{133,196},{134,197},{135,1... | collective-permute-start | bytes 393224 | tf_op jit(solution)/shard_map/ppermute | solution.py:358
  39.2 2.1 %collective-permute-start.18 = (bf16[8,64,256]{2,1,0:T(8,128)(2,1)S(1)}, bf16[8,64,256]{2,1,0:T(8,128)(2,1)S(1)}, u32[]{:S(2)}, u32[]{:S(2)}) collective-permute-start(bf16[8,64,256]{2,1,0:T(8,128)(2,1)S(1)} %get-tuple-element.114), channel_id=1, source_target_pairs={{128,192},{129,193},{130,194},{131,195},{132,196},{133,197},{134,1... | collective-permute-start | bytes 786440 | tf_op jit(solution)/shard_map/ppermute | solution.py:356
  39.9 5.6 %collective-permute-start.17 = (bf16[8,64,256]{2,1,0:T(8,128)(2,1)S(1)}, bf16[8,64,256]{2,1,0:T(8,128)(2,1)S(1)}, u32[]{:S(2)}, u32[]{:S(2)}) collective-permute-start(bf16[8,64,256]{2,1,0:T(8,128)(2,1)S(1)} %get-tuple-element.113), channel_id=1, source_target_pairs={{128,192},{129,193},{130,194},{131,195},{132,196},{133,197},{134,1... | collective-permute-start | bytes 786440 | tf_op jit(solution)/shard_map/ppermute | solution.py:359
  40.6 58.0 %collective-permute-start.26 = (f32[12,64,256]{2,1,0:T(8,128)S(1)}, f32[12,64,256]{2,1,0:T(8,128)S(1)}, u32[]{:S(2)}, u32[]{:S(2)}) collective-permute-start(f32[12,64,256]{2,1,0:T(8,128)S(1)} %get-tuple-element.134), channel_id=1, source_target_pairs={{0,32},{1,33},{2,34},{3,35},{4,36},{5,37},{6,38},{7,39},{8,40},{9,... | collective-permute-start | bytes 2359304 | tf_op jit(solution)/shard_map/ppermute | solution.py:366
  41.6 49.8 %collective-permute-start.23 = (bf16[3,64,256]{2,1,0:T(8,128)(2,1)S(1)}, bf16[3,64,256]{2,1,0:T(8,128)(2,1)S(1)}, u32[]{:S(2)}, u32[]{:S(2)}) collective-permute-start(bf16[3,64,256]{2,1,0:T(8,128)(2,1)S(1)} %get-tuple-element.126), channel_id=1, source_target_pairs={{192,225},{193,226},{194,227},{195,228},{196,229},{197,230},{198,2... | collective-permute-start | bytes 294920 | tf_op jit(solution)/shard_map/ppermute | solution.py:357
  42.9 49.2 %collective-permute-start.24 = (bf16[3,64,256]{2,1,0:T(8,128)(2,1)S(1)}, bf16[3,64,256]{2,1,0:T(8,128)(2,1)S(1)}, u32[]{:S(2)}, u32[]{:S(2)}) collective-permute-start(bf16[3,64,256]{2,1,0:T(8,128)(2,1)S(1)} %get-tuple-element.127), channel_id=1, source_target_pairs={{193,224},{194,225},{195,226},{196,227},{197,228},{198,229},{199,2... | collective-permute-start | bytes 294920 | tf_op jit(solution)/shard_map/ppermute | solution.py:358
  44.2 50.1 %collective-permute-start.22 = (bf16[8,64,256]{2,1,0:T(8,128)(2,1)S(1)}, bf16[8,64,256]{2,1,0:T(8,128)(2,1)S(1)}, u32[]{:S(2)}, u32[]{:S(2)}) collective-permute-start(bf16[8,64,256]{2,1,0:T(8,128)(2,1)S(1)} %get-tuple-element.125), channel_id=1, source_target_pairs={{192,224},{193,225},{194,226},{195,227},{196,228},{197,229},{198,2... | collective-permute-start | bytes 786440 | tf_op jit(solution)/shard_map/ppermute | solution.py:356
  45.5 51.5 %collective-permute-start.21 = (bf16[8,64,256]{2,1,0:T(8,128)(2,1)S(1)}, bf16[8,64,256]{2,1,0:T(8,128)(2,1)S(1)}, u32[]{:S(2)}, u32[]{:S(2)}) collective-permute-start(bf16[8,64,256]{2,1,0:T(8,128)(2,1)S(1)} %get-tuple-element.124), channel_id=1, source_target_pairs={{192,224},{193,225},{194,226},{195,227},{196,228},{197,229},{198,2... | collective-permute-start | bytes 786440 | tf_op jit(solution)/shard_map/ppermute | solution.py:359
  91.4 7.2 %collective-permute-start.27 = (f32[12,64,256]{2,1,0:T(8,128)S(1)}, f32[12,64,256]{2,1,0:T(8,128)S(1)}, u32[]{:S(2)}, u32[]{:S(2)}) collective-permute-start(f32[12,64,256]{2,1,0:T(8,128)S(1)} %get-tuple-element.135), channel_id=1, source_target_pairs={{64,48},{65,49},{66,50},{67,51},{68,52},{69,53},{70,54},{71,55},{7... | collective-permute-start | bytes 2359304 | tf_op jit(solution)/shard_map/ppermute | solution.py:366
  97.2 3.2 %collective-permute-start.25 = (f32[12,64,256]{2,1,0:T(8,128)S(1)}, f32[12,64,256]{2,1,0:T(8,128)S(1)}, u32[]{:S(2)}, u32[]{:S(2)}) collective-permute-start(f32[12,64,256]{2,1,0:T(8,128)S(1)} %get-tuple-element.133), channel_id=1, source_target_pairs={{0,16},{1,17},{2,18},{3,19},{4,20},{5,21},{6,22},{7,23},{8,24},{9,... | collective-permute-start | bytes 2359304 | tf_op jit(solution)/shard_map/ppermute | solution.py:366

commit v11 on v9

--- a/solution.py
+++ b/solution.py
@@ -168,7 +168,8 @@
             new[KEPT : KEPT + rows] = old[KEPT : KEPT + rows] + part
 
 
-def pack_kernel(own, core, after, prev, packed, state):
+def pack_kernel(own, core, after, prev, *rest):
+    packs, state = rest[:-1], rest[-1]
     depth = lax.axis_index("depth")
     final = 4 * ((lax.axis_size("depth") - 1) // 4) + 2
     role = jnp.where(depth < final, depth % 4, depth - final)
@@ -178,48 +179,57 @@
         def _():
             state[...] = source[...]
 
-    ncols = packed.shape[0]
+    ncols = len(packs)
     deep, width, channels = state.shape
     wide = width // ncols
     rows = deep - 2 * KEPT
-    first = lax.axis_index("cols") == 0
+    mine = lax.axis_index("cols")
     group = lax.broadcasted_iota(jnp.int32, (8, channels), 0)
     span = wide + 8
-    for k in range(ncols):
+    for away, packed in enumerate(packs):
+        k = lax.rem(mine + away, ncols)
+        middle = pl.multiple_of(k * wide, 8)
+        before = pl.multiple_of(jnp.maximum(middle - 8, 0), 8)
+        after_it = pl.multiple_of(jnp.minimum(middle + wide, width - 8), 8)
         for row in range(rows + KEPT):
             if row < rows:
-                line = lambda a, b: state[KEPT + row, a:b]
+                place = KEPT + row
             else:
-                line = lambda a, b: jnp.where(first, state[row - rows, a:b], state[KEPT + row, a:b])
-            mine = line(k * wide, (k + 1) * wide)
-            right = line((k + 1) * wide, (k + 1) * wide + 8) if k < ncols - 1 else jnp.zeros((8, channels), F32)
-            left = line(k * wide - 8, k * wide) if k > 0 else jnp.zeros((8, channels), F32)
-            high = mine.astype(BF16)
-            packed[k, row * span : row * span + wide] = high
-            packed[k, row * span + wide : (row + 1) * span] = jnp.where(group < 4, right, left).astype(BF16)
+                place = jnp.where(mine == 0, row - rows, KEPT + row)
+            here = state[place, pl.ds(middle, wide)]
+            right = jnp.where(k < ncols - 1, state[place, pl.ds(after_it, 8)], 0.0)
+            left = jnp.where(k > 0, state[place, pl.ds(before, 8)], 0.0)
+            high = here.astype(BF16)
+            packed[row * span : row * span + wide] = high
+            packed[row * span + wide : (row + 1) * span] = jnp.where(group < 4, right, left).astype(BF16)
             if row < rows:
                 start = (rows + KEPT) * span + row * wide
-                packed[k, start : start + wide] = (mine - high.astype(F32)).astype(BF16)
-
-
-def tail_kernel(step, height, width, packed, layers, fine, coarse, state, patch, second):
-    ncols = packed.shape[0]
+                packed[start : start + wide] = (here - high.astype(F32)).astype(BF16)
+
+
+def tail_kernel(step, height, width, *rest):
+    *packs, layers, fine, coarse, state, patch, second = rest
+    ncols = len(packs)
     tile_rows, wide = coarse.shape[:2]
     rows = tile_rows // ncols
     span = wide + 8
-    for k in range(ncols):
+    for away, packed in enumerate(packs):
+        k = lax.rem(lax.axis_index("cols") + ncols - away, ncols)
         for row in range(rows):
             start = (rows + KEPT) * span + row * wide
-            high = packed[k, row * span : (row + 1) * span].astype(F32)
-            whole = high[:wide] + packed[k, start : start + wide].astype(F32)
+            high = packed[row * span : (row + 1) * span].astype(F32)
+            whole = high[:wide] + packed[start : start + wide].astype(F32)
             place = k * rows + row
             coarse[place] = whole
             state[KEPT + place, :wide] = whole
             state[KEPT + place, wide:] = high[wide:]
-    for row in range(KEPT):
-        cut = slice((rows + row) * span, (rows + row + 1) * span)
-        state[row] = packed[0, cut].astype(F32)
-        state[KEPT + tile_rows + row] = packed[ncols - 1, cut].astype(F32)
+        for end, first in ((0, 0), (ncols - 1, KEPT + tile_rows)):
+
+            @pl.when(k == end)
+            def _():
+                for row in range(KEPT):
+                    state[first + row] = packed[(rows + row) * span : (rows + row + 1) * span].astype(F32)
+
     top = lax.axis_index("rows") * tile_rows - KEPT
     column = lax.broadcasted_iota(jnp.int32, (span, state.shape[2]), 0)
     place = lax.axis_index("cols") * wide + jnp.where(column < span - 4, column, column - span)
@@ -366,19 +376,20 @@
 
     span = tile_cols + 8
     pixels = (rows + KEPT) * span + rows * tile_cols
-    (packed,) = call(
+    packs = list(call(
         pack_kernel,
-        [((ncols, pixels, channels), BF16)],
+        [((pixels, channels), BF16)] * ncols,
         [vm(rows + 2 * KEPT)],
         (saved["own"], give("core"), give("next"), give("prev")),
-    )
-    packed = lax.all_to_all(packed, "cols", 0, 0, tiled=True)
+    ))
+    for away in (2, 1, 3):
+        packs[away] = lax.ppermute(packs[away], "cols", [(c, (c + away) % ncols) for c in range(ncols)])
     tall = lambda n, t=F32, taps=1: pltpu.VMEM((n, span, taps * channels), t)
     fine, coarse = call(
         functools.partial(tail_kernel, step, height, width),
         [((2, *tile.shape), F32), (tile.shape, F32)],
         [tall(tile_rows + 4), tall(tile_rows + 4, BF16, 3), tall(tile_rows + 4, BF16, 3)],
-        (packed, flat),
+        (*packs, flat),
     )
     return fine, coarse[None]
 

time: 122 us -> 120 us (0.984)
  blocking collectives: 29.1 us -> 14 us
  waiting for transfers between devices: 53.5 us -> 63.1 us
  starting transfers between devices: 25.2 us -> 28.5 us
    all_to_all x1 -> x0, blocking collectives: 15.1 us -> none  [on_device(): packed = lax.all_to_all(packed, 'cols', 0, 0, tiled=True)]
    ppermute x0 -> x3, waiting for transfers between devices: none -> 9.61 us  [on_device(): lax.ppermute(packs[away], 'cols', [(c, (c + away) % ncols) for c in range...]
    ppermute x0 -> x3, starting transfers between devices: none -> 3.32 us  [on_device(): lax.ppermute(packs[away], 'cols', [(c, (c + away) % ncols) for c in range...]
  transfers between devices with their start and end apart: 28 -> 31, of which waited for: 5 -> 7; matrix products, arithmetic and copies ran while one was open for 0% -> 0% of each run, Pallas kernels for 5% -> 5%
where the time goes in v11:
time: 120 us; the launch traced here: 119 us
  waiting for transfers between devices  63.1 us (53%)
  starting transfers between devices  28.5 us (24%)
  blocking collectives  14 us (12%)
  Pallas kernels  11.3 us (9%)
  local copies, waits for them, and re-layouts  1.5 us (1%)
    ppermute x4, waiting for transfers between devices, on_device(): top = lax.ppermute(results[2], AXES, route(pair, 1))  44.9 us
    all_to_all x1, blocking collectives, on_device(): lax.all_to_all(tile.reshape(ncols, rows, tile_cols, channels), 'cols', 0,...  14 us
    pallas_call x14, Pallas kernels, call(): pl.pallas_call(kernel, out_shape=[jax.ShapeDtypeStruct(*o) for o in outs]...  11.3 us
    ppermute x3, waiting for transfers between devices, on_device(): lax.ppermute(packs[away], 'cols', [(c, (c + away) % ncols) for c in range...  9.61 us
    ppermute x7, starting transfers between devices, fetch(): return lax.ppermute(x, AXES, route(pairs, 0))  4.96 us
    ppermute x2, starting transfers between devices, ring(): lax.ppermute(x, ('rows', 'cols'), [(s, (s + shift) % strips) for s in ran...  4.21 us
    ppermute x4, waiting for transfers between devices, on_device(): main = lax.ppermute(results[0], AXES, route(pair, 0))  3.44 us
    ppermute x4, starting transfers between devices, on_device(): main = lax.ppermute(results[0], AXES, route(pair, 0))  3.32 us
  transfers between devices with their start and end apart: 31, of which 7 were waited for; matrix products, arithmetic and copies ran while one was open for 0% of the time, Pallas kernels for 5%

profile of v11, /device:TPU:226, one launch (start us, length us, event | category | flops | bytes accessed | tf_op | source)
XLA Modules:
  0.0 119.4 jit_solution(12311274648538033405)
XLA Ops:
  0.6 1.5 %slice.4 = bf16[1,3,3,256,256]{4,3,2,1,0:T(8,128)(2,1)S(1)} slice(bf16[2,3,3,256,256]{4,3,2,1,0:T(8,128)(2,1)} %param.3), slice={[0:1], [0:3], [0:3], [0:256], [0:256]} | slice | bytes 2359296 | tf_op jit(solution)/shard_map/slice | solution.py:274
  2.1 0.7 collective-permute-start.2
  2.9 14.0 %all_to_all.5.pieces = f32[4,8,16,256]{3,2,1,0:T(8,128)S(1)} all-to-all(f32[4,8,16,256]{3,2,1,0:T(8,128)} %bitcast.14), channel_id=1, replica_groups=mesh['depth'=16,'rows'=4,'cols'=4] {'cols'}, dimensions={0} | all-to-all | bytes 1048576 | tf_op jit(solution)/shard_map/all_to_all | solution.py:301
  16.9 0.6 collective-permute-start
  17.5 3.6 %collective-permute-start.1 = (bf16[4,6,16,256]{3,2,1,0:T(8,128)(2,1)S(1)}, bf16[4,6,16,256]{3,2,1,0:T(8,128)(2,1)S(1)}, u32[]{:S(2)}, u32[]{:S(2)}) collective-permute-start(bf16[4,6,16,256]{3,2,1,0:T(8,128)(2,1)S(1)} %get-tuple-element.74), channel_id=1, source_target_pairs={{0,15},{1,0},{2,1},{3,2},{4,3},{5,4},{6,5},{7,6},{8,7},{9,8},{10,9... | collective-permute-start | bytes 589832 | tf_op jit(solution)/shard_map/ppermute | solution.py:296
  21.1 0.7 collective-permute-start.10
  21.8 0.7 collective-permute-start.3
  22.6 2.2 %collective-permute-done.above = bf16[4,6,16,256]{3,2,1,0:T(8,128)(2,1)S(1)} collective-permute-done((bf16[4,6,16,256]{3,2,1,0:T(8,128)(2,1)S(1)}, bf16[4,6,16,256]{3,2,1,0:T(8,128)(2,1)S(1)}, u32[]{:S(2)}, u32[]{:S(2)}) %collective-permute-start) | collective-permute-done | bytes 196640 | tf_op jit(solution)/shard_map/ppermute | solution.py:296
  24.7 0.0 collective-permute-done.1.below
  24.7 3.6 %shard_map.42 = (f32[8,64,256]{2,1,0:T(8,128)S(1)}, bf16[4,64,256]{2,1,0:T(8,128)(2,1)S(1)}, bf16[4,64,256]{2,1,0:T(8,128)(2,1)S(1)}, bf16[16,64,256]{2,1,0:T(8,...) custom-call(f32[4,8,16,256]{3,2,1,0:T(8,128)S(1)} %all_to_all.5.pieces, ...), custom_call_target="tpu_custom_call" | custom-call | flops 15000000512 | tf_op jit(solution)/shard_map/pallas_call | solution.py:253
  28.4 0.7 collective-permute-start.4
  29.1 0.7 collective-permute-start.5
  29.8 0.7 collective-permute-start.11
  30.5 0.7 collective-permute-start.12
  31.3 0.7 collective-permute-start.7
  31.9 0.7 collective-permute-start.8
  32.6 0.7 collective-permute-start.9
  33.3 0.7 collective-permute-start.6
  34.0 0.2 shard_map.45
  34.3 0.7 collective-permute-start.15
  34.9 0.7 collective-permute-start.16
  35.6 0.7 collective-permute-start.14
  36.3 0.7 collective-permute-start.13
  37.1 0.7 collective-permute-start.19
  37.8 0.7 collective-permute-start.20
  38.4 0.7 collective-permute-start.18
  39.2 0.7 collective-permute-start.17
  39.8 0.7 collective-permute-start.26
  40.6 0.2 shard_map.49
  40.8 1.3 %collective-permute-start.23 = (bf16[3,64,256]{2,1,0:T(8,128)(2,1)S(1)}, bf16[3,64,256]{2,1,0:T(8,128)(2,1)S(1)}, u32[]{:S(2)}, u32[]{:S(2)}) collective-permute-start(bf16[3,64,256]{2,1,0:T(8,128)(2,1)S(1)} %get-tuple-element.128), channel_id=1, source_target_pairs={{192,225},{193,226},{194,227},{195,228},{196,229},{197,230},{198,2... | collective-permute-start | bytes 294920 | tf_op jit(solution)/shard_map/ppermute | solution.py:366
  42.1 1.3 %collective-permute-start.24 = (bf16[3,64,256]{2,1,0:T(8,128)(2,1)S(1)}, bf16[3,64,256]{2,1,0:T(8,128)(2,1)S(1)}, u32[]{:S(2)}, u32[]{:S(2)}) collective-permute-start(bf16[3,64,256]{2,1,0:T(8,128)(2,1)S(1)} %get-tuple-element.129), channel_id=1, source_target_pairs={{193,224},{194,225},{195,226},{196,227},{197,228},{198,229},{199,2... | collective-permute-start | bytes 294920 | tf_op jit(solution)/shard_map/ppermute | solution.py:367
  43.4 1.3 %collective-permute-start.22 = (bf16[8,64,256]{2,1,0:T(8,128)(2,1)S(1)}, bf16[8,64,256]{2,1,0:T(8,128)(2,1)S(1)}, u32[]{:S(2)}, u32[]{:S(2)}) collective-permute-start(bf16[8,64,256]{2,1,0:T(8,128)(2,1)S(1)} %get-tuple-element.127), channel_id=1, source_target_pairs={{192,224},{193,225},{194,226},{195,227},{196,228},{197,229},{198,2... | collective-permute-start | bytes 786440 | tf_op jit(solution)/shard_map/ppermute | solution.py:365
  44.8 1.3 %collective-permute-start.21 = (bf16[8,64,256]{2,1,0:T(8,128)(2,1)S(1)}, bf16[8,64,256]{2,1,0:T(8,128)(2,1)S(1)}, u32[]{:S(2)}, u32[]{:S(2)}) collective-permute-start(bf16[8,64,256]{2,1,0:T(8,128)(2,1)S(1)} %get-tuple-element.126), channel_id=1, source_target_pairs={{192,224},{193,225},{194,226},{195,227},{196,228},{197,229},{198,2... | collective-permute-start | bytes 786440 | tf_op jit(solution)/shard_map/ppermute | solution.py:368
  46.1 44.9 %collective-permute-done.23.rest_1_ = bf16[3,64,256]{2,1,0:T(8,128)(2,1)S(1)} collective-permute-done((bf16[3,64,256]{2,1,0:T(8,128)(2,1)S(1)}, bf16[3,64,256]{2,1,0:T(8,128)(2,1)S(1)}, u32[]{:S(2)}, u32[]{:S(2)}) %collective-permute-start.23) | collective-permute-done | bytes 98336 | tf_op jit(solution)/shard_map/ppermute | solution.py:366
  90.9 0.7 collective-permute-start.27
  91.7 3.4 %collective-permute-done.22.rest_0_ = bf16[8,64,256]{2,1,0:T(8,128)(2,1)S(1)} collective-permute-done((bf16[8,64,256]{2,1,0:T(8,128)(2,1)S(1)}, bf16[8,64,256]{2,1,0:T(8,128)(2,1)S(1)}, u32[]{:S(2)}, u32[]{:S(2)}) %collective-permute-start.22) | collective-permute-done | bytes 262176 | tf_op jit(solution)/shard_map/ppermute | solution.py:365
  95.1 1.7 %shard_map.51 = (f32[12,64,256]{2,1,0:T(8,128)S(1)}, f32[12,64,256]{2,1,0:T(8,128)S(1)}) custom-call(bf16[8,64,256]{2,1,0:T(8,128)(2,1)S(1)} %collective-permute-done.22.rest_0_, bf16[3,64,256]{2,1,0:T(8,128)(2,1)S(1)} %collective-permute-done.23.rest_1_, ...), custom_call_target="tpu_custom_call", output_to_operand_aliasing={{0}: (5, {}), {1}: (6, {})} | custom-call | flops 20000000000 | tf_op jit(solution)/shard_map/pallas_call | solution.py:253
  96.8 1.1 collective-permute-done.21.low
  97.9 0.2 shard_map.52
  98.1 1.3 %collective-permute-start.25 = (f32[12,64,256]{2,1,0:T(8,128)S(1)}, f32[12,64,256]{2,1,0:T(8,128)S(1)}, u32[]{:S(2)}, u32[]{:S(2)}) collective-permute-start(f32[12,64,256]{2,1,0:T(8,128)S(1)} %get-tuple-element.135), channel_id=1, source_target_pairs={{0,16},{1,17},{2,18},{3,19},{4,20},{5,21},{6,22},{7,23},{8,24},{9,... | collective-permute-start | bytes 2359304 | tf_op jit(solution)/shard_map/ppermute | solution.py:375
  99.4 1.8 %collective-permute-done.25.core = f32[12,64,256]{2,1,0:T(8,128)S(1)} collective-permute-done((f32[12,64,256]{2,1,0:T(8,128)S(1)}, f32[12,64,256]{2,1,0:T(8,128)S(1)}, u32[]{:S(2)}, u32[]{:S(2)}) %collective-permute-start.25) | collective-permute-done | bytes 786464 | tf_op jit(solution)/shard_map/ppermute | solution.py:375
  101.3 0.2 shard_map.53
  101.4 0.1 collective-permute-start.28
  101.5 2.3 %collective-permute-start.29 = (bf16[368,256]{1,0:T(8,128)(2,1)S(1)}, bf16[368,256]{1,0:T(8,128)(2,1)S(1)}, u32[]{:S(2)}, u32[]{:S(2)}) collective-permute-start(bf16[368,256]{1,0:T(8,128)(2,1)S(1)} %get-tuple-element.140), channel_id=1, source_target_pairs={{0,2},{1,3},{2,0},{3,1},{4,6},{5,7},{6,4},{7,5},{8,10},{9,11},{10,... | collective-permute-start | bytes 565256 | tf_op jit(solution)/shard_map/ppermute | solution.py:386
  103.8 1.0 collective-permute-start.30
  104.8 9.0 %collective-permute-done.28.rest_1_ = bf16[368,256]{1,0:T(8,128)(2,1)S(1)} collective-permute-done((bf16[368,256]{1,0:T(8,128)(2,1)S(1)}, bf16[368,256]{1,0:T(8,128)(2,1)S(1)}, u32[]{:S(2)}, u32[]{:S(2)}) %collective-permute-start.28) | collective-permute-done | bytes 188448 | tf_op jit(solution)/shard_map/ppermute | solution.py:386
  113.8 0.6 collective-permute-done.30.rest_3_
  114.4 5.1 %shard_map.54 = (f32[2,32,16,256]{3,2,1,0:T(8,128)}, f32[32,16,256]{2,1,0:T(8,128)}) custom-call(bf16[368,256]{1,0:T(8,128)(2,1)S(1)} %get-tuple-element.138.rest_0_, bf16[368,256]{1,0:T(8,128)(2,1)S(1)} %collective-permute-done.28.rest_1_, bf16[368,256]{1,0:T(8,128)(2,1)S(1)} %collective-permute-done.29.rest_2_, ...), custom_call_target="tpu_custom_call" | custom-call | tf_op jit(solution)/shard_map/pallas_call | solution.py:253
  (32 shorter events, 0.2 us)
Async XLA Ops:
  0.6 24.1 %copy-start = (bf16[2,3,3,256,256]{4,3,2,1,0:T(8,128)(2,1)S(1)}, bf16[2,3,3,256,256]{4,3,2,1,0:T(8,128)(2,1)}, u32[]{:S(2)}) copy-start(bf16[2,3,3,256,256]{4,3,2,1,0:T(8,128)(2,1)} %param.3) | copy-start | bytes 7077892
  2.1 22.6 %collective-permute-start.2 = (bf16[3,768,256]{2,1,0:T(8,128)(2,1)S(1)}, bf16[3,768,256]{2,1,0:T(8,128)(2,1)S(1)}, u32[]{:S(2)}, u32[]{:S(2)}) collective-permute-start(bf16[3,768,256]{2,1,0:T(8,128)(2,1)S(1)} %bitcast.11), channel_id=1, source_target_pairs={{32,0},{33,1},{34,2},{35,3},{36,4},{37,5},{38,6},{39,7},{40,8},{41... | collective-permute-start | bytes 3538952 | tf_op jit(solution)/shard_map/ppermute | solution.py:293
  16.9 7.9 %collective-permute-start = (bf16[4,6,16,256]{3,2,1,0:T(8,128)(2,1)S(1)}, bf16[4,6,16,256]{3,2,1,0:T(8,128)(2,1)S(1)}, u32[]{:S(2)}, u32[]{:S(2)}) collective-permute-start(bf16[4,6,16,256]{3,2,1,0:T(8,128)(2,1)S(1)} %get-tuple-element.73), channel_id=1, source_target_pairs={{0,1},{1,2},{2,3},{3,4},{4,5},{5,6},{6,7},{7,8},{8,9},{9,10},{10,1... | collective-permute-start | bytes 589832 | tf_op jit(solution)/shard_map/ppermute | solution.py:296
  17.5 7.2 %collective-permute-start.1 = (bf16[4,6,16,256]{3,2,1,0:T(8,128)(2,1)S(1)}, bf16[4,6,16,256]{3,2,1,0:T(8,128)(2,1)S(1)}, u32[]{:S(2)}, u32[]{:S(2)}) collective-permute-start(bf16[4,6,16,256]{3,2,1,0:T(8,128)(2,1)S(1)} %get-tuple-element.74), channel_id=1, source_target_pairs={{0,15},{1,0},{2,1},{3,2},{4,3},{5,4},{6,5},{7,6},{8,7},{9,8},{10,9... | collective-permute-start | bytes 589832 | tf_op jit(solution)/shard_map/ppermute | solution.py:296
  21.1 11.5 %collective-permute-start.10 = (bf16[3,768,256]{2,1,0:T(8,128)(2,1)S(1)}, bf16[3,768,256]{2,1,0:T(8,128)(2,1)S(1)}, u32[]{:S(2)}, u32[]{:S(2)}) collective-permute-start(bf16[3,768,256]{2,1,0:T(8,128)(2,1)S(1)} %bitcast.12), channel_id=1, source_target_pairs={{48,64},{49,65},{50,66},{51,67},{52,68},{53,69},{54,70},{55,71},{5... | collective-permute-start | bytes 3538952 | tf_op jit(solution)/shard_map/ppermute | solution.py:293
  21.8 6.6 %collective-permute-start.3 = (bf16[3,768,256]{2,1,0:T(8,128)(2,1)S(1)}, bf16[3,768,256]{2,1,0:T(8,128)(2,1)S(1)}, u32[]{:S(2)}, u32[]{:S(2)}) collective-permute-start(bf16[3,768,256]{2,1,0:T(8,128)(2,1)S(1)} %bitcast.13), channel_id=1, source_target_pairs={{16,0},{17,1},{18,2},{19,3},{20,4},{21,5},{22,6},{23,7},{24,8},{25... | collective-permute-start | bytes 3538952 | tf_op jit(solution)/shard_map/ppermute | solution.py:293
  28.4 2.8 %collective-permute-start.4 = (f32[12,64,256]{2,1,0:T(8,128)S(1)}, f32[12,64,256]{2,1,0:T(8,128)S(1)}, u32[]{:S(2)}, u32[]{:S(2)}) collective-permute-start(f32[12,64,256]{2,1,0:T(8,128)S(1)} %get-tuple-element.86), channel_id=1, source_target_pairs={{16,0},{17,1},{18,2},{19,3},{20,4},{21,5},{22,6},{23,7},{24,8},{25... | collective-permute-start | bytes 2359304 | tf_op jit(solution)/shard_map/ppermute | solution.py:293
  29.1 2.1 %collective-permute-start.5 = (bf16[8,64,256]{2,1,0:T(8,128)(2,1)S(1)}, bf16[8,64,256]{2,1,0:T(8,128)(2,1)S(1)}, u32[]{:S(2)}, u32[]{:S(2)}) collective-permute-start(bf16[8,64,256]{2,1,0:T(8,128)(2,1)S(1)} %get-tuple-element.89), channel_id=1, source_target_pairs={{32,0},{33,1},{34,2},{35,3},{36,4},{37,5},{38,6},{39,7},{40,8},{41... | collective-permute-start | bytes 786440 | tf_op jit(solution)/shard_map/ppermute | solution.py:293
  29.8 4.2 %collective-permute-start.11 = (bf16[16,64,256]{2,1,0:T(8,128)(2,1)S(1)}, bf16[16,64,256]{2,1,0:T(8,128)(2,1)S(1)}, u32[]{:S(2)}, u32[]{:S(2)}) collective-permute-start(bf16[16,64,256]{2,1,0:T(8,128)(2,1)S(1)} %get-tuple-element.94), channel_id=1, source_target_pairs={{48,64},{49,65},{50,66},{51,67},{52,68},{53,69},{54,70},{55,71},{5... | collective-permute-start | bytes 1572872 | tf_op jit(solution)/shard_map/ppermute | solution.py:293
  30.5 2.8 %collective-permute-start.12 = (bf16[8,64,256]{2,1,0:T(8,128)(2,1)S(1)}, bf16[8,64,256]{2,1,0:T(8,128)(2,1)S(1)}, u32[]{:S(2)}, u32[]{:S(2)}) collective-permute-start(bf16[8,64,256]{2,1,0:T(8,128)(2,1)S(1)} %get-tuple-element.89), channel_id=1, source_target_pairs={{96,64},{97,65},{98,66},{99,67},{100,68},{101,69},{102,70},{103,71... | collective-permute-start | bytes 786440 | tf_op jit(solution)/shard_map/ppermute | solution.py:293
  31.3 2.8 %collective-permute-start.7 = (bf16[8,64,256]{2,1,0:T(8,128)(2,1)S(1)}, bf16[8,64,256]{2,1,0:T(8,128)(2,1)S(1)}, u32[]{:S(2)}, u32[]{:S(2)}) collective-permute-start(bf16[8,64,256]{2,1,0:T(8,128)(2,1)S(1)} %get-tuple-element.91), channel_id=1, source_target_pairs={{0,64},{1,65},{2,66},{3,67},{4,68},{5,69},{6,70},{7,71},{8,72},{9,... | collective-permute-start | bytes 786440 | tf_op jit(solution)/shard_map/ppermute | solution.py:365
  31.9 2.1 %collective-permute-start.8 = (bf16[5,64,256]{2,1,0:T(8,128)(2,1)S(1)}, bf16[5,64,256]{2,1,0:T(8,128)(2,1)S(1)}, u32[]{:S(2)}, u32[]{:S(2)}) collective-permute-start(bf16[5,64,256]{2,1,0:T(8,128)(2,1)S(1)} %get-tuple-element.92), channel_id=1, source_target_pairs={{0,65},{1,66},{2,67},{3,68},{4,69},{5,70},{6,71},{7,72},{8,73},{9,... | collective-permute-start | bytes 491528 | tf_op jit(solution)/shard_map/ppermute | solution.py:366
  32.6 1.4 %collective-permute-start.9 = (bf16[5,64,256]{2,1,0:T(8,128)(2,1)S(1)}, bf16[5,64,256]{2,1,0:T(8,128)(2,1)S(1)}, u32[]{:S(2)}, u32[]{:S(2)}) collective-permute-start(bf16[5,64,256]{2,1,0:T(8,128)(2,1)S(1)} %get-tuple-element.93), channel_id=1, source_target_pairs={{1,64},{2,65},{3,66},{4,67},{5,68},{6,69},{7,70},{8,71},{9,72},{10... | collective-permute-start | bytes 491528 | tf_op jit(solution)/shard_map/ppermute | solution.py:367
  33.3 3.0 %collective-permute-start.6 = (bf16[8,64,256]{2,1,0:T(8,128)(2,1)S(1)}, bf16[8,64,256]{2,1,0:T(8,128)(2,1)S(1)}, u32[]{:S(2)}, u32[]{:S(2)}) collective-permute-start(bf16[8,64,256]{2,1,0:T(8,128)(2,1)S(1)} %get-tuple-element.90), channel_id=1, source_target_pairs={{0,64},{1,65},{2,66},{3,67},{4,68},{5,69},{6,70},{7,71},{8,72},{9,... | collective-permute-start | bytes 786440 | tf_op jit(solution)/shard_map/ppermute | solution.py:368
  34.3 2.8 %collective-permute-start.15 = (bf16[5,64,256]{2,1,0:T(8,128)(2,1)S(1)}, bf16[5,64,256]{2,1,0:T(8,128)(2,1)S(1)}, u32[]{:S(2)}, u32[]{:S(2)}) collective-permute-start(bf16[5,64,256]{2,1,0:T(8,128)(2,1)S(1)} %get-tuple-element.104), channel_id=1, source_target_pairs={{64,129},{65,130},{66,131},{67,132},{68,133},{69,134},{70,135},{71... | collective-permute-start | bytes 491528 | tf_op jit(solution)/shard_map/ppermute | solution.py:366
  34.9 2.1 %collective-permute-start.16 = (bf16[5,64,256]{2,1,0:T(8,128)(2,1)S(1)}, bf16[5,64,256]{2,1,0:T(8,128)(2,1)S(1)}, u32[]{:S(2)}, u32[]{:S(2)}) collective-permute-start(bf16[5,64,256]{2,1,0:T(8,128)(2,1)S(1)} %get-tuple-element.105), channel_id=1, source_target_pairs={{65,128},{66,129},{67,130},{68,131},{69,132},{70,133},{71,134},{72... | collective-permute-start | bytes 491528 | tf_op jit(solution)/shard_map/ppermute | solution.py:367
  35.6 1.4 %collective-permute-start.14 = (bf16[8,64,256]{2,1,0:T(8,128)(2,1)S(1)}, bf16[8,64,256]{2,1,0:T(8,128)(2,1)S(1)}, u32[]{:S(2)}, u32[]{:S(2)}) collective-permute-start(bf16[8,64,256]{2,1,0:T(8,128)(2,1)S(1)} %get-tuple-element.103), channel_id=1, source_target_pairs={{64,128},{65,129},{66,130},{67,131},{68,132},{69,133},{70,134},{71... | collective-permute-start | bytes 786440 | tf_op jit(solution)/shard_map/ppermute | solution.py:365
  36.3 2.8 %collective-permute-start.13 = (bf16[8,64,256]{2,1,0:T(8,128)(2,1)S(1)}, bf16[8,64,256]{2,1,0:T(8,128)(2,1)S(1)}, u32[]{:S(2)}, u32[]{:S(2)}) collective-permute-start(bf16[8,64,256]{2,1,0:T(8,128)(2,1)S(1)} %get-tuple-element.102), channel_id=1, source_target_pairs={{64,128},{65,129},{66,130},{67,131},{68,132},{69,133},{70,134},{71... | collective-permute-start | bytes 786440 | tf_op jit(solution)/shard_map/ppermute | solution.py:368
  37.1 3.5 %collective-permute-start.19 = (bf16[4,64,256]{2,1,0:T(8,128)(2,1)S(1)}, bf16[4,64,256]{2,1,0:T(8,128)(2,1)S(1)}, u32[]{:S(2)}, u32[]{:S(2)}) collective-permute-start(bf16[4,64,256]{2,1,0:T(8,128)(2,1)S(1)} %get-tuple-element.117), channel_id=1, source_target_pairs={{128,193},{129,194},{130,195},{131,196},{132,197},{133,198},{134,1... | collective-permute-start | bytes 393224 | tf_op jit(solution)/shard_map/ppermute | solution.py:366
  37.8 2.8 %collective-permute-start.20 = (bf16[4,64,256]{2,1,0:T(8,128)(2,1)S(1)}, bf16[4,64,256]{2,1,0:T(8,128)(2,1)S(1)}, u32[]{:S(2)}, u32[]{:S(2)}) collective-permute-start(bf16[4,64,256]{2,1,0:T(8,128)(2,1)S(1)} %get-tuple-element.118), channel_id=1, source_target_pairs={{129,192},{130,193},{131,194},{132,195},{133,196},{134,197},{135,1... | collective-permute-start | bytes 393224 | tf_op jit(solution)/shard_map/ppermute | solution.py:367
  38.4 2.1 %collective-permute-start.18 = (bf16[8,64,256]{2,1,0:T(8,128)(2,1)S(1)}, bf16[8,64,256]{2,1,0:T(8,128)(2,1)S(1)}, u32[]{:S(2)}, u32[]{:S(2)}) collective-permute-start(bf16[8,64,256]{2,1,0:T(8,128)(2,1)S(1)} %get-tuple-element.116), channel_id=1, source_target_pairs={{128,192},{129,193},{130,194},{131,195},{132,196},{133,197},{134,1... | collective-permute-start | bytes 786440 | tf_op jit(solution)/shard_map/ppermute | solution.py:365
  39.2 5.6 %collective-permute-start.17 = (bf16[8,64,256]{2,1,0:T(8,128)(2,1)S(1)}, bf16[8,64,256]{2,1,0:T(8,128)(2,1)S(1)}, u32[]{:S(2)}, u32[]{:S(2)}) collective-permute-start(bf16[8,64,256]{2,1,0:T(8,128)(2,1)S(1)} %get-tuple-element.115), channel_id=1, source_target_pairs={{128,192},{129,193},{130,194},{131,195},{132,196},{133,197},{134,1... | collective-permute-start | bytes 786440 | tf_op jit(solution)/shard_map/ppermute | solution.py:368
  39.8 59.6 %collective-permute-start.26 = (f32[12,64,256]{2,1,0:T(8,128)S(1)}, f32[12,64,256]{2,1,0:T(8,128)S(1)}, u32[]{:S(2)}, u32[]{:S(2)}) collective-permute-start(f32[12,64,256]{2,1,0:T(8,128)S(1)} %get-tuple-element.136), channel_id=1, source_target_pairs={{0,32},{1,33},{2,34},{3,35},{4,36},{5,37},{6,38},{7,39},{8,40},{9,... | collective-permute-start | bytes 2359304 | tf_op jit(solution)/shard_map/ppermute | solution.py:375
  40.8 50.1 %collective-permute-start.23 = (bf16[3,64,256]{2,1,0:T(8,128)(2,1)S(1)}, bf16[3,64,256]{2,1,0:T(8,128)(2,1)S(1)}, u32[]{:S(2)}, u32[]{:S(2)}) collective-permute-start(bf16[3,64,256]{2,1,0:T(8,128)(2,1)S(1)} %get-tuple-element.128), channel_id=1, source_target_pairs={{192,225},{193,226},{194,227},{195,228},{196,229},{197,230},{198,2... | collective-permute-start | bytes 294920 | tf_op jit(solution)/shard_map/ppermute | solution.py:366
  42.1 49.5 %collective-permute-start.24 = (bf16[3,64,256]{2,1,0:T(8,128)(2,1)S(1)}, bf16[3,64,256]{2,1,0:T(8,128)(2,1)S(1)}, u32[]{:S(2)}, u32[]{:S(2)}) collective-permute-start(bf16[3,64,256]{2,1,0:T(8,128)(2,1)S(1)} %get-tuple-element.129), channel_id=1, source_target_pairs={{193,224},{194,225},{195,226},{196,227},{197,228},{198,229},{199,2... | collective-permute-start | bytes 294920 | tf_op jit(solution)/shard_map/ppermute | solution.py:367
  43.4 51.6 %collective-permute-start.22 = (bf16[8,64,256]{2,1,0:T(8,128)(2,1)S(1)}, bf16[8,64,256]{2,1,0:T(8,128)(2,1)S(1)}, u32[]{:S(2)}, u32[]{:S(2)}) collective-permute-start(bf16[8,64,256]{2,1,0:T(8,128)(2,1)S(1)} %get-tuple-element.127), channel_id=1, source_target_pairs={{192,224},{193,225},{194,226},{195,227},{196,228},{197,229},{198,2... | collective-permute-start | bytes 786440 | tf_op jit(solution)/shard_map/ppermute | solution.py:365
  44.8 53.1 %collective-permute-start.21 = (bf16[8,64,256]{2,1,0:T(8,128)(2,1)S(1)}, bf16[8,64,256]{2,1,0:T(8,128)(2,1)S(1)}, u32[]{:S(2)}, u32[]{:S(2)}) collective-permute-start(bf16[8,64,256]{2,1,0:T(8,128)(2,1)S(1)} %get-tuple-element.126), channel_id=1, source_target_pairs={{192,224},{193,225},{194,226},{195,227},{196,228},{197,229},{198,2... | collective-permute-start | bytes 786440 | tf_op jit(solution)/shard_map/ppermute | solution.py:368
  90.9 8.5 %collective-permute-start.27 = (f32[12,64,256]{2,1,0:T(8,128)S(1)}, f32[12,64,256]{2,1,0:T(8,128)S(1)}, u32[]{:S(2)}, u32[]{:S(2)}) collective-permute-start(f32[12,64,256]{2,1,0:T(8,128)S(1)} %get-tuple-element.137), channel_id=1, source_target_pairs={{64,48},{65,49},{66,50},{67,51},{68,52},{69,53},{70,54},{71,55},{7... | collective-permute-start | bytes 2359304 | tf_op jit(solution)/shard_map/ppermute | solution.py:375
  98.1 3.2 %collective-permute-start.25 = (f32[12,64,256]{2,1,0:T(8,128)S(1)}, f32[12,64,256]{2,1,0:T(8,128)S(1)}, u32[]{:S(2)}, u32[]{:S(2)}) collective-permute-start(f32[12,64,256]{2,1,0:T(8,128)S(1)} %get-tuple-element.135), channel_id=1, source_target_pairs={{0,16},{1,17},{2,18},{3,19},{4,20},{5,21},{6,22},{7,23},{8,24},{9,... | collective-permute-start | bytes 2359304 | tf_op jit(solution)/shard_map/ppermute | solution.py:375
  101.4 12.3 %collective-permute-start.28 = (bf16[368,256]{1,0:T(8,128)(2,1)S(1)}, bf16[368,256]{1,0:T(8,128)(2,1)S(1)}, u32[]{:S(2)}, u32[]{:S(2)}) collective-permute-start(bf16[368,256]{1,0:T(8,128)(2,1)S(1)} %get-tuple-element.139), channel_id=1, source_target_pairs={{0,1},{1,2},{2,3},{3,0},{4,5},{5,6},{6,7},{7,4},{8,9},{9,10},{10,1... | collective-permute-start | bytes 565256 | tf_op jit(solution)/shard_map/ppermute | solution.py:386
  101.5 12.2 %collective-permute-start.29 = (bf16[368,256]{1,0:T(8,128)(2,1)S(1)}, bf16[368,256]{1,0:T(8,128)(2,1)S(1)}, u32[]{:S(2)}, u32[]{:S(2)}) collective-permute-start(bf16[368,256]{1,0:T(8,128)(2,1)S(1)} %get-tuple-element.140), channel_id=1, source_target_pairs={{0,2},{1,3},{2,0},{3,1},{4,6},{5,7},{6,4},{7,5},{8,10},{9,11},{10,... | collective-permute-start | bytes 565256 | tf_op jit(solution)/shard_map/ppermute | solution.py:386
  103.8 10.6 %collective-permute-start.30 = (bf16[368,256]{1,0:T(8,128)(2,1)S(1)}, bf16[368,256]{1,0:T(8,128)(2,1)S(1)}, u32[]{:S(2)}, u32[]{:S(2)}) collective-permute-start(bf16[368,256]{1,0:T(8,128)(2,1)S(1)} %get-tuple-element.141), channel_id=1, source_target_pairs={{0,3},{1,0},{2,1},{3,2},{4,7},{5,4},{6,5},{7,6},{8,11},{9,8},{10,9... | collective-permute-start | bytes 565256 | tf_op jit(solution)/shard_map/ppermute | solution.py:386
